TPU v7x, 32 devices: a whole 2x2x4 slice. The times are simulated.
32 devices in a mesh: grp: 4 (over y, core), rep: 8 (over z, x).
Axes of the slice: x: 2, y: 2, z: 4, core: 2. Of those that a mesh axis runs over, the one named last changes fastest.
Arguments:
- tokens: bfloat16 [16, 1024, 960], P('rep', 'grp'), may hold values from -6 to 6
- w_query: bfloat16 [960, 960], P('grp'), may hold values from -0.1875 to 0.1875
- w_key: bfloat16 [960, 320], P('grp'), may hold values from -0.1875 to 0.1875
- w_value: bfloat16 [960, 320], P('grp'), may hold values from -0.1875 to 0.1875
- w_out: bfloat16 [960, 960], P('grp'), may hold values from -2.5 to 2.5
- w_gate: bfloat16 [960, 2560], P(None, 'grp'), may hold values from -0.1875 to 0.1875
- w_up: bfloat16 [960, 2560], P(None, 'grp'), may hold values from -0.1875 to 0.1875
- w_down: bfloat16 [2560, 960], P('grp'), may hold values from -0.125 to 0.125
- gain_attn: bfloat16 [960], P('grp'), may hold values from 0.25 to 1.75
- gain_mlp: bfloat16 [960], P('grp'), may hold values from 0.25 to 1.75
- span_order: int32 [16, 4], P('rep'), may hold values from 0 to 3, each once within a row
- piece_starts: int32 [16, 2], P('rep'), may hold values from 0 to 768, as said below
- cotangent: bfloat16 [16, 1024, 960], P('rep', 'grp'), may hold values from -6 to 6
Outputs:
- block_out: float32 [16, 1024, 960], P('rep', 'grp')
- grad_tokens: float32 [16, 1024, 960], P('rep', 'grp')
- grad_w_query: float32 [960, 960], P('grp')
- grad_w_key: float32 [960, 320], P('grp')
- grad_w_value: float32 [960, 320], P('grp')
- grad_w_out: float32 [960, 960], P('grp')
- grad_w_gate: float32 [960, 2560], P(None, 'grp')
- grad_w_up: float32 [960, 2560], P(None, 'grp')
- grad_w_down: float32 [2560, 960], P('grp')
- grad_gain_attn: float32 [960], P('grp')
- grad_gain_mlp: float32 [960], P('grp')
Inputs may be any that keep to these rules, and one draw needn't show every extreme that they name: `span_order`: each row names every one of the sequence's 4 spans once. `piece_starts`: each sequence holds 2 pieces of 256 places at these starts, inside the sequence, in increasing order, not intersecting; some sequence has a piece at its start and some sequence has a piece at its end.
All inputs are finite; a program needn't handle non-finite values.
Results may differ from a plain program's by a relative error of at most 0.019.
Values may be sent and summed in bfloat16 or wider, within the bound.
No kernel may reach another device: no remote copies, remote signals or barrier semaphores. Data moves between devices by JAX's collectives and lax.ppermute only.
A program may use at most 256 MiB of HBM per device.

v0:
```python
import jax
import jax.numpy as jnp
from jax import lax
from jax.sharding import PartitionSpec as P

HD = 64
PIECE = 256


NORM_EPS = 1e-05
ROPE_BASE = 10000.0
MASKED_SCORE = -1e30


def rotate(values, places, direction):
    half_dim = HD // 2
    shaped = values.reshape(values.shape[:-1] + (values.shape[-1] // HD, HD))
    frequency = ROPE_BASE ** (-2.0 * jnp.arange(half_dim, dtype=jnp.float32) / HD)
    angles = places.astype(jnp.float32)[..., None, None] * frequency
    cosine = jnp.cos(angles)
    sine_val = jnp.sin(angles)
    leading = shaped[..., :half_dim]
    second = shaped[..., half_dim:]
    turned = jnp.concatenate(
        [
            leading * cosine - direction * second * sine_val,
            second * cosine + direction * leading * sine_val,
        ],
        axis=-1,
    )
    return turned.reshape(values.shape)


def allowed_mask(query_pos, key_pos, starts):
    causal = key_pos[None, :] <= query_pos[:, None]
    query_in = (query_pos[:, None] >= starts[None, :]) & (
        query_pos[:, None] < starts[None, :] + PIECE
    )
    key_in = (key_pos[:, None] >= starts[None, :]) & (key_pos[:, None] < starts[None, :] + PIECE)
    inside = jnp.any(query_in[:, None, :] & key_in[None, :, :], axis=-1)
    return causal | inside


def norm_scale(hidden_in, gain_vec):
    inverse = lax.rsqrt(jnp.mean(hidden_in * hidden_in, axis=-1, keepdims=True) + NORM_EPS)
    return (hidden_in * inverse * gain_vec, inverse)


def norm_back(hidden_in, inverse, gain_vec, grad_norm):
    scaled = grad_norm * gain_vec
    grad_in = inverse * scaled - hidden_in * inverse * inverse * inverse * jnp.mean(
        scaled * hidden_in, axis=-1, keepdims=True
    )
    grad_gain = jnp.sum(grad_norm * hidden_in * inverse, axis=0)
    return (grad_in, grad_gain)


def score_block(queries, key_rows, query_pos, key_pos, starts):
    q_count = queries.shape[0]
    heads_kv = key_rows.shape[-1] // HD
    grouped = queries.reshape(q_count, heads_kv, -1, HD)
    key_heads = key_rows.reshape(-1, heads_kv, HD)
    scores = jnp.einsum(
        "qkgd,pkd->kgqp", grouped, key_heads, preferred_element_type=jnp.float32
    ) * HD ** (-0.5)
    masked = jnp.where(allowed_mask(query_pos, key_pos, starts)[None, None], scores, MASKED_SCORE)
    return (masked, grouped, key_heads)


def attend_forward(bundle):
    queries, key_rows, value_rows, query_pos, key_pos, starts = bundle
    q_count = queries.shape[0]
    masked, grouped, key_heads = score_block(queries, key_rows, query_pos, key_pos, starts)
    value_heads = value_rows.reshape(-1, key_heads.shape[1], HD)
    row_peak = jnp.max(masked, axis=-1, keepdims=True)
    exponent = jnp.exp(masked - row_peak)
    total_sum = jnp.sum(exponent, axis=-1, keepdims=True)
    probability = (exponent / total_sum).astype(jnp.bfloat16)
    mixed_out = jnp.einsum(
        "kgqp,pkd->qkgd", probability, value_heads, preferred_element_type=jnp.float32
    )
    log_total = row_peak + jnp.log(total_sum)
    return (mixed_out.reshape(q_count, -1).astype(jnp.bfloat16), log_total)


def attend_backward(bundle):
    queries, key_rows, value_rows, query_pos, key_pos, starts, log_total, grad_mixed = bundle
    q_count = queries.shape[0]
    masked, grouped, key_heads = score_block(queries, key_rows, query_pos, key_pos, starts)
    heads_kv = key_heads.shape[1]
    value_heads = value_rows.reshape(-1, heads_kv, HD)
    probability = jnp.exp(masked - log_total)
    prob_low = probability.astype(jnp.bfloat16)
    grad_heads = grad_mixed.reshape(q_count, heads_kv, -1, HD)
    grad_prob = jnp.einsum(
        "qkgd,pkd->kgqp", grad_heads, value_heads, preferred_element_type=jnp.float32
    )
    inner_sum = jnp.sum(probability * grad_prob, axis=-1, keepdims=True)
    grad_scores = (probability * (grad_prob - inner_sum)).astype(jnp.bfloat16)
    scale_val = HD ** (-0.5)
    grad_query = (
        jnp.einsum("kgqp,pkd->qkgd", grad_scores, key_heads, preferred_element_type=jnp.float32)
        * scale_val
    )
    grad_key = (
        jnp.einsum("kgqp,qkgd->pkd", grad_scores, grouped, preferred_element_type=jnp.float32)
        * scale_val
    )
    grad_value = jnp.einsum(
        "kgqp,qkgd->pkd", prob_low, grad_heads, preferred_element_type=jnp.float32
    )
    return (
        grad_query.reshape(q_count, -1),
        grad_key.reshape(grad_key.shape[0], -1),
        grad_value.reshape(grad_value.shape[0], -1),
    )


def left_dot(left_mat, right_mat):
    return lax.dot_general(
        left_mat, right_mat, (((0,), (0,)), ((), ())), preferred_element_type=jnp.float32
    )


def right_dot(left_mat, right_mat):
    return lax.dot_general(
        left_mat, right_mat, (((1,), (1,)), ((), ())), preferred_element_type=jnp.float32
    )


def body(
    tokens,
    w_query,
    w_key,
    w_value,
    w_out,
    w_gate,
    w_up,
    w_down,
    gain_attn,
    gain_mlp,
    span_order,
    piece_starts,
    cotangent,
):
    groups = lax.axis_size("grp")
    rank_grp = lax.axis_index("grp")
    seq_count, span_len, width = tokens.shape
    shards = (w_query, w_key, w_value, w_out, w_gate, w_up, w_down, gain_attn, gain_mlp)
    gathered = (
        lax.all_gather(shards[0], "grp", axis=0, tiled=True),
        lax.all_gather(shards[1], "grp", axis=0, tiled=True),
        lax.all_gather(shards[2], "grp", axis=0, tiled=True),
        lax.all_gather(shards[3], "grp", axis=0, tiled=True),
        lax.all_gather(shards[4], "grp", axis=1, tiled=True),
        lax.all_gather(shards[5], "grp", axis=1, tiled=True),
        lax.all_gather(shards[6], "grp", axis=0, tiled=True),
        lax.all_gather(shards[7], "grp", axis=0, tiled=True),
        lax.all_gather(shards[8], "grp", axis=0, tiled=True),
    )
    (
        full_query,
        full_key,
        full_value,
        full_out,
        full_gate,
        full_up,
        full_down,
        full_gain_one,
        full_gain_two,
    ) = gathered
    gain_one = full_gain_one.astype(jnp.float32)
    gain_two = full_gain_two.astype(jnp.float32)
    offsets = jnp.arange(span_len, dtype=jnp.int32)
    own_span = jnp.sum(
        jnp.where(jnp.arange(groups, dtype=jnp.int32)[None, :] == rank_grp, span_order, 0), axis=1
    )
    query_pos = own_span[:, None] * span_len + offsets[None, :]
    key_pos = (span_order[:, :, None] * span_len + offsets[None, None, :]).reshape(seq_count, -1)
    token_rows = tokens.reshape(-1, width).astype(jnp.float32)
    norm_one, inverse_one = norm_scale(token_rows, gain_one)
    norm_low = norm_one.astype(jnp.bfloat16)
    query_lin = jnp.dot(norm_low, full_query, preferred_element_type=jnp.float32)
    key_lin = jnp.dot(norm_low, full_key, preferred_element_type=jnp.float32)
    value_lin = jnp.dot(norm_low, full_value, preferred_element_type=jnp.float32)
    queries = rotate(query_lin.reshape(seq_count, span_len, -1), query_pos, 1.0).astype(
        jnp.bfloat16
    )
    key_local = rotate(key_lin.reshape(seq_count, span_len, -1), query_pos, 1.0).astype(
        jnp.bfloat16
    )
    value_local = value_lin.reshape(seq_count, span_len, -1).astype(jnp.bfloat16)
    key_all, value_all = (
        lax.all_gather(key_local, "grp", axis=1, tiled=True),
        lax.all_gather(value_local, "grp", axis=1, tiled=True),
    )
    attended, log_total = lax.map(
        attend_forward, (queries, key_all, value_all, query_pos, key_pos, piece_starts)
    )
    attended_rows = attended.reshape(-1, attended.shape[-1])
    middle = token_rows + jnp.dot(attended_rows, full_out, preferred_element_type=jnp.float32)
    norm_two, inverse_two = norm_scale(middle, gain_two)
    norm_two_low = norm_two.astype(jnp.bfloat16)
    gate_lin = jnp.dot(norm_two_low, full_gate, preferred_element_type=jnp.float32)
    up_lin = jnp.dot(norm_two_low, full_up, preferred_element_type=jnp.float32)
    gate_sig = jax.nn.sigmoid(gate_lin)
    swish = gate_lin * gate_sig
    hidden = (swish * up_lin).astype(jnp.bfloat16)
    block_out = middle + jnp.dot(hidden, full_down, preferred_element_type=jnp.float32)
    again = (
        lax.all_gather(shards[0], "grp", axis=0, tiled=True),
        lax.all_gather(shards[1], "grp", axis=0, tiled=True),
        lax.all_gather(shards[2], "grp", axis=0, tiled=True),
        lax.all_gather(shards[3], "grp", axis=0, tiled=True),
        lax.all_gather(shards[4], "grp", axis=1, tiled=True),
        lax.all_gather(shards[5], "grp", axis=1, tiled=True),
        lax.all_gather(shards[6], "grp", axis=0, tiled=True),
        lax.all_gather(shards[7], "grp", axis=0, tiled=True),
        lax.all_gather(shards[8], "grp", axis=0, tiled=True),
    )
    (
        back_query,
        back_key,
        back_value,
        back_out,
        back_gate,
        back_up,
        back_down,
        spare_one,
        spare_two,
    ) = again
    grad_rows = cotangent.reshape(-1, width)
    grad_down_w = left_dot(hidden, grad_rows)
    grad_hidden = right_dot(grad_rows, back_down)
    grad_gate = (grad_hidden * up_lin * gate_sig * (1.0 + gate_lin * (1.0 - gate_sig))).astype(
        jnp.bfloat16
    )
    grad_up = (grad_hidden * swish).astype(jnp.bfloat16)
    ff_part = back_gate.shape[1] // groups
    grad_gate_w = jnp.einsum(
        "td,tgf->gdf",
        norm_two_low,
        grad_gate.reshape(-1, groups, ff_part),
        preferred_element_type=jnp.float32,
    )
    grad_up_w = jnp.einsum(
        "td,tgf->gdf",
        norm_two_low,
        grad_up.reshape(-1, groups, ff_part),
        preferred_element_type=jnp.float32,
    )
    grad_norm_two = right_dot(grad_gate, back_gate) + right_dot(grad_up, back_up)
    grad_mid_norm, grad_gain_two = norm_back(middle, inverse_two, gain_two, grad_norm_two)
    grad_middle = grad_rows.astype(jnp.float32) + grad_mid_norm
    grad_branch = grad_middle.astype(jnp.bfloat16)
    grad_out_w = left_dot(attended_rows, grad_branch)
    grad_attended = (
        right_dot(grad_branch, back_out).astype(jnp.bfloat16).reshape(seq_count, span_len, -1)
    )
    grad_query_rot, grad_key_all, grad_value_all = lax.map(
        attend_backward,
        (queries, key_all, value_all, query_pos, key_pos, piece_starts, log_total, grad_attended),
    )
    grad_key_rot, grad_value_own = (
        lax.psum_scatter(
            grad_key_all.astype(jnp.bfloat16), "grp", scatter_dimension=1, tiled=True
        ).astype(jnp.float32),
        lax.psum_scatter(
            grad_value_all.astype(jnp.bfloat16), "grp", scatter_dimension=1, tiled=True
        ).astype(jnp.float32),
    )
    grad_q_low = (
        rotate(grad_query_rot, query_pos, -1.0)
        .astype(jnp.bfloat16)
        .reshape(-1, grad_query_rot.shape[-1])
    )
    grad_k_low = (
        rotate(grad_key_rot, query_pos, -1.0)
        .astype(jnp.bfloat16)
        .reshape(-1, grad_key_rot.shape[-1])
    )
    grad_v_low = grad_value_own.astype(jnp.bfloat16).reshape(-1, grad_value_own.shape[-1])
    grad_query_w = left_dot(norm_low, grad_q_low)
    grad_key_w = left_dot(norm_low, grad_k_low)
    grad_value_w = left_dot(norm_low, grad_v_low)
    grad_norm_one = (
        right_dot(grad_q_low, back_query)
        + right_dot(grad_k_low, back_key)
        + right_dot(grad_v_low, back_value)
    )
    grad_tok_norm, grad_gain_one = norm_back(token_rows, inverse_one, gain_one, grad_norm_one)
    grad_tokens = grad_middle + grad_tok_norm
    pieces = [
        grad_query_w.reshape(groups, -1),
        grad_key_w.reshape(groups, -1),
        grad_value_w.reshape(groups, -1),
        grad_out_w.reshape(groups, -1),
        grad_gate_w.reshape(groups, -1),
        grad_up_w.reshape(groups, -1),
        grad_down_w.reshape(groups, -1),
        grad_gain_one.reshape(groups, -1),
        grad_gain_two.reshape(groups, -1),
    ]
    packed = jnp.concatenate(pieces, axis=1)
    owned = lax.psum_scatter(
        packed.astype(jnp.bfloat16), "grp", scatter_dimension=0, tiled=True
    ).astype(jnp.float32)
    summed = lax.psum(owned, "rep")[0]
    results = []
    position = 0
    for shard_arr in shards:
        extent = shard_arr.size
        results.append(summed[position : position + extent].reshape(shard_arr.shape))
        position = position + extent
    return (
        block_out.reshape(tokens.shape),
        grad_tokens.reshape(tokens.shape),
        results[0],
        results[1],
        results[2],
        results[3],
        results[4],
        results[5],
        results[6],
        results[7],
        results[8],
    )


def solution(mesh):
    placed = (
        P("rep", "grp", None),
        P("grp", None),
        P("grp", None),
        P("grp", None),
        P("grp", None),
        P(None, "grp"),
        P(None, "grp"),
        P("grp", None),
        P("grp"),
        P("grp"),
        P("rep", None),
        P("rep", None),
        P("rep", "grp", None),
    )
    return jax.shard_map(
        body,
        mesh=mesh,
        in_specs=placed,
        out_specs=(
            P("rep", "grp", None),
            P("rep", "grp", None),
            P("grp", None),
            P("grp", None),
            P("grp", None),
            P("grp", None),
            P(None, "grp"),
            P(None, "grp"),
            P("grp", None),
            P("grp"),
            P("grp"),
        ),
        check_vma=False,
    )
```

profile of v0, /device:TPU:0, one launch (start us, length us, event | category | flops | bytes accessed | tf_op | source)
XLA Modules:
  0.0 1175.1 jit_solution(9615888078784373299)
XLA Ops:
  11.7 8.3 all-reduce.3
  20.0 11.6 all-gather.1
  35.7 8.0 all-gather
  52.7 2.2 copy.134
  57.5 3.1 copy.96
  62.4 16.3 %all-gather.10.cloned.1.call-done = bf16[2,1024,320]{1,2,0:T(8,128)(2,1)} async-done(((bf16[2,256,320]{1,2,0:T(8,128)(2,1)}), bf16[2,1024,320]{1,2,0:T(8,128)(2,1)}) %all-gather.10.cloned.1.call-update) | async-done | bytes 1310736 | tf_op jit(solution)/shard_map/all_gather | solution.py:195
  78.7 54.8 %while.26 = (s32[]{:T(128)}, bf16[2,256,960]{1,2,0:T(8,128)(2,1)}, f32[2,5,3,256,1]{3,2,1,4,0:T(4,128)S(1)}, bf16[2,1024,320]{1,2,0:T(8,128)(2,1)}, s32[2,1024]{...) while((s32[]{:T(128)}, bf16[2,256,960]{1,2,0:T(8,128)(2,1)}, ...), condition=%wide.region_6.7_spmd, body=%wide.region_2.6_spmd.sunk | while | flops 1055379200 | bytes 69435672 | solution.py:197
  81.2 7.1 fusion.119
  88.3 8.6 fusion.120
  97.0 7.8 fusion.121
  108.3 7.6 fusion.119
  116.0 8.7 fusion.120
  124.6 7.8 fusion.121
  134.8 3.8 multiply_reduce_fusion.4
  142.0 7.4 fusion.44
  149.4 32.6 %all-gather.18.cloned.1.call-done = bf16[960,2560]{1,0:T(8,128)(2,1)} async-done(((bf16[960,640]{1,0:T(8,128)(2,1)}), bf16[960,2560]{1,0:T(8,128)(2,1)}) %all-gather.18.cloned.1.call-update) | async-done | bytes 4915216 | tf_op jit(solution)/shard_map/all_gather | solution.py:155
  182.0 7.0 fusion.43
  189.0 33.1 %all-gather.22.cloned.1.call-done = bf16[2560,960]{0,1:T(8,128)(2,1)} async-done(((bf16[640,960]{0,1:T(8,128)(2,1)}), bf16[2560,960]{0,1:T(8,128)(2,1)}) %all-gather.22.cloned.1.call-update) | async-done | bytes 4915216 | tf_op jit(solution)/shard_map/all_gather | solution.py:157
  222.1 10.4 multiply_convert_fusion
  232.6 2.7 fusion.45
  235.6 6.0 multiply_reduce_fusion
  245.5 83.4 %while.27 = (s32[]{:T(128)}, f32[2,256,960]{1,2,0:T(8,128)}, bf16[2,1024,320]{1,2,0:T(8,128)(2,1)}, bf16[2,1024,320]{1,2,0:T(8,128)(2,1)}, bf16[2,1024,320]{1,2,...) while((s32[]{:T(128)}, f32[2,256,960]{1,2,0:T(8,128)}, ...), condition=%wide.region_12.13_spmd, body=%wide.region_9.12_spmd.sunk | while | flops 2554187520 | bytes 203198896 | solution.py:260
  249.1 7.8 fusion.132
  256.9 8.1 fusion.134
  265.0 9.4 fusion.135
  274.4 2.5 fusion.136
  276.9 5.9 fusion.137
  290.7 7.8 fusion.132
  298.5 8.1 fusion.134
  306.6 9.4 fusion.135
  316.0 2.5 fusion.136
  318.5 5.9 fusion.137
  333.4 2.4 convolution_convert_fusion.2
  335.8 3.4 reshape.767
  339.2 2.3 reshape.681
  343.2 7.0 convolution_convert_fusion
  350.4 3.7 convolution_convert_fusion.1
  354.1 3.9 reshape.769
  359.8 7.8 copy.108
  367.7 10.5 reshape.771
  378.2 6.6 reshape.689
  384.8 4.7 convert_bitcast_fusion.1
  389.5 5.9 copy.140
  395.4 3.1 convert_bitcast_fusion
  398.5 6.1 copy.141
  404.6 2.4 fusion.47
  410.0 2.0 fusion.46
  413.8 2.4 fusion.24
  421.3 4.8 multiply_reduce_fusion.1
  426.2 2.2 constant_dynamic-update-slice_fusion.9
  431.1 7.6 constant_dynamic-update-slice_fusion.6
  438.7 4.0 constant_dynamic-update-slice_fusion.5
  442.8 4.0 constant_dynamic-update-slice_fusion.4
  449.8 335.7 %all-reduce.9.cloned.1.call-done = bf16[4,2458080]{1,0:T(4,128)(2,1)} async-done(((bf16[4,2458080]{1,0:T(4,128)(2,1)}), bf16[4,2458080]{1,0:T(4,128)(2,1)}) %all-reduce.9.cloned.1.call-update) | async-done | bytes 19664656
  785.5 12.1 %dynamic-slice_convert_fusion = f32[1,2458080]{1,0:T(1,128)} fusion(bf16[4,2458080]{1,0:T(4,128)(2,1)} %all-reduce.9.cloned.1.call-done, u32[]{:T(128)} %bitcast.79), kind=kLoop, calls=%fused_computation.53 | loop fusion | flops 2458080 | bytes 14748484 | tf_op jit(solution)/shard_map/convert_element_type | solution.py:307
  797.6 6.6 convolution_add_fusion.1
  804.9 2.3 copy_bitcast_fusion
  807.2 301.0 %all-reduce.7.cloned.1.call-done = f32[1,2458080]{1,0:T(1,128)} async-done(((f32[1,2458080]{1,0:T(1,128)}), f32[1,2458080]{1,0:T(1,128)}) %all-reduce.7.cloned.1.call-update) | async-done | bytes 9832336 | tf_op jit(solution)/shard_map/psum | solution.py:308
  1108.1 2.7 slice_reduce_fusion.5
  1112.8 10.8 slice_reduce_fusion.3
  1124.9 30.6 %slice_reduce_fusion = (f32[614400]{0:T(1024)}, f32[614400]{0:T(1024)}, f32[614400]{0:T(1024)}) fusion(f32[1,2458080]{1,0:T(1,128)} %all-reduce.7.cloned.1.call-done), kind=kLoop, calls=%fused_computation.69 | loop fusion | bytes 14745600 | tf_op jit(solution)/shard_map/slice | solution.py:313
  1155.5 2.7 reshape.698
  1158.2 2.0 copy.113
  1161.5 3.6 reshape.697
  (300 shorter events, 84.2 us)
Async XLA Ops:
  7.2 25.5 %copy-start.7 = (bf16[2,256,960]{1,2,0:T(8,128)(2,1)S(1)}, bf16[2,256,960]{1,2,0:T(8,128)(2,1)}, u32[]{:S(2)}) copy-start(bf16[2,256,960]{1,2,0:T(8,128)(2,1)} %param.17) | copy-start | bytes 2949124
  7.2 25.8 %copy-start.47 = (s32[2,4]{1,0:T(2,128)S(1)}, s32[2,4]{1,0:T(2,128)}, u32[]{:S(2)}) copy-start(s32[2,4]{1,0:T(2,128)} %param.27) | copy-start | bytes 100
  7.2 50.3 %all-gather.14.cloned.1.call-start = ((), (), s32[]{:S(2)}) async-start(), calls=%async_computation.4 | async-start | bytes 2457600 | tf_op jit(solution)/shard_map/all_gather | solution.py:151
  7.9 54.5 %all-gather.12.cloned.1.call-start = ((), (), s32[]{:S(2)}) async-start(), calls=%async_computation.3 | async-start | bytes 1638400 | tf_op jit(solution)/shard_map/all_gather | solution.py:194
  20.0 40.6 %copy-start.39 = (f32[960]{0:T(1024)}, f32[960]{0:T(1024)S(1)}, u32[]{:S(2)}) copy-start(f32[960]{0:T(1024)S(1)} %convert_element_type.143) | copy-start | bytes 11524
  32.7 2.1 copy-start.19
  33.1 27.5 %copy-start.44 = (f32[2,256]{1,0:T(2,128)}, f32[2,256]{1,0:T(2,128)S(1)}, u32[]{:S(2)}) copy-start(f32[2,256]{1,0:T(2,128)S(1)} %get-tuple-element.304) | copy-start | bytes 6148
  34.1 27.8 %copy-start.26 = (f32[2,256,32]{1,2,0:T(8,128)}, f32[2,256,32]{1,2,0:T(8,128)S(1)}, u32[]{:S(2)}) copy-start(f32[2,256,32]{1,2,0:T(8,128)S(1)} %get-tuple-element.302) | copy-start | bytes 196612
  35.6 43.1 %all-gather.10.cloned.1.call-start = ((), (), s32[]{:S(2)}) async-start(), calls=%async_computation.2 | async-start | bytes 1638400 | tf_op jit(solution)/shard_map/all_gather | solution.py:195
  46.1 88.7 %all-gather.16.cloned.1.call-start = ((), (), s32[]{:S(2)}) async-start(), calls=%async_computation.5 | async-start | bytes 2457600 | tf_op jit(solution)/shard_map/all_gather | solution.py:154
  46.7 95.3 %all-gather.20.cloned.1.call-start = ((), (), s32[]{:S(2)}) async-start(), calls=%async_computation.7 | async-start | bytes 6144000 | tf_op jit(solution)/shard_map/all_gather | solution.py:156
  47.2 134.7 %all-gather.18.cloned.1.call-start = ((), (), s32[]{:S(2)}) async-start(), calls=%async_computation.6 | async-start | bytes 6144000 | tf_op jit(solution)/shard_map/all_gather | solution.py:155
  47.8 174.3 %all-gather.22.cloned.1.call-start = ((), (), s32[]{:S(2)}) async-start(), calls=%async_computation.8 | async-start | bytes 6144000 | tf_op jit(solution)/shard_map/all_gather | solution.py:157
  48.6 358.5 %reduce-scatter.3.cloned.1.call-start = ((), (), s32[]{:S(2)}) async-start(), calls=%async_computation.9 | async-start | bytes 1638400 | tf_op jit(solution)/shard_map/reduce_scatter | solution.py:265
  51.4 3.5 copy-start.32
  61.9 16.8 %copy-start.42 = (s32[2,2]{1,0:T(2,128)S(1)}, s32[2,2]{1,0:T(2,128)}, u32[]{:S(2)}) copy-start(s32[2,2]{1,0:T(2,128)} %param.28) | copy-start | bytes 52
  96.9 7.9 copy-start.34
  124.6 7.9 copy-start.34
  134.8 3.8 copy-start.33
  134.8 5.1 copy-start.41
  140.1 41.8 %copy-start.5 = (bf16[512,960]{0,1:T(8,128)(2,1)}, bf16[512,960]{0,1:T(8,128)(2,1)S(1)}, u32[]{:S(2)}) copy-start(bf16[512,960]{0,1:T(8,128)(2,1)S(1)} %multiply_convert_fusion.3) | copy-start | bytes 2949124
  149.4 72.7 %copy-start.18 = (bf16[2,120,8,256]{3,2,0,1:T(8,128)(2,1)S(1)}, bf16[2,120,8,256]{3,2,0,1:T(8,128)(2,1)}, u32[]{:S(2)}) copy-start(bf16[2,120,8,256]{3,2,0,1:T(8,128)(2,1)} %copy.132) | copy-start | bytes 2949124
  222.1 10.4 copy-start.16
  232.6 2.8 copy-start.51
  232.6 2.8 copy-start.49
  232.6 3.0 copy-start.11
  243.2 2.3 copy-start.2
  245.5 83.4 %copy-start.27 = (f32[2,256,32]{1,2,0:T(8,128)S(1)}, f32[2,256,32]{1,2,0:T(8,128)}, u32[]{:S(2)}) copy-start(f32[2,256,32]{1,2,0:T(8,128)} %copy-done.26) | copy-start | bytes 196612
  245.5 83.4 %copy-start.37 = (f32[2,256,32]{1,2,0:T(8,128)S(1)}, f32[2,256,32]{1,2,0:T(8,128)}, u32[]{:S(2)}) copy-start(f32[2,256,32]{1,2,0:T(8,128)} %get-tuple-element.300) | copy-start | bytes 196612
  276.9 5.9 copy-start
  282.8 1.9 copy-start.28
  282.8 2.3 copy-start.30
  285.2 1.6 copy-start.29
  285.2 2.0 copy-start.31
  318.5 5.9 copy-start
  324.4 1.9 copy-start.28
  324.4 2.3 copy-start.30
  326.8 2.0 copy-start.31
  330.7 2.7 copy-start.17
  332.9 79.1 %reduce-scatter.5.cloned.1.call-start = ((), (), s32[]{:S(2)}) async-start(), calls=%async_computation.10 | async-start | bytes 1638400 | tf_op jit(solution)/shard_map/reduce_scatter | solution.py:268
  341.5 1.6 copy-start.46
  343.2 7.1 copy-start.13
  350.3 435.2 %all-reduce.9.cloned.1.call-start = ((), (), s32[]{:S(2)}) async-start(), calls=%async_computation.12 | async-start | bytes 39329792
  378.2 6.6 copy-start.6
  389.5 6.0 copy-start.50
  398.5 6.1 copy-start.23
  398.5 6.1 copy-start.36
  408.1 2.0 copy-start.20
  408.6 5.1 copy-start.8
  408.6 5.1 copy-start.40
  408.6 5.1 copy-start.45
  416.2 3.2 copy-start.21
  416.2 5.1 copy-start.3
  416.2 5.1 copy-start.43
  421.3 7.2 copy-start.22
  421.3 17.4 %slice-start.2 = ((s8[4915200]{0:T(1024)(128)(4,1)}), s8[720896]{0:T(1024)(128)(4,1)S(1)}, s32[]{:S(2)}) async-start(s8[4915200]{0:T(1024)(128)(4,1)} %bitcast.318), calls=%async_computation.15 | async-start | bytes 1441792
  426.2 3.3 copy-start.15
  429.5 9.2 slice-start.3
  431.1 11.7 slice-start
  438.7 4.1 slice-start.1
  449.8 658.4 %all-reduce.7.cloned.1.call-start = ((), (), s32[]{:S(2)}) async-start(), calls=%async_computation.11 | async-start | bytes 19664896 | tf_op jit(solution)/shard_map/psum | solution.py:308
  797.6 6.7 copy-start.9
  797.6 6.7 copy-start.14
  1161.5 3.6 copy-start.4
  (13 other events, 17.4 us)
Sparse Core Ops, SparseCore 0:
  9.6 28.0 all-gather.13
  39.8 18.3 all-gather.11
  60.3 18.3 all-gather.9
  80.1 21.8 all-gather.15
  103.4 38.5 all-gather.19
  143.4 38.5 all-gather.17
  183.5 38.5 all-gather.21
  333.1 26.5 reduce-scatter.2
  362.3 26.5 reduce-scatter.4
  449.9 335.6 all-reduce.8
  797.7 310.3 all-reduce.6
where the time goes:
time: 1180 us
  waiting for transfers between devices  724 us (61%)
  local copies, waits for them, and re-layouts  182 us (15%)
  matrix products  164 us (14%)
  other arithmetic  60 us (5%)
  blocking collectives  28 us (2%)
  between operations  15.7 us (1%)
    unnamed x12, waiting for transfers between devices  339 us
    psum x1, waiting for transfers between devices, body(): summed = lax.psum(owned, 'rep')[0]  301 us
    unnamed x124, local copies, waits for them, and re-layouts  69.6 us
    slice x4, local copies, waits for them, and re-layouts, body(): results.append(summed[position:position + extent].reshape(shard_arr.shape))  45.4 us
    all_gather x1, waiting for transfers between devices, body(): lax.all_gather(shards[6], 'grp', axis=0, tiled=True)  33.1 us
    all_gather x1, waiting for transfers between devices, body(): lax.all_gather(shards[4], 'grp', axis=1, tiled=True)  32.6 us
    dot_general x4, matrix products, score_block(): jnp.einsum('qkgd,pkd->kgqp', grouped, key_heads, preferred_element_type=j...  31 us
    dot_general x7, matrix products, right_dot(): lax.dot_general(left_mat, right_mat, (((1,), (1,)), ((), ())), preferred_...  29.7 us
  transfers between devices with their start and end apart: 11, of which 6 were waited for; matrix products, arithmetic and copies ran while one was open for 16% of the time, Pallas kernels for 0%

commit v1 on v0

v1 whole, which is shorter than its diff:
```python
import jax
import jax.numpy as jnp
from jax import lax
from jax.sharding import PartitionSpec as P

HD = 64
PIECE = 256


NORM_EPS = 1e-05
ROPE_BASE = 10000.0
MASKED_SCORE = -1e30


def rotate(values, places, direction):
    half_dim = HD // 2
    shaped = values.reshape(values.shape[:-1] + (values.shape[-1] // HD, HD))
    frequency = ROPE_BASE ** (-2.0 * jnp.arange(half_dim, dtype=jnp.float32) / HD)
    angles = places.astype(jnp.float32)[..., None, None] * frequency
    cosine = jnp.cos(angles)
    sine_val = jnp.sin(angles)
    leading = shaped[..., :half_dim]
    second = shaped[..., half_dim:]
    turned = jnp.concatenate(
        [
            leading * cosine - direction * second * sine_val,
            second * cosine + direction * leading * sine_val,
        ],
        axis=-1,
    )
    return turned.reshape(values.shape)


def allowed_mask(query_pos, key_pos, starts):
    causal = key_pos[None, :] <= query_pos[:, None]
    query_in = (query_pos[:, None] >= starts[None, :]) & (
        query_pos[:, None] < starts[None, :] + PIECE
    )
    key_in = (key_pos[:, None] >= starts[None, :]) & (key_pos[:, None] < starts[None, :] + PIECE)
    inside = jnp.any(query_in[:, None, :] & key_in[None, :, :], axis=-1)
    return causal | inside


def norm_scale(hidden_in, gain_vec):
    inverse = lax.rsqrt(jnp.mean(hidden_in * hidden_in, axis=-1, keepdims=True) + NORM_EPS)
    return (hidden_in * inverse * gain_vec, inverse)


def norm_back(hidden_in, inverse, gain_vec, grad_norm):
    scaled = grad_norm * gain_vec
    grad_in = inverse * scaled - hidden_in * inverse * inverse * inverse * jnp.mean(
        scaled * hidden_in, axis=-1, keepdims=True
    )
    grad_gain = jnp.sum(grad_norm * hidden_in * inverse, axis=0)
    return (grad_in, grad_gain)


def score_block(queries, key_rows, query_pos, key_pos, starts):
    q_count = queries.shape[0]
    heads_kv = key_rows.shape[-1] // HD
    grouped = queries.reshape(q_count, heads_kv, -1, HD)
    key_heads = key_rows.reshape(-1, heads_kv, HD)
    scores = jnp.einsum(
        "qkgd,pkd->kgqp", grouped, key_heads, preferred_element_type=jnp.float32
    ) * HD ** (-0.5)
    masked = jnp.where(allowed_mask(query_pos, key_pos, starts)[None, None], scores, MASKED_SCORE)
    return (masked, grouped, key_heads)


def attend_forward(bundle):
    queries, key_rows, value_rows, query_pos, key_pos, starts = bundle
    q_count = queries.shape[0]
    masked, grouped, key_heads = score_block(queries, key_rows, query_pos, key_pos, starts)
    value_heads = value_rows.reshape(-1, key_heads.shape[1], HD)
    row_peak = jnp.max(masked, axis=-1, keepdims=True)
    exponent = jnp.exp(masked - row_peak)
    total_sum = jnp.sum(exponent, axis=-1, keepdims=True)
    probability = (exponent / total_sum).astype(jnp.bfloat16)
    mixed_out = jnp.einsum(
        "kgqp,pkd->qkgd", probability, value_heads, preferred_element_type=jnp.float32
    )
    log_total = row_peak + jnp.log(total_sum)
    return (mixed_out.reshape(q_count, -1).astype(jnp.bfloat16), log_total)


def attend_backward(bundle):
    queries, key_rows, value_rows, query_pos, key_pos, starts, log_total, grad_mixed = bundle
    q_count = queries.shape[0]
    masked, grouped, key_heads = score_block(queries, key_rows, query_pos, key_pos, starts)
    heads_kv = key_heads.shape[1]
    value_heads = value_rows.reshape(-1, heads_kv, HD)
    probability = jnp.exp(masked - log_total)
    prob_low = probability.astype(jnp.bfloat16)
    grad_heads = grad_mixed.reshape(q_count, heads_kv, -1, HD)
    grad_prob = jnp.einsum(
        "qkgd,pkd->kgqp", grad_heads, value_heads, preferred_element_type=jnp.float32
    )
    inner_sum = jnp.sum(probability * grad_prob, axis=-1, keepdims=True)
    grad_scores = (probability * (grad_prob - inner_sum)).astype(jnp.bfloat16)
    scale_val = HD ** (-0.5)
    grad_query = (
        jnp.einsum("kgqp,pkd->qkgd", grad_scores, key_heads, preferred_element_type=jnp.float32)
        * scale_val
    )
    grad_key = (
        jnp.einsum("kgqp,qkgd->pkd", grad_scores, grouped, preferred_element_type=jnp.float32)
        * scale_val
    )
    grad_value = jnp.einsum(
        "kgqp,qkgd->pkd", prob_low, grad_heads, preferred_element_type=jnp.float32
    )
    return (
        grad_query.reshape(q_count, -1),
        grad_key.reshape(grad_key.shape[0], -1),
        grad_value.reshape(grad_value.shape[0], -1),
    )


def left_dot(left_mat, right_mat):
    return lax.dot_general(
        left_mat, right_mat, (((0,), (0,)), ((), ())), preferred_element_type=jnp.float32
    )


def right_dot(left_mat, right_mat):
    return lax.dot_general(
        left_mat, right_mat, (((1,), (1,)), ((), ())), preferred_element_type=jnp.float32
    )


def swap(values, axis, count, mask):
    return lax.ppermute(values, axis, [(i, i ^ mask) for i in range(count)])


def group_blocks(own):
    across = swap(own, "grp", 4, 2)
    beside = swap(own, "grp", 4, 1)
    corner = swap(across, "grp", 4, 1)
    return own, beside, across, corner


def group_sum(parts):
    low = jnp.bfloat16
    beside = swap(jnp.stack([parts[1], parts[3]]).astype(low), "grp", 4, 1).astype(jnp.float32)
    across = swap((parts[2] + beside[1]).astype(low), "grp", 4, 2).astype(jnp.float32)
    return parts[0] + beside[0] + across


def absolute(blocks, rank):
    stacked = jnp.stack(blocks)
    return jnp.take(stacked, jnp.arange(len(blocks)) ^ rank, axis=0)


def rep_sum(chunks, ranks):
    low = jnp.bfloat16
    rank = lax.axis_index("rep")
    low_rank = rank & 7
    slots = jnp.take(chunks, jnp.arange(8) ^ low_rank, axis=0)
    one = swap(slots[jnp.array([1, 3, 5, 7])].astype(low), "rep", ranks, 1)
    slots = slots[jnp.array([0, 2, 4, 6])] + one.astype(jnp.float32)
    two = swap(slots[jnp.array([1, 3])].astype(low), "rep", ranks, 2)
    slots = slots[jnp.array([0, 2])] + two.astype(jnp.float32)
    three = swap(slots[1:2].astype(low), "rep", ranks, 4)
    mine = slots[0:1] + three.astype(jnp.float32)
    mine = mine.astype(low)
    if ranks > 8:
        others = [[j * 8 + i for j in range(ranks // 8)] for i in range(8)]
        mine = lax.psum(mine, "rep", axis_index_groups=others)
    held = jnp.stack([mine[0], swap(mine, "rep", ranks, 4)[0]])
    other = swap(held, "rep", ranks, 2)
    held = jnp.stack([held[0], other[0], held[1], other[1]])
    other = swap(held, "rep", ranks, 1)
    held = jnp.stack([held[0], other[0], held[1], other[1], held[2], other[2], held[3], other[3]])
    return jnp.take(held, jnp.arange(8) ^ low_rank, axis=0)


def body(
    tokens,
    w_query,
    w_key,
    w_value,
    w_out,
    w_gate,
    w_up,
    w_down,
    gain_attn,
    gain_mlp,
    span_order,
    piece_starts,
    cotangent,
):
    groups = lax.axis_size("grp")
    ranks = lax.axis_size("rep")
    rank_grp = lax.axis_index("grp")
    seq_count, span_len, width = tokens.shape
    low = jnp.bfloat16
    shard_rows = w_query.shape[0]
    gains = jnp.zeros((16, w_key.shape[1] + w_value.shape[1]), low)
    gains = gains.at[0, :shard_rows].set(gain_attn).at[1, :shard_rows].set(gain_mlp)
    kv_shard = jnp.concatenate([jnp.concatenate([w_key, w_value], axis=1), gains], axis=0)
    kv_full = absolute(group_blocks(kv_shard), rank_grp)
    full_kv = kv_full[:, :shard_rows].reshape(width, -1)
    gain_one = kv_full[:, shard_rows, :shard_rows].reshape(width).astype(jnp.float32)
    gain_two = kv_full[:, shard_rows + 1, :shard_rows].reshape(width).astype(jnp.float32)
    full_query = absolute(group_blocks(w_query), rank_grp).reshape(width, -1)
    full_out = absolute(group_blocks(w_out), rank_grp).reshape(-1, width)
    kw = w_key.shape[1]

    rel = jnp.arange(groups, dtype=jnp.int32) ^ rank_grp
    order = jnp.take(span_order, rel, axis=1)
    offsets = jnp.arange(span_len, dtype=jnp.int32)
    query_pos = order[:, 0, None] * span_len + offsets[None, :]
    key_pos = (order[:, :, None] * span_len + offsets[None, None, :]).reshape(seq_count, -1)
    token_rows = tokens.reshape(-1, width).astype(jnp.float32)
    norm_one, inverse_one = norm_scale(token_rows, gain_one)
    norm_low = norm_one.astype(low)
    kv_lin = jnp.dot(norm_low, full_kv, preferred_element_type=jnp.float32)
    query_lin = jnp.dot(norm_low, full_query, preferred_element_type=jnp.float32)
    queries = rotate(query_lin.reshape(seq_count, span_len, -1), query_pos, 1.0).astype(low)
    key_local = rotate(kv_lin[:, :kw].reshape(seq_count, span_len, -1), query_pos, 1.0).astype(low)
    value_local = kv_lin[:, kw:].reshape(seq_count, span_len, -1).astype(low)
    kv_local = jnp.concatenate([key_local, value_local], axis=-1)
    kv_all = [jnp.concatenate(group_blocks(kv_local[s]), axis=0) for s in range(seq_count)]
    cot_blocks = group_blocks(cotangent)

    middles, x_blocks, logs, attendeds, inverse_twos = [], [], [], [], []
    for s in range(seq_count):
        attended, log_total = attend_forward(
            (queries[s], kv_all[s][:, :kw], kv_all[s][:, kw:], query_pos[s], key_pos[s], piece_starts[s])
        )
        middle = tokens[s].astype(jnp.float32) + jnp.dot(
            attended, full_out, preferred_element_type=jnp.float32
        )
        norm_two, inverse_two = norm_scale(middle, gain_two)
        x_blocks.append(group_blocks(norm_two.astype(low)))
        middles.append(middle)
        logs.append(log_total)
        attendeds.append(attended)
        inverse_twos.append(inverse_two)

    outs, grad_norms, hid, gg, gu, xs, cs = [], [], [], [], [], [], []
    for s in range(seq_count):
        x = jnp.concatenate(x_blocks[s], axis=0)
        cot = jnp.concatenate([c[s] for c in cot_blocks], axis=0)
        gate_lin = jnp.dot(x, w_gate, preferred_element_type=jnp.float32)
        up_lin = jnp.dot(x, w_up, preferred_element_type=jnp.float32)
        gate_sig = jax.nn.sigmoid(gate_lin)
        swish = gate_lin * gate_sig
        hidden = (swish * up_lin).astype(low)
        out_part = jnp.dot(hidden, w_down, preferred_element_type=jnp.float32)
        grad_hidden = right_dot(cot, w_down)
        grad_gate = (grad_hidden * up_lin * gate_sig * (1.0 + gate_lin * (1.0 - gate_sig))).astype(low)
        grad_up = (grad_hidden * swish).astype(low)
        grad_x = right_dot(grad_gate, w_gate) + right_dot(grad_up, w_up)
        outs.append(middles[s] + group_sum(out_part.reshape(groups, span_len, -1)))
        grad_norms.append(group_sum(grad_x.reshape(groups, span_len, -1)))
        hid.append(hidden)
        gg.append(grad_gate)
        gu.append(grad_up)
        xs.append(x)
        cs.append(cot)
    x_all, cot_all = jnp.concatenate(xs), jnp.concatenate(cs)
    grad_gate_w = left_dot(x_all, jnp.concatenate(gg))
    grad_up_w = left_dot(x_all, jnp.concatenate(gu))
    grad_down_w = left_dot(jnp.concatenate(hid), cot_all)
    ff = grad_gate_w.shape[1]
    gate_up = rep_sum(jnp.concatenate([grad_gate_w, grad_up_w], axis=1).reshape(8, -1, 2 * ff), ranks)
    gate_up = gate_up.reshape(width, 2 * ff).astype(jnp.float32)
    down = rep_sum(grad_down_w.reshape(8, -1, width), ranks).reshape(ff, width).astype(jnp.float32)

    gq, gkv, grad_mids, gain_twos, branches = [], [], [], [], []
    for s in range(seq_count):
        grad_mid_norm, grad_gain_two = norm_back(middles[s], inverse_twos[s], gain_two, grad_norms[s])
        grad_middle = cotangent[s].astype(jnp.float32) + grad_mid_norm
        grad_branch = grad_middle.astype(low)
        grad_attended = right_dot(grad_branch, full_out).astype(low)
        grad_query_rot, grad_key_all, grad_value_all = attend_backward(
            (
                queries[s],
                kv_all[s][:, :kw],
                kv_all[s][:, kw:],
                query_pos[s],
                key_pos[s],
                piece_starts[s],
                logs[s],
                grad_attended,
            )
        )
        both = jnp.concatenate([grad_key_all, grad_value_all], axis=-1)
        own = group_sum(both.reshape(groups, span_len, -1))
        gq.append(rotate(grad_query_rot, query_pos[s], -1.0).astype(low))
        gkv.append(
            jnp.concatenate([rotate(own[:, :kw], query_pos[s], -1.0), own[:, kw:]], axis=1).astype(low)
        )
        grad_mids.append(grad_middle)
        gain_twos.append(grad_gain_two)
        branches.append(grad_branch)
    grad_q_low, grad_kv_low = jnp.concatenate(gq), jnp.concatenate(gkv)
    grad_out_w = left_dot(jnp.concatenate(attendeds), jnp.concatenate(branches))
    grad_query_w = left_dot(norm_low, grad_q_low)
    grad_kv_w = left_dot(norm_low, grad_kv_low)
    grad_norm_one = right_dot(grad_q_low, full_query) + right_dot(grad_kv_low, full_kv)
    grad_middle = jnp.concatenate(grad_mids)
    grad_tok_norm, grad_gain_one = norm_back(token_rows, inverse_one, gain_one, grad_norm_one)
    grad_tokens = grad_middle + grad_tok_norm
    grad_gain_two = gain_twos[0] + gain_twos[1]

    gain_rows = jnp.zeros((groups, 8, 2 * width + 2 * kw), jnp.float32)
    gain_rows = gain_rows.at[:, 0, :shard_rows].set(grad_gain_one.reshape(groups, -1))
    gain_rows = gain_rows.at[:, 1, :shard_rows].set(grad_gain_two.reshape(groups, -1))
    attn_w = jnp.concatenate([grad_query_w, grad_out_w, grad_kv_w], axis=1).reshape(groups, shard_rows, -1)
    attn_w = jnp.concatenate([attn_w, gain_rows], axis=1)
    attn_w = jnp.take(attn_w, rel, axis=0)
    own_w = group_sum([attn_w[k] for k in range(groups)])
    own_w = rep_sum(own_w.reshape(8, -1, own_w.shape[1]), ranks).reshape(own_w.shape)
    own_w = own_w.astype(jnp.float32)
    return (
        jnp.stack(outs),
        grad_tokens.reshape(tokens.shape),
        own_w[:shard_rows, :width],
        own_w[:shard_rows, 2 * width : 2 * width + kw],
        own_w[:shard_rows, 2 * width + kw :],
        own_w[:shard_rows, width : 2 * width],
        gate_up[:, :ff],
        gate_up[:, ff:],
        down,
        own_w[shard_rows, :shard_rows],
        own_w[shard_rows + 1, :shard_rows],
    )


def solution(mesh):
    placed = (
        P("rep", "grp", None),
        P("grp", None),
        P("grp", None),
        P("grp", None),
        P("grp", None),
        P(None, "grp"),
        P(None, "grp"),
        P("grp", None),
        P("grp"),
        P("grp"),
        P("rep", None),
        P("rep", None),
        P("rep", "grp", None),
    )
    return jax.shard_map(
        body,
        mesh=mesh,
        in_specs=placed,
        out_specs=(
            P("rep", "grp", None),
            P("rep", "grp", None),
            P("grp", None),
            P("grp", None),
            P("grp", None),
            P("grp", None),
            P(None, "grp"),
            P(None, "grp"),
            P("grp", None),
            P("grp"),
            P("grp"),
        ),
        check_vma=False,
    )
```

time: 1180 us -> 665 us (0.56)
  waiting for transfers between devices: 724 us -> 85.5 us
  other arithmetic: 60 us -> 174 us
  starting transfers between devices: 0.84 us -> 44.1 us
  blocking collectives: 28 us -> 0 us
  matrix products: 164 us -> 151 us
  local copies, waits for them, and re-layouts: 182 us -> 195 us
  between operations: 15.7 us -> 3.59 us
    unnamed x12 -> x0, waiting for transfers between devices: 339 us -> none
    psum x1 -> x0, waiting for transfers between devices: 301 us -> none  [body(): summed = lax.psum(owned, 'rep')[0]]
    ppermute x0 -> x56, waiting for transfers between devices: none -> 85.5 us  [swap(): return lax.ppermute(values, axis, [(i, i ^ mask) for i in range(count)])]
    all_gather x7 -> x0, waiting for transfers between devices: 83.9 us -> none  [the longest x1 33.1 us: body(): lax.all_gather(shards[6], 'grp', axis=0, tiled=True)]
    gather x0 -> x25, local copies, waits for them, and re-layouts: none -> 79.5 us  [the longest x3 13.6 us: rep_sum(): slots = jnp.take(chunks, jnp.arange(8) ^ low_rank, axis=0)]
    ppermute x0 -> x56, starting transfers between devices: none -> 44.1 us  [swap(): return lax.ppermute(values, axis, [(i, i ^ mask) for i in range(count)])]
    another operation x4 -> x27, other arithmetic: 0.45 us -> 37 us
    slice x4 -> x29, local copies, waits for them, and re-layouts: 45.4 us -> 16.8 us  [the longest x2 3.15 us: body(): kv_lin[:, :kw].reshape(seq_count, span_len, -1)]
  transfers between devices with their start and end apart: 11 -> 56, of which waited for: 6 -> 13; matrix products, arithmetic and copies ran while one was open for 16% -> 74% of each run, Pallas kernels for 0% -> 0%
where the time goes in v1:
time: 665 us; the launch traced here: 653 us
  local copies, waits for them, and re-layouts  195 us (29%)
  other arithmetic  174 us (26%)
  matrix products  151 us (23%)
  waiting for transfers between devices  85.5 us (13%)
  starting transfers between devices  44.1 us (7%)
    ppermute x56, waiting for transfers between devices, swap(): return lax.ppermute(values, axis, [(i, i ^ mask) for i in range(count)])  85.5 us
    unnamed x292, local copies, waits for them, and re-layouts  50.1 us
    ppermute x56, starting transfers between devices, swap(): return lax.ppermute(values, axis, [(i, i ^ mask) for i in range(count)])  44.1 us
    dot_general x10, matrix products, right_dot(): lax.dot_general(left_mat, right_mat, (((1,), (1,)), ((), ())), preferred_...  34.4 us
    dot_general x6, matrix products, left_dot(): lax.dot_general(left_mat, right_mat, (((0,), (0,)), ((), ())), preferred_...  19.4 us
    convert_element_type x2, other arithmetic, attend_backward(): grad_scores = (probability * (grad_prob - inner_sum)).astype(jnp.bfloat16)  18.1 us
    dot_general x2, matrix products, attend_backward(): jnp.einsum('qkgd,pkd->kgqp', grad_heads, value_heads, preferred_element_t...  18 us
    reduce_sum x2, other arithmetic, attend_forward(): total_sum = jnp.sum(exponent, axis=-1, keepdims=True)  15.1 us
  transfers between devices with their start and end apart: 56, of which 13 were waited for; matrix products, arithmetic and copies ran while one was open for 74% of the time, Pallas kernels for 0%

profile of v1, /device:TPU:0, one launch (start us, length us, event | category | flops | bytes accessed | tf_op | source)
XLA Modules:
  0.0 653.1 jit_solution(11710616537266952100)
XLA Ops:
  31.4 3.2 copy.263
  72.4 3.6 gather_fusion.21
  79.5 3.6 gather_fusion.22
  83.1 4.5 broadcast_select_fusion.2
  87.6 4.0 copy.216
  106.9 6.7 %fusion.162 = (f32[5,3,256]{2,1,0:T(4,128)S(1)}, f32[5,3,256,1024]{2,3,1,0:T(8,128)}) fusion(bf16[1024,5,64,1]{0,2,3,1:T(8,128)(2,1)S(1)} %bitcast.406, bf16[256,5,3,64]{0,3,2,1:T(8,128)(2,1)S(1)} %bitcast.412, pred[256,1024]{0,1:T(8,128)(4,1)S(1)} %copy-done.57), kind=kOutput, calls=%fused_computation.436 | convolution fusion | flops 515109120 | bytes 17153024 | tf_op jit(solution)/shard_map/qkgd,pkd->kgqp/dot_general | solution.py:63
  113.7 7.6 %fusion.6 = f32[5,3,256]{2,1,0:T(4,128)S(1)} fusion(f32[5,3,256,1024]{2,3,1,0:T(8,128)} %get-tuple-element.261, f32[5,3,256]{2,1,0:T(4,128)S(1)} %get-tuple-element.260), kind=kLoop, calls=%fused_computation.41 | loop fusion | flops 7860480 | bytes 15759360 | tf_op jit(solution)/shard_map/reduce_sum | solution.py:77
  121.3 7.1 %fusion.61 = bf16[5,64,3,256]{3,1,2,0:T(8,128)(2,1)S(1)} fusion(bf16[1024,5,64,1]{0,2,3,1:T(8,128)(2,1)S(1)} %bitcast.418, f32[5,3,256,1024]{2,3,1,0:T(8,128)} %get-tuple-element.261, f32[5,3,256]{2,1,0:T(4,128)S(1)} %fusion.6, f32[5,3,256]{2,1,0:T(4,128)S(1)} %get-tuple-element.260), kind=kOutput, calls=%fused_computation.158 | convolution fusion | flops 515358720 | bytes 16906240 | tf_op jit(solution)/shard_map/kgqp,pkd->qkgd/dot_general | solution.py:79
  134.7 7.2 %fusion.164 = (f32[5,3,256]{2,1,0:T(4,128)S(1)}, f32[5,3,256,1024]{2,3,1,0:T(8,128)}) fusion(bf16[1024,5,64,1]{0,2,3,1:T(8,128)(2,1)S(1)} %bitcast.408, bf16[256,5,3,64]{0,3,2,1:T(8,128)(2,1)S(1)} %bitcast.410, pred[256,1024]{0,1:T(8,128)(4,1)S(1)} %copy.218), kind=kOutput, calls=%fused_computation.438 | convolution fusion | flops 515109120 | bytes 17153024 | tf_op jit(solution)/shard_map/qkgd,pkd->kgqp/dot_general | solution.py:63
  141.9 7.5 %fusion.7 = f32[5,3,256]{2,1,0:T(4,128)S(1)} fusion(f32[5,3,256,1024]{2,3,1,0:T(8,128)} %get-tuple-element.267, f32[5,3,256]{2,1,0:T(4,128)S(1)} %get-tuple-element.266), kind=kLoop, calls=%fused_computation.42 | loop fusion | flops 7860480 | bytes 15759360 | tf_op jit(solution)/shard_map/reduce_sum | solution.py:77
  149.5 7.0 %fusion.60 = bf16[5,64,3,256]{3,1,2,0:T(8,128)(2,1)S(1)} fusion(bf16[1024,5,64,1]{0,2,3,1:T(8,128)(2,1)S(1)} %bitcast.420, f32[5,3,256,1024]{2,3,1,0:T(8,128)} %get-tuple-element.267, f32[5,3,256]{2,1,0:T(4,128)S(1)} %fusion.7, f32[5,3,256]{2,1,0:T(4,128)S(1)} %get-tuple-element.266), kind=kOutput, calls=%fused_computation.157 | convolution fusion | flops 515358720 | bytes 16906240 | tf_op jit(solution)/shard_map/kgqp,pkd->qkgd/dot_general | solution.py:79
  166.7 3.1 fusion.110
  169.9 3.2 fusion.111
  173.1 3.5 multiply_convert_fusion.2
  176.5 3.7 fusion.167
  183.6 3.6 fusion.163
  194.4 4.5 multiply_convert_fusion
  198.9 4.3 fusion.166
  203.2 4.4 fusion.28
  207.6 4.0 gather_fusion.15
  211.6 3.7 broadcast_select_fusion.4
  215.4 3.3 gather_fusion.17
  220.4 5.4 fusion.170
  225.9 3.2 fusion.20
  229.2 3.2 fusion.24
  235.0 5.6 gather_fusion.9
  240.6 5.2 broadcast_select_fusion.1
  246.9 3.5 gather_fusion.16
  250.8 6.1 fusion.165
  269.6 4.2 gather_fusion.11
  273.8 4.7 gather_fusion.10
  301.3 6.3 collective-permute-done.44
  310.1 3.1 convert_add_fusion
  313.3 3.4 gather_fusion.13
  316.6 3.5 gather_fusion.12
  323.6 3.4 multiply_reduce_fusion.3
  327.1 5.3 fusion.146
  337.5 7.3 %fusion.3 = (f32[5,3,256]{2,1,0:T(4,128)S(1)}, f32[5,1024,256,3]{2,1,3,0:T(8,128)}) fusion(f32[5,3,256,1024]{2,3,1,0:T(8,128)S(1)} %bitcast.384, f32[5,3,256]{2,1,0:T(4,128)S(1)} %log_add_fusion.1, bf16[1024,5,64,1]{0,2,3,1:T(8,128)(2,1)S(1)} %bitcast.419, bf16[256,5,3,64]{0,3,2,1:T(8,128)(2,1)S(1)} %bitcast.417), kind=kOutput, calls=%fused_computation.30 | convolution fusion | flops 515109120 | bytes 32634880 | tf_op jit(solution)/shard_map/qkgd,pkd->kgqp/dot_general | solution.py:95
  347.1 8.1 %fusion.10 = f32[5,64,1024,1]{2,1,3,0:T(8,128)S(1)} fusion(bf16[256,5,3,64]{0,3,2,1:T(8,128)(2,1)S(1)} %bitcast.414, f32[5,3,256,1024]{2,3,1,0:T(8,128)} %get-tuple-element.267, f32[5,3,256]{2,1,0:T(4,128)S(1)} %log_add_fusion), kind=kOutput, calls=%fused_computation.46 | convolution fusion | flops 511180800 | bytes 17546240 | tf_op jit(solution)/shard_map/kgqp,qkgd->pkd/dot_general | solution.py:109
  355.2 10.7 %fusion = (f32[5,3,256]{2,1,0:T(4,128)S(1)}, f32[5,1024,256,3]{2,1,3,0:T(8,128)}) fusion(f32[5,3,256,1024]{2,3,1,0:T(8,128)} %get-tuple-element.267, f32[5,3,256]{2,1,0:T(4,128)S(1)} %log_add_fusion, bf16[1024,5,64,1]{0,2,3,1:T(8,128)(2,1)S(1)} %bitcast.421, bf16[256,5,3,64]{0,3,2,1:T(8,128)(2,1)S(1)} %bitcast.415), kind=kOutput, calls=%fused_computation.25 | convolution fusion | flops 515109120 | bytes 32634880 | tf_op jit(solution)/shard_map/qkgd,pkd->kgqp/dot_general | solution.py:95
  365.9 10.1 %fusion.5 = bf16[5,3,256,1024]{2,3,1,0:T(8,128)(2,1)} fusion(f32[5,1024,256,3]{2,1,3,0:T(8,128)} %get-tuple-element.279, f32[5,3,256,1024]{2,3,1,0:T(8,128)S(1)} %bitcast.384, f32[5,3,256]{2,1,0:T(4,128)S(1)} %get-tuple-element.278, f32[5,3,256]{2,1,0:T(4,128)S(1)} %log_add_fusion.1), kind=kLoop, calls=%fused_computation.32 | loop fusion | flops 15728640 | bytes 39352320 | tf_op jit(solution)/shard_map/convert_element_type | solution.py:99
  376.0 5.8 fusion.58
  381.9 6.8 %convolution_multiply_fusion.1 = f32[5,64,3,256]{3,1,2,0:T(8,128)} fusion(bf16[1024,5,64,1]{0,2,3,1:T(8,128)(2,1)S(1)} %bitcast.407, bf16[5,3,256,1024]{2,3,1,0:T(8,128)(2,1)} %fusion.5), kind=kOutput, calls=%fused_computation.142 | convolution fusion | flops 503562240 | bytes 9502720 | tf_op jit(solution)/shard_map/kgqp,pkd->qkgd/dot_general | solution.py:102
  388.7 7.9 %fusion.2 = bf16[5,3,256,1024]{2,3,1,0:T(8,128)(2,1)S(1)} fusion(f32[5,1024,256,3]{2,1,3,0:T(8,128)S(1)} %copy-done.2, f32[5,3,256,1024]{2,3,1,0:T(8,128)} %get-tuple-element.267, f32[5,3,256]{2,1,0:T(4,128)S(1)} %get-tuple-element.276, f32[5,3,256]{2,1,0:T(4,128)S(1)} %log_add_fusion), kind=kLoop, calls=%fused_computation.27 | loop fusion | flops 15728640 | bytes 39352320 | tf_op jit(solution)/shard_map/convert_element_type | solution.py:99
  407.7 3.1 fusion.104
  431.3 6.0 collective-permute-done.35
  443.0 11.4 %concatenate.139 = f32[960,2560]{1,0:T(8,128)} concatenate(f32[960,960]{1,0:T(8,128)} %fusion.104, f32[960,960]{1,0:T(8,128)} %fusion.83, f32[960,640]{1,0:T(8,128)} %fusion.119), dimensions={1} | concatenate | bytes 19660800 | tf_op jit(solution)/shard_map/concatenate | solution.py:311
  454.5 8.6 %pad_maximum_fusion = f32[4,248,2560]{2,1,0:T(8,128)} fusion(f32[4,8,2560]{2,1,0:T(8,128)S(1)} %scatter.19, f32[4,240,2560]{2,1,0:T(8,128)} %bitcast.389), kind=kLoop, calls=%fused_computation.45 | loop fusion | flops 2539520 | bytes 20316160 | tf_op jit(solution)/shard_map/concatenate | solution.py:312
  463.1 9.0 %gather_fusion.2 = f32[4,248,2560]{2,1,0:T(8,128)} fusion(f32[4,248,2560]{2,1,0:T(8,128)} %pad_maximum_fusion, s32[1024]{0:T(1024)} %copy-done.99), kind=kCustom, calls=%fused_computation.4 | custom fusion | bytes 20316176 | tf_op jit(solution)/shard_map/jit(_take)/gather | solution.py:313
  472.1 11.1 %fusion.145 = (bf16[4,248,2560]{2,1,0:T(8,128)(2,1)}, f32[4,248,2560]{2,1,0:T(8,128)}) fusion(f32[4,248,2560]{2,1,0:T(8,128)} %gather_fusion.2, pred[4]{0:T(512)(128)(4,1)S(1)} %copy-done.98), kind=kLoop, calls=%fused_computation.421 | loop fusion | flops 5079040 | bytes 25395204 | tf_op jit(solution)/shard_map/convert.11
  506.4 3.2 copy.238
  509.5 9.7 %collective-permute-done.47 = bf16[1,120,1280]{2,1,0:T(8,128)(2,1)S(1)} collective-permute-done((bf16[1,120,1280]{2,1,0:T(8,128)(2,1)}, bf16[1,120,1280]{2,1,0:T(8,128)(2,1)S(1)}, u32[]{:S(2)}, u32[]{:S(2)}) %collective-permute-start.47) | collective-permute-done | bytes 307232 | tf_op jit(solution)/shard_map/ppermute | solution.py:132
  528.5 7.7 %collective-permute-done.48 = bf16[2,120,1280]{2,1,0:T(8,128)(2,1)S(1)} collective-permute-done((bf16[2,120,1280]{2,1,0:T(8,128)(2,1)S(1)}, bf16[2,120,1280]{2,1,0:T(8,128)(2,1)S(1)}, u32[]{:S(2)}, u32[]{:S(2)}) %collective-permute-start.48) | collective-permute-done | bytes 614432 | tf_op jit(solution)/shard_map/ppermute | solution.py:132
  539.7 15.2 %collective-permute-done.37 = bf16[248,2560]{1,0:T(8,128)(2,1)S(1)} collective-permute-done((bf16[248,2560]{1,0:T(8,128)(2,1)S(1)}, bf16[248,2560]{1,0:T(8,128)(2,1)S(1)}, u32[]{:S(2)}, u32[]{:S(2)}) %collective-permute-start.37) | collective-permute-done | bytes 1269792 | tf_op jit(solution)/shard_map/ppermute | solution.py:132
  554.9 3.7 fusion.36
  558.6 3.6 reshape.994
  562.2 3.9 gather_fusion.3
  566.2 3.6 broadcast_select_fusion.5
  578.6 10.8 %collective-permute-done.38 = bf16[4,31,2560]{2,0,1:T(4,128)(2,1)S(1)} collective-permute-done((bf16[4,31,2560]{2,0,1:T(4,128)(2,1)}, bf16[4,31,2560]{2,0,1:T(4,128)(2,1)S(1)}, u32[]{:S(2)}, u32[]{:S(2)}) %collective-permute-start.38) | collective-permute-done | bytes 634912 | tf_op jit(solution)/shard_map/ppermute | solution.py:132
  597.4 3.4 collective-permute-done.39
  603.7 8.9 %collective-permute-done.40 = bf16[1,31,2560]{2,1,0:T(8,128)(2,1)S(1)} collective-permute-done((bf16[1,31,2560]{2,1,0:T(8,128)(2,1)S(1)}, bf16[1,31,2560]{2,1,0:T(8,128)(2,1)S(1)}, u32[]{:S(2)}, u32[]{:S(2)}) %collective-permute-start.40) | collective-permute-done | bytes 158752 | tf_op jit(solution)/shard_map/ppermute | solution.py:132
  614.0 5.6 collective-permute-done.41
  620.5 3.8 gather_fusion.14
  631.2 6.8 %collective-permute-done.43 = bf16[4,31,2560]{2,0,1:T(4,128)(2,1)S(1)} collective-permute-done((bf16[4,31,2560]{2,0,1:T(4,128)(2,1)S(1)}, bf16[4,31,2560]{2,0,1:T(4,128)(2,1)S(1)}, u32[]{:S(2)}, u32[]{:S(2)}) %collective-permute-start.43) | collective-permute-done | bytes 634912 | tf_op jit(solution)/shard_map/ppermute | solution.py:132
  (597 shorter events, 283.9 us)
Async XLA Ops:
  0.6 172.4 %copy-start = (bf16[640,960]{0,1:T(8,128)(2,1)S(1)}, bf16[640,960]{0,1:T(8,128)(2,1)}, u32[]{:S(2)}) copy-start(bf16[640,960]{0,1:T(8,128)(2,1)} %param.42) | copy-start | bytes 3686404
  5.4 33.4 %collective-permute-start.1 = (bf16[256,640]{1,0:T(8,128)(2,1)}, bf16[256,640]{1,0:T(8,128)(2,1)}, u32[]{:S(2)}, u32[]{:S(2)}) collective-permute-start(bf16[256,640]{1,0:T(8,128)(2,1)} %pad_maximum_fusion.34), channel_id=1, source_target_pairs={{0,16},{8,24},{16,0},{24,8},{1,17},{9,25},{17,1},{25,9},{2,18},{10... | collective-permute-start | bytes 983048 | tf_op jit(solution)/shard_map/ppermute | solution.py:132
  8.4 32.2 %collective-permute-start = (bf16[256,640]{1,0:T(8,128)(2,1)}, bf16[256,640]{1,0:T(8,128)(2,1)}, u32[]{:S(2)}, u32[]{:S(2)}) collective-permute-start(bf16[256,640]{1,0:T(8,128)(2,1)} %pad_maximum_fusion.34), channel_id=1, source_target_pairs={{0,8},{8,0},{16,24},{24,16},{1,9},{9,1},{17,25},{25,17},{2,10},{10... | collective-permute-start | bytes 983048 | tf_op jit(solution)/shard_map/ppermute | solution.py:132
  8.4 32.7 %collective-permute-start.7 = (bf16[240,960]{1,0:T(8,128)(2,1)}, bf16[240,960]{1,0:T(8,128)(2,1)}, u32[]{:S(2)}, u32[]{:S(2)}) collective-permute-start(bf16[240,960]{1,0:T(8,128)(2,1)} %param.36), channel_id=1, source_target_pairs={{0,16},{8,24},{16,0},{24,8},{1,17},{9,25},{17,1},{25,9},{2,18},{10... | collective-permute-start | bytes 1382408 | tf_op jit(solution)/shard_map/ppermute | solution.py:132
  8.4 59.2 %collective-permute-start.6 = (bf16[240,960]{1,0:T(8,128)(2,1)}, bf16[240,960]{1,0:T(8,128)(2,1)}, u32[]{:S(2)}, u32[]{:S(2)}) collective-permute-start(bf16[240,960]{1,0:T(8,128)(2,1)} %param.36), channel_id=1, source_target_pairs={{0,8},{8,0},{16,24},{24,16},{1,9},{9,1},{17,25},{25,17},{2,10},{10... | collective-permute-start | bytes 1382408 | tf_op jit(solution)/shard_map/ppermute | solution.py:132
  8.9 32.4 %collective-permute-start.10 = (bf16[240,960]{1,0:T(8,128)(2,1)}, bf16[240,960]{1,0:T(8,128)(2,1)}, u32[]{:S(2)}, u32[]{:S(2)}) collective-permute-start(bf16[240,960]{1,0:T(8,128)(2,1)} %param.39), channel_id=1, source_target_pairs={{0,16},{8,24},{16,0},{24,8},{1,17},{9,25},{17,1},{25,9},{2,18},{10... | collective-permute-start | bytes 1382408 | tf_op jit(solution)/shard_map/ppermute | solution.py:132
  11.5 71.6 %copy-start.97 = (pred[4]{0:T(512)(128)(4,1)}, pred[4]{0:T(512)(128)(4,1)S(1)}, u32[]{:S(2)}) copy-start(pred[4]{0:T(512)(128)(4,1)S(1)} %compare_and_fusion.5) | copy-start | bytes 16
  14.8 29.4 %copy-start.99 = (s32[1024]{0:T(1024)}, s32[1024]{0:T(1024)S(1)}, u32[]{:S(2)}) copy-start(s32[1024]{0:T(1024)S(1)} %pad_clamp_fusion.6) | copy-start | bytes 12292
  38.8 2.5 collective-permute-start.2
  40.5 35.5 %collective-permute-start.9 = (bf16[240,960]{1,0:T(8,128)(2,1)}, bf16[240,960]{1,0:T(8,128)(2,1)}, u32[]{:S(2)}, u32[]{:S(2)}) collective-permute-start(bf16[240,960]{1,0:T(8,128)(2,1)} %param.39), channel_id=1, source_target_pairs={{0,8},{8,0},{16,24},{24,16},{1,9},{9,1},{17,25},{25,17},{2,10},{10... | collective-permute-start | bytes 1382408 | tf_op jit(solution)/shard_map/ppermute | solution.py:132
  41.0 53.9 %collective-permute-start.26 = (bf16[2,256,960]{1,2,0:T(8,128)(2,1)S(1)}, bf16[2,256,960]{1,2,0:T(8,128)(2,1)}, u32[]{:S(2)}, u32[]{:S(2)}) collective-permute-start(bf16[2,256,960]{1,2,0:T(8,128)(2,1)S(1)} %copy-done.15), channel_id=1, source_target_pairs={{0,16},{8,24},{16,0},{24,8},{1,17},{9,25},{17,1},{25,9},{2,18},{10... | collective-permute-start | bytes 2949128 | tf_op jit(solution)/shard_map/ppermute | solution.py:132
  41.3 26.3 %collective-permute-start.8 = (bf16[240,960]{1,0:T(8,128)(2,1)}, bf16[240,960]{1,0:T(8,128)(2,1)}, u32[]{:S(2)}, u32[]{:S(2)}) collective-permute-start(bf16[240,960]{1,0:T(8,128)(2,1)} %collective-permute-done.7), channel_id=1, source_target_pairs={{0,8},{8,0},{16,24},{24,16},{1,9},{9,1},{17,25},{25,17},{2,10},{10... | collective-permute-start | bytes 1382408 | tf_op jit(solution)/shard_map/ppermute | solution.py:132
  41.3 34.9 %collective-permute-start.11 = (bf16[240,960]{1,0:T(8,128)(2,1)}, bf16[240,960]{1,0:T(8,128)(2,1)}, u32[]{:S(2)}, u32[]{:S(2)}) collective-permute-start(bf16[240,960]{1,0:T(8,128)(2,1)} %collective-permute-done.10), channel_id=1, source_target_pairs={{0,8},{8,0},{16,24},{24,16},{1,9},{9,1},{17,25},{25,17},{2,10},{10... | collective-permute-start | bytes 1382408 | tf_op jit(solution)/shard_map/ppermute | solution.py:132
  50.0 41.6 %copy-start.73 = (f32[960]{0:T(1024)}, f32[960]{0:T(1024)S(1)}, u32[]{:S(2)}) copy-start(f32[960]{0:T(1024)S(1)} %reshape.998) | copy-start | bytes 11524
  67.6 30.6 %collective-permute-start.25 = (bf16[2,256,960]{1,2,0:T(8,128)(2,1)S(1)}, bf16[2,256,960]{1,2,0:T(8,128)(2,1)}, u32[]{:S(2)}, u32[]{:S(2)}) collective-permute-start(bf16[2,256,960]{1,2,0:T(8,128)(2,1)S(1)} %copy-done.15), channel_id=1, source_target_pairs={{0,8},{8,0},{16,24},{24,16},{1,9},{9,1},{17,25},{25,17},{2,10},{10... | collective-permute-start | bytes 2949128 | tf_op jit(solution)/shard_map/ppermute | solution.py:132
  67.7 30.0 %collective-permute-start.4 = (bf16[256,640]{0,1:T(8,128)(2,1)}, bf16[256,640]{0,1:T(8,128)(2,1)}, u32[]{:S(2)}, u32[]{:S(2)}) collective-permute-start(bf16[256,640]{0,1:T(8,128)(2,1)} %get-tuple-element.219), channel_id=1, source_target_pairs={{0,16},{8,24},{16,0},{24,8},{1,17},{9,25},{17,1},{25,9},{2,18},{10... | collective-permute-start | bytes 983048 | tf_op jit(solution)/shard_map/ppermute | solution.py:132
  76.1 28.6 %collective-permute-start.3 = (bf16[256,640]{0,1:T(8,128)(2,1)}, bf16[256,640]{0,1:T(8,128)(2,1)}, u32[]{:S(2)}, u32[]{:S(2)}) collective-permute-start(bf16[256,640]{0,1:T(8,128)(2,1)} %get-tuple-element.219), channel_id=1, source_target_pairs={{0,8},{8,0},{16,24},{24,16},{1,9},{9,1},{17,25},{25,17},{2,10},{10... | collective-permute-start | bytes 983048 | tf_op jit(solution)/shard_map/ppermute | solution.py:132
  76.2 21.9 %collective-permute-start.18 = (bf16[256,640]{0,1:T(8,128)(2,1)}, bf16[256,640]{0,1:T(8,128)(2,1)}, u32[]{:S(2)}, u32[]{:S(2)}) collective-permute-start(bf16[256,640]{0,1:T(8,128)(2,1)} %get-tuple-element.220), channel_id=1, source_target_pairs={{0,16},{8,24},{16,0},{24,8},{1,17},{9,25},{17,1},{25,9},{2,18},{10... | collective-permute-start | bytes 983048 | tf_op jit(solution)/shard_map/ppermute | solution.py:132
  95.0 39.7 %copy-start.31 = (bf16[1,256,15,64]{1,3,2,0:T(8,128)(2,1)}, bf16[1,256,15,64]{1,3,2,0:T(8,128)(2,1)S(1)}, u32[]{:S(2)}) copy-start(bf16[1,256,15,64]{1,3,2,0:T(8,128)(2,1)S(1)} %get-tuple-element.216) | copy-start | bytes 1474564
  95.5 37.7 %collective-permute-start.17 = (bf16[256,640]{0,1:T(8,128)(2,1)S(1)}, bf16[256,640]{0,1:T(8,128)(2,1)}, u32[]{:S(2)}, u32[]{:S(2)}) collective-permute-start(bf16[256,640]{0,1:T(8,128)(2,1)S(1)} %copy-done.64), channel_id=1, source_target_pairs={{0,8},{8,0},{16,24},{24,16},{1,9},{9,1},{17,25},{25,17},{2,10},{10... | collective-permute-start | bytes 983048 | tf_op jit(solution)/shard_map/ppermute | solution.py:132
  97.7 64.3 %collective-permute-start.27 = (bf16[2,256,960]{1,2,0:T(8,128)(2,1)}, bf16[2,256,960]{1,2,0:T(8,128)(2,1)S(1)}, u32[]{:S(2)}, u32[]{:S(2)}) collective-permute-start(bf16[2,256,960]{1,2,0:T(8,128)(2,1)} %collective-permute-done.26), channel_id=1, source_target_pairs={{0,8},{8,0},{16,24},{24,16},{1,9},{9,1},{17,25},{25,17},{2,10},{10... | collective-permute-start | bytes 2949128 | tf_op jit(solution)/shard_map/ppermute | solution.py:132
  98.2 6.5 collective-permute-start.5
  98.2 35.0 %collective-permute-start.19 = (bf16[256,640]{0,1:T(8,128)(2,1)}, bf16[256,640]{0,1:T(8,128)(2,1)}, u32[]{:S(2)}, u32[]{:S(2)}) collective-permute-start(bf16[256,640]{0,1:T(8,128)(2,1)} %collective-permute-done.18), channel_id=1, source_target_pairs={{0,8},{8,0},{16,24},{24,16},{1,9},{9,1},{17,25},{25,17},{2,10},{10... | collective-permute-start | bytes 983048 | tf_op jit(solution)/shard_map/ppermute | solution.py:132
  131.4 26.4 %collective-permute-start.12 = (bf16[256,960]{0,1:T(8,128)(2,1)S(1)}, bf16[256,960]{0,1:T(8,128)(2,1)}, u32[]{:S(2)}, u32[]{:S(2)}) collective-permute-start(bf16[256,960]{0,1:T(8,128)(2,1)S(1)} %get-tuple-element.152), channel_id=1, source_target_pairs={{0,8},{8,0},{16,24},{24,16},{1,9},{9,1},{17,25},{25,17},{2,10},{10... | collective-permute-start | bytes 1474568 | tf_op jit(solution)/shard_map/ppermute | solution.py:132
  131.5 26.1 %collective-permute-start.13 = (bf16[256,960]{0,1:T(8,128)(2,1)S(1)}, bf16[256,960]{0,1:T(8,128)(2,1)}, u32[]{:S(2)}, u32[]{:S(2)}) collective-permute-start(bf16[256,960]{0,1:T(8,128)(2,1)S(1)} %get-tuple-element.152), channel_id=1, source_target_pairs={{0,16},{8,24},{16,0},{24,8},{1,17},{9,25},{17,1},{25,9},{2,18},{10... | collective-permute-start | bytes 1474568 | tf_op jit(solution)/shard_map/ppermute | solution.py:132
  157.5 7.0 %collective-permute-start.14 = (bf16[256,960]{0,1:T(8,128)(2,1)}, bf16[256,960]{0,1:T(8,128)(2,1)S(1)}, u32[]{:S(2)}, u32[]{:S(2)}) collective-permute-start(bf16[256,960]{0,1:T(8,128)(2,1)} %collective-permute-done.13), channel_id=1, source_target_pairs={{0,8},{8,0},{16,24},{24,16},{1,9},{9,1},{17,25},{25,17},{2,10},{10... | collective-permute-start | bytes 1474568 | tf_op jit(solution)/shard_map/ppermute | solution.py:132
  166.4 20.8 %collective-permute-start.21 = (bf16[256,960]{0,1:T(8,128)(2,1)S(1)}, bf16[256,960]{0,1:T(8,128)(2,1)S(1)}, u32[]{:S(2)}, u32[]{:S(2)}) collective-permute-start(bf16[256,960]{0,1:T(8,128)(2,1)S(1)} %get-tuple-element.150), channel_id=1, source_target_pairs={{0,16},{8,24},{16,0},{24,8},{1,17},{9,25},{17,1},{25,9},{2,18},{10... | collective-permute-start | bytes 1474568 | tf_op jit(solution)/shard_map/ppermute | solution.py:132
  166.7 22.1 %collective-permute-start.20 = (bf16[256,960]{0,1:T(8,128)(2,1)S(1)}, bf16[256,960]{0,1:T(8,128)(2,1)S(1)}, u32[]{:S(2)}, u32[]{:S(2)}) collective-permute-start(bf16[256,960]{0,1:T(8,128)(2,1)S(1)} %get-tuple-element.150), channel_id=1, source_target_pairs={{0,8},{8,0},{16,24},{24,16},{1,9},{9,1},{17,25},{25,17},{2,10},{10... | collective-permute-start | bytes 1474568 | tf_op jit(solution)/shard_map/ppermute | solution.py:132
  181.4 77.2 %collective-permute-start.15 = (bf16[2,256,960]{1,2,0:T(8,128)(2,1)}, bf16[2,256,960]{1,2,0:T(8,128)(2,1)}, u32[]{:S(2)}, u32[]{:S(2)}) collective-permute-start(bf16[2,256,960]{1,2,0:T(8,128)(2,1)} %pad_maximum_fusion.14), channel_id=1, source_target_pairs={{0,8},{8,0},{16,24},{24,16},{1,9},{9,1},{17,25},{25,17},{2,10},{10... | collective-permute-start | bytes 2949128 | tf_op jit(solution)/shard_map/ppermute | solution.py:132
  187.2 3.4 collective-permute-start.22
  188.3 90.7 %collective-permute-start.28 = (bf16[2,256,960]{1,2,0:T(8,128)(2,1)}, bf16[2,256,960]{1,2,0:T(8,128)(2,1)S(1)}, u32[]{:S(2)}, u32[]{:S(2)}) collective-permute-start(bf16[2,256,960]{1,2,0:T(8,128)(2,1)} %pad_maximum_fusion.16), channel_id=1, source_target_pairs={{0,8},{8,0},{16,24},{24,16},{1,9},{9,1},{17,25},{25,17},{2,10},{10... | collective-permute-start | bytes 2949128 | tf_op jit(solution)/shard_map/ppermute | solution.py:132
  218.7 42.5 %collective-permute-start.50 = (bf16[4,80,960]{2,1,0:T(8,128)(2,1)}, bf16[4,80,960]{2,1,0:T(8,128)(2,1)}, u32[]{:S(2)}, u32[]{:S(2)}) collective-permute-start(bf16[4,80,960]{2,1,0:T(8,128)(2,1)} %gather_fusion.17), channel_id=1, source_target_pairs={{0,1},{1,0},{2,3},{3,2},{4,5},{5,4},{6,7},{7,6},{8,9},{9,8},{10,11... | collective-permute-start | bytes 1843208 | tf_op jit(solution)/shard_map/ppermute | solution.py:132
  250.4 36.4 %collective-permute-start.23 = (bf16[2,256,960]{1,2,0:T(8,128)(2,1)}, bf16[2,256,960]{1,2,0:T(8,128)(2,1)}, u32[]{:S(2)}, u32[]{:S(2)}) collective-permute-start(bf16[2,256,960]{1,2,0:T(8,128)(2,1)} %pad_maximum_fusion.15), channel_id=1, source_target_pairs={{0,8},{8,0},{16,24},{24,16},{1,9},{9,1},{17,25},{25,17},{2,10},{10... | collective-permute-start | bytes 2949128 | tf_op jit(solution)/shard_map/ppermute | solution.py:132
  258.1 35.5 %collective-permute-start.30 = (bf16[2,256,960]{1,2,0:T(8,128)(2,1)}, bf16[2,256,960]{1,2,0:T(8,128)(2,1)}, u32[]{:S(2)}, u32[]{:S(2)}) collective-permute-start(bf16[2,256,960]{1,2,0:T(8,128)(2,1)} %pad_maximum_fusion.17), channel_id=1, source_target_pairs={{0,8},{8,0},{16,24},{24,16},{1,9},{9,1},{17,25},{25,17},{2,10},{10... | collective-permute-start | bytes 2949128 | tf_op jit(solution)/shard_map/ppermute | solution.py:132
  265.6 20.5 %collective-permute-start.51 = (bf16[2,80,960]{2,1,0:T(8,128)(2,1)S(1)}, bf16[2,80,960]{2,1,0:T(8,128)(2,1)S(1)}, u32[]{:S(2)}, u32[]{:S(2)}) collective-permute-start(bf16[2,80,960]{2,1,0:T(8,128)(2,1)S(1)} %gather_fusion.19), channel_id=1, source_target_pairs={{0,2},{1,3},{2,0},{3,1},{4,6},{5,7},{6,4},{7,5},{8,10},{9,11},{10,... | collective-permute-start | bytes 921608 | tf_op jit(solution)/shard_map/ppermute | solution.py:132
  278.5 29.1 %collective-permute-start.44 = (bf16[4,120,1280]{2,1,0:T(8,128)(2,1)}, bf16[4,120,1280]{2,1,0:T(8,128)(2,1)}, u32[]{:S(2)}, u32[]{:S(2)}) collective-permute-start(bf16[4,120,1280]{2,1,0:T(8,128)(2,1)} %gather_fusion.11), channel_id=1, source_target_pairs={{0,1},{1,0},{2,3},{3,2},{4,5},{5,4},{6,7},{7,6},{8,9},{9,8},{10,11... | collective-permute-start | bytes 3686408 | tf_op jit(solution)/shard_map/ppermute | solution.py:132
  279.0 48.0 %collective-permute-start.16 = (bf16[256,960]{0,1:T(8,128)(2,1)}, bf16[256,960]{0,1:T(8,128)(2,1)}, u32[]{:S(2)}, u32[]{:S(2)}) collective-permute-start(bf16[256,960]{0,1:T(8,128)(2,1)} %fusion.78), channel_id=1, source_target_pairs={{0,16},{8,24},{16,0},{24,8},{1,17},{9,25},{17,1},{25,9},{2,18},{10... | collective-permute-start | bytes 1474568 | tf_op jit(solution)/shard_map/ppermute | solution.py:132
  286.1 35.3 %collective-permute-start.29 = (bf16[256,960]{0,1:T(8,128)(2,1)}, bf16[256,960]{0,1:T(8,128)(2,1)}, u32[]{:S(2)}, u32[]{:S(2)}) collective-permute-start(bf16[256,960]{0,1:T(8,128)(2,1)} %fusion.68), channel_id=1, source_target_pairs={{0,16},{8,24},{16,0},{24,8},{1,17},{9,25},{17,1},{25,9},{2,18},{10... | collective-permute-start | bytes 1474568 | tf_op jit(solution)/shard_map/ppermute | solution.py:132
  286.8 13.3 %collective-permute-start.52 = (bf16[1,80,960]{2,1,0:T(8,128)(2,1)S(1)}, bf16[1,80,960]{2,1,0:T(8,128)(2,1)S(1)}, u32[]{:S(2)}, u32[]{:S(2)}) collective-permute-start(bf16[1,80,960]{2,1,0:T(8,128)(2,1)S(1)} %slice.1076), channel_id=1, source_target_pairs={{0,4},{1,5},{2,6},{3,7},{4,0},{5,1},{6,2},{7,3},{8,12},{9,13},{10,... | collective-permute-start | bytes 460808 | tf_op jit(solution)/shard_map/ppermute | solution.py:132
  293.6 33.4 %collective-permute-start.24 = (bf16[256,960]{0,1:T(8,128)(2,1)}, bf16[256,960]{0,1:T(8,128)(2,1)}, u32[]{:S(2)}, u32[]{:S(2)}) collective-permute-start(bf16[256,960]{0,1:T(8,128)(2,1)} %fusion.72), channel_id=1, source_target_pairs={{0,16},{8,24},{16,0},{24,8},{1,17},{9,25},{17,1},{25,9},{2,18},{10... | collective-permute-start | bytes 1474568 | tf_op jit(solution)/shard_map/ppermute | solution.py:132
  300.1 23.6 %collective-permute-start.31 = (bf16[256,960]{0,1:T(8,128)(2,1)}, bf16[256,960]{0,1:T(8,128)(2,1)}, u32[]{:S(2)}, u32[]{:S(2)}) collective-permute-start(bf16[256,960]{0,1:T(8,128)(2,1)} %fusion.64), channel_id=1, source_target_pairs={{0,16},{8,24},{16,0},{24,8},{1,17},{9,25},{17,1},{25,9},{2,18},{10... | collective-permute-start | bytes 1474568 | tf_op jit(solution)/shard_map/ppermute | solution.py:132
  301.3 18.8 %copy-start.62 = (bf16[1,80,960]{2,1,0:T(8,128)(2,1)}, bf16[1,80,960]{2,1,0:T(8,128)(2,1)S(1)}, u32[]{:S(2)}) copy-start(bf16[1,80,960]{2,1,0:T(8,128)(2,1)S(1)} %get-tuple-element.146) | copy-start | bytes 460804
  307.6 12.6 %collective-permute-start.53 = (bf16[1,80,960]{2,1,0:T(8,128)(2,1)S(1)}, bf16[1,80,960]{2,1,0:T(8,128)(2,1)S(1)}, u32[]{:S(2)}, u32[]{:S(2)}) collective-permute-start(bf16[1,80,960]{2,1,0:T(8,128)(2,1)S(1)} %get-tuple-element.146), channel_id=1, source_target_pairs={{0,4},{1,5},{2,6},{3,7},{4,0},{5,1},{6,2},{7,3},{8,12},{9,13},{10,... | collective-permute-start | bytes 460808 | tf_op jit(solution)/shard_map/ppermute | solution.py:132
  320.9 94.5 %collective-permute-start.54 = (bf16[2,80,960]{2,1,0:T(8,128)(2,1)}, bf16[2,80,960]{2,1,0:T(8,128)(2,1)}, u32[]{:S(2)}, u32[]{:S(2)}) collective-permute-start(bf16[2,80,960]{2,1,0:T(8,128)(2,1)} %pad_maximum_fusion.37), channel_id=1, source_target_pairs={{0,2},{1,3},{2,0},{3,1},{4,6},{5,7},{6,4},{7,5},{8,10},{9,11},{10,... | collective-permute-start | bytes 921608 | tf_op jit(solution)/shard_map/ppermute | solution.py:132
  321.4 102.7 %collective-permute-start.45 = (bf16[2,120,1280]{2,1,0:T(8,128)(2,1)}, bf16[2,120,1280]{2,1,0:T(8,128)(2,1)}, u32[]{:S(2)}, u32[]{:S(2)}) collective-permute-start(bf16[2,120,1280]{2,1,0:T(8,128)(2,1)} %gather_fusion.13), channel_id=1, source_target_pairs={{0,2},{1,3},{2,0},{3,1},{4,6},{5,7},{6,4},{7,5},{8,10},{9,11},{10,... | collective-permute-start | bytes 1843208 | tf_op jit(solution)/shard_map/ppermute | solution.py:132
  337.5 63.1 %copy-start.6 = (f32[5,64,1024,1]{2,1,3,0:T(8,128)}, f32[5,64,1024,1]{2,1,3,0:T(8,128)S(1)}, u32[]{:S(2)}) copy-start(f32[5,64,1024,1]{2,1,3,0:T(8,128)S(1)} %fusion.12) | copy-start | bytes 3932164
  355.1 46.6 %copy-start.4 = (f32[5,64,1024,1]{2,1,3,0:T(8,128)}, f32[5,64,1024,1]{2,1,3,0:T(8,128)S(1)}, u32[]{:S(2)}) copy-start(f32[5,64,1024,1]{2,1,3,0:T(8,128)S(1)} %fusion.10) | copy-start | bytes 3932164
  401.8 17.3 %collective-permute-start.32 = (bf16[2,256,640]{1,2,0:T(8,128)(2,1)}, bf16[2,256,640]{1,2,0:T(8,128)(2,1)}, u32[]{:S(2)}, u32[]{:S(2)}) collective-permute-start(bf16[2,256,640]{1,2,0:T(8,128)(2,1)} %pad_maximum_fusion.19), channel_id=1, source_target_pairs={{0,8},{8,0},{16,24},{24,16},{1,9},{9,1},{17,25},{25,17},{2,10},{10... | collective-permute-start | bytes 1966088 | tf_op jit(solution)/shard_map/ppermute | solution.py:132
  403.0 19.1 %collective-permute-start.34 = (bf16[2,256,640]{1,2,0:T(8,128)(2,1)}, bf16[2,256,640]{1,2,0:T(8,128)(2,1)}, u32[]{:S(2)}, u32[]{:S(2)}) collective-permute-start(bf16[2,256,640]{1,2,0:T(8,128)(2,1)} %pad_maximum_fusion.20), channel_id=1, source_target_pairs={{0,8},{8,0},{16,24},{24,16},{1,9},{9,1},{17,25},{25,17},{2,10},{10... | collective-permute-start | bytes 1966088 | tf_op jit(solution)/shard_map/ppermute | solution.py:132
  417.6 69.2 %collective-permute-start.55 = (bf16[4,80,960]{2,1,0:T(8,128)(2,1)}, bf16[4,80,960]{2,1,0:T(8,128)(2,1)}, u32[]{:S(2)}, u32[]{:S(2)}) collective-permute-start(bf16[4,80,960]{2,1,0:T(8,128)(2,1)} %pad_maximum_fusion.22), channel_id=1, source_target_pairs={{0,1},{1,0},{2,3},{3,2},{4,5},{5,4},{6,7},{7,6},{8,9},{9,8},{10,11... | collective-permute-start | bytes 1843208 | tf_op jit(solution)/shard_map/ppermute | solution.py:132
  420.5 10.6 %collective-permute-start.33 = (bf16[256,640]{0,1:T(8,128)(2,1)S(1)}, bf16[256,640]{0,1:T(8,128)(2,1)S(1)}, u32[]{:S(2)}, u32[]{:S(2)}) collective-permute-start(bf16[256,640]{0,1:T(8,128)(2,1)S(1)} %fusion.103), channel_id=1, source_target_pairs={{0,16},{8,24},{16,0},{24,8},{1,17},{9,25},{17,1},{25,9},{2,18},{10... | collective-permute-start | bytes 983048 | tf_op jit(solution)/shard_map/ppermute | solution.py:132
  423.4 13.9 %collective-permute-start.35 = (bf16[256,640]{0,1:T(8,128)(2,1)S(1)}, bf16[256,640]{0,1:T(8,128)(2,1)S(1)}, u32[]{:S(2)}, u32[]{:S(2)}) collective-permute-start(bf16[256,640]{0,1:T(8,128)(2,1)S(1)} %fusion.97), channel_id=1, source_target_pairs={{0,16},{8,24},{16,0},{24,8},{1,17},{9,25},{17,1},{25,9},{2,18},{10... | collective-permute-start | bytes 983048 | tf_op jit(solution)/shard_map/ppermute | solution.py:132
  426.6 73.5 %collective-permute-start.46 = (bf16[1,120,1280]{2,1,0:T(8,128)(2,1)}, bf16[1,120,1280]{2,1,0:T(8,128)(2,1)}, u32[]{:S(2)}, u32[]{:S(2)}) collective-permute-start(bf16[1,120,1280]{2,1,0:T(8,128)(2,1)} %slice.1075), channel_id=1, source_target_pairs={{0,4},{1,5},{2,6},{3,7},{4,0},{5,1},{6,2},{7,3},{8,12},{9,13},{10,... | collective-permute-start | bytes 921608 | tf_op jit(solution)/shard_map/ppermute | solution.py:132
  486.8 33.6 %collective-permute-start.36 = (bf16[2,248,2560]{2,1,0:T(8,128)(2,1)}, bf16[2,248,2560]{2,1,0:T(8,128)(2,1)}, u32[]{:S(2)}, u32[]{:S(2)}) collective-permute-start(bf16[2,248,2560]{2,1,0:T(8,128)(2,1)} %pad_maximum_fusion.4), channel_id=1, source_target_pairs={{0,8},{8,0},{16,24},{24,16},{1,9},{9,1},{17,25},{25,17},{2,10},{10... | collective-permute-start | bytes 7618568 | tf_op jit(solution)/shard_map/ppermute | solution.py:132
  502.0 17.3 %collective-permute-start.47 = (bf16[1,120,1280]{2,1,0:T(8,128)(2,1)}, bf16[1,120,1280]{2,1,0:T(8,128)(2,1)S(1)}, u32[]{:S(2)}, u32[]{:S(2)}) collective-permute-start(bf16[1,120,1280]{2,1,0:T(8,128)(2,1)} %get-tuple-element.148), channel_id=1, source_target_pairs={{0,4},{1,5},{2,6},{3,7},{4,0},{5,1},{6,2},{7,3},{8,12},{9,13},{10,... | collective-permute-start | bytes 921608 | tf_op jit(solution)/shard_map/ppermute | solution.py:132
  520.3 15.9 %collective-permute-start.48 = (bf16[2,120,1280]{2,1,0:T(8,128)(2,1)S(1)}, bf16[2,120,1280]{2,1,0:T(8,128)(2,1)S(1)}, u32[]{:S(2)}, u32[]{:S(2)}) collective-permute-start(bf16[2,120,1280]{2,1,0:T(8,128)(2,1)S(1)} %pad_maximum_fusion.25), channel_id=1, source_target_pairs={{0,2},{1,3},{2,0},{3,1},{4,6},{5,7},{6,4},{7,5},{8,10},{9,11},{10,... | collective-permute-start | bytes 1843208 | tf_op jit(solution)/shard_map/ppermute | solution.py:132
  524.9 29.9 %collective-permute-start.37 = (bf16[248,2560]{1,0:T(8,128)(2,1)S(1)}, bf16[248,2560]{1,0:T(8,128)(2,1)S(1)}, u32[]{:S(2)}, u32[]{:S(2)}) collective-permute-start(bf16[248,2560]{1,0:T(8,128)(2,1)S(1)} %fusion.62), channel_id=1, source_target_pairs={{0,16},{8,24},{16,0},{24,8},{1,17},{9,25},{17,1},{25,9},{2,18},{10... | collective-permute-start | bytes 3809288 | tf_op jit(solution)/shard_map/ppermute | solution.py:132
  539.2 34.9 %collective-permute-start.49 = (bf16[4,120,1280]{2,1,0:T(8,128)(2,1)}, bf16[4,120,1280]{2,1,0:T(8,128)(2,1)S(1)}, u32[]{:S(2)}, u32[]{:S(2)}) collective-permute-start(bf16[4,120,1280]{2,1,0:T(8,128)(2,1)} %pad_maximum_fusion.13), channel_id=1, source_target_pairs={{0,1},{1,0},{2,3},{3,2},{4,5},{5,4},{6,7},{7,6},{8,9},{9,8},{10,11... | collective-permute-start | bytes 3686408 | tf_op jit(solution)/shard_map/ppermute | solution.py:132
  573.7 15.6 %collective-permute-start.38 = (bf16[4,31,2560]{2,0,1:T(4,128)(2,1)}, bf16[4,31,2560]{2,0,1:T(4,128)(2,1)S(1)}, u32[]{:S(2)}, u32[]{:S(2)}) collective-permute-start(bf16[4,31,2560]{2,0,1:T(4,128)(2,1)} %copy.274), channel_id=1, source_target_pairs={{0,1},{1,0},{2,3},{3,2},{4,5},{5,4},{6,7},{7,6},{8,9},{9,8},{10,11... | collective-permute-start | bytes 1904648 | tf_op jit(solution)/shard_map/ppermute | solution.py:132
  592.7 8.1 %collective-permute-start.39 = (bf16[2,31,2560]{2,1,0:T(8,128)(2,1)S(1)}, bf16[2,31,2560]{2,1,0:T(8,128)(2,1)}, u32[]{:S(2)}, u32[]{:S(2)}) collective-permute-start(bf16[2,31,2560]{2,1,0:T(8,128)(2,1)S(1)} %gather_fusion.7), channel_id=1, source_target_pairs={{0,2},{1,3},{2,0},{3,1},{4,6},{5,7},{6,4},{7,5},{8,10},{9,11},{10,... | collective-permute-start | bytes 952328 | tf_op jit(solution)/shard_map/ppermute | solution.py:132
  601.9 10.7 %collective-permute-start.40 = (bf16[1,31,2560]{2,1,0:T(8,128)(2,1)S(1)}, bf16[1,31,2560]{2,1,0:T(8,128)(2,1)S(1)}, u32[]{:S(2)}, u32[]{:S(2)}) collective-permute-start(bf16[1,31,2560]{2,1,0:T(8,128)(2,1)S(1)} %slice.1077), channel_id=1, source_target_pairs={{0,4},{1,5},{2,6},{3,7},{4,0},{5,1},{6,2},{7,3},{8,12},{9,13},{10,... | collective-permute-start | bytes 476168 | tf_op jit(solution)/shard_map/ppermute | solution.py:132
  613.3 6.3 collective-permute-start.41
  619.7 7.1 %collective-permute-start.42 = (bf16[2,31,2560]{2,1,0:T(8,128)(2,1)S(1)}, bf16[2,31,2560]{2,1,0:T(8,128)(2,1)S(1)}, u32[]{:S(2)}, u32[]{:S(2)}) collective-permute-start(bf16[2,31,2560]{2,1,0:T(8,128)(2,1)S(1)} %pad_maximum_fusion.36), channel_id=1, source_target_pairs={{0,2},{1,3},{2,0},{3,1},{4,6},{5,7},{6,4},{7,5},{8,10},{9,11},{10,... | collective-permute-start | bytes 952328 | tf_op jit(solution)/shard_map/ppermute | solution.py:132
  627.4 10.5 %collective-permute-start.43 = (bf16[4,31,2560]{2,0,1:T(4,128)(2,1)S(1)}, bf16[4,31,2560]{2,0,1:T(4,128)(2,1)S(1)}, u32[]{:S(2)}, u32[]{:S(2)}) collective-permute-start(bf16[4,31,2560]{2,0,1:T(4,128)(2,1)S(1)} %copy.229), channel_id=1, source_target_pairs={{0,1},{1,0},{2,3},{3,2},{4,5},{5,4},{6,7},{7,6},{8,9},{9,8},{10,11... | collective-permute-start | bytes 1904648 | tf_op jit(solution)/shard_map/ppermute | solution.py:132
  (118 other events, 598.1 us)

commit v2 on v1

v2 whole, which is shorter than its diff:
```python
import functools

import jax
import jax.numpy as jnp
from jax import lax
from jax.experimental import pallas as pl
from jax.experimental.pallas import tpu as pltpu
from jax.sharding import PartitionSpec as P

HD = 64
PIECE = 256
LANES = 128
GROUP = 4
PARTS = 8
GAIN_ROWS = 16
SLOTS = (7, 3, 5, 1, 6, 2, 4, 0)


NORM_EPS = 1e-05
ROPE_BASE = 10000.0
MASKED_SCORE = -1e30
SCALE = HD ** (-0.5)

LOW = jnp.bfloat16
FULL = jnp.float32
NN = (((1,), (0,)), ((), ()))
NT = (((1,), (1,)), ((), ()))
TN = (((0,), (0,)), ((), ()))
TT = (((0,), (1,)), ((), ()))


def dot(left_mat, right_mat, form=NN):
    return lax.dot_general(left_mat, right_mat, form, preferred_element_type=FULL)


def swap(values, axis, count, mask):
    return lax.ppermute(values, axis, [(i, i ^ mask) for i in range(count)])


def group_blocks(own):
    across = swap(own, "grp", GROUP, 2)
    beside = swap(own, "grp", GROUP, 1)
    corner = swap(across, "grp", GROUP, 1)
    return own, beside, across, corner


def group_terms(keep, send):
    beside = swap(send, "grp", GROUP, 1)
    across = (keep[1].astype(FULL) + beside[1].astype(FULL)).astype(LOW)
    return keep[0], beside[0], swap(across, "grp", GROUP, 2)


def three(terms):
    return terms[0].astype(FULL) + terms[1].astype(FULL) + terms[2].astype(FULL)


def rep_sum(first, second, third, last, ranks):
    one = swap(first, "rep", ranks, 1)
    two = (second.astype(FULL) + one[0:2].astype(FULL)).astype(LOW)
    two = swap(two, "rep", ranks, 2)
    four = (third.astype(FULL) + one[2:3].astype(FULL) + two[0:1].astype(FULL)).astype(LOW)
    four = swap(four, "rep", ranks, 4)
    mine = last.astype(FULL) + one[3:4].astype(FULL) + two[1:2].astype(FULL) + four.astype(FULL)
    mine = mine.astype(LOW)
    if ranks > PARTS:
        others = [[j * PARTS + i for j in range(ranks // PARTS)] for i in range(PARTS)]
        mine = lax.psum(mine, "rep", axis_index_groups=others)
    held = jnp.concatenate([mine, swap(mine, "rep", ranks, 4)])
    held = jnp.concatenate([held, swap(held, "rep", ranks, 2)])
    return held, swap(held, "rep", ranks, 1)


def call(kernel, name, out_shape, *, grid=(), prefetch=0, in_specs, out_specs, scratch=(), flops=0, moved=0, vmem=56):
    return pl.pallas_call(
        kernel,
        name=name,
        out_shape=out_shape,
        grid_spec=pltpu.PrefetchScalarGridSpec(
            num_scalar_prefetch=prefetch,
            grid=grid,
            in_specs=in_specs,
            out_specs=out_specs,
            scratch_shapes=list(scratch),
        ),
        compiler_params=pltpu.CompilerParams(vmem_limit_bytes=vmem << 20),
        cost_estimate=pl.CostEstimate(flops=int(flops), bytes_accessed=int(moved), transcendentals=0),
    )


def whole(shape):
    return pl.BlockSpec(shape, lambda *_: (0,) * len(shape))


def shape_of(shape, kind=LOW):
    return jax.ShapeDtypeStruct(shape, kind)


def lane_index(rows):
    return lax.broadcasted_iota(jnp.int32, (rows, LANES), 1)


def turn(slab, cosine, sine_val, lane):
    swapped = jnp.where(
        lane % HD < HD // 2, pltpu.roll(slab, LANES - HD // 2, 1), pltpu.roll(slab, HD // 2, 1)
    )
    return slab * cosine + swapped * sine_val


def assemble(rank, blocks, scratch, rows, columns):
    for k in range(GROUP):
        start = pl.multiple_of((rank ^ k) * rows, 16)
        scratch[pl.ds(start, rows), 0:columns] = blocks[k][0:rows, :]


def keys_values_kernel(ranks, tok_ref, b0, b1, b2, b3, cos_ref, sin_ref, norm_ref, kv_refs_a, kv_refs_b, gain_ref, w_ref):
    width = tok_ref.shape[1]
    kw2 = b0.shape[1]
    shard = b0.shape[0] - GAIN_ROWS
    span = kv_refs_a.shape[0]
    blocks = (b0, b1, b2, b3)
    rows = sum(b[shard : shard + GAIN_ROWS, :].astype(FULL) for b in blocks)
    gain_one = jnp.concatenate([rows[0:1, :], rows[1:2, : width - kw2]], axis=1)
    gain_two = jnp.concatenate([rows[2:3, :], rows[3:4, : width - kw2]], axis=1)
    gain_ref[0:1, :] = gain_one
    gain_ref[1:2, :] = gain_two
    gain_ref[2:8, :] = jnp.zeros((6, width), FULL)
    assemble(ranks[0], blocks, w_ref, shard, kw2)
    lane = lane_index(span)
    heads = kw2 // LANES
    for s, out in enumerate((kv_refs_a, kv_refs_b)):
        part = slice(s * span, (s + 1) * span)
        x = tok_ref[part, :].astype(FULL)
        inverse = lax.rsqrt(jnp.mean(x * x, axis=-1, keepdims=True) + NORM_EPS)
        norm = (x * inverse * gain_one).astype(LOW)
        norm_ref[part, :] = norm
        kv = dot(norm, w_ref[...])
        cosine, sine_val = cos_ref[part, :], sin_ref[part, :]
        for h in range(heads):
            key = kv[:, (h // 2) * LANES : (h // 2 + 1) * LANES]
            key = turn(key, cosine, sine_val, lane)
            if h % 2:
                key = pltpu.roll(key, HD, 1)
            v = heads + h
            value = kv[:, (v // 2) * LANES : (v // 2 + 1) * LANES]
            if v % 2 == 0:
                value = pltpu.roll(value, HD, 1)
            out[:, h * LANES : (h + 1) * LANES] = jnp.where(lane < HD, key, value).astype(LOW)


def queries_kernel(ranks, norm_ref, b0, b1, b2, b3, cos_ref, sin_ref, q_ref, w_ref):
    width = b0.shape[1]
    shard = b0.shape[0]
    span = norm_ref.shape[0] // 2
    padded = w_ref.shape[1]
    assemble(ranks[0], (b0, b1, b2, b3), w_ref, shard, width)
    if padded > width:
        w_ref[:, width:padded] = jnp.zeros((w_ref.shape[0], padded - width), LOW)
    lane = lane_index(span)
    heads = width // HD
    for s in range(2):
        part = slice(s * span, (s + 1) * span)
        query = dot(norm_ref[part, :], w_ref[...])
        cosine, sine_val = cos_ref[part, :], sin_ref[part, :]
        for j in range(padded // LANES):
            slab = turn(query[:, j * LANES : (j + 1) * LANES], cosine, sine_val, lane) * SCALE
            even = jnp.where(lane < HD, slab, 0.0)
            q_ref[part, 2 * j * LANES : (2 * j + 1) * LANES] = even.astype(LOW)
            if 2 * j + 1 < heads:
                odd = jnp.where(lane < HD, pltpu.roll(slab, HD, 1), 0.0)
                q_ref[part, (2 * j + 1) * LANES : (2 * j + 2) * LANES] = odd.astype(LOW)


def attend_kernel(seq, ranks, order, starts, q_ref, b0, b1, b2, b3, p_ref, o_ref, bias_ref):
    span = q_ref.shape[0]
    per = q_ref.shape[1] // LANES
    rank = ranks[0]

    @pl.when(pl.program_id(0) == 0)
    def _():
        query_pos = order[seq, rank] * span + lax.broadcasted_iota(jnp.int32, (span, span), 1)
        query_in = []
        for m in range(2):
            start = starts[seq, m]
            query_in.append((query_pos >= start) & (query_pos < start + PIECE))
        for k in range(GROUP):
            key_pos = order[seq, rank ^ k] * span + lax.broadcasted_iota(jnp.int32, (span, span), 0)
            allowed = key_pos <= query_pos
            for m in range(2):
                start = starts[seq, m]
                key_in = (key_pos >= start) & (key_pos < start + PIECE)
                allowed = allowed | (query_in[m] & key_in)
            bias_ref[k * span : (k + 1) * span, :] = jnp.where(allowed, 0.0, MASKED_SCORE)

    kv = jnp.concatenate([b0[...], b1[...], b2[...], b3[...]], axis=0)
    kv_t = kv.T
    for i in range(per):
        scores = dot(kv, q_ref[:, i * LANES : (i + 1) * LANES], NT) + bias_ref[...]
        peak = jnp.max(scores, axis=0, keepdims=True)
        exponent = jnp.exp(scores - peak)
        total = jnp.sum(exponent, axis=0, keepdims=True)
        probs = (exponent * (1.0 / total)).astype(LOW)
        p_ref[0, :, i * span : (i + 1) * span] = probs
        mixed = dot(kv_t, probs)
        o_ref[i * HD : (i + 1) * HD, :] = mixed[HD : 2 * HD, :].astype(LOW)


def middle_kernel(ranks, att_ref, b0, b1, b2, b3, tok_ref, gain_ref, mid_ref, x_ref, w_ref):
    width = b0.shape[1]
    shard = b0.shape[0]
    assemble(ranks[0], (b0, b1, b2, b3), w_ref, shard, width)
    middle = tok_ref[0].astype(FULL) + dot(att_ref[...], w_ref[...], TN)
    mid_ref[...] = middle
    inverse = lax.rsqrt(jnp.mean(middle * middle, axis=-1, keepdims=True) + NORM_EPS)
    x_ref[...] = (middle * inverse * gain_ref[1:2, :]).astype(LOW)


def forward_back_kernel(x0, x1, x2, x3, c0, c1, c2, c3, wg_ref, wu_ref, wd_ref, ko_ref, so_ref, kg_ref, sg_ref, hid_ref, gg_ref, gu_ref, xs, cs):
    k = pl.program_id(0)
    for i, (x, c) in enumerate(((x0, c0), (x1, c1), (x2, c2), (x3, c3))):

        @pl.when(k == i)
        def _(x=x, c=c):
            xs[...] = x[...]
            cs[...] = c[0]

    x = xs[...]
    gate = dot(x, wg_ref[...])
    up = dot(x, wu_ref[...])
    grad_hidden = dot(cs[...], wd_ref[...], NT)
    sig = 1.0 / (1.0 + jnp.exp(-gate))
    swish = gate * sig
    hidden = (swish * up).astype(LOW)
    grad_gate = (grad_hidden * up * sig * (1.0 + gate * (1.0 - sig))).astype(LOW)
    grad_up = (grad_hidden * swish).astype(LOW)
    hid_ref[...] = hidden
    gg_ref[...] = grad_gate
    gu_ref[...] = grad_up
    grad_x = (dot(grad_gate, wg_ref[...], NT) + dot(grad_up, wu_ref[...], NT)).astype(LOW)
    out = dot(hidden, wd_ref[...]).astype(LOW)
    half = k // 2

    @pl.when(k % 2 == 0)
    def _():
        kg_ref[half] = grad_x
        ko_ref[half] = out

    @pl.when(k % 2 == 1)
    def _():
        sg_ref[half] = grad_x
        so_ref[half] = out


def weight_kernel(ranks, *refs):
    xs = refs[0:8]
    cs = refs[8:12]
    rows = refs[12:18]
    first, second, third, last = refs[18:22]
    left, left_t, right, acc, sem = refs[22:27]
    m = pl.program_id(0)
    span = left.shape[2]
    copies = []
    for s in range(2):
        for k in range(GROUP):
            b = s * GROUP + k
            copies.append(pltpu.make_async_copy(xs[b], left.at[0, b], sem.at[b]))
            copies.append(pltpu.make_async_copy(cs[k].at[s], left.at[1, b], sem.at[8 + b]))
        for n in range(3):
            copies.append(
                pltpu.make_async_copy(
                    rows[s * 3 + n], right.at[n, pl.ds(s * GROUP * span, GROUP * span)], sem.at[16 + s * 3 + n]
                )
            )

    @pl.when(m == 0)
    def _():
        for copy in copies:
            copy.start()
        for copy in copies:
            copy.wait()

    @pl.when(m != 1)
    def _():
        side = m // 2

        def flip(b, carry):
            start = pl.multiple_of(b * span, LANES)
            left_t[:, pl.ds(start, span)] = left[side, b].T
            return carry

        lax.fori_loop(0, 2 * GROUP, flip, 0)

    acc[...] = dot(left_t[...], right[m])
    part = acc.shape[0] // PARTS
    outs = [(first, i) for i in range(4)] + [(second, 0), (second, 1), (third, 0), (last, 0)]
    for (out, i), slot in zip(outs, SLOTS):
        start = pl.multiple_of((slot ^ ranks[1]) * part, 8)
        out[i] = acc[pl.ds(start, part), :].astype(LOW)


def branch_kernel(ranks, mid_ref, cot_ref, e0, e1, e2, gain_ref, b0, b1, b2, b3, att_ref, gm_ref, gb_ref, do_ref, delta_ref, gain_out, w_ref):
    width = b0.shape[1]
    shard = b0.shape[0]
    span = mid_ref.shape[0]
    padded = w_ref.shape[0]
    assemble(ranks[0], (b0, b1, b2, b3), w_ref, shard, width)
    if padded > width:
        w_ref[width:padded, :] = jnp.zeros((padded - width, width), LOW)
    middle = mid_ref[...]
    grad = e0[0].astype(FULL) + e1[0].astype(FULL) + e2[...].astype(FULL)
    inverse = lax.rsqrt(jnp.mean(middle * middle, axis=-1, keepdims=True) + NORM_EPS)
    scaled = grad * gain_ref[1:2, :]
    turned = jnp.mean(scaled * middle, axis=-1, keepdims=True)
    grad_middle = cot_ref[0].astype(FULL) + inverse * scaled - middle * (inverse * inverse * inverse * turned)
    gain_out[0:1, :] = jnp.sum(grad * middle * inverse, axis=0, keepdims=True)
    gain_out[1:8, :] = jnp.zeros((7, width), FULL)
    gm_ref[...] = grad_middle
    branch = grad_middle.astype(LOW)
    gb_ref[...] = branch
    lane = lane_index(span)
    grad_att = dot(branch, w_ref[...], NT)
    heads = width // HD
    for j in range(padded // LANES):
        slab = grad_att[:, j * LANES : (j + 1) * LANES]
        even = jnp.where(lane >= HD, pltpu.roll(slab, HD, 1), 0.0)
        do_ref[:, 2 * j * LANES : (2 * j + 1) * LANES] = even.astype(LOW)
        if 2 * j + 1 < heads:
            odd = jnp.where(lane >= HD, slab, 0.0)
            do_ref[:, (2 * j + 1) * LANES : (2 * j + 2) * LANES] = odd.astype(LOW)
    grad_att_t = dot(w_ref[0:width, :], branch, NT).astype(LOW).astype(FULL)
    both = grad_att_t * att_ref[...].astype(FULL)
    for h in range(heads):
        delta_ref[h : h + 1, :] = jnp.sum(both[h * HD : (h + 1) * HD, :], axis=0, keepdims=True)
    delta_ref[heads:, :] = jnp.zeros((delta_ref.shape[0] - heads, span), FULL)


def attend_back_kernel(q_ref, b0, b1, b2, b3, p_ref, do_ref, delta_ref, cos_ref, sin_ref, gq_ref, keep_ref, send_ref):
    span = q_ref.shape[0]
    per = q_ref.shape[1] // LANES
    h = pl.program_id(0)
    kv = jnp.concatenate([b0[...], b1[...], b2[...], b3[...]], axis=0)
    kv_t = kv.T
    cosine, sine_val = cos_ref[0], sin_ref[0]
    total = None
    for i in range(per):
        out_grad = do_ref[:, i * LANES : (i + 1) * LANES]
        probs = p_ref[0, :, i * span : (i + 1) * span]
        grad_probs = dot(kv, out_grad, NT)
        delta = delta_ref[pl.ds(per * h + i, 1), :]
        grad_scores = (probs.astype(FULL) * (grad_probs - delta)).astype(LOW)
        grad_q = dot(kv_t, grad_scores)
        one = grad_q[0 : HD // 2, :] * SCALE
        two = grad_q[HD // 2 : HD, :] * SCALE
        gq_ref[i * HD : i * HD + HD // 2, :] = (one * cosine + two * sine_val).astype(LOW)
        gq_ref[i * HD + HD // 2 : (i + 1) * HD, :] = (two * cosine - one * sine_val).astype(LOW)
        both = dot(grad_scores, q_ref[:, i * LANES : (i + 1) * LANES]) + dot(probs, out_grad)
        total = both if total is None else total + both
    total = total.astype(LOW)
    keep_ref[0] = total[0:span, :]
    send_ref[0] = total[span : 2 * span, :]
    keep_ref[1] = total[2 * span : 3 * span, :]
    send_ref[1] = total[3 * span : 4 * span, :]


def spread(ranks, acc, keep_ref, send_ref):
    part = acc.shape[1] // PARTS
    for k in range(GROUP):
        out = send_ref if k % 2 else keep_ref
        for i, slot in enumerate(SLOTS):
            start = pl.multiple_of((slot ^ ranks[1]) * part, 8)
            out[k // 2, i] = acc[ranks[0] ^ k, pl.ds(start, part), :].astype(LOW)


def out_weight_kernel(ranks, att_a, att_b, gb_a, gb_b, keep_ref, send_ref, acc):
    width = gb_a.shape[1]
    shard = width // GROUP
    for b in range(GROUP):
        rows = slice(b * shard, (b + 1) * shard)
        acc[b, 0:shard, :] = dot(att_a[rows, :], gb_a[...]) + dot(att_b[rows, :], gb_b[...])
        acc[b, shard:, :] = jnp.zeros((acc.shape[1] - shard, width), FULL)
    spread(ranks, acc, keep_ref, send_ref)


def last_kernel(ranks, *refs):
    (norm_ref, gq_a, gq_b) = refs[0:3]
    kv_terms = (refs[3:6], refs[6:9])
    cos_ref, sin_ref = refs[9:11]
    q_blocks, kv_blocks = refs[11:15], refs[15:19]
    tok_ref, gm_a, gm_b, gain_ref, gain_a, gain_b = refs[19:25]
    out_ref, keep_ref, send_ref = refs[25:28]
    wq_ref, wkv_ref, gkv_ref, acc = refs[28:32]
    width = norm_ref.shape[1]
    span = gq_a.shape[1]
    shard = width // GROUP
    kw2 = wkv_ref.shape[1]
    heads = kw2 // LANES
    assemble(ranks[0], q_blocks, wq_ref, shard, width)
    assemble(ranks[0], kv_blocks, wkv_ref, shard, kw2)
    lane = lane_index(span)
    grad_gain = jnp.zeros((1, width), FULL)
    for s in range(2):
        part = slice(s * span, (s + 1) * span)
        e0, e1, e2 = kv_terms[s]
        keys, values = [], []
        for h in range(heads):
            cut = slice(h * LANES, (h + 1) * LANES)
            slab = e0[0, :, cut].astype(FULL) + e1[0, :, cut].astype(FULL) + e2[:, cut].astype(FULL)
            keys.append(turn(slab, cos_ref[part, :], -sin_ref[part, :], lane))
            values.append(slab)
        plain = []
        for t in range(2 * heads):
            if t < heads:
                plain.append(keys[t] if t % 2 == 0 else pltpu.roll(keys[t], HD, 1))
            else:
                plain.append(values[t - heads] if t % 2 else pltpu.roll(values[t - heads], HD, 1))
        for j in range(heads):
            pair = jnp.where(lane < HD, plain[2 * j], plain[2 * j + 1])
            gkv_ref[part, j * LANES : (j + 1) * LANES] = pair.astype(LOW)
        gq = (gq_a, gq_b)[s]
        grad_norm = dot(gq[...], wq_ref[...], TT) + dot(gkv_ref[part, :], wkv_ref[...], NT)
        x = tok_ref[part, :].astype(FULL)
        inverse = lax.rsqrt(jnp.mean(x * x, axis=-1, keepdims=True) + NORM_EPS)
        scaled = grad_norm * gain_ref[0:1, :]
        turned = jnp.mean(scaled * x, axis=-1, keepdims=True)
        out_ref[part, :] = (gm_a, gm_b)[s][...] + inverse * scaled - x * (inverse * inverse * inverse * turned)
        grad_gain = grad_gain + jnp.sum(grad_norm * x * inverse, axis=0, keepdims=True)
    norm_t = norm_ref[...].T
    gain_two = gain_a[0:1, :] + gain_b[0:1, :]
    for b in range(GROUP):
        rows = norm_t[b * shard : (b + 1) * shard, :]
        acc[b, 0:shard, 0:width] = dot(rows[:, 0:span], gq_a[...], NT) + dot(rows[:, span:], gq_b[...], NT)
        acc[b, 0:shard, width:] = dot(rows, gkv_ref[...])
        acc[b, shard:, :] = jnp.zeros((acc.shape[1] - shard, acc.shape[2]), FULL)
        acc[b, shard : shard + 1, 0:width] = grad_gain
        acc[b, shard + 1 : shard + 2, 0:width] = gain_two
    spread(ranks, acc, keep_ref, send_ref)


def place(slot):
    return ((slot >> 2) & 1) + ((slot >> 1) & 1) * 2


def forward_weights_kernel(ranks, even, odd, gate_ref, up_ref, down_ref, scratch):
    part = even.shape[1]
    columns = gate_ref.shape[1]
    for a in range(PARTS):
        slot = ranks[1] ^ a
        index = place(slot)
        rows = slice(a * part, (a + 1) * part)

        @pl.when(slot % 2 == 0)
        def _(rows=rows, index=index):
            gate_ref[rows, :] = even[index, :, 0:columns].astype(FULL)
            up_ref[rows, :] = even[index, :, columns : 2 * columns].astype(FULL)
            scratch[rows, :] = even[index, :, 2 * columns :].astype(FULL)

        @pl.when(slot % 2 == 1)
        def _(rows=rows, index=index):
            gate_ref[rows, :] = odd[index, :, 0:columns].astype(FULL)
            up_ref[rows, :] = odd[index, :, columns : 2 * columns].astype(FULL)
            scratch[rows, :] = odd[index, :, 2 * columns :].astype(FULL)

    down_ref[...] = scratch[...].T


def attention_weights_kernel(ranks, even, odd, even_o, odd_o, q_ref, k_ref, v_ref, o_ref, gain_ref, scratch, scratch_o):
    part = even.shape[1]
    shard, width = q_ref.shape
    kw = k_ref.shape[1]
    for a in range(PARTS):
        slot = ranks[1] ^ a
        index = place(slot)
        rows = slice(a * part, (a + 1) * part)

        @pl.when(slot % 2 == 0)
        def _(rows=rows, index=index):
            scratch[rows, :] = even[index].astype(FULL)
            scratch_o[rows, :] = even_o[index].astype(FULL)

        @pl.when(slot % 2 == 1)
        def _(rows=rows, index=index):
            scratch[rows, :] = odd[index].astype(FULL)
            scratch_o[rows, :] = odd_o[index].astype(FULL)

    q_ref[...] = scratch[0:shard, 0:width]
    k_ref[...] = scratch[0:shard, width : width + kw]
    v_ref[...] = scratch[0:shard, width + kw : width + 2 * kw]
    o_ref[...] = scratch_o[0:shard, :]
    gain_ref[...] = scratch[shard : shard + 8, 0:width]


def tables(places):
    half = HD // 2
    frequency = ROPE_BASE ** (-2.0 * jnp.arange(half, dtype=FULL) / HD)
    spots = places.astype(FULL)
    angles = spots.reshape(-1, 1) * frequency
    cosine, sine_val = jnp.cos(angles), jnp.sin(angles)
    cos_rows = jnp.concatenate([cosine] * 4, axis=1)
    sin_rows = jnp.concatenate([-sine_val, sine_val, -sine_val, sine_val], axis=1)
    cols = spots[:, None, :] * frequency[None, :, None]
    return cos_rows, sin_rows, jnp.cos(cols), jnp.sin(cols)


def body(
    tokens,
    w_query,
    w_key,
    w_value,
    w_out,
    w_gate,
    w_up,
    w_down,
    gain_attn,
    gain_mlp,
    span_order,
    piece_starts,
    cotangent,
):
    ranks = lax.axis_size("rep")
    rank_grp = lax.axis_index("grp")
    seq_count, span, width = tokens.shape
    shard = w_query.shape[0]
    kw = w_key.shape[1]
    kw2 = 2 * kw
    kv_heads = kw // HD
    per = width // kw
    ff = w_gate.shape[1]
    rows = seq_count * span
    length = GROUP * span
    padded = -(-width // LANES) * LANES
    place_of = jnp.stack([rank_grp, lax.axis_index("rep") % PARTS]).astype(jnp.int32)
    any_spec = pl.BlockSpec(memory_space=pl.ANY)

    gains = jnp.zeros((2, 2 * kw2), LOW)
    gains = lax.dynamic_update_slice(gains, jnp.stack([gain_attn, gain_mlp]), (0, rank_grp * shard))
    gains = jnp.pad(gains.reshape(4, kw2), ((0, GAIN_ROWS - 4), (0, 0)))
    kv_shard = jnp.concatenate([jnp.concatenate([w_key, w_value], axis=1), gains], axis=0)
    kv_blocks = group_blocks(kv_shard)
    q_blocks = group_blocks(w_query)
    o_blocks = group_blocks(w_out)
    own_span = lax.dynamic_slice(span_order, (0, rank_grp), (seq_count, 1))
    places = own_span * span + jnp.arange(span, dtype=jnp.int32)[None, :]
    cos_rows, sin_rows, cos_cols, sin_cols = tables(places)
    token_rows = tokens.reshape(rows, width)

    table = whole((rows, LANES))
    norm_low, kv_a, kv_b, gain_rows = call(
        keys_values_kernel,
        "keys_values",
        (shape_of((rows, width)), shape_of((span, kw2)), shape_of((span, kw2)), shape_of((8, width), FULL)),
        prefetch=1,
        grid=(1,),
        in_specs=[whole((rows, width))] + [whole(kv_shard.shape)] * 4 + [table, table],
        out_specs=(whole((rows, width)), whole((span, kw2)), whole((span, kw2)), whole((8, width))),
        scratch=[pltpu.VMEM((width, kw2), LOW)],
        flops=2 * rows * width * kw2,
        moved=4 * rows * width + 2 * width * kw2 + 2 * rows * kw2,
    )(place_of, token_rows, *kv_blocks, cos_rows, sin_rows)
    queries = call(
        queries_kernel,
        "queries",
        shape_of((rows, per * kv_heads * LANES)),
        prefetch=1,
        grid=(1,),
        in_specs=[whole((rows, width))] + [whole((shard, width))] * 4 + [table, table],
        out_specs=whole((rows, per * kv_heads * LANES)),
        scratch=[pltpu.VMEM((width, padded), LOW)],
        flops=2 * rows * width * padded,
        moved=2 * rows * width + 2 * width * width + 4 * rows * width,
    )(place_of, norm_low, *q_blocks, cos_rows, sin_rows)

    kv_all = [group_blocks(kv_a), group_blocks(kv_b)]
    cot_blocks = group_blocks(cotangent)
    head = pl.BlockSpec((span, LANES), lambda h, *_: (0, h))
    stats, attended, middles, x_blocks = [], [], [], []
    for s in range(seq_count):
        probs, att = call(
            functools.partial(attend_kernel, s),
            "attend",
            (shape_of((kv_heads, length, per * span)), shape_of((width, span))),
            prefetch=3,
            grid=(kv_heads,),
            in_specs=[pl.BlockSpec((span, per * LANES), lambda h, *_, s=s: (s, h))] + [head] * 4,
            out_specs=(
                pl.BlockSpec((1, length, per * span), lambda h, *_: (h, 0, 0)),
                pl.BlockSpec((per * HD, span), lambda h, *_: (h, 0)),
            ),
            scratch=[pltpu.VMEM((length, span), FULL)],
            flops=8 * span * length * width * 2,
            moved=2 * kv_heads * length * per * span + 2 * length * kw2 + 6 * span * width,
        )(place_of, span_order, piece_starts, queries, *kv_all[s])
        middle, x = call(
            middle_kernel,
            "middle",
            (shape_of((span, width), FULL), shape_of((span, width))),
            prefetch=1,
            grid=(1,),
            in_specs=[whole((width, span))]
            + [whole((shard, width))] * 4
            + [pl.BlockSpec((1, span, width), lambda *_, s=s: (s, 0, 0)), whole((8, width))],
            out_specs=(whole((span, width)), whole((span, width))),
            scratch=[pltpu.VMEM((width, width), LOW)],
            flops=2 * span * width * width,
            moved=10 * span * width + 2 * width * width,
        )(place_of, att, *o_blocks, tokens, gain_rows)
        stats.append(probs)
        attended.append(att)
        middles.append(middle)
        x_blocks.append(group_blocks(x))

    outs, grads, saved = [], [], []
    for s in range(seq_count):
        block = whole((span, width))
        both = whole((2, span, width))
        per_block = pl.BlockSpec((span, ff), lambda k, *_: (k, 0))
        ko, so, kg, sg, hid, gg, gu = call(
            forward_back_kernel,
            "forward_back",
            (shape_of((2, span, width)),) * 4 + (shape_of((length, ff)),) * 3,
            grid=(GROUP,),
            in_specs=[block] * 4
            + [pl.BlockSpec((1, span, width), lambda *_, s=s: (s, 0, 0))] * 4
            + [whole((width, ff)), whole((width, ff)), whole((ff, width))],
            out_specs=(both,) * 4 + (per_block,) * 3,
            scratch=[pltpu.VMEM((span, width), LOW), pltpu.VMEM((span, width), LOW)],
            flops=12 * length * width * ff,
            moved=6 * width * ff + 8 * length * width + 6 * length * ff,
        )(*x_blocks[s], *cot_blocks, w_gate, w_up, w_down)
        grads.append(group_terms(kg, sg) + (kg, sg))
        outs.append((ko, so))
        saved.append((hid, gg, gu))

    part = width // PARTS
    pieces = call(
        weight_kernel,
        "weights",
        tuple(shape_of((n, part, 3 * ff)) for n in (4, 2, 1, 1)),
        prefetch=1,
        grid=(3,),
        in_specs=[any_spec] * 18,
        out_specs=tuple(pl.BlockSpec((n, part, ff), lambda m, *_: (0, 0, m)) for n in (4, 2, 1, 1)),
        scratch=[
            pltpu.VMEM((2, 2 * GROUP, span, width), LOW),
            pltpu.VMEM((width, 2 * length), LOW),
            pltpu.VMEM((3, 2 * length, ff), LOW),
            pltpu.VMEM((width, ff), FULL),
            pltpu.SemaphoreType.DMA((22,)),
        ],
        flops=12 * length * width * ff,
        moved=8 * length * width + 12 * length * ff + 6 * width * ff,
    )(
        place_of,
        *x_blocks[0],
        *x_blocks[1],
        *cot_blocks,
        saved[0][1],
        saved[0][2],
        saved[0][0],
        saved[1][1],
        saved[1][2],
        saved[1][0],
    )
    ff_even, ff_odd = rep_sum(*pieces, ranks)

    block_out = jnp.stack([middles[s] + three(group_terms(*outs[s])) for s in range(seq_count)])

    branches, mids, gain_twos, kv_grads, q_grads = [], [], [], [], []
    for s in range(seq_count):
        keep_term, beside_term, across_term = grads[s][0:3]
        block = whole((span, width))
        grad_middle, branch, out_grad, delta, gain_two = call(
            branch_kernel,
            "branch",
            (
                shape_of((span, width), FULL),
                shape_of((span, width)),
                shape_of((span, per * kv_heads * LANES)),
                shape_of((16, span), FULL),
                shape_of((8, width), FULL),
            ),
            prefetch=1,
            grid=(1,),
            in_specs=[
                block,
                pl.BlockSpec((1, span, width), lambda *_, s=s: (s, 0, 0)),
                pl.BlockSpec((1, span, width), lambda *_: (0, 0, 0)),
                pl.BlockSpec((1, span, width), lambda *_: (0, 0, 0)),
                block,
                whole((8, width)),
            ]
            + [whole((shard, width))] * 4
            + [whole((width, span))],
            out_specs=(block, block, whole((span, per * kv_heads * LANES)), whole((16, span)), whole((8, width))),
            scratch=[pltpu.VMEM((padded, width), LOW)],
            flops=4 * span * width * width,
            moved=20 * span * width + 2 * width * width,
        )(place_of, middles[s], cotangent, keep_term[None], beside_term[None], across_term, gain_rows, *o_blocks, attended[s])
        column = pl.BlockSpec((1, HD // 2, span), lambda *_, s=s: (s, 0, 0))
        halves = pl.BlockSpec((2, span, LANES), lambda h, *_: (0, 0, h))
        grad_q, kv_keep, kv_send = call(
            attend_back_kernel,
            "attend_back",
            (shape_of((width, span)), shape_of((2, span, kw2)), shape_of((2, span, kw2))),
            grid=(kv_heads,),
            in_specs=[pl.BlockSpec((span, per * LANES), lambda h, *_, s=s: (s, h))]
            + [head] * 4
            + [
                pl.BlockSpec((1, length, per * span), lambda h, *_: (h, 0, 0)),
                pl.BlockSpec((span, per * LANES), lambda h, *_: (0, h)),
                whole((16, span)),
                column,
                column,
            ],
            out_specs=(pl.BlockSpec((per * HD, span), lambda h, *_: (h, 0)), halves, halves),
            flops=16 * span * length * width * 2,
            moved=2 * kv_heads * length * per * span + 4 * length * kw2 + 8 * span * width,
        )(queries, *kv_all[s], stats[s], out_grad, delta, cos_cols, sin_cols)
        q_grads.append(grad_q)
        kv_grads.append(group_terms(kv_keep, kv_send))
        branches.append(branch)
        mids.append(grad_middle)
        gain_twos.append(gain_two)

    grown = shard + GAIN_ROWS
    cut = grown // PARTS
    spread_out = lambda columns: (shape_of((2, PARTS, cut, columns)),) * 2
    spread_spec = lambda columns: (whole((2, PARTS, cut, columns)),) * 2
    out_keep, out_send = call(
        out_weight_kernel,
        "out_weights",
        spread_out(width),
        prefetch=1,
        grid=(1,),
        in_specs=[whole((width, span))] * 2 + [whole((span, width))] * 2,
        out_specs=spread_spec(width),
        scratch=[pltpu.VMEM((GROUP, grown, width), FULL)],
        flops=2 * rows * width * width,
        moved=4 * rows * width + 2 * width * width,
    )(place_of, *attended, *branches)

    def owned(keep, send):
        terms = group_terms(keep, send)
        cuts = (slice(0, 4), slice(4, 6), slice(6, 7), slice(7, 8))
        return [three([t[c] for t in terms]).astype(LOW) for c in cuts]

    o_even, o_odd = rep_sum(*owned(out_keep, out_send), ranks)

    block = whole((span, width))
    one = pl.BlockSpec((1, span, kw2), lambda *_: (0, 0, 0))
    kv_term = [one, one, whole((span, kw2))]
    terms = []
    for keep_term, beside_term, across_term in kv_grads:
        terms += [keep_term[None], beside_term[None], across_term]
    total = width + kw2
    grad_tokens, w_keep, w_send = call(
        last_kernel,
        "last",
        (shape_of((rows, width), FULL),) + spread_out(total),
        prefetch=1,
        grid=(1,),
        in_specs=[whole((rows, width)), whole((width, span)), whole((width, span))]
        + kv_term * 2
        + [table, table]
        + [whole((shard, width))] * 4
        + [whole(kv_shard.shape)] * 4
        + [whole((rows, width)), block, block]
        + [whole((8, width))] * 3,
        out_specs=(whole((rows, width)),) + spread_spec(total),
        scratch=[
            pltpu.VMEM((width, width), LOW),
            pltpu.VMEM((width, kw2), LOW),
            pltpu.VMEM((rows, kw2), LOW),
            pltpu.VMEM((GROUP, grown, total), FULL),
        ],
        flops=4 * rows * width * total,
        moved=14 * rows * width + 4 * width * total,
    )(
        place_of,
        norm_low,
        *q_grads,
        *terms,
        cos_rows,
        sin_rows,
        *q_blocks,
        *kv_blocks,
        token_rows,
        *mids,
        gain_rows,
        *gain_twos,
    )
    w_even, w_odd = rep_sum(*owned(w_keep, w_send), ranks)

    grad_gate, grad_up, grad_down = call(
        forward_weights_kernel,
        "forward_weights",
        (shape_of((width, ff), FULL), shape_of((width, ff), FULL), shape_of((ff, width), FULL)),
        prefetch=1,
        grid=(1,),
        in_specs=[whole((4, part, 3 * ff))] * 2,
        out_specs=(whole((width, ff)), whole((width, ff)), whole((ff, width))),
        scratch=[pltpu.VMEM((width, ff), FULL)],
        moved=18 * width * ff,
    )(place_of, ff_even, ff_odd)
    grad_query, grad_key, grad_value, grad_out, grad_gains = call(
        attention_weights_kernel,
        "attention_weights",
        (
            shape_of((shard, width), FULL),
            shape_of((shard, kw), FULL),
            shape_of((shard, kw), FULL),
            shape_of((shard, width), FULL),
            shape_of((8, width), FULL),
        ),
        prefetch=1,
        grid=(1,),
        in_specs=[whole((4, cut, total))] * 2 + [whole((4, cut, width))] * 2,
        out_specs=(
            whole((shard, width)),
            whole((shard, kw)),
            whole((shard, kw)),
            whole((shard, width)),
            whole((8, width)),
        ),
        scratch=[pltpu.VMEM((grown, total), FULL), pltpu.VMEM((grown, width), FULL)],
        moved=6 * shard * (total + width),
    )(place_of, w_even, w_odd, o_even, o_odd)
    own_gains = lax.dynamic_slice(grad_gains, (0, rank_grp * shard), (2, shard))
    return (
        block_out,
        grad_tokens.reshape(tokens.shape),
        grad_query,
        grad_key,
        grad_value,
        grad_out,
        grad_gate,
        grad_up,
        grad_down,
        own_gains[0],
        own_gains[1],
    )


def solution(mesh):
    placed = (
        P("rep", "grp", None),
        P("grp", None),
        P("grp", None),
        P("grp", None),
        P("grp", None),
        P(None, "grp"),
        P(None, "grp"),
        P("grp", None),
        P("grp"),
        P("grp"),
        P("rep", None),
        P("rep", None),
        P("rep", "grp", None),
    )
    return jax.shard_map(
        body,
        mesh=mesh,
        in_specs=placed,
        out_specs=(
            P("rep", "grp", None),
            P("rep", "grp", None),
            P("grp", None),
            P("grp", None),
            P("grp", None),
            P("grp", None),
            P(None, "grp"),
            P(None, "grp"),
            P("grp", None),
            P("grp"),
            P("grp"),
        ),
        check_vma=False,
    )
```

time: 665 us -> 490 us (0.74)
  Pallas kernels: 0 us -> 175 us
  matrix products: 151 us -> 0 us
  other arithmetic: 174 us -> 34.5 us
  local copies, waits for them, and re-layouts: 195 us -> 58.9 us
  waiting for transfers between devices: 85.5 us -> 166 us
    pallas_call x0 -> x17, Pallas kernels: none -> 175 us  [the longest x2 37.3 us: body(): call(forward_back_kernel, 'forward_back', (shape_of((2, span, width)),) *...]
    dot_general x38 -> x0, matrix products: 151 us -> none  [the longest x10 34.4 us: right_dot(): lax.dot_general(left_mat, right_mat, (((1,), (1,)), ((), ())), preferred_...]
    ppermute x56 -> x58, waiting for transfers between devices: 85.5 us -> 166 us  [swap(): return lax.ppermute(values, axis, [(i, i ^ mask) for i in range(count)])]
    gather x25 -> x0, local copies, waits for them, and re-layouts: 79.5 us -> none  [the longest x3 13.6 us: rep_sum(): slots = jnp.take(chunks, jnp.arange(8) ^ low_rank, axis=0)]
    another operation x27 -> x5, other arithmetic: 37 us -> 2.68 us  [the longest x3 2.05 us: body(): jnp.stack([middles[s] + three(group_terms(*outs[s])) for s in range(seq_c...]
    convert_element_type x23 -> x20, other arithmetic: 50.6 us -> 25.7 us  [the longest x8 11.2 us: group_terms(): across = (keep[1].astype(FULL) + beside[1].astype(FULL)).astype(LOW)]
    unnamed x292 -> x107, local copies, waits for them, and re-layouts: 50.1 us -> 30 us
    select_n x10 -> x0, other arithmetic: 19.6 us -> none  [the longest x3 12.5 us: rep_sum(): slots = jnp.take(chunks, jnp.arange(8) ^ low_rank, axis=0)]
  transfers between devices with their start and end apart: 56 -> 58, of which waited for: 13 -> 18; matrix products, arithmetic and copies ran while one was open for 74% -> 16% of each run, Pallas kernels for 0% -> 35%
where the time goes in v2:
time: 490 us; the launch traced here: 480 us
  Pallas kernels  175 us (36%)
  waiting for transfers between devices  166 us (34%)
  local copies, waits for them, and re-layouts  58.9 us (12%)
  starting transfers between devices  44.5 us (9%)
  other arithmetic  34.5 us (7%)
    ppermute x58, waiting for transfers between devices, swap(): return lax.ppermute(values, axis, [(i, i ^ mask) for i in range(count)])  166 us
    ppermute x58, starting transfers between devices, swap(): return lax.ppermute(values, axis, [(i, i ^ mask) for i in range(count)])  44.5 us
    pallas_call x2, Pallas kernels, body(): call(forward_back_kernel, 'forward_back', (shape_of((2, span, width)),) *...  37.3 us
    pallas_call x2, Pallas kernels, body(): call(functools.partial(attend_kernel, s), 'attend', (shape_of((kv_heads,...  33.2 us
    unnamed x107, local copies, waits for them, and re-layouts  30 us
    pallas_call x2, Pallas kernels, body(): call(attend_back_kernel, 'attend_back', (shape_of((width, span)), shape_o...  24.7 us
    pallas_call x1, Pallas kernels, body(): call(weight_kernel, 'weights', tuple((shape_of((n, part, 3 * ff)) for n i...  20.8 us
    pallas_call x1, Pallas kernels, body(): call(last_kernel, 'last', (shape_of((rows, width), FULL),) + spread_out(t...  12.6 us
  transfers between devices with their start and end apart: 58, of which 18 were waited for; matrix products, arithmetic and copies ran while one was open for 16% of the time, Pallas kernels for 35%

profile of v2, /device:TPU:0, one launch (start us, length us, event | category | flops | bytes accessed | tf_op | source)
XLA Modules:
  0.0 480.2 jit_solution(12388855728910979107)
XLA Ops:
  4.6 3.2 collective-permute-start.1
  8.2 1.7 collective-permute-start.10
  10.9 5.3 %collective-permute-done.1.b2.refs_17_ = bf16[256,640]{1,0:T(8,128)(2,1)S(1)} collective-permute-done((bf16[256,640]{1,0:T(8,128)(2,1)S(1)}, bf16[256,640]{1,0:T(8,128)(2,1)S(1)}, u32[]{:S(2)}, u32[]{:S(2)}) %collective-permute-start.1) | collective-permute-done | bytes 327712 | tf_op jit(solution)/shard_map/ppermute | solution.py:37
  21.4 4.6 keys_values.1
  26.0 2.1 collective-permute-start.21
  28.3 1.8 collective-permute-start.7
  30.1 7.2 %collective-permute-done.10.b2 = bf16[240,960]{1,0:T(8,128)(2,1)S(1)} collective-permute-done((bf16[240,960]{1,0:T(8,128)(2,1)}, bf16[240,960]{1,0:T(8,128)(2,1)S(1)}, u32[]{:S(2)}, u32[]{:S(2)}) %collective-permute-start.10) | collective-permute-done | bytes 460832 | tf_op jit(solution)/shard_map/ppermute | solution.py:37
  37.3 7.0 %collective-permute-done.21.b2 = bf16[256,640]{1,0:T(8,128)(2,1)S(1)} collective-permute-done((bf16[256,640]{1,0:T(8,128)(2,1)}, bf16[256,640]{1,0:T(8,128)(2,1)S(1)}, u32[]{:S(2)}, u32[]{:S(2)}) %collective-permute-start.21) | collective-permute-done | bytes 327712 | tf_op jit(solution)/shard_map/ppermute | solution.py:37
  44.9 26.7 %collective-permute-done.7.b2 = bf16[256,640]{1,0:T(8,128)(2,1)S(1)} collective-permute-done((bf16[256,640]{1,0:T(8,128)(2,1)}, bf16[256,640]{1,0:T(8,128)(2,1)S(1)}, u32[]{:S(2)}, u32[]{:S(2)}) %collective-permute-start.7) | collective-permute-done | bytes 327712 | tf_op jit(solution)/shard_map/ppermute | solution.py:37
  71.6 6.0 %queries.1.q_ref = bf16[512,1920]{1,0:T(8,128)(2,1)} custom-call(s32[2]{0:T(128)} %pad_add_fusion.ranks, bf16[512,960]{1,0:T(8,128)(2,1)} %get-tuple-element.70.norm_ref.refs_0_, bf16[240,960]{1,0:T(8,128)(2,1)} %refs_11_.1, bf16[240,960]{1,0:T(8,128)(2,1)} %collective-permute-done.3.b1.refs_12_, bf16[240,960]{1,0:T(8,128)(2,1)} %collective-permute-done.4.b2.refs_13_, ...), custom_call_target="tpu_custom_call" | custom-call | flops 1006632960 | bytes 4792320 | tf_op jit(solution)/shard_map/queries/pallas_call | solution.py:558
  78.9 16.5 %attend.3 = (bf16[5,1024,768]{2,1,0:T(8,128)(2,1)}, bf16[960,256]{1,0:T(8,128)(2,1)}) custom-call(s32[2]{0:T(128)} %pad_add_fusion.ranks, s32[2,4]{1,0:T(2,128)} %order.3, s32[2,2]{1,0:T(2,128)} %starts.3, bf16[512,1920]{1,0:T(8,128)(2,1)} %queries.1.q_ref, bf16[256,640]{1,0:T(8,128)(2,1)} %get-tuple-element.78.b0, bf16[256,640]{1,0:T(8,128)(2,1)} %copy-done.39, ...), custom_call_target="tpu_custom_call" | custom-call | flops 4026531840 | bytes 10649600 | tf_op jit(solution)/shard_map/attend/pallas_call | solution.py:576
  96.8 4.5 middle.3
  101.3 1.7 collective-permute-start.24
  104.5 16.7 %attend.2 = (bf16[5,1024,768]{2,1,0:T(8,128)(2,1)}, bf16[960,256]{1,0:T(8,128)(2,1)}) custom-call(s32[2]{0:T(128)} %pad_add_fusion.ranks, s32[2,4]{1,0:T(2,128)} %order.3, s32[2,2]{1,0:T(2,128)} %starts.3, bf16[512,1920]{1,0:T(8,128)(2,1)} %queries.1.q_ref, bf16[256,640]{1,0:T(8,128)(2,1)} %get-tuple-element.71.b0, bf16[256,640]{1,0:T(8,128)(2,1)} %copy-done.38, ...), custom_call_target="tpu_custom_call" | custom-call | flops 4026531840 | bytes 10649600 | tf_op jit(solution)/shard_map/attend/pallas_call | solution.py:576
  121.3 4.4 middle.2
  127.8 1.9 copy.90.wd_ref
  132.0 2.3 copy.87.c1.refs_9_
  134.3 5.3 %collective-permute-done.13.x2.refs_2_ = bf16[256,960]{1,0:T(8,128)(2,1)} collective-permute-done((bf16[256,960]{1,0:T(8,128)(2,1)}, bf16[256,960]{1,0:T(8,128)(2,1)}, u32[]{:S(2)}, u32[]{:S(2)}) %collective-permute-start.13) | collective-permute-done | bytes 491552 | tf_op jit(solution)/shard_map/ppermute | solution.py:37
  139.7 2.3 copy.89.c3.refs_11_
  142.0 18.5 %forward_back.3 = (bf16[2,256,960]{2,1,0:T(8,128)(2,1)}, bf16[2,256,960]{2,1,0:T(8,128)(2,1)}, bf16[2,256,960]{2,1,0:T(8,128)(2,1)}, bf16[2,256,960]{2,1,0:T(8,1...) custom-call(bf16[256,960]{1,0:T(8,128)(2,1)} %get-tuple-element.81.x0.refs_4_, ...), custom_call_target="tpu_custom_call" | custom-call | flops 7549747200 | bytes 15482880 | tf_op jit(solution)/shard_map/forward_back/pallas_call | solution.py:615
  160.4 2.2 copy.107
  164.8 18.8 %forward_back.2 = (bf16[2,256,960]{2,1,0:T(8,128)(2,1)}, bf16[2,256,960]{2,1,0:T(8,128)(2,1)}, bf16[2,256,960]{2,1,0:T(8,128)(2,1)}, bf16[2,256,960]{2,1,0:T(8,1...) custom-call(bf16[256,960]{1,0:T(8,128)(2,1)} %get-tuple-element.75.x0.refs_0_, ...), custom_call_target="tpu_custom_call" | custom-call | flops 7549747200 | bytes 15482880 | tf_op jit(solution)/shard_map/forward_back/pallas_call | solution.py:615
  184.4 1.9 slice.251.e0
  187.6 20.8 %weights.1 = (bf16[4,120,1920]{2,1,0:T(8,128)(2,1)}, bf16[2,120,1920]{2,1,0:T(8,128)(2,1)}, bf16[1,120,1920]{2,1,0:T(8,128)(2,1)}, bf16[1,120,1920]{2,1,0:T(8,128)(2,1)}) custom-call(s32[2]{0:T(128)} %pad_add_fusion.ranks, bf16[256,960]{1,0:T(8,128)(2,1)} %get-tuple-element.75.x0.refs_0_, bf16[256,960]{1,0:T(8,128)(2,1)} %copy-done.33, ...), custom_call_target="tpu_custom_call" | custom-call | flops 7549747200 | bytes 19415040 | tf_op jit(solution)/shard_map/weights/pallas_call | solution.py:633
  212.5 2.0 fusion.10
  220.3 9.3 %collective-permute-done.31.e2 = bf16[256,960]{1,0:T(8,128)(2,1)} collective-permute-done((bf16[256,960]{1,0:T(8,128)(2,1)}, bf16[256,960]{1,0:T(8,128)(2,1)}, u32[]{:S(2)}, u32[]{:S(2)}) %collective-permute-start.31) | collective-permute-done | bytes 491552 | tf_op jit(solution)/shard_map/ppermute | solution.py:37
  229.6 5.8 %branch.3 = (f32[256,960]{1,0:T(8,128)}, bf16[256,960]{1,0:T(8,128)(2,1)}, bf16[256,1920]{1,0:T(8,128)(2,1)}, f32[16,256]{1,0:T(8,128)}, f32[8,960]{1,0:T(8,128)}) custom-call(s32[2]{0:T(128)} %pad_add_fusion.ranks, f32[256,960]{1,0:T(8,128)} %get-tuple-element.80.mid_ref, bf16[2,256,960]{2,1,0:T(8,128)(2,1)} %copy.86.c0.cot_ref.refs_8_, ...), custom_call_target="tpu_custom_call" | custom-call | flops 943718400 | bytes 6758400 | tf_op jit(solution)/shard_map/branch/pallas_call | solution.py:670
  235.4 12.3 %attend_back.3 = (bf16[960,256]{1,0:T(8,128)(2,1)}, bf16[2,256,640]{2,1,0:T(8,128)(2,1)}, bf16[2,256,640]{2,1,0:T(8,128)(2,1)}) custom-call(bf16[512,1920]{1,0:T(8,128)(2,1)} %queries.1.q_ref, bf16[256,640]{1,0:T(8,128)(2,1)} %get-tuple-element.78.b0, bf16[256,640]{1,0:T(8,128)(2,1)} %copy-done.39, bf16[256,640]{1,0:T(8,128)(2,1)} %copy-done.37, ...), custom_call_target="tpu_custom_call" | custom-call | flops 8053063680 | bytes 12451840 | tf_op jit(solution)/shard_map/attend_back/pallas_call | solution.py:699
  248.6 5.8 %branch.2 = (f32[256,960]{1,0:T(8,128)}, bf16[256,960]{1,0:T(8,128)(2,1)}, bf16[256,1920]{1,0:T(8,128)(2,1)}, f32[16,256]{1,0:T(8,128)}, f32[8,960]{1,0:T(8,128)}) custom-call(s32[2]{0:T(128)} %pad_add_fusion.ranks, f32[256,960]{1,0:T(8,128)} %get-tuple-element.74.mid_ref, bf16[2,256,960]{2,1,0:T(8,128)(2,1)} %copy.86.c0.cot_ref.refs_8_, ...), custom_call_target="tpu_custom_call" | custom-call | flops 943718400 | bytes 6758400 | tf_op jit(solution)/shard_map/branch/pallas_call | solution.py:670
  254.4 12.4 %attend_back.2 = (bf16[960,256]{1,0:T(8,128)(2,1)}, bf16[2,256,640]{2,1,0:T(8,128)(2,1)}, bf16[2,256,640]{2,1,0:T(8,128)(2,1)}) custom-call(bf16[512,1920]{1,0:T(8,128)(2,1)} %queries.1.q_ref, bf16[256,640]{1,0:T(8,128)(2,1)} %get-tuple-element.71.b0, bf16[256,640]{1,0:T(8,128)(2,1)} %copy-done.38, bf16[256,640]{1,0:T(8,128)(2,1)} %copy-done.36, ...), custom_call_target="tpu_custom_call" | custom-call | flops 8053063680 | bytes 12451840 | tf_op jit(solution)/shard_map/attend_back/pallas_call | solution.py:699
  268.6 2.5 copy.91
  273.1 4.7 out_weights.1
  283.5 1.7 slice.322.refs_7_
  285.2 1.7 slice.320.refs_4_
  286.9 2.7 collective-permute-done.35.refs_8_
  291.3 4.8 %collective-permute-done.33.refs_5_ = bf16[256,640]{1,0:T(8,128)(2,1)S(1)} collective-permute-done((bf16[256,640]{1,0:T(8,128)(2,1)S(1)}, bf16[256,640]{1,0:T(8,128)(2,1)S(1)}, u32[]{:S(2)}, u32[]{:S(2)}) %collective-permute-start.33) | collective-permute-done | bytes 327712 | tf_op jit(solution)/shard_map/ppermute | solution.py:37
  296.8 12.6 %last.1 = (f32[512,960]{1,0:T(8,128)}, bf16[2,8,32,1600]{3,2,1,0:T(8,128)(2,1)}, bf16[2,8,32,1600]{3,2,1,0:T(8,128)(2,1)}) custom-call(s32[2]{0:T(128)} %pad_add_fusion.ranks, bf16[512,960]{1,0:T(8,128)(2,1)} %get-tuple-element.70.norm_ref.refs_0_, bf16[960,256]{1,0:T(8,128)(2,1)} %get-tuple-element.89.refs_1_, bf16[960,256]{1,0:T(8,128)(2,1)} %get-tuple-element.95.refs_2_, ...), custom_call_target="tpu_custom_call" | custom-call | flops 3145728000 | bytes 13025280 | tf_op jit(solution)/shard_map/last/pallas_call | solution.py:754
  317.2 2.3 add_convert_fusion.8
  319.4 2.6 collective-permute-start.54
  322.0 15.8 %collective-permute-done.45 = bf16[8,32,960]{2,1,0:T(8,128)(2,1)S(1)} collective-permute-done((bf16[8,32,960]{2,1,0:T(8,128)(2,1)S(1)}, bf16[8,32,960]{2,1,0:T(8,128)(2,1)S(1)}, u32[]{:S(2)}, u32[]{:S(2)}) %collective-permute-start.45) | collective-permute-done | bytes 491552 | tf_op jit(solution)/shard_map/ppermute | solution.py:37
  338.6 1.9 fusion.12
  340.9 2.3 fusion.4
  344.9 1.8 collective-permute-start.19
  346.7 1.9 collective-permute-done.46
  351.2 1.7 add_convert_fusion.7
  352.9 2.7 collective-permute-start.55
  355.6 9.8 %collective-permute-done.37 = bf16[8,32,1600]{2,1,0:T(8,128)(2,1)} collective-permute-done((bf16[8,32,1600]{2,1,0:T(8,128)(2,1)}, bf16[8,32,1600]{2,1,0:T(8,128)(2,1)}, u32[]{:S(2)}, u32[]{:S(2)}) %collective-permute-start.37) | collective-permute-done | bytes 819232 | tf_op jit(solution)/shard_map/ppermute | solution.py:37
  369.2 2.6 collective-permute-start.48
  371.9 5.1 %collective-permute-done.55 = bf16[1,120,1920]{2,1,0:T(8,128)(2,1)S(1)} collective-permute-done((bf16[1,120,1920]{2,1,0:T(8,128)(2,1)S(1)}, bf16[1,120,1920]{2,1,0:T(8,128)(2,1)S(1)}, u32[]{:S(2)}, u32[]{:S(2)}) %collective-permute-start.55) | collective-permute-done | bytes 460832 | tf_op jit(solution)/shard_map/ppermute | solution.py:37
  378.3 2.1 collective-permute-start.39
  382.5 20.9 %collective-permute-done.39 = bf16[2,32,1600]{2,1,0:T(8,128)(2,1)S(1)} collective-permute-done((bf16[2,32,1600]{2,1,0:T(8,128)(2,1)S(1)}, bf16[2,32,1600]{2,1,0:T(8,128)(2,1)S(1)}, u32[]{:S(2)}, u32[]{:S(2)}) %collective-permute-start.39) | collective-permute-done | bytes 204832 | tf_op jit(solution)/shard_map/ppermute | solution.py:37
  405.1 1.7 pad_maximum_fusion.1.even
  407.2 5.0 %collective-permute-done.40 = bf16[1,32,1600]{2,1,0:T(8,128)(2,1)S(1)} collective-permute-done((bf16[1,32,1600]{2,1,0:T(8,128)(2,1)S(1)}, bf16[1,32,1600]{2,1,0:T(8,128)(2,1)S(1)}, u32[]{:S(2)}, u32[]{:S(2)}) %collective-permute-start.40) | collective-permute-done | bytes 102432 | tf_op jit(solution)/shard_map/ppermute | solution.py:37
  414.5 4.5 collective-permute-done.41
  420.8 4.2 collective-permute-done.42
  425.8 1.7 copy.115
  427.5 2.8 copy.116
  430.4 25.3 %collective-permute-done.51.odd_o = bf16[4,32,960]{2,1,0:T(8,128)(2,1)S(1)} collective-permute-done((bf16[4,32,960]{2,1,0:T(8,128)(2,1)S(1)}, bf16[4,32,960]{2,1,0:T(8,128)(2,1)S(1)}, u32[]{:S(2)}, u32[]{:S(2)}) %collective-permute-start.51) | collective-permute-done | bytes 245792 | tf_op jit(solution)/shard_map/ppermute | solution.py:37
  455.7 4.8 %collective-permute-done.43.odd = bf16[4,32,1600]{2,1,0:T(8,128)(2,1)S(1)} collective-permute-done((bf16[4,32,1600]{2,1,0:T(8,128)(2,1)S(1)}, bf16[4,32,1600]{2,1,0:T(8,128)(2,1)S(1)}, u32[]{:S(2)}, u32[]{:S(2)}) %collective-permute-start.43) | collective-permute-done | bytes 409632 | tf_op jit(solution)/shard_map/ppermute | solution.py:37
  461.3 3.9 attention_weights.1
  465.2 1.9 copy.117
  467.1 1.9 copy.118
  470.4 6.4 %forward_weights.1 = (f32[960,640]{1,0:T(8,128)}, f32[960,640]{1,0:T(8,128)}, f32[640,960]{1,0:T(8,128)}) custom-call(s32[2]{0:T(128)} %pad_add_fusion.ranks, bf16[4,120,1920]{2,1,0:T(8,128)(2,1)} %pad_maximum_fusion.1.even, bf16[4,120,1920]{2,1,0:T(8,128)(2,1)} %collective-permute-done.57.odd), custom_call_target="tpu_custom_call" | custom-call | bytes 11059200 | tf_op jit(solution)/shard_map/forward_weights/pallas_call | solution.py:792
  476.8 3.2 copy.119
  (236 shorter events, 76.1 us)
Async XLA Ops:
  4.6 11.7 %collective-permute-start.1 = (bf16[256,640]{1,0:T(8,128)(2,1)S(1)}, bf16[256,640]{1,0:T(8,128)(2,1)S(1)}, u32[]{:S(2)}, u32[]{:S(2)}) collective-permute-start(bf16[256,640]{1,0:T(8,128)(2,1)S(1)} %fusion.14.b0.refs_15_), channel_id=1, source_target_pairs={{0,16},{8,24},{16,0},{24,8},{1,17},{9,25},{17,1},{25,9},{2,18},{10... | collective-permute-start | bytes 983048 | tf_op jit(solution)/shard_map/ppermute | solution.py:37
  7.7 12.8 %collective-permute-start = (bf16[256,640]{1,0:T(8,128)(2,1)S(1)}, bf16[256,640]{1,0:T(8,128)(2,1)S(1)}, u32[]{:S(2)}, u32[]{:S(2)}) collective-permute-start(bf16[256,640]{1,0:T(8,128)(2,1)S(1)} %fusion.14.b0.refs_15_), channel_id=1, source_target_pairs={{0,8},{8,0},{16,24},{24,16},{1,9},{9,1},{17,25},{25,17},{2,10},{10... | collective-permute-start | bytes 983048 | tf_op jit(solution)/shard_map/ppermute | solution.py:37
  7.7 20.4 %collective-permute-start.4 = (bf16[240,960]{1,0:T(8,128)(2,1)}, bf16[240,960]{1,0:T(8,128)(2,1)}, u32[]{:S(2)}, u32[]{:S(2)}) collective-permute-start(bf16[240,960]{1,0:T(8,128)(2,1)} %refs_11_.1), channel_id=1, source_target_pairs={{0,16},{8,24},{16,0},{24,8},{1,17},{9,25},{17,1},{25,9},{2,18},{10... | collective-permute-start | bytes 1382408 | tf_op jit(solution)/shard_map/ppermute | solution.py:37
  7.9 20.4 %collective-permute-start.3 = (bf16[240,960]{1,0:T(8,128)(2,1)}, bf16[240,960]{1,0:T(8,128)(2,1)}, u32[]{:S(2)}, u32[]{:S(2)}) collective-permute-start(bf16[240,960]{1,0:T(8,128)(2,1)} %refs_11_.1), channel_id=1, source_target_pairs={{0,8},{8,0},{16,24},{24,16},{1,9},{9,1},{17,25},{25,17},{2,10},{10... | collective-permute-start | bytes 1382408 | tf_op jit(solution)/shard_map/ppermute | solution.py:37
  8.2 29.1 %collective-permute-start.10 = (bf16[240,960]{1,0:T(8,128)(2,1)}, bf16[240,960]{1,0:T(8,128)(2,1)S(1)}, u32[]{:S(2)}, u32[]{:S(2)}) collective-permute-start(bf16[240,960]{1,0:T(8,128)(2,1)} %b0.9), channel_id=1, source_target_pairs={{0,16},{8,24},{16,0},{24,8},{1,17},{9,25},{17,1},{25,9},{2,18},{10... | collective-permute-start | bytes 1382408 | tf_op jit(solution)/shard_map/ppermute | solution.py:37
  16.3 4.2 collective-permute-start.2
  19.9 24.5 %copy-start = (bf16[240,960]{1,0:T(8,128)(2,1)S(1)}, bf16[240,960]{1,0:T(8,128)(2,1)}, u32[]{:S(2)}) copy-start(bf16[240,960]{1,0:T(8,128)(2,1)} %b0.9) | copy-start | bytes 1382404
  26.0 18.4 %collective-permute-start.21 = (bf16[256,640]{1,0:T(8,128)(2,1)}, bf16[256,640]{1,0:T(8,128)(2,1)S(1)}, u32[]{:S(2)}, u32[]{:S(2)}) collective-permute-start(bf16[256,640]{1,0:T(8,128)(2,1)} %get-tuple-element.78.b0), channel_id=1, source_target_pairs={{0,16},{8,24},{16,0},{24,8},{1,17},{9,25},{17,1},{25,9},{2,18},{10... | collective-permute-start | bytes 983048 | tf_op jit(solution)/shard_map/ppermute | solution.py:37
  28.0 67.5 %collective-permute-start.16 = (bf16[2,256,960]{1,2,0:T(8,128)(2,1)S(1)}, bf16[2,256,960]{1,2,0:T(8,128)(2,1)S(1)}, u32[]{:S(2)}, u32[]{:S(2)}) collective-permute-start(bf16[2,256,960]{1,2,0:T(8,128)(2,1)S(1)} %copy-done.20), channel_id=1, source_target_pairs={{0,16},{8,24},{16,0},{24,8},{1,17},{9,25},{17,1},{25,9},{2,18},{10... | collective-permute-start | bytes 2949128 | tf_op jit(solution)/shard_map/ppermute | solution.py:37
  28.1 16.3 %collective-permute-start.5 = (bf16[240,960]{1,0:T(8,128)(2,1)}, bf16[240,960]{1,0:T(8,128)(2,1)S(1)}, u32[]{:S(2)}, u32[]{:S(2)}) collective-permute-start(bf16[240,960]{1,0:T(8,128)(2,1)} %collective-permute-done.4.b2.refs_13_), channel_id=1, source_target_pairs={{0,8},{8,0},{16,24},{24,16},{1,9},{9,1},{17,25},{25,17},{2,10},{10... | collective-permute-start | bytes 1382408 | tf_op jit(solution)/shard_map/ppermute | solution.py:37
  28.3 43.3 %collective-permute-start.7 = (bf16[256,640]{1,0:T(8,128)(2,1)}, bf16[256,640]{1,0:T(8,128)(2,1)S(1)}, u32[]{:S(2)}, u32[]{:S(2)}) collective-permute-start(bf16[256,640]{1,0:T(8,128)(2,1)} %get-tuple-element.71.b0), channel_id=1, source_target_pairs={{0,16},{8,24},{16,0},{24,8},{1,17},{9,25},{17,1},{25,9},{2,18},{10... | collective-permute-start | bytes 983048 | tf_op jit(solution)/shard_map/ppermute | solution.py:37
  37.3 40.3 %copy-start.1 = (bf16[240,960]{1,0:T(8,128)(2,1)}, bf16[240,960]{1,0:T(8,128)(2,1)S(1)}, u32[]{:S(2)}) copy-start(bf16[240,960]{1,0:T(8,128)(2,1)S(1)} %collective-permute-done.10.b2) | copy-start | bytes 1382404
  37.3 40.3 %collective-permute-start.20 = (bf16[256,640]{1,0:T(8,128)(2,1)}, bf16[256,640]{1,0:T(8,128)(2,1)S(1)}, u32[]{:S(2)}, u32[]{:S(2)}) collective-permute-start(bf16[256,640]{1,0:T(8,128)(2,1)} %get-tuple-element.78.b0), channel_id=1, source_target_pairs={{0,8},{8,0},{16,24},{24,16},{1,9},{9,1},{17,25},{25,17},{2,10},{10... | collective-permute-start | bytes 983048 | tf_op jit(solution)/shard_map/ppermute | solution.py:37
  44.4 34.0 %copy-start.37 = (bf16[256,640]{1,0:T(8,128)(2,1)}, bf16[256,640]{1,0:T(8,128)(2,1)S(1)}, u32[]{:S(2)}) copy-start(bf16[256,640]{1,0:T(8,128)(2,1)S(1)} %collective-permute-done.21.b2) | copy-start | bytes 983044
  44.4 33.8 %collective-permute-start.22 = (bf16[256,640]{1,0:T(8,128)(2,1)S(1)}, bf16[256,640]{1,0:T(8,128)(2,1)S(1)}, u32[]{:S(2)}, u32[]{:S(2)}) collective-permute-start(bf16[256,640]{1,0:T(8,128)(2,1)S(1)} %collective-permute-done.21.b2), channel_id=1, source_target_pairs={{0,8},{8,0},{16,24},{24,16},{1,9},{9,1},{17,25},{25,17},{2,10},{10... | collective-permute-start | bytes 983048 | tf_op jit(solution)/shard_map/ppermute | solution.py:37
  44.4 27.2 %copy-start.26 = (bf16[240,960]{1,0:T(8,128)(2,1)}, bf16[240,960]{1,0:T(8,128)(2,1)S(1)}, u32[]{:S(2)}) copy-start(bf16[240,960]{1,0:T(8,128)(2,1)S(1)} %collective-permute-done.5.b3.refs_14_) | copy-start | bytes 1382404
  44.4 51.0 %collective-permute-start.9 = (bf16[240,960]{1,0:T(8,128)(2,1)S(1)}, bf16[240,960]{1,0:T(8,128)(2,1)S(1)}, u32[]{:S(2)}, u32[]{:S(2)}) collective-permute-start(bf16[240,960]{1,0:T(8,128)(2,1)S(1)} %copy-done), channel_id=1, source_target_pairs={{0,8},{8,0},{16,24},{24,16},{1,9},{9,1},{17,25},{25,17},{2,10},{10... | collective-permute-start | bytes 1382408 | tf_op jit(solution)/shard_map/ppermute | solution.py:37
  71.6 24.4 %collective-permute-start.11 = (bf16[240,960]{1,0:T(8,128)(2,1)S(1)}, bf16[240,960]{1,0:T(8,128)(2,1)S(1)}, u32[]{:S(2)}, u32[]{:S(2)}) collective-permute-start(bf16[240,960]{1,0:T(8,128)(2,1)S(1)} %collective-permute-done.10.b2), channel_id=1, source_target_pairs={{0,8},{8,0},{16,24},{24,16},{1,9},{9,1},{17,25},{25,17},{2,10},{10... | collective-permute-start | bytes 1382408 | tf_op jit(solution)/shard_map/ppermute | solution.py:37
  77.6 25.4 %collective-permute-start.6 = (bf16[256,640]{1,0:T(8,128)(2,1)S(1)}, bf16[256,640]{1,0:T(8,128)(2,1)S(1)}, u32[]{:S(2)}, u32[]{:S(2)}) collective-permute-start(bf16[256,640]{1,0:T(8,128)(2,1)S(1)} %copy-done.35), channel_id=1, source_target_pairs={{0,8},{8,0},{16,24},{24,16},{1,9},{9,1},{17,25},{25,17},{2,10},{10... | collective-permute-start | bytes 983048 | tf_op jit(solution)/shard_map/ppermute | solution.py:37
  78.2 24.8 %collective-permute-start.8 = (bf16[256,640]{1,0:T(8,128)(2,1)S(1)}, bf16[256,640]{1,0:T(8,128)(2,1)S(1)}, u32[]{:S(2)}, u32[]{:S(2)}) collective-permute-start(bf16[256,640]{1,0:T(8,128)(2,1)S(1)} %collective-permute-done.7.b2), channel_id=1, source_target_pairs={{0,8},{8,0},{16,24},{24,16},{1,9},{9,1},{17,25},{25,17},{2,10},{10... | collective-permute-start | bytes 983048 | tf_op jit(solution)/shard_map/ppermute | solution.py:37
  95.4 36.6 %collective-permute-start.15 = (bf16[2,256,960]{1,2,0:T(8,128)(2,1)S(1)}, bf16[2,256,960]{1,2,0:T(8,128)(2,1)}, u32[]{:S(2)}, u32[]{:S(2)}) collective-permute-start(bf16[2,256,960]{1,2,0:T(8,128)(2,1)S(1)} %copy-done.20), channel_id=1, source_target_pairs={{0,8},{8,0},{16,24},{24,16},{1,9},{9,1},{17,25},{25,17},{2,10},{10... | collective-permute-start | bytes 2949128 | tf_op jit(solution)/shard_map/ppermute | solution.py:37
  95.5 44.1 %collective-permute-start.17 = (bf16[2,256,960]{1,2,0:T(8,128)(2,1)S(1)}, bf16[2,256,960]{1,2,0:T(8,128)(2,1)}, u32[]{:S(2)}, u32[]{:S(2)}) collective-permute-start(bf16[2,256,960]{1,2,0:T(8,128)(2,1)S(1)} %collective-permute-done.16), channel_id=1, source_target_pairs={{0,8},{8,0},{16,24},{24,16},{1,9},{9,1},{17,25},{25,17},{2,10},{10... | collective-permute-start | bytes 2949128 | tf_op jit(solution)/shard_map/ppermute | solution.py:37
  101.3 24.7 %collective-permute-start.24 = (bf16[256,960]{1,0:T(8,128)(2,1)}, bf16[256,960]{1,0:T(8,128)(2,1)}, u32[]{:S(2)}, u32[]{:S(2)}) collective-permute-start(bf16[256,960]{1,0:T(8,128)(2,1)} %get-tuple-element.81.x0.refs_4_), channel_id=1, source_target_pairs={{0,16},{8,24},{16,0},{24,8},{1,17},{9,25},{17,1},{25,9},{2,18},{10... | collective-permute-start | bytes 1474568 | tf_op jit(solution)/shard_map/ppermute | solution.py:37
  125.7 14.0 %collective-permute-start.13 = (bf16[256,960]{1,0:T(8,128)(2,1)}, bf16[256,960]{1,0:T(8,128)(2,1)}, u32[]{:S(2)}, u32[]{:S(2)}) collective-permute-start(bf16[256,960]{1,0:T(8,128)(2,1)} %get-tuple-element.75.x0.refs_0_), channel_id=1, source_target_pairs={{0,16},{8,24},{16,0},{24,8},{1,17},{9,25},{17,1},{25,9},{2,18},{10... | collective-permute-start | bytes 1474568 | tf_op jit(solution)/shard_map/ppermute | solution.py:37
  126.0 16.0 %collective-permute-start.23 = (bf16[256,960]{1,0:T(8,128)(2,1)}, bf16[256,960]{1,0:T(8,128)(2,1)}, u32[]{:S(2)}, u32[]{:S(2)}) collective-permute-start(bf16[256,960]{1,0:T(8,128)(2,1)} %get-tuple-element.81.x0.refs_4_), channel_id=1, source_target_pairs={{0,8},{8,0},{16,24},{24,16},{1,9},{9,1},{17,25},{25,17},{2,10},{10... | collective-permute-start | bytes 1474568 | tf_op jit(solution)/shard_map/ppermute | solution.py:37
  126.0 16.0 %collective-permute-start.25 = (bf16[256,960]{1,0:T(8,128)(2,1)}, bf16[256,960]{1,0:T(8,128)(2,1)}, u32[]{:S(2)}, u32[]{:S(2)}) collective-permute-start(bf16[256,960]{1,0:T(8,128)(2,1)} %collective-permute-done.24.x2.refs_6_), channel_id=1, source_target_pairs={{0,8},{8,0},{16,24},{24,16},{1,9},{9,1},{17,25},{25,17},{2,10},{10... | collective-permute-start | bytes 1474568 | tf_op jit(solution)/shard_map/ppermute | solution.py:37
  134.3 28.9 %collective-permute-start.12 = (bf16[256,960]{1,0:T(8,128)(2,1)S(1)}, bf16[256,960]{1,0:T(8,128)(2,1)S(1)}, u32[]{:S(2)}, u32[]{:S(2)}) collective-permute-start(bf16[256,960]{1,0:T(8,128)(2,1)S(1)} %copy-done.32), channel_id=1, source_target_pairs={{0,8},{8,0},{16,24},{24,16},{1,9},{9,1},{17,25},{25,17},{2,10},{10... | collective-permute-start | bytes 1474568 | tf_op jit(solution)/shard_map/ppermute | solution.py:37
  139.6 23.5 %collective-permute-start.14 = (bf16[256,960]{1,0:T(8,128)(2,1)}, bf16[256,960]{1,0:T(8,128)(2,1)S(1)}, u32[]{:S(2)}, u32[]{:S(2)}) collective-permute-start(bf16[256,960]{1,0:T(8,128)(2,1)} %collective-permute-done.13.x2.refs_2_), channel_id=1, source_target_pairs={{0,8},{8,0},{16,24},{24,16},{1,9},{9,1},{17,25},{25,17},{2,10},{10... | collective-permute-start | bytes 1474568 | tf_op jit(solution)/shard_map/ppermute | solution.py:37
  162.7 47.3 %collective-permute-start.30 = (bf16[2,256,960]{1,2,0:T(8,128)(2,1)}, bf16[2,256,960]{1,2,0:T(8,128)(2,1)}, u32[]{:S(2)}, u32[]{:S(2)}) collective-permute-start(bf16[2,256,960]{1,2,0:T(8,128)(2,1)} %copy.107), channel_id=1, source_target_pairs={{0,8},{8,0},{16,24},{24,16},{1,9},{9,1},{17,25},{25,17},{2,10},{10... | collective-permute-start | bytes 2949128 | tf_op jit(solution)/shard_map/ppermute | solution.py:37
  187.6 27.4 %collective-permute-start.28 = (bf16[2,256,960]{1,2,0:T(8,128)(2,1)}, bf16[2,256,960]{1,2,0:T(8,128)(2,1)}, u32[]{:S(2)}, u32[]{:S(2)}) collective-permute-start(bf16[2,256,960]{1,2,0:T(8,128)(2,1)} %copy.103), channel_id=1, source_target_pairs={{0,8},{8,0},{16,24},{24,16},{1,9},{9,1},{17,25},{25,17},{2,10},{10... | collective-permute-start | bytes 2949128 | tf_op jit(solution)/shard_map/ppermute | solution.py:37
  208.4 72.3 %collective-permute-start.52 = (bf16[4,120,1920]{2,1,0:T(8,128)(2,1)}, bf16[4,120,1920]{2,1,0:T(8,128)(2,1)S(1)}, u32[]{:S(2)}, u32[]{:S(2)}) collective-permute-start(bf16[4,120,1920]{2,1,0:T(8,128)(2,1)} %get-tuple-element.122), channel_id=1, source_target_pairs={{0,1},{1,0},{2,3},{3,2},{4,5},{5,4},{6,7},{7,6},{8,9},{9,8},{10,11... | collective-permute-start | bytes 5529608 | tf_op jit(solution)/shard_map/ppermute | solution.py:37
  214.5 15.1 %collective-permute-start.31 = (bf16[256,960]{1,0:T(8,128)(2,1)}, bf16[256,960]{1,0:T(8,128)(2,1)}, u32[]{:S(2)}, u32[]{:S(2)}) collective-permute-start(bf16[256,960]{1,0:T(8,128)(2,1)} %fusion.10), channel_id=1, source_target_pairs={{0,16},{8,24},{16,0},{24,8},{1,17},{9,25},{17,1},{25,9},{2,18},{10... | collective-permute-start | bytes 1474568 | tf_op jit(solution)/shard_map/ppermute | solution.py:37
  218.7 29.0 %collective-permute-start.29 = (bf16[256,960]{1,0:T(8,128)(2,1)S(1)}, bf16[256,960]{1,0:T(8,128)(2,1)S(1)}, u32[]{:S(2)}, u32[]{:S(2)}) collective-permute-start(bf16[256,960]{1,0:T(8,128)(2,1)S(1)} %fusion.9), channel_id=1, source_target_pairs={{0,16},{8,24},{16,0},{24,8},{1,17},{9,25},{17,1},{25,9},{2,18},{10... | collective-permute-start | bytes 1474568 | tf_op jit(solution)/shard_map/ppermute | solution.py:37
  247.7 30.1 %collective-permute-start.34 = (bf16[2,256,640]{2,1,0:T(8,128)(2,1)}, bf16[2,256,640]{2,1,0:T(8,128)(2,1)}, u32[]{:S(2)}, u32[]{:S(2)}) collective-permute-start(bf16[2,256,640]{2,1,0:T(8,128)(2,1)} %get-tuple-element.99), channel_id=1, source_target_pairs={{0,8},{8,0},{16,24},{24,16},{1,9},{9,1},{17,25},{25,17},{2,10},{10... | collective-permute-start | bytes 1966088 | tf_op jit(solution)/shard_map/ppermute | solution.py:37
  266.8 12.3 %collective-permute-start.32 = (bf16[2,256,640]{2,1,0:T(8,128)(2,1)}, bf16[2,256,640]{2,1,0:T(8,128)(2,1)}, u32[]{:S(2)}, u32[]{:S(2)}) collective-permute-start(bf16[2,256,640]{2,1,0:T(8,128)(2,1)} %get-tuple-element.97), channel_id=1, source_target_pairs={{0,8},{8,0},{16,24},{24,16},{1,9},{9,1},{17,25},{25,17},{2,10},{10... | collective-permute-start | bytes 1966088 | tf_op jit(solution)/shard_map/ppermute | solution.py:37
  268.6 41.0 %collective-permute-start.26 = (bf16[2,256,960]{1,2,0:T(8,128)(2,1)}, bf16[2,256,960]{1,2,0:T(8,128)(2,1)}, u32[]{:S(2)}, u32[]{:S(2)}) collective-permute-start(bf16[2,256,960]{1,2,0:T(8,128)(2,1)} %copy.100), channel_id=1, source_target_pairs={{0,8},{8,0},{16,24},{24,16},{1,9},{9,1},{17,25},{25,17},{2,10},{10... | collective-permute-start | bytes 2949128 | tf_op jit(solution)/shard_map/ppermute | solution.py:37
  271.1 41.5 %collective-permute-start.18 = (bf16[2,256,960]{1,2,0:T(8,128)(2,1)}, bf16[2,256,960]{1,2,0:T(8,128)(2,1)}, u32[]{:S(2)}, u32[]{:S(2)}) collective-permute-start(bf16[2,256,960]{1,2,0:T(8,128)(2,1)} %copy.91), channel_id=1, source_target_pairs={{0,8},{8,0},{16,24},{24,16},{1,9},{9,1},{17,25},{25,17},{2,10},{10... | collective-permute-start | bytes 2949128 | tf_op jit(solution)/shard_map/ppermute | solution.py:37
  277.8 36.2 %collective-permute-start.44 = (bf16[2,8,32,960]{3,2,1,0:T(8,128)(2,1)}, bf16[2,8,32,960]{3,2,1,0:T(8,128)(2,1)}, u32[]{:S(2)}, u32[]{:S(2)}) collective-permute-start(bf16[2,8,32,960]{3,2,1,0:T(8,128)(2,1)} %get-tuple-element.110), channel_id=1, source_target_pairs={{0,8},{8,0},{16,24},{24,16},{1,9},{9,1},{17,25},{25,17},{2,10},{10... | collective-permute-start | bytes 2949128 | tf_op jit(solution)/shard_map/ppermute | solution.py:37
  279.1 10.6 %collective-permute-start.35 = (bf16[256,640]{1,0:T(8,128)(2,1)S(1)}, bf16[256,640]{1,0:T(8,128)(2,1)S(1)}, u32[]{:S(2)}, u32[]{:S(2)}) collective-permute-start(bf16[256,640]{1,0:T(8,128)(2,1)S(1)} %fusion.16), channel_id=1, source_target_pairs={{0,16},{8,24},{16,0},{24,8},{1,17},{9,25},{17,1},{25,9},{2,18},{10... | collective-permute-start | bytes 983048 | tf_op jit(solution)/shard_map/ppermute | solution.py:37
  280.7 15.4 %collective-permute-start.33 = (bf16[256,640]{1,0:T(8,128)(2,1)S(1)}, bf16[256,640]{1,0:T(8,128)(2,1)S(1)}, u32[]{:S(2)}, u32[]{:S(2)}) collective-permute-start(bf16[256,640]{1,0:T(8,128)(2,1)S(1)} %fusion.15), channel_id=1, source_target_pairs={{0,16},{8,24},{16,0},{24,8},{1,17},{9,25},{17,1},{25,9},{2,18},{10... | collective-permute-start | bytes 983048 | tf_op jit(solution)/shard_map/ppermute | solution.py:37
  289.7 27.5 %collective-permute-start.53 = (bf16[2,120,1920]{2,1,0:T(8,128)(2,1)}, bf16[2,120,1920]{2,1,0:T(8,128)(2,1)}, u32[]{:S(2)}, u32[]{:S(2)}) collective-permute-start(bf16[2,120,1920]{2,1,0:T(8,128)(2,1)} %add_convert_fusion), channel_id=1, source_target_pairs={{0,2},{1,3},{2,0},{3,1},{4,6},{5,7},{6,4},{7,5},{8,10},{9,11},{10,... | collective-permute-start | bytes 2764808 | tf_op jit(solution)/shard_map/ppermute | solution.py:37
  309.4 31.5 %collective-permute-start.36 = (bf16[2,8,32,1600]{3,2,1,0:T(8,128)(2,1)}, bf16[2,8,32,1600]{3,2,1,0:T(8,128)(2,1)}, u32[]{:S(2)}, u32[]{:S(2)}) collective-permute-start(bf16[2,8,32,1600]{3,2,1,0:T(8,128)(2,1)} %get-tuple-element.106), channel_id=1, source_target_pairs={{0,8},{8,0},{16,24},{24,16},{1,9},{9,1},{17,25},{25,17},{2,10},{10... | collective-permute-start | bytes 4915208 | tf_op jit(solution)/shard_map/ppermute | solution.py:37
  312.1 107.0 %collective-permute-start.27 = (bf16[256,960]{1,0:T(8,128)(2,1)}, bf16[256,960]{1,0:T(8,128)(2,1)}, u32[]{:S(2)}, u32[]{:S(2)}) collective-permute-start(bf16[256,960]{1,0:T(8,128)(2,1)} %fusion.8), channel_id=1, source_target_pairs={{0,16},{8,24},{16,0},{24,8},{1,17},{9,25},{17,1},{25,9},{2,18},{10... | collective-permute-start | bytes 1474568 | tf_op jit(solution)/shard_map/ppermute | solution.py:37
  314.0 26.9 %copy-start.7 = (bf16[2,8,32,1600]{3,2,1,0:T(8,128)(2,1)S(1)}, bf16[2,8,32,1600]{3,2,1,0:T(8,128)(2,1)}, u32[]{:S(2)}) copy-start(bf16[2,8,32,1600]{3,2,1,0:T(8,128)(2,1)} %get-tuple-element.105) | copy-start | bytes 4915204
  315.6 22.2 %collective-permute-start.45 = (bf16[8,32,960]{2,1,0:T(8,128)(2,1)S(1)}, bf16[8,32,960]{2,1,0:T(8,128)(2,1)S(1)}, u32[]{:S(2)}, u32[]{:S(2)}) collective-permute-start(bf16[8,32,960]{2,1,0:T(8,128)(2,1)S(1)} %fusion.11), channel_id=1, source_target_pairs={{0,16},{8,24},{16,0},{24,8},{1,17},{9,25},{17,1},{25,9},{2,18},{10... | collective-permute-start | bytes 1474568 | tf_op jit(solution)/shard_map/ppermute | solution.py:37
  319.4 24.1 %copy-start.11 = (bf16[2,256,960]{2,1,0:T(8,128)(2,1)S(1)}, bf16[2,256,960]{2,1,0:T(8,128)(2,1)}, u32[]{:S(2)}) copy-start(bf16[2,256,960]{2,1,0:T(8,128)(2,1)} %get-tuple-element.76) | copy-start | bytes 2949124
  319.4 31.8 %collective-permute-start.54 = (bf16[1,120,1920]{2,1,0:T(8,128)(2,1)}, bf16[1,120,1920]{2,1,0:T(8,128)(2,1)}, u32[]{:S(2)}, u32[]{:S(2)}) collective-permute-start(bf16[1,120,1920]{2,1,0:T(8,128)(2,1)} %add_convert_fusion.8), channel_id=1, source_target_pairs={{0,4},{1,5},{2,6},{3,7},{4,0},{5,1},{6,2},{7,3},{8,12},{9,13},{10,... | collective-permute-start | bytes 1382408 | tf_op jit(solution)/shard_map/ppermute | solution.py:37
  340.4 8.2 %collective-permute-start.46 = (bf16[4,32,960]{2,1,0:T(8,128)(2,1)}, bf16[4,32,960]{2,1,0:T(8,128)(2,1)S(1)}, u32[]{:S(2)}, u32[]{:S(2)}) collective-permute-start(bf16[4,32,960]{2,1,0:T(8,128)(2,1)} %fusion.12), channel_id=1, source_target_pairs={{0,1},{1,0},{2,3},{3,2},{4,5},{5,4},{6,7},{7,6},{8,9},{9,8},{10,11... | collective-permute-start | bytes 737288 | tf_op jit(solution)/shard_map/ppermute | solution.py:37
  343.2 22.2 %collective-permute-start.37 = (bf16[8,32,1600]{2,1,0:T(8,128)(2,1)}, bf16[8,32,1600]{2,1,0:T(8,128)(2,1)}, u32[]{:S(2)}, u32[]{:S(2)}) collective-permute-start(bf16[8,32,1600]{2,1,0:T(8,128)(2,1)} %fusion.4), channel_id=1, source_target_pairs={{0,16},{8,24},{16,0},{24,8},{1,17},{9,25},{17,1},{25,9},{2,18},{10... | collective-permute-start | bytes 2457608 | tf_op jit(solution)/shard_map/ppermute | solution.py:37
  344.9 80.2 %collective-permute-start.19 = (bf16[256,960]{1,0:T(8,128)(2,1)}, bf16[256,960]{1,0:T(8,128)(2,1)S(1)}, u32[]{:S(2)}, u32[]{:S(2)}) collective-permute-start(bf16[256,960]{1,0:T(8,128)(2,1)} %fusion.7), channel_id=1, source_target_pairs={{0,16},{8,24},{16,0},{24,8},{1,17},{9,25},{17,1},{25,9},{2,18},{10... | collective-permute-start | bytes 1474568 | tf_op jit(solution)/shard_map/ppermute | solution.py:37
  349.7 18.6 %collective-permute-start.47 = (bf16[2,32,960]{2,1,0:T(8,128)(2,1)S(1)}, bf16[2,32,960]{2,1,0:T(8,128)(2,1)S(1)}, u32[]{:S(2)}, u32[]{:S(2)}) collective-permute-start(bf16[2,32,960]{2,1,0:T(8,128)(2,1)S(1)} %add_convert_fusion.12), channel_id=1, source_target_pairs={{0,2},{1,3},{2,0},{3,1},{4,6},{5,7},{6,4},{7,5},{8,10},{9,11},{10,... | collective-permute-start | bytes 368648 | tf_op jit(solution)/shard_map/ppermute | solution.py:37
  352.9 24.1 %collective-permute-start.55 = (bf16[1,120,1920]{2,1,0:T(8,128)(2,1)S(1)}, bf16[1,120,1920]{2,1,0:T(8,128)(2,1)S(1)}, u32[]{:S(2)}, u32[]{:S(2)}) collective-permute-start(bf16[1,120,1920]{2,1,0:T(8,128)(2,1)S(1)} %add_convert_fusion.7), channel_id=1, source_target_pairs={{0,4},{1,5},{2,6},{3,7},{4,0},{5,1},{6,2},{7,3},{8,12},{9,13},{10,... | collective-permute-start | bytes 1382408 | tf_op jit(solution)/shard_map/ppermute | solution.py:37
  366.7 10.5 %collective-permute-start.38 = (bf16[4,32,1600]{2,1,0:T(8,128)(2,1)S(1)}, bf16[4,32,1600]{2,1,0:T(8,128)(2,1)S(1)}, u32[]{:S(2)}, u32[]{:S(2)}) collective-permute-start(bf16[4,32,1600]{2,1,0:T(8,128)(2,1)S(1)} %fusion.5), channel_id=1, source_target_pairs={{0,1},{1,0},{2,3},{3,2},{4,5},{5,4},{6,7},{7,6},{8,9},{9,8},{10,11... | collective-permute-start | bytes 1228808 | tf_op jit(solution)/shard_map/ppermute | solution.py:37
  369.2 11.2 %collective-permute-start.48 = (bf16[1,32,960]{2,1,0:T(8,128)(2,1)S(1)}, bf16[1,32,960]{2,1,0:T(8,128)(2,1)S(1)}, u32[]{:S(2)}, u32[]{:S(2)}) collective-permute-start(bf16[1,32,960]{2,1,0:T(8,128)(2,1)S(1)} %add_convert_fusion.16), channel_id=1, source_target_pairs={{0,4},{1,5},{2,6},{3,7},{4,0},{5,1},{6,2},{7,3},{8,12},{9,13},{10,... | collective-permute-start | bytes 184328 | tf_op jit(solution)/shard_map/ppermute | solution.py:37
  377.1 28.0 %collective-permute-start.56 = (bf16[2,120,1920]{2,1,0:T(8,128)(2,1)S(1)}, bf16[2,120,1920]{2,1,0:T(8,128)(2,1)S(1)}, u32[]{:S(2)}, u32[]{:S(2)}) collective-permute-start(bf16[2,120,1920]{2,1,0:T(8,128)(2,1)S(1)} %pad_maximum_fusion.2), channel_id=1, source_target_pairs={{0,2},{1,3},{2,0},{3,1},{4,6},{5,7},{6,4},{7,5},{8,10},{9,11},{10,... | collective-permute-start | bytes 2764808 | tf_op jit(solution)/shard_map/ppermute | solution.py:37
  378.3 25.1 %collective-permute-start.39 = (bf16[2,32,1600]{2,1,0:T(8,128)(2,1)S(1)}, bf16[2,32,1600]{2,1,0:T(8,128)(2,1)S(1)}, u32[]{:S(2)}, u32[]{:S(2)}) collective-permute-start(bf16[2,32,1600]{2,1,0:T(8,128)(2,1)S(1)} %add_convert_fusion.11), channel_id=1, source_target_pairs={{0,2},{1,3},{2,0},{3,1},{4,6},{5,7},{6,4},{7,5},{8,10},{9,11},{10,... | collective-permute-start | bytes 614408 | tf_op jit(solution)/shard_map/ppermute | solution.py:37
  381.4 31.9 %collective-permute-start.49 = (bf16[1,32,960]{2,1,0:T(8,128)(2,1)S(1)}, bf16[1,32,960]{2,1,0:T(8,128)(2,1)S(1)}, u32[]{:S(2)}, u32[]{:S(2)}) collective-permute-start(bf16[1,32,960]{2,1,0:T(8,128)(2,1)S(1)} %add_convert_fusion.15), channel_id=1, source_target_pairs={{0,4},{1,5},{2,6},{3,7},{4,0},{5,1},{6,2},{7,3},{8,12},{9,13},{10,... | collective-permute-start | bytes 184328 | tf_op jit(solution)/shard_map/ppermute | solution.py:37
  404.4 7.7 %collective-permute-start.40 = (bf16[1,32,1600]{2,1,0:T(8,128)(2,1)S(1)}, bf16[1,32,1600]{2,1,0:T(8,128)(2,1)S(1)}, u32[]{:S(2)}, u32[]{:S(2)}) collective-permute-start(bf16[1,32,1600]{2,1,0:T(8,128)(2,1)S(1)} %add_convert_fusion.14), channel_id=1, source_target_pairs={{0,4},{1,5},{2,6},{3,7},{4,0},{5,1},{6,2},{7,3},{8,12},{9,13},{10,... | collective-permute-start | bytes 307208 | tf_op jit(solution)/shard_map/ppermute | solution.py:37
  406.8 63.6 %collective-permute-start.57 = (bf16[4,120,1920]{2,1,0:T(8,128)(2,1)}, bf16[4,120,1920]{2,1,0:T(8,128)(2,1)}, u32[]{:S(2)}, u32[]{:S(2)}) collective-permute-start(bf16[4,120,1920]{2,1,0:T(8,128)(2,1)} %pad_maximum_fusion.1.even), channel_id=1, source_target_pairs={{0,1},{1,0},{2,3},{3,2},{4,5},{5,4},{6,7},{7,6},{8,9},{9,8},{10,11... | collective-permute-start | bytes 5529608 | tf_op jit(solution)/shard_map/ppermute | solution.py:37
  413.2 5.8 %collective-permute-start.41 = (bf16[1,32,1600]{2,1,0:T(8,128)(2,1)S(1)}, bf16[1,32,1600]{2,1,0:T(8,128)(2,1)S(1)}, u32[]{:S(2)}, u32[]{:S(2)}) collective-permute-start(bf16[1,32,1600]{2,1,0:T(8,128)(2,1)S(1)} %add_convert_fusion.13), channel_id=1, source_target_pairs={{0,4},{1,5},{2,6},{3,7},{4,0},{5,1},{6,2},{7,3},{8,12},{9,13},{10,... | collective-permute-start | bytes 307208 | tf_op jit(solution)/shard_map/ppermute | solution.py:37
  413.3 7.3 %collective-permute-start.50 = (bf16[2,32,960]{2,1,0:T(8,128)(2,1)S(1)}, bf16[2,32,960]{2,1,0:T(8,128)(2,1)S(1)}, u32[]{:S(2)}, u32[]{:S(2)}) collective-permute-start(bf16[2,32,960]{2,1,0:T(8,128)(2,1)S(1)} %pad_maximum_fusion.8), channel_id=1, source_target_pairs={{0,2},{1,3},{2,0},{3,1},{4,6},{5,7},{6,4},{7,5},{8,10},{9,11},{10,... | collective-permute-start | bytes 368648 | tf_op jit(solution)/shard_map/ppermute | solution.py:37
  419.0 5.9 %collective-permute-start.42 = (bf16[2,32,1600]{2,1,0:T(8,128)(2,1)S(1)}, bf16[2,32,1600]{2,1,0:T(8,128)(2,1)S(1)}, u32[]{:S(2)}, u32[]{:S(2)}) collective-permute-start(bf16[2,32,1600]{2,1,0:T(8,128)(2,1)S(1)} %pad_maximum_fusion.7), channel_id=1, source_target_pairs={{0,2},{1,3},{2,0},{3,1},{4,6},{5,7},{6,4},{7,5},{8,10},{9,11},{10,... | collective-permute-start | bytes 614408 | tf_op jit(solution)/shard_map/ppermute | solution.py:37
  420.7 35.0 %collective-permute-start.51 = (bf16[4,32,960]{2,1,0:T(8,128)(2,1)S(1)}, bf16[4,32,960]{2,1,0:T(8,128)(2,1)S(1)}, u32[]{:S(2)}, u32[]{:S(2)}) collective-permute-start(bf16[4,32,960]{2,1,0:T(8,128)(2,1)S(1)} %pad_maximum_fusion.6.even_o), channel_id=1, source_target_pairs={{0,1},{1,0},{2,3},{3,2},{4,5},{5,4},{6,7},{7,6},{8,9},{9,8},{10,11... | collective-permute-start | bytes 737288 | tf_op jit(solution)/shard_map/ppermute | solution.py:37
  425.0 35.5 %collective-permute-start.43 = (bf16[4,32,1600]{2,1,0:T(8,128)(2,1)S(1)}, bf16[4,32,1600]{2,1,0:T(8,128)(2,1)S(1)}, u32[]{:S(2)}, u32[]{:S(2)}) collective-permute-start(bf16[4,32,1600]{2,1,0:T(8,128)(2,1)S(1)} %pad_maximum_fusion.3.even), channel_id=1, source_target_pairs={{0,1},{1,0},{2,3},{3,2},{4,5},{5,4},{6,7},{7,6},{8,9},{9,8},{10,11... | collective-permute-start | bytes 1228808 | tf_op jit(solution)/shard_map/ppermute | solution.py:37
  (38 other events, 188.1 us)

commit v3 on v1

v3 whole, which is shorter than its diff:
```python
import functools

import jax
import jax.numpy as jnp
from jax import lax
from jax.experimental import pallas as pl
from jax.experimental.pallas import tpu as pltpu
from jax.sharding import PartitionSpec as P

HD = 64
PIECE = 256
LANES = 128
GROUP = 4
PARTS = 8
GAIN_ROWS = 16
RATE = 1.0e9
SLOTS = (7, 3, 5, 1, 6, 2, 4, 0)


NORM_EPS = 1e-05
ROPE_BASE = 10000.0
MASKED_SCORE = -1e30
SCALE = HD ** (-0.5)

LOW = jnp.bfloat16
FULL = jnp.float32
NN = (((1,), (0,)), ((), ()))
NT = (((1,), (1,)), ((), ()))
TN = (((0,), (0,)), ((), ()))


def dot(left_mat, right_mat, form=NN):
    return lax.dot_general(left_mat, right_mat, form, preferred_element_type=FULL)


def swap(values, axis, count, mask):
    return lax.ppermute(values, axis, [(i, i ^ mask) for i in range(count)])


def after(values, *others):
    return lax.optimization_barrier((values,) + others)[0] if others else values


class Blocks:
    def __init__(self, own, *others):
        self.own = own
        sent = after(own, *others)
        self.across = swap(sent, "grp", GROUP, 2)
        self.sent = sent

    def finish(self, *others):
        pair = after((self.sent, self.across), *others)
        return self.own, swap(pair[0], "grp", GROUP, 1), self.across, swap(pair[1], "grp", GROUP, 1)


class Terms:
    def __init__(self, keep, send):
        self.keep = keep
        self.beside = swap(send, "grp", GROUP, 1)

    def cross(self, *others):
        keep, beside = after((self.keep, self.beside), *others)
        across = (keep[1].astype(FULL) + beside[1].astype(FULL)).astype(LOW)
        self.across = swap(across, "grp", GROUP, 2)
        return across

    def all(self):
        return self.keep, self.beside, self.across


def three(terms):
    return terms[0][0].astype(FULL) + terms[1][0].astype(FULL) + terms[2].astype(FULL)


class RepSum:
    def __init__(self, pieces, ranks):
        self.pieces, self.ranks = pieces, ranks
        self.one = swap(pieces[0], "rep", ranks, 1)

    def second(self, *others):
        self.one = after(self.one, *others)
        two = (self.pieces[1].astype(FULL) + self.one[0:2].astype(FULL)).astype(LOW)
        self.two = swap(two, "rep", self.ranks, 2)
        return two

    def third(self, *others):
        self.two = after(self.two, *others)
        four = self.pieces[2].astype(FULL) + self.one[2:3].astype(FULL) + self.two[0:1].astype(FULL)
        four = four.astype(LOW)
        self.four = swap(four, "rep", self.ranks, 4)
        return four

    def own(self, *others):
        ranks = self.ranks
        self.four = after(self.four, *others)
        mine = self.pieces[3].astype(FULL) + self.one[3:4].astype(FULL) + self.two[1:2].astype(FULL)
        mine = (mine + self.four.astype(FULL)).astype(LOW)
        if ranks > PARTS:
            others = [[j * PARTS + i for j in range(ranks // PARTS)] for i in range(PARTS)]
            mine = lax.psum(mine, "rep", axis_index_groups=others)
        self.mine = mine
        self.back = swap(mine, "rep", ranks, 4)
        return mine

    def spread(self, *others):
        self.back = after(self.back, *others)
        held = jnp.concatenate([self.mine, self.back])
        self.held = held
        self.wide = swap(held, "rep", self.ranks, 2)
        return held

    def done(self, *others):
        self.wide = after(self.wide, *others)
        held = jnp.concatenate([self.held, self.wide])
        return held, swap(held, "rep", self.ranks, 1)


def all_sum(values, ranks):
    for mask in (1, 2):
        values = values + swap(values, "grp", GROUP, mask)
    mask = 1
    while mask < ranks:
        values = values + swap(values, "rep", ranks, mask)
        mask *= 2
    return values


def call(kernel, name, out_shape, *, grid=(1,), prefetch=0, in_specs, out_specs, scratch=(), micros=1, vmem=56):
    return pl.pallas_call(
        kernel,
        name=name,
        out_shape=out_shape,
        grid_spec=pltpu.PrefetchScalarGridSpec(
            num_scalar_prefetch=prefetch,
            grid=grid,
            in_specs=in_specs,
            out_specs=out_specs,
            scratch_shapes=list(scratch),
        ),
        compiler_params=pltpu.CompilerParams(vmem_limit_bytes=vmem << 20),
        cost_estimate=pl.CostEstimate(flops=int(micros * RATE), bytes_accessed=1 << 20, transcendentals=0),
    )


def whole(shape):
    return pl.BlockSpec(shape, lambda *_: (0,) * len(shape))


def shape_of(shape, kind=LOW):
    return jax.ShapeDtypeStruct(shape, kind)


def turn(rows, cosine, sine_val, sign):
    one, two = rows[0 : HD // 2, :], rows[HD // 2 : HD, :]
    sine_val = sine_val * sign
    return one * cosine - two * sine_val, two * cosine + one * sine_val


def assemble(rank, blocks, scratch):
    rows = blocks[0].shape[0]
    for k in range(GROUP):
        start = pl.multiple_of((rank ^ k) * rows, 16)
        scratch[pl.ds(start, rows), :] = blocks[k][...]


def flip_kernel(wg_ref, wu_ref, wdt_ref, wgut_ref, wgu_ref, wd_ref):
    ff = wg_ref.shape[1]
    wgut_ref[0:ff, :] = wg_ref[...].T
    wgut_ref[ff:, :] = wu_ref[...].T
    wgu_ref[:, 0:ff] = wg_ref[...]
    wgu_ref[:, ff:] = wu_ref[...]
    wd_ref[...] = wdt_ref[...].T


def keys_values_kernel(ranks, tok_ref, b0, b1, b2, b3, cos_ref, sin_ref, norm_ref, kv_a, kv_b, gain_ref, w_ref):
    span = tok_ref.shape[2]
    kw2 = kv_a.shape[0]
    kw = kw2 // 2
    assemble(ranks[0], (b0, b1, b2, b3), w_ref)
    gains = w_ref[:, kw2:]
    gain_ref[...] = gains
    gain_one = gains[:, 0:1].astype(FULL)
    for s, out in enumerate((kv_a, kv_b)):
        x = tok_ref[s].astype(FULL)
        inverse = lax.rsqrt(jnp.mean(x * x, axis=0, keepdims=True) + NORM_EPS)
        norm = (x * inverse * gain_one).astype(LOW)
        norm_ref[:, s * span : (s + 1) * span] = norm
        kv = dot(w_ref[:, 0:kw2], norm, TN)
        for h in range(kw // HD):
            one, two = turn(kv[h * HD : (h + 1) * HD, :], cos_ref[s], sin_ref[s], 1.0)
            top = h * 2 * HD
            out[top : top + HD // 2, :] = one.astype(LOW)
            out[top + HD // 2 : top + HD, :] = two.astype(LOW)
            out[top + HD : top + 2 * HD, :] = kv[kw + h * HD : kw + (h + 1) * HD, :].astype(LOW)


def queries_kernel(ranks, norm_ref, b0, b1, b2, b3, cos_ref, sin_ref, q_ref, w_ref):
    width = b0.shape[1]
    span = cos_ref.shape[2]
    assemble(ranks[0], (b0, b1, b2, b3), w_ref)
    for s in range(2):
        part = slice(s * span, (s + 1) * span)
        query = dot(w_ref[...], norm_ref[:, part], TN)
        for h in range(width // HD):
            one, two = turn(query[h * HD : (h + 1) * HD, :], cos_ref[s], sin_ref[s], 1.0)
            q_ref[h * HD : h * HD + HD // 2, part] = (one * SCALE).astype(LOW)
            q_ref[h * HD + HD // 2 : (h + 1) * HD, part] = (two * SCALE).astype(LOW)


def attend_kernel(seq, ranks, order, starts, q_ref, b0, b1, b2, b3, p_ref, o_ref, bias_ref):
    span = q_ref.shape[1]
    per = q_ref.shape[0] // HD
    rank = ranks[0]

    @pl.when(pl.program_id(0) == 0)
    def _():
        query_pos = order[seq, rank] * span + lax.broadcasted_iota(jnp.int32, (span, span), 1)
        query_in = []
        for m in range(2):
            start = starts[seq, m]
            query_in.append((query_pos >= start) & (query_pos < start + PIECE))
        for k in range(GROUP):
            key_pos = order[seq, rank ^ k] * span + lax.broadcasted_iota(jnp.int32, (span, span), 0)
            allowed = key_pos <= query_pos
            for m in range(2):
                start = starts[seq, m]
                key_in = (key_pos >= start) & (key_pos < start + PIECE)
                allowed = allowed | (query_in[m] & key_in)
            bias_ref[k * span : (k + 1) * span, :] = jnp.where(allowed, 0.0, MASKED_SCORE)

    kv_t = jnp.concatenate([b0[...], b1[...], b2[...], b3[...]], axis=1)
    keys = kv_t.T[:, 0:HD]
    values_t = kv_t[HD : 2 * HD, :]
    for i in range(per):
        scores = dot(keys, q_ref[i * HD : (i + 1) * HD, :]) + bias_ref[...]
        peak = jnp.max(scores, axis=0, keepdims=True)
        exponent = jnp.exp(scores - peak)
        total = jnp.sum(exponent, axis=0, keepdims=True)
        probs = (exponent * (1.0 / total)).astype(LOW)
        p_ref[0, :, i * span : (i + 1) * span] = probs
        o_ref[i * HD : (i + 1) * HD, :] = dot(values_t, probs).astype(LOW)


def middle_kernel(ranks, att_ref, b0, b1, b2, b3, tok_ref, gain_ref, mid_ref, x_ref, w_ref):
    assemble(ranks[0], (b0, b1, b2, b3), w_ref)
    middle = tok_ref[0].astype(FULL) + dot(w_ref[...], att_ref[...], TN)
    mid_ref[...] = middle
    inverse = lax.rsqrt(jnp.mean(middle * middle, axis=0, keepdims=True) + NORM_EPS)
    x_ref[...] = (middle * inverse * gain_ref[:, 1:2].astype(FULL)).astype(LOW)


def forward_back_kernel(x0, x1, x2, x3, c0, c1, c2, c3, wgut_ref, wgu_ref, wdt_ref, wd_ref, ko_ref, so_ref, kg_ref, sg_ref, hid_ref, gg_ref, gu_ref, xs, cs, both):
    k = pl.program_id(0)
    ff = wd_ref.shape[0]
    for i, (x, c) in enumerate(((x0, c0), (x1, c1), (x2, c2), (x3, c3))):

        @pl.when(k == i)
        def _(x=x, c=c):
            xs[...] = x[...]
            cs[...] = c[...]

    gate_up = dot(wgut_ref[...], xs[...])
    grad_hidden = dot(wd_ref[...], cs[...])
    gate, up = gate_up[0:ff, :], gate_up[ff:, :]
    sig = 1.0 / (1.0 + jnp.exp(-gate))
    swish = gate * sig
    hidden = (swish * up).astype(LOW)
    grad_gate = (grad_hidden * up * sig * (1.0 + gate * (1.0 - sig))).astype(LOW)
    grad_up = (grad_hidden * swish).astype(LOW)
    hid_ref[...] = hidden
    gg_ref[...] = grad_gate
    gu_ref[...] = grad_up
    both[0:ff, :] = grad_gate
    both[ff:, :] = grad_up
    grad_x = dot(wgu_ref[...], both[...]).astype(LOW)
    out = dot(wdt_ref[...], hid_ref[...]).astype(LOW)
    half = k // 2

    @pl.when(k % 2 == 0)
    def _():
        kg_ref[half] = grad_x
        ko_ref[half] = out

    @pl.when(k % 2 == 1)
    def _():
        sg_ref[half] = grad_x
        so_ref[half] = out


def weight_kernel(stacked, ranks, *refs):
    count = GROUP if stacked else 2 * GROUP
    blocks = refs[0:count]
    rights = refs[count : count + 2]
    outs = refs[count + 2 : count + 6]
    left, right, acc, sem = refs[count + 6 : count + 10]
    span = left.shape[2] // GROUP
    copies = []
    for s in range(2):
        own = []
        for k in range(GROUP):
            source = blocks[k].at[s] if stacked else blocks[s * GROUP + k]
            own.append(pltpu.make_async_copy(source, left.at[s, :, pl.ds(k * span, span)], sem.at[s * 5 + k]))
        own.append(pltpu.make_async_copy(rights[s], right.at[s], sem.at[s * 5 + 4]))
        copies.append(own)
    for own in copies:
        for copy in own:
            copy.start()
    for copy in copies[0]:
        copy.wait()
    acc[...] = dot(left[0], right[0], NT)
    for copy in copies[1]:
        copy.wait()
    acc[...] += dot(left[1], right[1], NT)
    part = acc.shape[0] // PARTS
    places = [(outs[0], i) for i in range(4)] + [(outs[1], 0), (outs[1], 1), (outs[2], 0), (outs[3], 0)]
    for (out, i), slot in zip(places, SLOTS):
        start = pl.multiple_of((slot ^ ranks[1]) * part, 8)
        out[i] = acc[pl.ds(start, part), :].astype(LOW)


def branch_kernel(ranks, mid_ref, cot_ref, e0, e1, e2, gain_ref, b0, b1, b2, b3, att_ref, gm_ref, gb_ref, do_ref, delta_ref, gain_out, w_ref):
    width, span = mid_ref.shape
    assemble(ranks[0], (b0, b1, b2, b3), w_ref)
    middle = mid_ref[...]
    grad = e0[0].astype(FULL) + e1[0].astype(FULL) + e2[...].astype(FULL)
    inverse = lax.rsqrt(jnp.mean(middle * middle, axis=0, keepdims=True) + NORM_EPS)
    scaled = grad * gain_ref[:, 1:2].astype(FULL)
    turned = jnp.mean(scaled * middle, axis=0, keepdims=True)
    grad_middle = cot_ref[0].astype(FULL) + inverse * scaled - middle * (inverse * inverse * inverse * turned)
    gain_out[...] = dot(jnp.ones((8, span), LOW), (grad * middle * inverse).astype(LOW), NT)
    gm_ref[...] = grad_middle
    branch = grad_middle.astype(LOW)
    gb_ref[...] = branch
    grad_att = dot(w_ref[...], branch).astype(LOW)
    do_ref[...] = grad_att
    both = grad_att.astype(FULL) * att_ref[...].astype(FULL)
    heads = width // HD
    for h in range(heads):
        delta_ref[h : h + 1, :] = jnp.sum(both[h * HD : (h + 1) * HD, :], axis=0, keepdims=True)
    delta_ref[heads:, :] = jnp.zeros((delta_ref.shape[0] - heads, span), FULL)


def attend_back_kernel(q_ref, b0, b1, b2, b3, p_ref, do_ref, delta_ref, cos_ref, sin_ref, gq_ref, keep_ref, send_ref, ds_ref):
    span = q_ref.shape[1]
    per = q_ref.shape[0] // HD
    h = pl.program_id(0)
    kv_t = jnp.concatenate([b0[...], b1[...], b2[...], b3[...]], axis=1)
    kv = kv_t.T
    keys_t = kv_t[0:HD, :]
    cosine, sine_val = cos_ref[0], sin_ref[0]
    none = jnp.zeros((HD, span), LOW)
    qs, dos = [], []
    for i in range(per):
        rows = slice(i * HD, (i + 1) * HD)
        out_grad = jnp.concatenate([none, do_ref[rows, :]], axis=0)
        probs = p_ref[0, :, i * span : (i + 1) * span]
        delta = delta_ref[pl.ds(per * h + i, 1), :]
        grad_scores = (probs.astype(FULL) * (dot(kv, out_grad) - delta)).astype(LOW)
        ds_ref[:, i * span : (i + 1) * span] = grad_scores
        one, two = turn(dot(keys_t, grad_scores) * SCALE, cosine, sine_val, -1.0)
        gq_ref[i * HD : i * HD + HD // 2, :] = one.astype(LOW)
        gq_ref[i * HD + HD // 2 : (i + 1) * HD, :] = two.astype(LOW)
        qs.append(jnp.concatenate([q_ref[rows, :], none], axis=0))
        dos.append(out_grad)
    total = dot(ds_ref[...], jnp.concatenate(qs, axis=1), NT)
    total = total + dot(p_ref[0], jnp.concatenate(dos, axis=1), NT)
    total = total.T.astype(LOW)
    keep_ref[0] = total[:, 0:span]
    send_ref[0] = total[:, span : 2 * span]
    keep_ref[1] = total[:, 2 * span : 3 * span]
    send_ref[1] = total[:, 3 * span : 4 * span]


def spread(ranks, acc, keep_ref, send_ref):
    part = acc.shape[1] // PARTS
    for k in range(GROUP):
        out = send_ref if k % 2 else keep_ref
        for i, slot in enumerate(SLOTS):
            start = pl.multiple_of((slot ^ ranks[1]) * part, 8)
            out[k // 2, i] = acc[ranks[0] ^ k, pl.ds(start, part), :].astype(LOW)


def out_weight_kernel(ranks, att_a, att_b, gb_a, gb_b, keep_ref, send_ref, acc):
    width = gb_a.shape[0]
    shard = width // GROUP
    for b in range(GROUP):
        rows = slice(b * shard, (b + 1) * shard)
        acc[b, 0:shard, :] = dot(att_a[rows, :], gb_a[...], NT) + dot(att_b[rows, :], gb_b[...], NT)
        acc[b, shard:, :] = jnp.zeros((acc.shape[1] - shard, width), FULL)
    spread(ranks, acc, keep_ref, send_ref)


def input_weight_kernel(ranks, norm_ref, gq_a, gq_b, a0, a1, a2, b0, b1, b2, cos_ref, sin_ref, keep_ref, send_ref, gkv_ref, acc):
    width = norm_ref.shape[0]
    span = gq_a.shape[1]
    shard = width // GROUP
    kw2 = gkv_ref.shape[0]
    kw = kw2 // 2
    for s, (e0, e1, e2) in enumerate(((a0, a1, a2), (b0, b1, b2))):
        part = slice(s * span, (s + 1) * span)
        grad = e0[0].astype(FULL) + e1[0].astype(FULL) + e2[...].astype(FULL)
        for h in range(kw // HD):
            top = h * 2 * HD
            one, two = turn(grad[top : top + HD, :], cos_ref[s], sin_ref[s], -1.0)
            gkv_ref[h * HD : h * HD + HD // 2, part] = one.astype(LOW)
            gkv_ref[h * HD + HD // 2 : (h + 1) * HD, part] = two.astype(LOW)
            gkv_ref[kw + h * HD : kw + (h + 1) * HD, part] = grad[top + HD : top + 2 * HD, :].astype(LOW)
    for b in range(GROUP):
        rows = slice(b * shard, (b + 1) * shard)
        acc[b, 0:shard, 0:width] = dot(norm_ref[rows, 0:span], gq_a[...], NT) + dot(norm_ref[rows, span:], gq_b[...], NT)
        acc[b, 0:shard, width:] = dot(norm_ref[rows, :], gkv_ref[...], NT)
        acc[b, shard:, :] = jnp.zeros((acc.shape[1] - shard, acc.shape[2]), FULL)
    spread(ranks, acc, keep_ref, send_ref)


def input_grad_kernel(ranks, gq_a, gq_b, gkv_ref, q0, q1, q2, q3, k0, k1, k2, k3, tok_ref, gm_a, gm_b, gain_a, gain_b, out_ref, gain_out, wq_ref, wkv_ref):
    span = gq_a.shape[1]
    kw2 = gkv_ref.shape[0]
    assemble(ranks[0], (q0, q1, q2, q3), wq_ref)
    assemble(ranks[0], (k0, k1, k2, k3), wkv_ref)
    gain_one = wkv_ref[:, kw2 : kw2 + 1].astype(FULL)
    total = None
    for s in range(2):
        part = slice(s * span, (s + 1) * span)
        grad_norm = dot(wq_ref[...], (gq_a, gq_b)[s][...]) + dot(wkv_ref[:, 0:kw2], gkv_ref[:, part])
        x = tok_ref[s].astype(FULL)
        inverse = lax.rsqrt(jnp.mean(x * x, axis=0, keepdims=True) + NORM_EPS)
        scaled = grad_norm * gain_one
        turned = jnp.mean(scaled * x, axis=0, keepdims=True)
        out_ref[s] = (gm_a, gm_b)[s][...] + inverse * scaled - x * (inverse * inverse * inverse * turned)
        row = dot(jnp.ones((8, span), LOW), (grad_norm * x * inverse).astype(LOW), NT)
        total = row if total is None else total + row
    gain_out[0:1, :] = total[0:1, :]
    gain_out[1:2, :] = gain_a[0:1, :] + gain_b[0:1, :]
    gain_out[2:8, :] = total[2:8, :]


def place(slot):
    return ((slot >> 2) & 1) + ((slot >> 1) & 1) * 2


def gathered(ranks, pairs):
    for a in range(PARTS):
        slot = ranks[1] ^ a
        index = place(slot)
        for parity in range(2):

            @pl.when(slot % 2 == parity)
            def _(parity=parity, index=index, a=a):
                for pair in pairs:
                    part = pair[parity].shape[1]
                    pair[2][a * part : (a + 1) * part, :] = pair[parity][index].astype(FULL)


def forward_weights_kernel(ranks, even, odd, out_ref):
    gathered(ranks, [(even, odd, out_ref)])


def attention_weights_kernel(ranks, even, odd, even_o, odd_o, q_ref, k_ref, v_ref, o_ref, scratch, scratch_o):
    shard, width = q_ref.shape
    kw = k_ref.shape[1]
    gathered(ranks, [(even, odd, scratch), (even_o, odd_o, scratch_o)])
    q_ref[...] = scratch[0:shard, 0:width]
    k_ref[...] = scratch[0:shard, width : width + kw]
    v_ref[...] = scratch[0:shard, width + kw : width + 2 * kw]
    o_ref[...] = scratch_o[0:shard, :]


def tables(places):
    half = HD // 2
    frequency = ROPE_BASE ** (-2.0 * jnp.arange(half, dtype=FULL) / HD)
    angles = places.astype(FULL)[:, None, :] * frequency[None, :, None]
    return jnp.cos(angles), jnp.sin(angles)


def body(
    tokens,
    w_query,
    w_key,
    w_value,
    w_out,
    w_gate,
    w_up,
    w_down,
    gain_attn,
    gain_mlp,
    span_order,
    piece_starts,
    cotangent,
):
    ranks = lax.axis_size("rep")
    rank_grp = lax.axis_index("grp")
    seq_count, span, width = tokens.shape
    shard = w_query.shape[0]
    kw = w_key.shape[1]
    kw2 = 2 * kw
    kv_heads = kw // HD
    per = width // kw
    ff = w_gate.shape[1]
    rows = seq_count * span
    length = GROUP * span
    place_of = jnp.stack([rank_grp, lax.axis_index("rep") % PARTS]).astype(jnp.int32)
    any_spec = pl.BlockSpec(memory_space=pl.ANY)
    tok_t = jnp.swapaxes(tokens, 1, 2)
    cot_t = jnp.swapaxes(cotangent, 1, 2)
    wd_t = w_down.T

    gains = jnp.pad(jnp.stack([gain_attn, gain_mlp], axis=1), ((0, 0), (0, LANES - 2)))
    kv_shard = jnp.concatenate([w_key, w_value, gains], axis=1)
    kv_flight = Blocks(kv_shard)
    q_flight = Blocks(w_query)
    own_span = lax.dynamic_slice(span_order, (0, rank_grp), (seq_count, 1))
    places = own_span * span + jnp.arange(span, dtype=jnp.int32)[None, :]
    cos_cols, sin_cols = tables(places)
    table = whole(cos_cols.shape)
    tok_spec = whole(tok_t.shape)
    wgut, wgu, wd = call(
        flip_kernel,
        "flip",
        (shape_of((2 * ff, width)), shape_of((width, 2 * ff)), shape_of((ff, width))),
        in_specs=[whole((width, ff))] * 3,
        out_specs=(whole((2 * ff, width)), whole((width, 2 * ff)), whole((ff, width))),
            micros=5,
    )(after(w_gate, kv_flight.sent), w_up, wd_t)
    kv_blocks = kv_flight.finish()

    one_seq = lambda s: pl.BlockSpec((1, width, span), lambda *_: (s, 0, 0))
    act = whole((width, span))
    norm_low, kv_a, kv_b, gain_cols = call(
        keys_values_kernel,
        "keys_values",
        (shape_of((width, rows)), shape_of((kw2, span)), shape_of((kw2, span)), shape_of((width, LANES))),
        prefetch=1,
        in_specs=[tok_spec] + [whole(kv_shard.shape)] * 4 + [table, table],
        out_specs=(whole((width, rows)), whole((kw2, span)), whole((kw2, span)), whole((width, LANES))),
        scratch=[pltpu.VMEM((width, kw2 + LANES), LOW)],
            micros=4.5,
    )(place_of, after(tok_t, wgut), *kv_blocks, cos_cols, sin_cols)
    kv_flight = [Blocks(kv_a), Blocks(kv_b, kv_a)]
    q_blocks = q_flight.finish(norm_low)
    queries = call(
        queries_kernel,
        "queries",
        shape_of((width, rows)),
        prefetch=1,
        in_specs=[whole((width, rows))] + [whole((shard, width))] * 4 + [table, table],
        out_specs=whole((width, rows)),
        scratch=[pltpu.VMEM((width, width), LOW)],
            micros=5,
    )(place_of, norm_low, *q_blocks, cos_cols, sin_cols)

    o_flight = Blocks(w_out, queries)
    cot_flight = [Blocks(cot_t[0], queries, o_flight.sent), None]
    kv_all = [kv_flight[0].finish(queries), None]
    cot_blocks = [None, None]
    head = pl.BlockSpec((2 * HD, span), lambda h, *_: (h, 0))
    probs_spec = pl.BlockSpec((1, length, per * span), lambda h, *_: (h, 0, 0))
    q_spec = lambda s: pl.BlockSpec((per * HD, span), lambda h, *_: (h, s))
    per_head = pl.BlockSpec((per * HD, span), lambda h, *_: (h, 0))
    def attend_of(s, query):
        return call(
            functools.partial(attend_kernel, s),
            "attend",
            (shape_of((kv_heads, length, per * span)), shape_of((width, span))),
            prefetch=3,
            grid=(kv_heads,),
            in_specs=[q_spec(s)] + [head] * 4,
            out_specs=(probs_spec, per_head),
            scratch=[pltpu.VMEM((length, span), FULL)],
            micros=16,
        )(place_of, span_order, piece_starts, query, *kv_all[s])

    def middle_of(s, att):
        return call(
            middle_kernel,
            "middle",
            (shape_of((width, span), FULL), shape_of((width, span))),
            prefetch=1,
            in_specs=[act] + [whole((shard, width))] * 4 + [one_seq(s), whole((width, LANES))],
            out_specs=(act, act),
            scratch=[pltpu.VMEM((width, width), LOW)],
            micros=4.6,
        )(place_of, att, *o_blocks, tok_t, gain_cols)

    probs_a, att_a = attend_of(0, queries)
    o_blocks = o_flight.finish(att_a)
    kv_all[1] = kv_flight[1].finish(att_a)
    middle_a, x_a = middle_of(0, att_a)
    x_flight = [Blocks(x_a), None]
    cot_flight[1] = Blocks(cot_t[1], x_flight[0].sent, x_a)
    probs_b, att_b = attend_of(1, after(queries, x_a))
    cot_blocks[0] = cot_flight[0].finish(att_b)
    middle_b, x_b = middle_of(1, att_b)
    x_blocks = [x_flight[0].finish(middle_b), None]
    x_flight[1] = Blocks(x_b)
    stats, attended, middles = (probs_a, probs_b), (att_a, att_b), (middle_a, middle_b)

    def forward_back(s, *others):
        both = whole((2, width, span))
        per_block = pl.BlockSpec((ff, span), lambda k, *_: (0, k))
        return call(
            forward_back_kernel,
            "forward_back",
            (shape_of((2, width, span)),) * 4 + (shape_of((ff, length)),) * 3,
            grid=(GROUP,),
            in_specs=[act] * 8
            + [whole((2 * ff, width)), whole((width, 2 * ff)), whole((width, ff)), whole((ff, width))],
            out_specs=(both,) * 4 + (per_block,) * 3,
            scratch=[pltpu.VMEM((width, span), LOW), pltpu.VMEM((width, span), LOW), pltpu.VMEM((2 * ff, span), LOW)],
            micros=19,
        )(*x_blocks[s], *cot_blocks[s], after(wgut, *others), wgu, wd_t, wd)

    ko_a, so_a, kg_a, sg_a, hid_a, gg_a, gu_a = forward_back(0, x_b)
    grad_a = Terms(kg_a, sg_a)
    x_blocks[1] = x_flight[1].finish(hid_a)
    cot_blocks[1] = cot_flight[1].finish(hid_a)
    ko_b, so_b, kg_b, sg_b, hid_b, gg_b, gu_b = forward_back(1, hid_a)
    grad_b = Terms(kg_b, sg_b)
    grad_a.cross(hid_b)
    grads = (grad_a, grad_b)

    part = width // PARTS

    def weights(name, stacked, blocks, rights):
        return call(
            functools.partial(weight_kernel, stacked),
            name,
            tuple(shape_of((n, part, ff)) for n in (4, 2, 1, 1)),
            prefetch=1,
            in_specs=[any_spec] * (len(blocks) + 2),
            out_specs=tuple(whole((n, part, ff)) for n in (4, 2, 1, 1)),
            scratch=[
                pltpu.VMEM((2, width, length), LOW),
                pltpu.VMEM((2, ff, length), LOW),
                pltpu.VMEM((width, ff), FULL),
                pltpu.SemaphoreType.DMA((10,)),
            ],
            micros=8,
        )(place_of, *blocks, *rights)

    def sums(name, stacked, blocks, rights, *others):
        return RepSum(weights(name, stacked, blocks, (after(rights[0], *others), rights[1])), ranks)

    x_all = x_blocks[0] + x_blocks[1]
    cot_all = cot_blocks[0] + cot_blocks[1]
    down_sum = sums("down_weights", False, cot_all, (hid_a, hid_b), grad_b.beside)
    grad_b.cross(down_sum.pieces[0])
    gate_sum = sums("gate_weights", False, x_all, (gg_a, gg_b), down_sum.pieces[0])
    up_sum = sums("up_weights", False, x_all, (gu_a, gu_b), gate_sum.pieces[0])
    out_a = Terms(ko_a, after(so_a, gate_sum.pieces[0]))
    out_b = Terms(ko_b, after(so_b, gate_sum.pieces[0]))

    def branch_of(s, middle):
        keep_term, beside_term, across_term = grads[s].all()
        return call(
            branch_kernel,
            "branch",
            (
                shape_of((width, span), FULL),
                shape_of((width, span)),
                shape_of((width, span)),
                shape_of((16, span), FULL),
                shape_of((8, width), FULL),
            ),
            prefetch=1,
            in_specs=[act, one_seq(s), one_seq(0), one_seq(0), act, whole((width, LANES))]
            + [whole((shard, width))] * 4
            + [act],
            out_specs=(act, act, act, whole((16, span)), whole((8, width))),
            scratch=[pltpu.VMEM((width, width), LOW)],
            micros=5.7,
        )(place_of, middle, cot_t, keep_term, beside_term, across_term, gain_cols, *o_blocks, attended[s])

    def attend_back_of(s, out_grad, delta):
        column = pl.BlockSpec((1, HD // 2, span), lambda *_: (s, 0, 0))
        halves = pl.BlockSpec((2, 2 * HD, span), lambda h, *_: (0, h, 0))
        grad_q, kv_keep, kv_send = call(
            attend_back_kernel,
            "attend_back",
            (shape_of((width, span)), shape_of((2, kw2, span)), shape_of((2, kw2, span))),
            grid=(kv_heads,),
            in_specs=[q_spec(s)] + [head] * 4 + [probs_spec, per_head, whole((16, span)), column, column],
            out_specs=(per_head, halves, halves),
            scratch=[pltpu.VMEM((length, per * span), LOW)],
            micros=15,
        )(queries, *kv_all[s], stats[s], out_grad, delta, cos_cols, sin_cols)
        return grad_q, Terms(kv_keep, kv_send)

    mid_a, branch_a, dout_a, delta_a, gain_a = branch_of(0, after(middles[0], up_sum.pieces[0]))
    out_a.cross(branch_a)
    out_b.cross(branch_a)
    dout_a = after(dout_a, down_sum.second(branch_a))
    gq_a, kv_grad_a = attend_back_of(0, dout_a, delta_a)
    mid_b, branch_b, dout_b, delta_b, gain_b = branch_of(1, after(middles[1], gq_a))
    kv_grad_a.cross(branch_b)
    block_out = jnp.stack(
        [middle + three(after(term.all(), gq_a)) for middle, term in zip(middles, (out_a, out_b))]
    )
    dout_b = after(dout_b, gate_sum.second(gq_a), down_sum.third(gq_a))
    grown = shard + GAIN_ROWS
    cut = grown // PARTS
    spread_out = lambda columns: (shape_of((2, PARTS, cut, columns)),) * 2
    spread_spec = lambda columns: (whole((2, PARTS, cut, columns)),) * 2
    out_parts = call(
        out_weight_kernel,
        "out_weights",
        spread_out(width),
        prefetch=1,
        in_specs=[act] * 4,
        out_specs=spread_spec(width),
        scratch=[pltpu.VMEM((GROUP, grown, width), FULL)],
            micros=5,
    )(place_of, *attended, branch_a, branch_b)

    def owned(terms):
        keep, beside, across = terms.all()
        cuts = (slice(0, 4), slice(4, 6), slice(6, 7), slice(7, 8))
        return [three((keep[:, c], beside[:, c], across[c])).astype(LOW) for c in cuts]

    out_terms = Terms(*out_parts)
    gq_b, kv_grad_b = attend_back_of(1, after(dout_b, out_parts[0]), delta_b)
    kv_grad_b.cross(gq_b)
    out_terms.cross(kv_grad_b.across)
    up_sum.second(gq_b)
    gate_sum.third(gq_b)
    down_sum.own(gq_b)

    one = pl.BlockSpec((1, kw2, span), lambda *_: (0, 0, 0))
    kv_term = [one, one, whole((kw2, span))]
    terms = []
    for term in (kv_grad_a, kv_grad_b):
        terms += term.all()
    total = width + kw2
    w_keep, w_send, gkv = call(
        input_weight_kernel,
        "input_weights",
        spread_out(total) + (shape_of((kw2, rows)),),
        prefetch=1,
        in_specs=[whole((width, rows)), act, act] + kv_term * 2 + [table, table],
        out_specs=spread_spec(total) + (whole((kw2, rows)),),
        scratch=[pltpu.VMEM((GROUP, grown, total), FULL)],
            micros=7,
    )(place_of, norm_low, gq_a, gq_b, *terms, cos_cols, sin_cols)
    w_terms = Terms(w_keep, w_send)
    grad_tokens, gain_part = call(
        input_grad_kernel,
        "input_grad",
        (shape_of((seq_count, width, span), FULL), shape_of((8, width), FULL)),
        prefetch=1,
        in_specs=[act, act, whole((kw2, rows))]
        + [whole((shard, width))] * 4
        + [whole(kv_shard.shape)] * 4
        + [tok_spec, act, act]
        + [whole((8, width))] * 2,
        out_specs=(tok_spec, whole((8, width))),
        scratch=[pltpu.VMEM((width, width), LOW), pltpu.VMEM((width, kw2 + LANES), LOW)],
            micros=8,
    )(place_of, gq_a, gq_b, gkv, *q_blocks, *kv_blocks, tok_t, mid_a, mid_b, gain_a, gain_b)
    w_terms.cross(grad_tokens)
    out_sum = RepSum(owned(out_terms), ranks)
    w_sum = RepSum(owned(w_terms), ranks)
    grad_gains = all_sum(gain_part, ranks)

    up_sum.third(w_keep)
    gate_sum.own(w_keep)
    for chain in (out_sum, w_sum):
        chain.second()
        chain.third()
    every = (down_sum, gate_sum, up_sum, out_sum, w_sum)
    for chain in (up_sum, out_sum, w_sum):
        chain.own()
    for chain in every:
        chain.spread()
    down_pair, gate_pair, up_pair, out_pair, w_pair = [chain.done() for chain in every]

    def finished(name, pair):
        return call(
            forward_weights_kernel,
            name,
            shape_of((width, ff), FULL),
            prefetch=1,
            in_specs=[whole((4, part, ff))] * 2,
            out_specs=whole((width, ff)),
            micros=3.6,
        )(place_of, *pair)

    grad_down = finished("down_done", down_pair).T
    grad_gate = finished("gate_done", gate_pair)
    grad_up = finished("up_done", up_pair)
    grad_query, grad_key, grad_value, grad_out = call(
        attention_weights_kernel,
        "attention_weights",
        (
            shape_of((shard, width), FULL),
            shape_of((shard, kw), FULL),
            shape_of((shard, kw), FULL),
            shape_of((shard, width), FULL),
        ),
        prefetch=1,
        in_specs=[whole((4, cut, total))] * 2 + [whole((4, cut, width))] * 2,
        out_specs=(whole((shard, width)), whole((shard, kw)), whole((shard, kw)), whole((shard, width))),
        scratch=[pltpu.VMEM((grown, total), FULL), pltpu.VMEM((grown, width), FULL)],
            micros=4,
    )(place_of, *w_pair, *out_pair)
    own_gains = lax.dynamic_slice(grad_gains, (0, rank_grp * shard), (2, shard))
    return (
        jnp.swapaxes(block_out, 1, 2),
        jnp.swapaxes(grad_tokens, 1, 2),
        grad_query,
        grad_key,
        grad_value,
        grad_out,
        grad_gate,
        grad_up,
        grad_down,
        own_gains[0],
        own_gains[1],
    )


def solution(mesh):
    placed = (
        P("rep", "grp", None),
        P("grp", None),
        P("grp", None),
        P("grp", None),
        P("grp", None),
        P(None, "grp"),
        P(None, "grp"),
        P("grp", None),
        P("grp"),
        P("grp"),
        P("rep", None),
        P("rep", None),
        P("rep", "grp", None),
    )
    return jax.shard_map(
        body,
        mesh=mesh,
        in_specs=placed,
        out_specs=(
            P("rep", "grp", None),
            P("rep", "grp", None),
            P("grp", None),
            P("grp", None),
            P("grp", None),
            P("grp", None),
            P(None, "grp"),
            P(None, "grp"),
            P("grp", None),
            P("grp"),
            P("grp"),
        ),
        check_vma=False,
    )
```

time: 665 us -> 415 us (0.62)
  Pallas kernels: 0 us -> 197 us
  local copies, waits for them, and re-layouts: 195 us -> 21.2 us
  other arithmetic: 174 us -> 22.2 us
  matrix products: 151 us -> 0 us
  waiting for transfers between devices: 85.5 us -> 110 us
  starting transfers between devices: 44.1 us -> 57.3 us
    pallas_call x0 -> x23, Pallas kernels: none -> 197 us  [the longest x2 38.4 us: forward_back(): call(forward_back_kernel, 'forward_back', (shape_of((2, width, span)),) *...]
    dot_general x38 -> x0, matrix products: 151 us -> none  [the longest x10 34.4 us: right_dot(): lax.dot_general(left_mat, right_mat, (((1,), (1,)), ((), ())), preferred_...]
    gather x25 -> x0, local copies, waits for them, and re-layouts: 79.5 us -> none  [the longest x3 13.6 us: rep_sum(): slots = jnp.take(chunks, jnp.arange(8) ^ low_rank, axis=0)]
    convert_element_type x23 -> x26, other arithmetic: 50.6 us -> 12.2 us  [the longest x5 3.16 us: own(): mine = (mine + self.four.astype(FULL)).astype(LOW)]
    another operation x27 -> x3, other arithmetic: 37 us -> 1.09 us  [the longest x1 0.59 us: body(): jnp.stack([rank_grp, lax.axis_index('rep') % PARTS]).astype(jnp.int32)]
    unnamed x292 -> x160, local copies, waits for them, and re-layouts: 50.1 us -> 19.1 us
    ppermute x56 -> x78, waiting for transfers between devices: 85.5 us -> 110 us  [swap(): return lax.ppermute(values, axis, [(i, i ^ mask) for i in range(count)])]
    select_n x10 -> x0, other arithmetic: 19.6 us -> none  [the longest x3 12.5 us: rep_sum(): slots = jnp.take(chunks, jnp.arange(8) ^ low_rank, axis=0)]
  transfers between devices with their start and end apart: 56 -> 78, of which waited for: 13 -> 31; matrix products, arithmetic and copies ran while one was open for 74% -> 6% of each run, Pallas kernels for 0% -> 47%
where the time goes in v3:
time: 415 us; the launch traced here: 410 us
  Pallas kernels  197 us (47%)
  waiting for transfers between devices  110 us (27%)
  starting transfers between devices  57.3 us (14%)
  other arithmetic  22.2 us (5%)
  local copies, waits for them, and re-layouts  21.2 us (5%)
    ppermute x78, waiting for transfers between devices, swap(): return lax.ppermute(values, axis, [(i, i ^ mask) for i in range(count)])  110 us
    ppermute x78, starting transfers between devices, swap(): return lax.ppermute(values, axis, [(i, i ^ mask) for i in range(count)])  57.3 us
    pallas_call x2, Pallas kernels, forward_back(): call(forward_back_kernel, 'forward_back', (shape_of((2, width, span)),) *...  38.4 us
    pallas_call x2, Pallas kernels, attend_of(): call(functools.partial(attend_kernel, s), 'attend', (shape_of((kv_heads,...  33 us
    pallas_call x2, Pallas kernels, attend_back_of(): call(attend_back_kernel, 'attend_back', (shape_of((width, span)), shape_o...  30.5 us
    pallas_call x3, Pallas kernels, weights(): call(functools.partial(weight_kernel, stacked), name, tuple((shape_of((n,...  24.3 us
    unnamed x160, local copies, waits for them, and re-layouts  19.1 us
    pallas_call x2, Pallas kernels, branch_of(): call(branch_kernel, 'branch', (shape_of((width, span), FULL), shape_of((w...  11.2 us
  transfers between devices with their start and end apart: 78, of which 31 were waited for; matrix products, arithmetic and copies ran while one was open for 6% of the time, Pallas kernels for 47%

profile of v3, /device:TPU:0, one launch (start us, length us, event | category | flops | bytes accessed | tf_op | source)
XLA Modules:
  0.0 409.6 jit_solution(18406952381346179610)
XLA Ops:
  4.5 3.0 collective-permute-start.1
  8.6 5.5 %flip.1 = (bf16[1280,960]{1,0:T(8,128)(2,1)}, bf16[960,1280]{1,0:T(8,128)(2,1)}, bf16[640,960]{1,0:T(8,128)(2,1)}) custom-call(bf16[960,640]{1,0:T(8,128)(2,1)} %wg_ref, bf16[960,640]{1,0:T(8,128)(2,1)} %wu_ref.1, bf16[960,640]{1,0:T(8,128)(2,1)} %bitcast.96), custom_call_target="tpu_custom_call" | custom-call | flops 5000000000 | bytes 1048576 | tf_op jit(solution)/shard_map/flip/pallas_call | solution.py:517
  14.1 2.8 collective-permute-done.1.b2.k2
  19.4 4.6 %keys_values.1 = (bf16[960,512]{1,0:T(8,128)(2,1)}, bf16[640,256]{1,0:T(8,128)(2,1)}, bf16[640,256]{1,0:T(8,128)(2,1)}, bf16[960,128]{1,0:T(8,128)(2,1)}) custom-call(s32[2]{0:T(128)} %pad_add_fusion.ranks, bf16[2,960,256]{2,1,0:T(8,128)(2,1)} %bitcast.99, bf16[240,768]{1,0:T(8,128)(2,1)} %copy-done.16, bf16[240,768]{1,0:T(8,128)(2,1)} %copy-done.65, ...), custom_call_target="tpu_custom_call" | custom-call | flops 4499999744 | bytes 1048576 | tf_op jit(solution)/shard_map/keys_values/pallas_call | solution.py:529
  23.9 2.7 collective-permute-done.3.b2.q2
  27.1 1.7 collective-permute-start.6
  30.5 5.0 %queries.1.q_ref = bf16[960,512]{1,0:T(8,128)(2,1)} custom-call(s32[2]{0:T(128)} %pad_add_fusion.ranks, bf16[960,512]{1,0:T(8,128)(2,1)} %get-tuple-element.147.norm_ref, bf16[240,960]{1,0:T(8,128)(2,1)} %q0.1, bf16[240,960]{1,0:T(8,128)(2,1)} %copy-done.42, bf16[240,960]{1,0:T(8,128)(2,1)} %copy-done.41, bf16[240,960]{1,0:T(8,128)(2,1)} %copy-done.43, ...), custom_call_target="tpu_custom_call" | custom-call | flops 5000000000 | bytes 1048576 | tf_op jit(solution)/shard_map/queries/pallas_call | solution.py:541
  35.5 1.6 collective-permute-done.6.b2
  37.6 1.7 collective-permute-start.9
  40.8 16.8 %attend.2 = (bf16[5,1024,768]{2,1,0:T(8,128)(2,1)}, bf16[960,256]{1,0:T(8,128)(2,1)}) custom-call(s32[2]{0:T(128)} %pad_add_fusion.ranks, s32[2,4]{1,0:T(2,128)} %order.3, s32[2,2]{1,0:T(2,128)} %starts.3, bf16[960,512]{1,0:T(8,128)(2,1)} %queries.1.q_ref, bf16[640,256]{1,0:T(8,128)(2,1)} %get-tuple-element.151.b0, bf16[640,256]{1,0:T(8,128)(2,1)} %copy-done.73, ...), custom_call_target="tpu_custom_call" | custom-call | flops 16000000000 | bytes 1048576 | tf_op jit(solution)/shard_map/attend/pallas_call | solution.py:561
  60.3 8.4 %collective-permute-done.13.b2 = bf16[640,256]{1,0:T(8,128)(2,1)S(1)} collective-permute-done((bf16[640,256]{1,0:T(8,128)(2,1)S(1)}, bf16[640,256]{1,0:T(8,128)(2,1)S(1)}, u32[]{:S(2)}, u32[]{:S(2)}) %collective-permute-start.13) | collective-permute-done | bytes 327712 | tf_op jit(solution)/shard_map/ppermute | solution.py:37
  70.2 4.6 %middle.2 = (f32[960,256]{1,0:T(8,128)}, bf16[960,256]{1,0:T(8,128)(2,1)}) custom-call(s32[2]{0:T(128)} %pad_add_fusion.ranks, bf16[960,256]{1,0:T(8,128)(2,1)} %get-tuple-element.153.att_ref.att_a, bf16[240,960]{1,0:T(8,128)(2,1)} %b0.9, bf16[240,960]{1,0:T(8,128)(2,1)} %copy-done.45, bf16[240,960]{1,0:T(8,128)(2,1)} %copy-done.44, ...), custom_call_target="tpu_custom_call" | custom-call | flops 4600000000 | bytes 1048576 | tf_op jit(solution)/shard_map/middle/pallas_call | solution.py:574
  77.4 16.2 %attend.3 = (bf16[5,1024,768]{2,1,0:T(8,128)(2,1)}, bf16[960,256]{1,0:T(8,128)(2,1)}) custom-call(s32[2]{0:T(128)} %pad_add_fusion.ranks, s32[2,4]{1,0:T(2,128)} %order.3, s32[2,2]{1,0:T(2,128)} %starts.3, bf16[960,512]{1,0:T(8,128)(2,1)} %queries.1.q_ref, bf16[640,256]{1,0:T(8,128)(2,1)} %get-tuple-element.163.b0, bf16[640,256]{1,0:T(8,128)(2,1)} %copy-done.70, ...), custom_call_target="tpu_custom_call" | custom-call | flops 16000000000 | bytes 1048576 | tf_op jit(solution)/shard_map/attend/pallas_call | solution.py:561
  94.2 4.5 %middle.3 = (f32[960,256]{1,0:T(8,128)}, bf16[960,256]{1,0:T(8,128)(2,1)}) custom-call(s32[2]{0:T(128)} %pad_add_fusion.ranks, bf16[960,256]{1,0:T(8,128)(2,1)} %get-tuple-element.165.att_ref.att_b, bf16[240,960]{1,0:T(8,128)(2,1)} %b0.9, bf16[240,960]{1,0:T(8,128)(2,1)} %copy-done.45, bf16[240,960]{1,0:T(8,128)(2,1)} %copy-done.44, ...), custom_call_target="tpu_custom_call" | custom-call | flops 4600000000 | bytes 1048576 | tf_op jit(solution)/shard_map/middle/pallas_call | solution.py:574
  102.5 19.1 %forward_back.2 = (bf16[2,960,256]{2,1,0:T(8,128)(2,1)}, bf16[2,960,256]{2,1,0:T(8,128)(2,1)}, bf16[2,960,256]{2,1,0:T(8,128)(2,1)}, bf16[2,960,256]{2,1,0:T(8,1...) custom-call(bf16[960,256]{1,0:T(8,128)(2,1)} %get-tuple-element.167.x0.refs_0_, ...), custom_call_target="tpu_custom_call" | custom-call | flops 19000000512 | bytes 1048576 | tf_op jit(solution)/shard_map/forward_back/pallas_call | solution.py:601
  121.6 1.7 collective-permute-done.24.c2.refs_6_
  126.0 1.4 collective-permute-done.25.c1.refs_5_
  127.4 1.4 collective-permute-done.26.c3.refs_7_
  129.6 19.3 %forward_back.3 = (bf16[2,960,256]{2,1,0:T(8,128)(2,1)}, bf16[2,960,256]{2,1,0:T(8,128)(2,1)}, bf16[2,960,256]{2,1,0:T(8,128)(2,1)}, bf16[2,960,256]{2,1,0:T(8,1...) custom-call(bf16[960,256]{1,0:T(8,128)(2,1)} %get-tuple-element.179.x0.refs_4_, ...), custom_call_target="tpu_custom_call" | custom-call | flops 19000000512 | bytes 1048576 | tf_op jit(solution)/shard_map/forward_back/pallas_call | solution.py:601
  150.2 1.5 collective-permute-done.27.e1
  151.7 8.1 %down_weights.1 = (bf16[4,120,640]{2,1,0:T(8,128)(2,1)}, bf16[2,120,640]{2,1,0:T(8,128)(2,1)}, bf16[1,120,640]{2,1,0:T(8,128)(2,1)}, bf16[1,120,640]{2,1,0:T(8,128)(2,1)}) custom-call(s32[2]{0:T(128)} %pad_add_fusion.ranks, bf16[960,256]{1,0:T(8,128)(2,1)} %copy-done.14, bf16[960,256]{1,0:T(8,128)(2,1)} %copy-done.54, bf16[960,256]{1,0:T(8,128)(2,1)} %copy-done.49, ...), custom_call_target="tpu_custom_call" | custom-call | flops 8000000000 | bytes 1048576 | tf_op jit(solution)/shard_map/down_weights/pallas_call | solution.py:625
  159.8 1.6 collective-permute-start.32
  161.4 8.1 %gate_weights.1 = (bf16[4,120,640]{2,1,0:T(8,128)(2,1)}, bf16[2,120,640]{2,1,0:T(8,128)(2,1)}, bf16[1,120,640]{2,1,0:T(8,128)(2,1)}, bf16[1,120,640]{2,1,0:T(8,128)(2,1)}) custom-call(s32[2]{0:T(128)} %pad_add_fusion.ranks, bf16[960,256]{1,0:T(8,128)(2,1)} %get-tuple-element.167.x0.refs_0_, bf16[960,256]{1,0:T(8,128)(2,1)} %copy-done.51, ...), custom_call_target="tpu_custom_call" | custom-call | flops 8000000000 | bytes 1048576 | tf_op jit(solution)/shard_map/gate_weights/pallas_call | solution.py:625
  170.0 8.2 %up_weights.1 = (bf16[4,120,640]{2,1,0:T(8,128)(2,1)}, bf16[2,120,640]{2,1,0:T(8,128)(2,1)}, bf16[1,120,640]{2,1,0:T(8,128)(2,1)}, bf16[1,120,640]{2,1,0:T(8,128)(2,1)}) custom-call(s32[2]{0:T(128)} %pad_add_fusion.ranks, bf16[960,256]{1,0:T(8,128)(2,1)} %get-tuple-element.167.x0.refs_0_, bf16[960,256]{1,0:T(8,128)(2,1)} %copy-done.51, ...), custom_call_target="tpu_custom_call" | custom-call | flops 8000000000 | bytes 1048576 | tf_op jit(solution)/shard_map/up_weights/pallas_call | solution.py:625
  178.2 1.6 collective-permute-start.63
  181.7 5.6 %branch.2 = (f32[960,256]{1,0:T(8,128)}, bf16[960,256]{1,0:T(8,128)(2,1)}, bf16[960,256]{1,0:T(8,128)(2,1)}, f32[16,256]{1,0:T(8,128)}, f32[8,960]{1,0:T(8,128)}) custom-call(s32[2]{0:T(128)} %pad_add_fusion.ranks, f32[960,256]{1,0:T(8,128)} %get-tuple-element.198.mid_ref, bf16[2,960,256]{2,1,0:T(8,128)(2,1)} %bitcast.91, ...), custom_call_target="tpu_custom_call" | custom-call | flops 5699999744 | bytes 1048576 | tf_op jit(solution)/shard_map/branch/pallas_call | solution.py:655
  187.5 15.3 %attend_back.2 = (bf16[960,256]{1,0:T(8,128)(2,1)}, bf16[2,640,256]{2,1,0:T(8,128)(2,1)}, bf16[2,640,256]{2,1,0:T(8,128)(2,1)}) custom-call(bf16[960,512]{1,0:T(8,128)(2,1)} %queries.1.q_ref, bf16[640,256]{1,0:T(8,128)(2,1)} %get-tuple-element.151.b0, bf16[640,256]{1,0:T(8,128)(2,1)} %copy-done.73, bf16[640,256]{1,0:T(8,128)(2,1)} %copy-done.71, ...), custom_call_target="tpu_custom_call" | custom-call | flops 15000000512 | bytes 1048576 | tf_op jit(solution)/shard_map/attend_back/pallas_call | solution.py:677
  202.8 1.6 collective-permute-start.37
  205.3 5.6 %branch.3 = (f32[960,256]{1,0:T(8,128)}, bf16[960,256]{1,0:T(8,128)(2,1)}, bf16[960,256]{1,0:T(8,128)(2,1)}, f32[16,256]{1,0:T(8,128)}, f32[8,960]{1,0:T(8,128)}) custom-call(s32[2]{0:T(128)} %pad_add_fusion.ranks, f32[960,256]{1,0:T(8,128)} %get-tuple-element.225.mid_ref, bf16[2,960,256]{2,1,0:T(8,128)(2,1)} %bitcast.92, ...), custom_call_target="tpu_custom_call" | custom-call | flops 5699999744 | bytes 1048576 | tf_op jit(solution)/shard_map/branch/pallas_call | solution.py:655
  211.0 5.0 %out_weights.1 = (bf16[2,8,32,960]{3,2,1,0:T(8,128)(2,1)}, bf16[2,8,32,960]{3,2,1,0:T(8,128)(2,1)}) custom-call(s32[2]{0:T(128)} %pad_add_fusion.ranks, bf16[960,256]{1,0:T(8,128)(2,1)} %get-tuple-element.153.att_ref.att_a, bf16[960,256]{1,0:T(8,128)(2,1)} %get-tuple-element.165.att_ref.att_b, bf16[960,256]{1,0:T(8,128)(2,1)} %get-tuple-element.203.gb_a, ...), custom_call_target="tpu_custom_call" | custom-call | flops 5000000000 | bytes 1048576 | tf_op jit(solution)/shard_map/out_weights/pallas_call | solution.py:704
  216.6 15.2 %attend_back.3 = (bf16[960,256]{1,0:T(8,128)(2,1)}, bf16[2,640,256]{2,1,0:T(8,128)(2,1)}, bf16[2,640,256]{2,1,0:T(8,128)(2,1)}) custom-call(bf16[960,512]{1,0:T(8,128)(2,1)} %queries.1.q_ref, bf16[640,256]{1,0:T(8,128)(2,1)} %get-tuple-element.163.b0, bf16[640,256]{1,0:T(8,128)(2,1)} %copy-done.70, bf16[640,256]{1,0:T(8,128)(2,1)} %copy-done.69, ...), custom_call_target="tpu_custom_call" | custom-call | flops 15000000512 | bytes 1048576 | tf_op jit(solution)/shard_map/attend_back/pallas_call | solution.py:677
  231.8 2.6 collective-permute-start.69
  237.8 4.4 %collective-permute-done.69 = bf16[1,120,640]{2,1,0:T(8,128)(2,1)S(1)} collective-permute-done((bf16[1,120,640]{2,1,0:T(8,128)(2,1)S(1)}, bf16[1,120,640]{2,1,0:T(8,128)(2,1)S(1)}, u32[]{:S(2)}, u32[]{:S(2)}) %collective-permute-start.69) | collective-permute-done | bytes 153632 | tf_op jit(solution)/shard_map/ppermute | solution.py:37
  243.1 8.9 %collective-permute-done.70 = bf16[1,120,640]{2,1,0:T(8,128)(2,1)S(1)} collective-permute-done((bf16[1,120,640]{2,1,0:T(8,128)(2,1)S(1)}, bf16[1,120,640]{2,1,0:T(8,128)(2,1)S(1)}, u32[]{:S(2)}, u32[]{:S(2)}) %collective-permute-start.70) | collective-permute-done | bytes 153632 | tf_op jit(solution)/shard_map/ppermute | solution.py:37
  253.8 1.8 collective-permute-start.64
  255.7 4.0 collective-permute-done.34
  263.1 1.4 maximum_bitcast_fusion
  264.5 5.8 %collective-permute-done.39.a2 = bf16[640,256]{1,0:T(8,128)(2,1)S(1)} collective-permute-done((bf16[640,256]{1,0:T(8,128)(2,1)S(1)}, bf16[640,256]{1,0:T(8,128)(2,1)S(1)}, u32[]{:S(2)}, u32[]{:S(2)}) %collective-permute-start.39) | collective-permute-done | bytes 327712 | tf_op jit(solution)/shard_map/ppermute | solution.py:37
  271.6 4.5 %collective-permute-done.41.b2 = bf16[640,256]{1,0:T(8,128)(2,1)S(1)} collective-permute-done((bf16[640,256]{1,0:T(8,128)(2,1)S(1)}, bf16[640,256]{1,0:T(8,128)(2,1)S(1)}, u32[]{:S(2)}, u32[]{:S(2)}) %collective-permute-start.41) | collective-permute-done | bytes 327712 | tf_op jit(solution)/shard_map/ppermute | solution.py:37
  276.9 7.1 %input_weights.1 = (bf16[2,8,32,1600]{3,2,1,0:T(8,128)(2,1)}, bf16[2,8,32,1600]{3,2,1,0:T(8,128)(2,1)}, bf16[640,512]{1,0:T(8,128)(2,1)}) custom-call(s32[2]{0:T(128)} %pad_add_fusion.ranks, bf16[960,512]{1,0:T(8,128)(2,1)} %get-tuple-element.147.norm_ref, bf16[960,256]{1,0:T(8,128)(2,1)} %get-tuple-element.212.gq_a, ...), custom_call_target="tpu_custom_call" | custom-call | flops 7000000000 | bytes 1048576 | tf_op jit(solution)/shard_map/input_weights/pallas_call | solution.py:734
  284.0 8.2 %input_grad.1 = (f32[2,960,256]{2,1,0:T(8,128)}, f32[8,960]{1,0:T(8,128)}) custom-call(s32[2]{0:T(128)} %pad_add_fusion.ranks, bf16[960,256]{1,0:T(8,128)(2,1)} %get-tuple-element.212.gq_a, bf16[960,256]{1,0:T(8,128)(2,1)} %get-tuple-element.239.gq_b, bf16[640,512]{1,0:T(8,128)(2,1)} %get-tuple-element.248.gkv_ref, bf16[240,960]{1,0:T(8,128)(2,1)} %q0.1, ...), custom_call_target="tpu_custom_call" | custom-call | flops 8000000000 | bytes 1048576 | tf_op jit(solution)/shard_map/input_grad/pallas_call | solution.py:745
  300.7 1.4 collective-permute-start.65
  302.1 7.4 %collective-permute-done.75 = f32[8,960]{1,0:T(8,128)S(1)} collective-permute-done((f32[8,960]{1,0:T(8,128)S(1)}, f32[8,960]{1,0:T(8,128)S(1)}, u32[]{:S(2)}, u32[]{:S(2)}) %collective-permute-start.75) | collective-permute-done | bytes 30752 | tf_op jit(solution)/shard_map/ppermute | solution.py:37
  311.8 2.5 collective-permute-done.76
  316.4 3.0 collective-permute-start.66
  320.1 2.8 collective-permute-done.77
  324.7 3.7 down_done.1
  329.3 2.1 collective-permute-start.67
  333.0 13.7 %collective-permute-done.43 = bf16[8,32,1600]{2,1,0:T(8,128)(2,1)S(1)} collective-permute-done((bf16[8,32,1600]{2,1,0:T(8,128)(2,1)S(1)}, bf16[8,32,1600]{2,1,0:T(8,128)(2,1)S(1)}, u32[]{:S(2)}, u32[]{:S(2)}) %collective-permute-start.43) | collective-permute-done | bytes 819232 | tf_op jit(solution)/shard_map/ppermute | solution.py:37
  348.5 1.6 collective-permute-start.62
  352.7 6.9 %collective-permute-done.44 = bf16[4,32,1600]{2,1,0:T(8,128)(2,1)S(1)} collective-permute-done((bf16[4,32,1600]{2,1,0:T(8,128)(2,1)S(1)}, bf16[4,32,1600]{2,1,0:T(8,128)(2,1)S(1)}, u32[]{:S(2)}, u32[]{:S(2)}) %collective-permute-start.44) | collective-permute-done | bytes 409632 | tf_op jit(solution)/shard_map/ppermute | solution.py:37
  360.8 1.7 collective-permute-start.54
  362.5 3.3 collective-permute-done.45
  366.4 2.3 collective-permute-done.54
  369.8 5.7 %collective-permute-done.46 = bf16[1,32,1600]{2,1,0:T(8,128)(2,1)S(1)} collective-permute-done((bf16[1,32,1600]{2,1,0:T(8,128)(2,1)S(1)}, bf16[1,32,1600]{2,1,0:T(8,128)(2,1)S(1)}, u32[]{:S(2)}, u32[]{:S(2)}) %collective-permute-start.46) | collective-permute-done | bytes 102432 | tf_op jit(solution)/shard_map/ppermute | solution.py:37
  377.5 4.1 %collective-permute-done.47 = bf16[1,32,1600]{2,1,0:T(8,128)(2,1)S(1)} collective-permute-done((bf16[1,32,1600]{2,1,0:T(8,128)(2,1)S(1)}, bf16[1,32,1600]{2,1,0:T(8,128)(2,1)S(1)}, u32[]{:S(2)}, u32[]{:S(2)}) %collective-permute-start.47) | collective-permute-done | bytes 102432 | tf_op jit(solution)/shard_map/ppermute | solution.py:37
  381.7 3.7 gate_done.1
  385.4 2.2 collective-permute-done.48
  388.3 1.6 collective-permute-start.57
  390.7 3.7 up_done.1
  394.3 6.0 %collective-permute-done.57.odd_o = bf16[4,32,960]{2,1,0:T(8,128)(2,1)S(1)} collective-permute-done((bf16[4,32,960]{2,1,0:T(8,128)(2,1)S(1)}, bf16[4,32,960]{2,1,0:T(8,128)(2,1)S(1)}, u32[]{:S(2)}, u32[]{:S(2)}) %collective-permute-start.57) | collective-permute-done | bytes 245792 | tf_op jit(solution)/shard_map/ppermute | solution.py:37
  401.8 3.9 attention_weights.1
  405.7 1.9 copy.37
  407.6 1.9 copy.38
  (329 shorter events, 73.0 us)
Async XLA Ops:
  4.5 12.4 %collective-permute-start.1 = (bf16[240,768]{1,0:T(8,128)(2,1)S(1)}, bf16[240,768]{1,0:T(8,128)(2,1)S(1)}, u32[]{:S(2)}, u32[]{:S(2)}) collective-permute-start(bf16[240,768]{1,0:T(8,128)(2,1)S(1)} %fusion.14.b0.k0), channel_id=1, source_target_pairs={{0,16},{8,24},{16,0},{24,8},{1,17},{9,25},{17,1},{25,9},{2,18},{10... | collective-permute-start | bytes 1105928 | tf_op jit(solution)/shard_map/ppermute | solution.py:37
  7.5 11.0 %collective-permute-start = (bf16[240,768]{1,0:T(8,128)(2,1)S(1)}, bf16[240,768]{1,0:T(8,128)(2,1)S(1)}, u32[]{:S(2)}, u32[]{:S(2)}) collective-permute-start(bf16[240,768]{1,0:T(8,128)(2,1)S(1)} %fusion.14.b0.k0), channel_id=1, source_target_pairs={{0,8},{8,0},{16,24},{24,16},{1,9},{9,1},{17,25},{25,17},{2,10},{10... | collective-permute-start | bytes 1105928 | tf_op jit(solution)/shard_map/ppermute | solution.py:37
  7.5 19.1 %collective-permute-start.3 = (bf16[240,960]{1,0:T(8,128)(2,1)}, bf16[240,960]{1,0:T(8,128)(2,1)S(1)}, u32[]{:S(2)}, u32[]{:S(2)}) collective-permute-start(bf16[240,960]{1,0:T(8,128)(2,1)} %q0.1), channel_id=1, source_target_pairs={{0,16},{8,24},{16,0},{24,8},{1,17},{9,25},{17,1},{25,9},{2,18},{10... | collective-permute-start | bytes 1382408 | tf_op jit(solution)/shard_map/ppermute | solution.py:37
  27.1 10.0 %collective-permute-start.6 = (bf16[640,256]{1,0:T(8,128)(2,1)}, bf16[640,256]{1,0:T(8,128)(2,1)S(1)}, u32[]{:S(2)}, u32[]{:S(2)}) collective-permute-start(bf16[640,256]{1,0:T(8,128)(2,1)} %get-tuple-element.151.b0), channel_id=1, source_target_pairs={{0,16},{8,24},{16,0},{24,8},{1,17},{9,25},{17,1},{25,9},{2,18},{10... | collective-permute-start | bytes 983048 | tf_op jit(solution)/shard_map/ppermute | solution.py:37
  37.6 19.9 %collective-permute-start.9 = (bf16[240,960]{1,0:T(8,128)(2,1)S(1)}, bf16[240,960]{1,0:T(8,128)(2,1)S(1)}, u32[]{:S(2)}, u32[]{:S(2)}) collective-permute-start(bf16[240,960]{1,0:T(8,128)(2,1)S(1)} %copy-done.39), channel_id=1, source_target_pairs={{0,16},{8,24},{16,0},{24,8},{1,17},{9,25},{17,1},{25,9},{2,18},{10... | collective-permute-start | bytes 1382408 | tf_op jit(solution)/shard_map/ppermute | solution.py:37
  57.6 11.7 %collective-permute-start.10 = (bf16[240,960]{1,0:T(8,128)(2,1)S(1)}, bf16[240,960]{1,0:T(8,128)(2,1)S(1)}, u32[]{:S(2)}, u32[]{:S(2)}) collective-permute-start(bf16[240,960]{1,0:T(8,128)(2,1)S(1)} %copy-done.39), channel_id=1, source_target_pairs={{0,8},{8,0},{16,24},{24,16},{1,9},{9,1},{17,25},{25,17},{2,10},{10... | collective-permute-start | bytes 1382408 | tf_op jit(solution)/shard_map/ppermute | solution.py:37
  57.7 11.6 %collective-permute-start.11 = (bf16[240,960]{1,0:T(8,128)(2,1)S(1)}, bf16[240,960]{1,0:T(8,128)(2,1)S(1)}, u32[]{:S(2)}, u32[]{:S(2)}) collective-permute-start(bf16[240,960]{1,0:T(8,128)(2,1)S(1)} %collective-permute-done.9.b2), channel_id=1, source_target_pairs={{0,8},{8,0},{16,24},{24,16},{1,9},{9,1},{17,25},{25,17},{2,10},{10... | collective-permute-start | bytes 1382408 | tf_op jit(solution)/shard_map/ppermute | solution.py:37
  58.2 10.6 %collective-permute-start.13 = (bf16[640,256]{1,0:T(8,128)(2,1)S(1)}, bf16[640,256]{1,0:T(8,128)(2,1)S(1)}, u32[]{:S(2)}, u32[]{:S(2)}) collective-permute-start(bf16[640,256]{1,0:T(8,128)(2,1)S(1)} %copy-done.67), channel_id=1, source_target_pairs={{0,16},{8,24},{16,0},{24,8},{1,17},{9,25},{17,1},{25,9},{2,18},{10... | collective-permute-start | bytes 983048 | tf_op jit(solution)/shard_map/ppermute | solution.py:37
  59.4 34.3 %collective-permute-start.18 = (bf16[960,256]{1,0:T(8,128)(2,1)S(1)}, bf16[960,256]{1,0:T(8,128)(2,1)S(1)}, u32[]{:S(2)}, u32[]{:S(2)}) collective-permute-start(bf16[960,256]{1,0:T(8,128)(2,1)S(1)} %get-tuple-element.170.c0.refs_0_), channel_id=1, source_target_pairs={{0,16},{8,24},{16,0},{24,8},{1,17},{9,25},{17,1},{25,9},{2,18},{10... | collective-permute-start | bytes 1474568 | tf_op jit(solution)/shard_map/ppermute | solution.py:37
  68.7 7.2 %collective-permute-start.14 = (bf16[640,256]{1,0:T(8,128)(2,1)S(1)}, bf16[640,256]{1,0:T(8,128)(2,1)S(1)}, u32[]{:S(2)}, u32[]{:S(2)}) collective-permute-start(bf16[640,256]{1,0:T(8,128)(2,1)S(1)} %copy-done.67), channel_id=1, source_target_pairs={{0,8},{8,0},{16,24},{24,16},{1,9},{9,1},{17,25},{25,17},{2,10},{10... | collective-permute-start | bytes 983048 | tf_op jit(solution)/shard_map/ppermute | solution.py:37
  68.7 7.2 %collective-permute-start.15 = (bf16[640,256]{1,0:T(8,128)(2,1)S(1)}, bf16[640,256]{1,0:T(8,128)(2,1)S(1)}, u32[]{:S(2)}, u32[]{:S(2)}) collective-permute-start(bf16[640,256]{1,0:T(8,128)(2,1)S(1)} %collective-permute-done.13.b2), channel_id=1, source_target_pairs={{0,8},{8,0},{16,24},{24,16},{1,9},{9,1},{17,25},{25,17},{2,10},{10... | collective-permute-start | bytes 983048 | tf_op jit(solution)/shard_map/ppermute | solution.py:37
  74.8 24.0 %collective-permute-start.12 = (bf16[960,256]{1,0:T(8,128)(2,1)}, bf16[960,256]{1,0:T(8,128)(2,1)S(1)}, u32[]{:S(2)}, u32[]{:S(2)}) collective-permute-start(bf16[960,256]{1,0:T(8,128)(2,1)} %get-tuple-element.167.x0.refs_0_), channel_id=1, source_target_pairs={{0,16},{8,24},{16,0},{24,8},{1,17},{9,25},{17,1},{25,9},{2,18},{10... | collective-permute-start | bytes 1474568 | tf_op jit(solution)/shard_map/ppermute | solution.py:37
  93.6 6.6 %collective-permute-start.19 = (bf16[960,256]{1,0:T(8,128)(2,1)S(1)}, bf16[960,256]{1,0:T(8,128)(2,1)S(1)}, u32[]{:S(2)}, u32[]{:S(2)}) collective-permute-start(bf16[960,256]{1,0:T(8,128)(2,1)S(1)} %get-tuple-element.170.c0.refs_0_), channel_id=1, source_target_pairs={{0,8},{8,0},{16,24},{24,16},{1,9},{9,1},{17,25},{25,17},{2,10},{10... | collective-permute-start | bytes 1474568 | tf_op jit(solution)/shard_map/ppermute | solution.py:37
  93.7 7.7 %collective-permute-start.20 = (bf16[960,256]{1,0:T(8,128)(2,1)S(1)}, bf16[960,256]{1,0:T(8,128)(2,1)S(1)}, u32[]{:S(2)}, u32[]{:S(2)}) collective-permute-start(bf16[960,256]{1,0:T(8,128)(2,1)S(1)} %collective-permute-done.18.c2.refs_2_), channel_id=1, source_target_pairs={{0,8},{8,0},{16,24},{24,16},{1,9},{9,1},{17,25},{25,17},{2,10},{10... | collective-permute-start | bytes 1474568 | tf_op jit(solution)/shard_map/ppermute | solution.py:37
  99.4 24.0 %collective-permute-start.21 = (bf16[960,256]{1,0:T(8,128)(2,1)}, bf16[960,256]{1,0:T(8,128)(2,1)S(1)}, u32[]{:S(2)}, u32[]{:S(2)}) collective-permute-start(bf16[960,256]{1,0:T(8,128)(2,1)} %get-tuple-element.179.x0.refs_4_), channel_id=1, source_target_pairs={{0,16},{8,24},{16,0},{24,8},{1,17},{9,25},{17,1},{25,9},{2,18},{10... | collective-permute-start | bytes 1474568 | tf_op jit(solution)/shard_map/ppermute | solution.py:37
  100.3 23.0 %collective-permute-start.24 = (bf16[960,256]{1,0:T(8,128)(2,1)S(1)}, bf16[960,256]{1,0:T(8,128)(2,1)S(1)}, u32[]{:S(2)}, u32[]{:S(2)}) collective-permute-start(bf16[960,256]{1,0:T(8,128)(2,1)S(1)} %get-tuple-element.183.c0.refs_4_), channel_id=1, source_target_pairs={{0,16},{8,24},{16,0},{24,8},{1,17},{9,25},{17,1},{25,9},{2,18},{10... | collective-permute-start | bytes 1474568 | tf_op jit(solution)/shard_map/ppermute | solution.py:37
  124.4 24.6 %collective-permute-start.29 = (bf16[2,960,256]{2,1,0:T(8,128)(2,1)}, bf16[2,960,256]{2,1,0:T(8,128)(2,1)S(1)}, u32[]{:S(2)}, u32[]{:S(2)}) collective-permute-start(bf16[2,960,256]{2,1,0:T(8,128)(2,1)} %get-tuple-element.200), channel_id=1, source_target_pairs={{0,8},{8,0},{16,24},{24,16},{1,9},{9,1},{17,25},{25,17},{2,10},{10... | collective-permute-start | bytes 2949128 | tf_op jit(solution)/shard_map/ppermute | solution.py:37
  149.2 31.7 %collective-permute-start.30 = (bf16[960,256]{1,0:T(8,128)(2,1)S(1)}, bf16[960,256]{1,0:T(8,128)(2,1)S(1)}, u32[]{:S(2)}, u32[]{:S(2)}) collective-permute-start(bf16[960,256]{1,0:T(8,128)(2,1)S(1)} %fusion.9), channel_id=1, source_target_pairs={{0,16},{8,24},{16,0},{24,8},{1,17},{9,25},{17,1},{25,9},{2,18},{10... | collective-permute-start | bytes 1474568 | tf_op jit(solution)/shard_map/ppermute | solution.py:37
  159.8 27.5 %collective-permute-start.32 = (bf16[4,120,640]{2,1,0:T(8,128)(2,1)}, bf16[4,120,640]{2,1,0:T(8,128)(2,1)S(1)}, u32[]{:S(2)}, u32[]{:S(2)}) collective-permute-start(bf16[4,120,640]{2,1,0:T(8,128)(2,1)} %get-tuple-element.189), channel_id=1, source_target_pairs={{0,1},{1,0},{2,3},{3,2},{4,5},{5,4},{6,7},{7,6},{8,9},{9,8},{10,11... | collective-permute-start | bytes 1843208 | tf_op jit(solution)/shard_map/ppermute | solution.py:37
  169.4 33.4 %collective-permute-start.36 = (bf16[4,120,640]{2,1,0:T(8,128)(2,1)}, bf16[4,120,640]{2,1,0:T(8,128)(2,1)S(1)}, u32[]{:S(2)}, u32[]{:S(2)}) collective-permute-start(bf16[4,120,640]{2,1,0:T(8,128)(2,1)} %get-tuple-element.192), channel_id=1, source_target_pairs={{0,1},{1,0},{2,3},{3,2},{4,5},{5,4},{6,7},{7,6},{8,9},{9,8},{10,11... | collective-permute-start | bytes 1843208 | tf_op jit(solution)/shard_map/ppermute | solution.py:37
  178.2 53.6 %collective-permute-start.63 = (bf16[4,120,640]{2,1,0:T(8,128)(2,1)}, bf16[4,120,640]{2,1,0:T(8,128)(2,1)S(1)}, u32[]{:S(2)}, u32[]{:S(2)}) collective-permute-start(bf16[4,120,640]{2,1,0:T(8,128)(2,1)} %get-tuple-element.197), channel_id=1, source_target_pairs={{0,1},{1,0},{2,3},{3,2},{4,5},{5,4},{6,7},{7,6},{8,9},{9,8},{10,11... | collective-permute-start | bytes 1843208 | tf_op jit(solution)/shard_map/ppermute | solution.py:37
  179.9 24.6 %collective-permute-start.35 = (bf16[960,256]{1,0:T(8,128)(2,1)S(1)}, bf16[960,256]{1,0:T(8,128)(2,1)S(1)}, u32[]{:S(2)}, u32[]{:S(2)}) collective-permute-start(bf16[960,256]{1,0:T(8,128)(2,1)S(1)} %fusion.12), channel_id=1, source_target_pairs={{0,16},{8,24},{16,0},{24,8},{1,17},{9,25},{17,1},{25,9},{2,18},{10... | collective-permute-start | bytes 1474568 | tf_op jit(solution)/shard_map/ppermute | solution.py:37
  180.9 54.4 %collective-permute-start.28 = (bf16[2,960,256]{2,1,0:T(8,128)(2,1)}, bf16[2,960,256]{2,1,0:T(8,128)(2,1)S(1)}, u32[]{:S(2)}, u32[]{:S(2)}) collective-permute-start(bf16[2,960,256]{2,1,0:T(8,128)(2,1)} %get-tuple-element.193), channel_id=1, source_target_pairs={{0,8},{8,0},{16,24},{24,16},{1,9},{9,1},{17,25},{25,17},{2,10},{10... | collective-permute-start | bytes 2949128 | tf_op jit(solution)/shard_map/ppermute | solution.py:37
  187.3 49.3 %collective-permute-start.33 = (bf16[2,960,256]{2,1,0:T(8,128)(2,1)}, bf16[2,960,256]{2,1,0:T(8,128)(2,1)S(1)}, u32[]{:S(2)}, u32[]{:S(2)}) collective-permute-start(bf16[2,960,256]{2,1,0:T(8,128)(2,1)} %get-tuple-element.218), channel_id=1, source_target_pairs={{0,8},{8,0},{16,24},{24,16},{1,9},{9,1},{17,25},{25,17},{2,10},{10... | collective-permute-start | bytes 2949128 | tf_op jit(solution)/shard_map/ppermute | solution.py:37
  202.8 13.1 %collective-permute-start.37 = (bf16[2,120,640]{2,1,0:T(8,128)(2,1)S(1)}, bf16[2,120,640]{2,1,0:T(8,128)(2,1)S(1)}, u32[]{:S(2)}, u32[]{:S(2)}) collective-permute-start(bf16[2,120,640]{2,1,0:T(8,128)(2,1)S(1)} %add_convert_fusion.10), channel_id=1, source_target_pairs={{0,2},{1,3},{2,0},{3,1},{4,6},{5,7},{6,4},{7,5},{8,10},{9,11},{10,... | collective-permute-start | bytes 921608 | tf_op jit(solution)/shard_map/ppermute | solution.py:37
  204.6 29.9 %collective-permute-start.58 = (bf16[2,120,640]{2,1,0:T(8,128)(2,1)S(1)}, bf16[2,120,640]{2,1,0:T(8,128)(2,1)S(1)}, u32[]{:S(2)}, u32[]{:S(2)}) collective-permute-start(bf16[2,120,640]{2,1,0:T(8,128)(2,1)S(1)} %add_convert_fusion.9), channel_id=1, source_target_pairs={{0,2},{1,3},{2,0},{3,1},{4,6},{5,7},{6,4},{7,5},{8,10},{9,11},{10,... | collective-permute-start | bytes 921608 | tf_op jit(solution)/shard_map/ppermute | solution.py:37
  215.9 36.8 %collective-permute-start.38 = (bf16[2,640,256]{2,1,0:T(8,128)(2,1)}, bf16[2,640,256]{2,1,0:T(8,128)(2,1)}, u32[]{:S(2)}, u32[]{:S(2)}) collective-permute-start(bf16[2,640,256]{2,1,0:T(8,128)(2,1)} %get-tuple-element.241), channel_id=1, source_target_pairs={{0,8},{8,0},{16,24},{24,16},{1,9},{9,1},{17,25},{25,17},{2,10},{10... | collective-permute-start | bytes 1966088 | tf_op jit(solution)/shard_map/ppermute | solution.py:37
  231.8 10.3 %collective-permute-start.69 = (bf16[1,120,640]{2,1,0:T(8,128)(2,1)S(1)}, bf16[1,120,640]{2,1,0:T(8,128)(2,1)S(1)}, u32[]{:S(2)}, u32[]{:S(2)}) collective-permute-start(bf16[1,120,640]{2,1,0:T(8,128)(2,1)S(1)} %add_convert_fusion.17), channel_id=1, source_target_pairs={{0,4},{1,5},{2,6},{3,7},{4,0},{5,1},{6,2},{7,3},{8,12},{9,13},{10,... | collective-permute-start | bytes 460808 | tf_op jit(solution)/shard_map/ppermute | solution.py:37
  234.5 26.3 %collective-permute-start.40 = (bf16[2,640,256]{2,1,0:T(8,128)(2,1)}, bf16[2,640,256]{2,1,0:T(8,128)(2,1)S(1)}, u32[]{:S(2)}, u32[]{:S(2)}) collective-permute-start(bf16[2,640,256]{2,1,0:T(8,128)(2,1)} %get-tuple-element.245), channel_id=1, source_target_pairs={{0,8},{8,0},{16,24},{24,16},{1,9},{9,1},{17,25},{25,17},{2,10},{10... | collective-permute-start | bytes 1966088 | tf_op jit(solution)/shard_map/ppermute | solution.py:37
  235.5 18.4 %collective-permute-start.31 = (bf16[960,256]{1,0:T(8,128)(2,1)S(1)}, bf16[960,256]{1,0:T(8,128)(2,1)S(1)}, u32[]{:S(2)}, u32[]{:S(2)}) collective-permute-start(bf16[960,256]{1,0:T(8,128)(2,1)S(1)} %fusion.10), channel_id=1, source_target_pairs={{0,16},{8,24},{16,0},{24,8},{1,17},{9,25},{17,1},{25,9},{2,18},{10... | collective-permute-start | bytes 1474568 | tf_op jit(solution)/shard_map/ppermute | solution.py:37
  236.8 22.9 %collective-permute-start.34 = (bf16[960,256]{1,0:T(8,128)(2,1)S(1)}, bf16[960,256]{1,0:T(8,128)(2,1)S(1)}, u32[]{:S(2)}, u32[]{:S(2)}) collective-permute-start(bf16[960,256]{1,0:T(8,128)(2,1)S(1)} %fusion.11), channel_id=1, source_target_pairs={{0,16},{8,24},{16,0},{24,8},{1,17},{9,25},{17,1},{25,9},{2,18},{10... | collective-permute-start | bytes 1474568 | tf_op jit(solution)/shard_map/ppermute | solution.py:37
  242.3 9.7 %collective-permute-start.70 = (bf16[1,120,640]{2,1,0:T(8,128)(2,1)S(1)}, bf16[1,120,640]{2,1,0:T(8,128)(2,1)S(1)}, u32[]{:S(2)}, u32[]{:S(2)}) collective-permute-start(bf16[1,120,640]{2,1,0:T(8,128)(2,1)S(1)} %add_convert_fusion.12), channel_id=1, source_target_pairs={{0,4},{1,5},{2,6},{3,7},{4,0},{5,1},{6,2},{7,3},{8,12},{9,13},{10,... | collective-permute-start | bytes 460808 | tf_op jit(solution)/shard_map/ppermute | solution.py:37
  252.0 48.7 %collective-permute-start.50 = (bf16[2,8,32,960]{3,2,1,0:T(8,128)(2,1)}, bf16[2,8,32,960]{3,2,1,0:T(8,128)(2,1)S(1)}, u32[]{:S(2)}, u32[]{:S(2)}) collective-permute-start(bf16[2,8,32,960]{3,2,1,0:T(8,128)(2,1)} %get-tuple-element.258), channel_id=1, source_target_pairs={{0,8},{8,0},{16,24},{24,16},{1,9},{9,1},{17,25},{25,17},{2,10},{10... | collective-permute-start | bytes 2949128 | tf_op jit(solution)/shard_map/ppermute | solution.py:37
  252.8 40.2 %collective-permute-start.59 = (bf16[1,120,640]{2,1,0:T(8,128)(2,1)}, bf16[1,120,640]{2,1,0:T(8,128)(2,1)}, u32[]{:S(2)}, u32[]{:S(2)}) collective-permute-start(bf16[1,120,640]{2,1,0:T(8,128)(2,1)} %add_convert_fusion.16), channel_id=1, source_target_pairs={{0,4},{1,5},{2,6},{3,7},{4,0},{5,1},{6,2},{7,3},{8,12},{9,13},{10,... | collective-permute-start | bytes 460808 | tf_op jit(solution)/shard_map/ppermute | solution.py:37
  253.8 43.0 %collective-permute-start.64 = (bf16[2,120,640]{2,1,0:T(8,128)(2,1)}, bf16[2,120,640]{2,1,0:T(8,128)(2,1)}, u32[]{:S(2)}, u32[]{:S(2)}) collective-permute-start(bf16[2,120,640]{2,1,0:T(8,128)(2,1)} %add_convert_fusion.8), channel_id=1, source_target_pairs={{0,2},{1,3},{2,0},{3,1},{4,6},{5,7},{6,4},{7,5},{8,10},{9,11},{10,... | collective-permute-start | bytes 921608 | tf_op jit(solution)/shard_map/ppermute | solution.py:37
  259.7 10.6 %collective-permute-start.39 = (bf16[640,256]{1,0:T(8,128)(2,1)S(1)}, bf16[640,256]{1,0:T(8,128)(2,1)S(1)}, u32[]{:S(2)}, u32[]{:S(2)}) collective-permute-start(bf16[640,256]{1,0:T(8,128)(2,1)S(1)} %fusion.15), channel_id=1, source_target_pairs={{0,16},{8,24},{16,0},{24,8},{1,17},{9,25},{17,1},{25,9},{2,18},{10... | collective-permute-start | bytes 983048 | tf_op jit(solution)/shard_map/ppermute | solution.py:37
  261.6 14.5 %collective-permute-start.41 = (bf16[640,256]{1,0:T(8,128)(2,1)S(1)}, bf16[640,256]{1,0:T(8,128)(2,1)S(1)}, u32[]{:S(2)}, u32[]{:S(2)}) collective-permute-start(bf16[640,256]{1,0:T(8,128)(2,1)S(1)} %fusion.16), channel_id=1, source_target_pairs={{0,16},{8,24},{16,0},{24,8},{1,17},{9,25},{17,1},{25,9},{2,18},{10... | collective-permute-start | bytes 983048 | tf_op jit(solution)/shard_map/ppermute | solution.py:37
  270.3 22.0 %collective-permute-start.71 = (bf16[2,120,640]{2,1,0:T(8,128)(2,1)}, bf16[2,120,640]{2,1,0:T(8,128)(2,1)S(1)}, u32[]{:S(2)}, u32[]{:S(2)}) collective-permute-start(bf16[2,120,640]{2,1,0:T(8,128)(2,1)} %pad_maximum_fusion.6), channel_id=1, source_target_pairs={{0,2},{1,3},{2,0},{3,1},{4,6},{5,7},{6,4},{7,5},{8,10},{9,11},{10,... | collective-permute-start | bytes 921608 | tf_op jit(solution)/shard_map/ppermute | solution.py:37
  284.0 39.0 %collective-permute-start.42 = (bf16[2,8,32,1600]{3,2,1,0:T(8,128)(2,1)}, bf16[2,8,32,1600]{3,2,1,0:T(8,128)(2,1)S(1)}, u32[]{:S(2)}, u32[]{:S(2)}) collective-permute-start(bf16[2,8,32,1600]{3,2,1,0:T(8,128)(2,1)} %get-tuple-element.255), channel_id=1, source_target_pairs={{0,8},{8,0},{16,24},{24,16},{1,9},{9,1},{17,25},{25,17},{2,10},{10... | collective-permute-start | bytes 4915208 | tf_op jit(solution)/shard_map/ppermute | solution.py:37
  292.9 31.7 %collective-permute-start.72 = (bf16[4,120,640]{2,1,0:T(8,128)(2,1)S(1)}, bf16[4,120,640]{2,1,0:T(8,128)(2,1)}, u32[]{:S(2)}, u32[]{:S(2)}) collective-permute-start(bf16[4,120,640]{2,1,0:T(8,128)(2,1)S(1)} %pad_maximum_fusion.2.even), channel_id=1, source_target_pairs={{0,1},{1,0},{2,3},{3,2},{4,5},{5,4},{6,7},{7,6},{8,9},{9,8},{10,11... | collective-permute-start | bytes 1843208 | tf_op jit(solution)/shard_map/ppermute | solution.py:37
  296.9 19.5 %collective-permute-start.60 = (bf16[1,120,640]{2,1,0:T(8,128)(2,1)S(1)}, bf16[1,120,640]{2,1,0:T(8,128)(2,1)S(1)}, u32[]{:S(2)}, u32[]{:S(2)}) collective-permute-start(bf16[1,120,640]{2,1,0:T(8,128)(2,1)S(1)} %add_convert_fusion.15), channel_id=1, source_target_pairs={{0,4},{1,5},{2,6},{3,7},{4,0},{5,1},{6,2},{7,3},{8,12},{9,13},{10,... | collective-permute-start | bytes 460808 | tf_op jit(solution)/shard_map/ppermute | solution.py:37
  298.6 10.9 %collective-permute-start.75 = (f32[8,960]{1,0:T(8,128)S(1)}, f32[8,960]{1,0:T(8,128)S(1)}, u32[]{:S(2)}, u32[]{:S(2)}) collective-permute-start(f32[8,960]{1,0:T(8,128)S(1)} %add.373), channel_id=1, source_target_pairs={{0,1},{1,0},{2,3},{3,2},{4,5},{5,4},{6,7},{7,6},{8,9},{9,8},{10,11... | collective-permute-start | bytes 92168 | tf_op jit(solution)/shard_map/ppermute | solution.py:37
  300.7 14.6 %collective-permute-start.65 = (bf16[1,120,640]{2,1,0:T(8,128)(2,1)S(1)}, bf16[1,120,640]{2,1,0:T(8,128)(2,1)S(1)}, u32[]{:S(2)}, u32[]{:S(2)}) collective-permute-start(bf16[1,120,640]{2,1,0:T(8,128)(2,1)S(1)} %add_convert_fusion.14), channel_id=1, source_target_pairs={{0,4},{1,5},{2,6},{3,7},{4,0},{5,1},{6,2},{7,3},{8,12},{9,13},{10,... | collective-permute-start | bytes 460808 | tf_op jit(solution)/shard_map/ppermute | solution.py:37
  309.5 4.9 %collective-permute-start.76 = (f32[8,960]{1,0:T(8,128)S(1)}, f32[8,960]{1,0:T(8,128)S(1)}, u32[]{:S(2)}, u32[]{:S(2)}) collective-permute-start(f32[8,960]{1,0:T(8,128)S(1)} %add.374), channel_id=1, source_target_pairs={{0,2},{1,3},{2,0},{3,1},{4,6},{5,7},{6,4},{7,5},{8,10},{9,11},{10,... | collective-permute-start | bytes 92168 | tf_op jit(solution)/shard_map/ppermute | solution.py:37
  314.4 17.0 %collective-permute-start.51 = (bf16[8,32,960]{2,1,0:T(8,128)(2,1)}, bf16[8,32,960]{2,1,0:T(8,128)(2,1)}, u32[]{:S(2)}, u32[]{:S(2)}) collective-permute-start(bf16[8,32,960]{2,1,0:T(8,128)(2,1)} %fusion.7), channel_id=1, source_target_pairs={{0,16},{8,24},{16,0},{24,8},{1,17},{9,25},{17,1},{25,9},{2,18},{10... | collective-permute-start | bytes 1474568 | tf_op jit(solution)/shard_map/ppermute | solution.py:37
  315.3 7.6 %collective-permute-start.77 = (f32[8,960]{1,0:T(8,128)S(1)}, f32[8,960]{1,0:T(8,128)S(1)}, u32[]{:S(2)}, u32[]{:S(2)}) collective-permute-start(f32[8,960]{1,0:T(8,128)S(1)} %add.375), channel_id=1, source_target_pairs={{0,4},{1,5},{2,6},{3,7},{4,0},{5,1},{6,2},{7,3},{8,12},{9,13},{10,... | collective-permute-start | bytes 92168 | tf_op jit(solution)/shard_map/ppermute | solution.py:37
  316.4 11.9 %collective-permute-start.66 = (bf16[1,120,640]{2,1,0:T(8,128)(2,1)S(1)}, bf16[1,120,640]{2,1,0:T(8,128)(2,1)}, u32[]{:S(2)}, u32[]{:S(2)}) collective-permute-start(bf16[1,120,640]{2,1,0:T(8,128)(2,1)S(1)} %add_convert_fusion.13), channel_id=1, source_target_pairs={{0,4},{1,5},{2,6},{3,7},{4,0},{5,1},{6,2},{7,3},{8,12},{9,13},{10,... | collective-permute-start | bytes 460808 | tf_op jit(solution)/shard_map/ppermute | solution.py:37
  322.9 24.5 %collective-permute-start.61 = (bf16[2,120,640]{2,1,0:T(8,128)(2,1)}, bf16[2,120,640]{2,1,0:T(8,128)(2,1)}, u32[]{:S(2)}, u32[]{:S(2)}) collective-permute-start(bf16[2,120,640]{2,1,0:T(8,128)(2,1)} %pad_maximum_fusion.4), channel_id=1, source_target_pairs={{0,2},{1,3},{2,0},{3,1},{4,6},{5,7},{6,4},{7,5},{8,10},{9,11},{10,... | collective-permute-start | bytes 921608 | tf_op jit(solution)/shard_map/ppermute | solution.py:37
  323.2 23.4 %collective-permute-start.43 = (bf16[8,32,1600]{2,1,0:T(8,128)(2,1)S(1)}, bf16[8,32,1600]{2,1,0:T(8,128)(2,1)S(1)}, u32[]{:S(2)}, u32[]{:S(2)}) collective-permute-start(bf16[8,32,1600]{2,1,0:T(8,128)(2,1)S(1)} %fusion.4), channel_id=1, source_target_pairs={{0,16},{8,24},{16,0},{24,8},{1,17},{9,25},{17,1},{25,9},{2,18},{10... | collective-permute-start | bytes 2457608 | tf_op jit(solution)/shard_map/ppermute | solution.py:37
  329.3 20.8 %collective-permute-start.67 = (bf16[2,120,640]{2,1,0:T(8,128)(2,1)S(1)}, bf16[2,120,640]{2,1,0:T(8,128)(2,1)S(1)}, u32[]{:S(2)}, u32[]{:S(2)}) collective-permute-start(bf16[2,120,640]{2,1,0:T(8,128)(2,1)S(1)} %pad_maximum_fusion.5), channel_id=1, source_target_pairs={{0,2},{1,3},{2,0},{3,1},{4,6},{5,7},{6,4},{7,5},{8,10},{9,11},{10,... | collective-permute-start | bytes 921608 | tf_op jit(solution)/shard_map/ppermute | solution.py:37
  332.4 19.2 %collective-permute-start.52 = (bf16[4,32,960]{2,1,0:T(8,128)(2,1)S(1)}, bf16[4,32,960]{2,1,0:T(8,128)(2,1)S(1)}, u32[]{:S(2)}, u32[]{:S(2)}) collective-permute-start(bf16[4,32,960]{2,1,0:T(8,128)(2,1)S(1)} %fusion.8), channel_id=1, source_target_pairs={{0,1},{1,0},{2,3},{3,2},{4,5},{5,4},{6,7},{7,6},{8,9},{9,8},{10,11... | collective-permute-start | bytes 737288 | tf_op jit(solution)/shard_map/ppermute | solution.py:37
  346.8 12.8 %collective-permute-start.44 = (bf16[4,32,1600]{2,1,0:T(8,128)(2,1)S(1)}, bf16[4,32,1600]{2,1,0:T(8,128)(2,1)S(1)}, u32[]{:S(2)}, u32[]{:S(2)}) collective-permute-start(bf16[4,32,1600]{2,1,0:T(8,128)(2,1)S(1)} %fusion.5), channel_id=1, source_target_pairs={{0,1},{1,0},{2,3},{3,2},{4,5},{5,4},{6,7},{7,6},{8,9},{9,8},{10,11... | collective-permute-start | bytes 1228808 | tf_op jit(solution)/shard_map/ppermute | solution.py:37
  348.5 33.2 %collective-permute-start.62 = (bf16[4,120,640]{2,1,0:T(8,128)(2,1)S(1)}, bf16[4,120,640]{2,1,0:T(8,128)(2,1)}, u32[]{:S(2)}, u32[]{:S(2)}) collective-permute-start(bf16[4,120,640]{2,1,0:T(8,128)(2,1)S(1)} %pad_maximum_fusion.even), channel_id=1, source_target_pairs={{0,1},{1,0},{2,3},{3,2},{4,5},{5,4},{6,7},{7,6},{8,9},{9,8},{10,11... | collective-permute-start | bytes 1843208 | tf_op jit(solution)/shard_map/ppermute | solution.py:37
  351.1 38.8 %collective-permute-start.68 = (bf16[4,120,640]{2,1,0:T(8,128)(2,1)S(1)}, bf16[4,120,640]{2,1,0:T(8,128)(2,1)S(1)}, u32[]{:S(2)}, u32[]{:S(2)}) collective-permute-start(bf16[4,120,640]{2,1,0:T(8,128)(2,1)S(1)} %pad_maximum_fusion.1.even), channel_id=1, source_target_pairs={{0,1},{1,0},{2,3},{3,2},{4,5},{5,4},{6,7},{7,6},{8,9},{9,8},{10,11... | collective-permute-start | bytes 1843208 | tf_op jit(solution)/shard_map/ppermute | solution.py:37
  352.6 7.2 %collective-permute-start.53 = (bf16[2,32,960]{2,1,0:T(8,128)(2,1)S(1)}, bf16[2,32,960]{2,1,0:T(8,128)(2,1)S(1)}, u32[]{:S(2)}, u32[]{:S(2)}) collective-permute-start(bf16[2,32,960]{2,1,0:T(8,128)(2,1)S(1)} %add_convert_fusion.18), channel_id=1, source_target_pairs={{0,2},{1,3},{2,0},{3,1},{4,6},{5,7},{6,4},{7,5},{8,10},{9,11},{10,... | collective-permute-start | bytes 368648 | tf_op jit(solution)/shard_map/ppermute | solution.py:37
  359.8 5.9 %collective-permute-start.45 = (bf16[2,32,1600]{2,1,0:T(8,128)(2,1)S(1)}, bf16[2,32,1600]{2,1,0:T(8,128)(2,1)S(1)}, u32[]{:S(2)}, u32[]{:S(2)}) collective-permute-start(bf16[2,32,1600]{2,1,0:T(8,128)(2,1)S(1)} %add_convert_fusion.11), channel_id=1, source_target_pairs={{0,2},{1,3},{2,0},{3,1},{4,6},{5,7},{6,4},{7,5},{8,10},{9,11},{10,... | collective-permute-start | bytes 614408 | tf_op jit(solution)/shard_map/ppermute | solution.py:37
  360.8 8.0 %collective-permute-start.54 = (bf16[1,32,960]{2,1,0:T(8,128)(2,1)S(1)}, bf16[1,32,960]{2,1,0:T(8,128)(2,1)S(1)}, u32[]{:S(2)}, u32[]{:S(2)}) collective-permute-start(bf16[1,32,960]{2,1,0:T(8,128)(2,1)S(1)} %add_convert_fusion.22), channel_id=1, source_target_pairs={{0,4},{1,5},{2,6},{3,7},{4,0},{5,1},{6,2},{7,3},{8,12},{9,13},{10,... | collective-permute-start | bytes 184328 | tf_op jit(solution)/shard_map/ppermute | solution.py:37
  365.8 9.7 %collective-permute-start.46 = (bf16[1,32,1600]{2,1,0:T(8,128)(2,1)S(1)}, bf16[1,32,1600]{2,1,0:T(8,128)(2,1)S(1)}, u32[]{:S(2)}, u32[]{:S(2)}) collective-permute-start(bf16[1,32,1600]{2,1,0:T(8,128)(2,1)S(1)} %add_convert_fusion.20), channel_id=1, source_target_pairs={{0,4},{1,5},{2,6},{3,7},{4,0},{5,1},{6,2},{7,3},{8,12},{9,13},{10,... | collective-permute-start | bytes 307208 | tf_op jit(solution)/shard_map/ppermute | solution.py:37
  369.7 6.7 %collective-permute-start.55 = (bf16[1,32,960]{2,1,0:T(8,128)(2,1)S(1)}, bf16[1,32,960]{2,1,0:T(8,128)(2,1)S(1)}, u32[]{:S(2)}, u32[]{:S(2)}) collective-permute-start(bf16[1,32,960]{2,1,0:T(8,128)(2,1)S(1)} %add_convert_fusion.21), channel_id=1, source_target_pairs={{0,4},{1,5},{2,6},{3,7},{4,0},{5,1},{6,2},{7,3},{8,12},{9,13},{10,... | collective-permute-start | bytes 184328 | tf_op jit(solution)/shard_map/ppermute | solution.py:37
  375.6 6.0 %collective-permute-start.47 = (bf16[1,32,1600]{2,1,0:T(8,128)(2,1)S(1)}, bf16[1,32,1600]{2,1,0:T(8,128)(2,1)S(1)}, u32[]{:S(2)}, u32[]{:S(2)}) collective-permute-start(bf16[1,32,1600]{2,1,0:T(8,128)(2,1)S(1)} %add_convert_fusion.19), channel_id=1, source_target_pairs={{0,4},{1,5},{2,6},{3,7},{4,0},{5,1},{6,2},{7,3},{8,12},{9,13},{10,... | collective-permute-start | bytes 307208 | tf_op jit(solution)/shard_map/ppermute | solution.py:37
  376.4 11.8 %collective-permute-start.56 = (bf16[2,32,960]{2,1,0:T(8,128)(2,1)S(1)}, bf16[2,32,960]{2,1,0:T(8,128)(2,1)S(1)}, u32[]{:S(2)}, u32[]{:S(2)}) collective-permute-start(bf16[2,32,960]{2,1,0:T(8,128)(2,1)S(1)} %pad_maximum_fusion.9), channel_id=1, source_target_pairs={{0,2},{1,3},{2,0},{3,1},{4,6},{5,7},{6,4},{7,5},{8,10},{9,11},{10,... | collective-permute-start | bytes 368648 | tf_op jit(solution)/shard_map/ppermute | solution.py:37
  381.6 5.9 %collective-permute-start.48 = (bf16[2,32,1600]{2,1,0:T(8,128)(2,1)S(1)}, bf16[2,32,1600]{2,1,0:T(8,128)(2,1)S(1)}, u32[]{:S(2)}, u32[]{:S(2)}) collective-permute-start(bf16[2,32,1600]{2,1,0:T(8,128)(2,1)S(1)} %pad_maximum_fusion.8), channel_id=1, source_target_pairs={{0,2},{1,3},{2,0},{3,1},{4,6},{5,7},{6,4},{7,5},{8,10},{9,11},{10,... | collective-permute-start | bytes 614408 | tf_op jit(solution)/shard_map/ppermute | solution.py:37
  387.6 12.7 %collective-permute-start.49 = (bf16[4,32,1600]{2,1,0:T(8,128)(2,1)S(1)}, bf16[4,32,1600]{2,1,0:T(8,128)(2,1)S(1)}, u32[]{:S(2)}, u32[]{:S(2)}) collective-permute-start(bf16[4,32,1600]{2,1,0:T(8,128)(2,1)S(1)} %pad_maximum_fusion.3.even), channel_id=1, source_target_pairs={{0,1},{1,0},{2,3},{3,2},{4,5},{5,4},{6,7},{7,6},{8,9},{9,8},{10,11... | collective-permute-start | bytes 1228808 | tf_op jit(solution)/shard_map/ppermute | solution.py:37
  388.3 12.1 %collective-permute-start.57 = (bf16[4,32,960]{2,1,0:T(8,128)(2,1)S(1)}, bf16[4,32,960]{2,1,0:T(8,128)(2,1)S(1)}, u32[]{:S(2)}, u32[]{:S(2)}) collective-permute-start(bf16[4,32,960]{2,1,0:T(8,128)(2,1)S(1)} %pad_maximum_fusion.7.even_o), channel_id=1, source_target_pairs={{0,1},{1,0},{2,3},{3,2},{4,5},{5,4},{6,7},{7,6},{8,9},{9,8},{10,11... | collective-permute-start | bytes 737288 | tf_op jit(solution)/shard_map/ppermute | solution.py:37
  (92 other events, 799.1 us)

commit v4 on v3

v4 whole, which is shorter than its diff:
```python
import functools

import jax
import jax.numpy as jnp
from jax import lax
from jax.experimental import pallas as pl
from jax.experimental.pallas import tpu as pltpu
from jax.sharding import PartitionSpec as P

HD = 64
PIECE = 256
LANES = 128
GROUP = 4
PARTS = 8
GAIN_ROWS = 16
RATE = 2.0e8
SLOTS = (7, 3, 5, 1, 6, 2, 4, 0)


NORM_EPS = 1e-05
ROPE_BASE = 10000.0
MASKED_SCORE = -1e30
SCALE = HD ** (-0.5)

LOW = jnp.bfloat16
FULL = jnp.float32
NN = (((1,), (0,)), ((), ()))
NT = (((1,), (1,)), ((), ()))
TN = (((0,), (0,)), ((), ()))


def dot(left_mat, right_mat, form=NN):
    return lax.dot_general(left_mat, right_mat, form, preferred_element_type=FULL)


def swap(values, axis, count, mask):
    return lax.ppermute(values, axis, [(i, i ^ mask) for i in range(count)])


def after(values, *others):
    return lax.optimization_barrier((values,) + others)[0] if others else values


class Blocks:
    def __init__(self, own, *others):
        self.own = own
        sent = after(own, *others)
        self.across = swap(sent, "grp", GROUP, 2)
        self.sent = sent

    def arrive(self, *others):
        pair = after((self.sent, self.across), *others)
        self.ready = pair
        self.core = swap(pair[0], "grp", GROUP, 1), swap(pair[1], "grp", GROUP, 1)

    def finish(self, *others):
        if not hasattr(self, "core"):
            self.arrive(*others)
        beside, corner = after(self.core, *others)
        return self.own, beside, self.across, corner


class Terms:
    def __init__(self, own, far, send):
        self.own, self.far = own, far
        self.beside = swap(send, "grp", GROUP, 1)

    def cross(self, *others):
        far, beside = after((self.far, self.beside), *others)
        across = (far.astype(FULL) + beside[1].astype(FULL)).astype(LOW)
        self.sent = across
        self.across = swap(across, "grp", GROUP, 2)
        return across

    def all(self):
        return self.own, self.beside, self.across


def three(terms):
    return terms[0].astype(FULL) + terms[1][0].astype(FULL) + terms[2].astype(FULL)


class RepSum:
    def __init__(self, pieces, ranks):
        self.pieces, self.ranks = pieces, ranks
        self.one = swap(pieces[0], "rep", ranks, 1)

    def second(self, *others):
        self.one = after(self.one, *others)
        two = (self.pieces[1].astype(FULL) + self.one[0:2].astype(FULL)).astype(LOW)
        self.held_two = two
        self.two = swap(two, "rep", self.ranks, 2)
        return two

    def third(self, *others):
        self.two = after(self.two, *others)
        four = self.pieces[2].astype(FULL) + self.one[2:3].astype(FULL) + self.two[0:1].astype(FULL)
        four = four.astype(LOW)
        self.four = swap(four, "rep", self.ranks, 4)
        return four

    def own(self, *others):
        ranks = self.ranks
        self.four = after(self.four, *others)
        mine = self.pieces[3].astype(FULL) + self.one[3:4].astype(FULL) + self.two[1:2].astype(FULL)
        mine = (mine + self.four.astype(FULL)).astype(LOW)
        if ranks > PARTS:
            others = [[j * PARTS + i for j in range(ranks // PARTS)] for i in range(PARTS)]
            mine = lax.psum(mine, "rep", axis_index_groups=others)
        self.mine = mine
        self.back = swap(mine, "rep", ranks, 4)
        return mine

    def spread(self, *others):
        self.back = after(self.back, *others)
        held = jnp.concatenate([self.mine, self.back])
        self.held = held
        self.wide = swap(held, "rep", self.ranks, 2)
        return held

    def done(self, *others):
        self.wide = after(self.wide, *others)
        held = jnp.concatenate([self.held, self.wide])
        return held, swap(held, "rep", self.ranks, 1)


class SmallSum:
    def __init__(self, values, ranks):
        self.values = values
        self.steps = [("grp", GROUP, 1), ("grp", GROUP, 2)]
        mask = 1
        while mask < ranks:
            self.steps.append(("rep", ranks, mask))
            mask *= 2
        self.flight = None

    def step(self, *others):
        if self.flight is not None:
            self.values = self.values + after(self.flight, *others)
        if self.steps:
            self.flight = swap(self.values, *self.steps.pop(0))
        return self.values

    def finish(self):
        while self.steps:
            self.step()
        self.step()
        return self.values


def call(kernel, name, out_shape, *, grid=(1,), prefetch=0, in_specs, out_specs, scratch=(), micros=1, vmem=30):
    def lies(shape):
        return pltpu.HBM(shape.shape, shape.dtype)

    several = isinstance(out_shape, tuple)
    run = pl.pallas_call(
        kernel,
        name=name,
        out_shape=tuple(map(lies, out_shape)) if several else lies(out_shape),
        grid_spec=pltpu.PrefetchScalarGridSpec(
            num_scalar_prefetch=prefetch,
            grid=grid,
            in_specs=in_specs,
            out_specs=out_specs,
            scratch_shapes=list(scratch),
        ),
        compiler_params=pltpu.CompilerParams(vmem_limit_bytes=vmem << 20),
        cost_estimate=pl.CostEstimate(flops=int(micros * RATE), bytes_accessed=1 << 10, transcendentals=0),
    )

    def placed(*args):
        rest = [
            arg if spec is NEAR else pltpu.with_memory_space_constraint(arg, pltpu.HBM)
            for arg, spec in zip(args[prefetch:], in_specs, strict=True)
        ]
        return run(*args[:prefetch], *rest)

    return placed


def whole(shape):
    return pl.BlockSpec(shape, lambda *_: (0,) * len(shape))


ANY = pl.BlockSpec(memory_space=pl.ANY)
NEAR = pl.BlockSpec(memory_space=pltpu.VMEM)


def shape_of(shape, kind=LOW):
    return jax.ShapeDtypeStruct(shape, kind)


def turn(rows, cosine, sine_val, sign):
    one, two = rows[0 : HD // 2, :], rows[HD // 2 : HD, :]
    sine_val = sine_val * sign
    return one * cosine - two * sine_val, two * cosine + one * sine_val


def assemble(rank, blocks, scratch):
    rows = blocks[0].shape[0]
    for k in range(GROUP):
        start = pl.multiple_of((rank ^ k) * rows, 16)
        scratch[pl.ds(start, rows), :] = blocks[k][...]


def pack_kernel(wk_ref, wv_ref, gains_ref, out_ref):
    kw, shard = wk_ref.shape
    out_ref[:, 0:kw] = wk_ref[...].T
    out_ref[:, kw : 2 * kw] = wv_ref[...].T
    gains = jnp.concatenate([gains_ref[...], jnp.zeros((LANES - 2, shard), FULL)], axis=0)
    out_ref[:, 2 * kw :] = gains.T.astype(LOW)


def flip_two_kernel(wg_ref, wu_ref, wgut_ref, wgu_ref):
    ff = wg_ref.shape[1]
    wgut_ref[0:ff, :] = wg_ref[...].T
    wgut_ref[ff:, :] = wu_ref[...].T
    wgu_ref[:, 0:ff] = wg_ref[...]
    wgu_ref[:, ff:] = wu_ref[...]


def flip_one_kernel(wdt_ref, wd_ref):
    wd_ref[...] = wdt_ref[...].T


def keys_values_kernel(ranks, tok_ref, b0, b1, b2, b3, cos_ref, sin_ref, norm_ref, kv_a, kv_b, gain_ref, w_ref):
    span = tok_ref.shape[2]
    kw2 = kv_a.shape[0]
    kw = kw2 // 2
    assemble(ranks[0], (b0, b1, b2, b3), w_ref)
    gains = w_ref[:, kw2:]
    gain_ref[...] = gains
    gain_one = gains[:, 0:1].astype(FULL)
    for s, out in enumerate((kv_a, kv_b)):
        x = tok_ref[s].astype(FULL)
        inverse = lax.rsqrt(jnp.mean(x * x, axis=0, keepdims=True) + NORM_EPS)
        norm = (x * inverse * gain_one).astype(LOW)
        norm_ref[:, s * span : (s + 1) * span] = norm
        kv = dot(w_ref[:, 0:kw2], norm, TN)
        for h in range(kw // HD):
            one, two = turn(kv[h * HD : (h + 1) * HD, :], cos_ref[s], sin_ref[s], 1.0)
            top = h * 2 * HD
            out[top : top + HD // 2, :] = one.astype(LOW)
            out[top + HD // 2 : top + HD, :] = two.astype(LOW)
            out[top + HD : top + 2 * HD, :] = kv[kw + h * HD : kw + (h + 1) * HD, :].astype(LOW)


def queries_kernel(ranks, norm_ref, b0, b1, b2, b3, cos_ref, sin_ref, q_ref, w_ref):
    width = b0.shape[1]
    span = cos_ref.shape[2]
    assemble(ranks[0], (b0, b1, b2, b3), w_ref)
    for s in range(2):
        part = slice(s * span, (s + 1) * span)
        query = dot(w_ref[...], norm_ref[:, part], TN)
        for h in range(width // HD):
            one, two = turn(query[h * HD : (h + 1) * HD, :], cos_ref[s], sin_ref[s], 1.0)
            q_ref[h * HD : h * HD + HD // 2, part] = (one * SCALE).astype(LOW)
            q_ref[h * HD + HD // 2 : (h + 1) * HD, part] = (two * SCALE).astype(LOW)


def beside(ref):
    return jnp.concatenate([ref[i : i + HD, :] for i in range(0, ref.shape[0], HD)], axis=1)


def attend_kernel(seq, ranks, order, starts, q_ref, b0, b1, b2, b3, p_ref, o_ref, bias_ref):
    span = q_ref.shape[1]
    per = q_ref.shape[0] // HD
    rank = ranks[0]

    @pl.when(pl.program_id(0) == 0)
    def _():
        query_pos = order[seq, rank] * span + lax.broadcasted_iota(jnp.int32, (span, span), 1)
        query_in = []
        for m in range(2):
            start = starts[seq, m]
            query_in.append((query_pos >= start) & (query_pos < start + PIECE))
        for k in range(GROUP):
            key_pos = order[seq, rank ^ k] * span + lax.broadcasted_iota(jnp.int32, (span, span), 0)
            allowed = key_pos <= query_pos
            for m in range(2):
                start = starts[seq, m]
                key_in = (key_pos >= start) & (key_pos < start + PIECE)
                allowed = allowed | (query_in[m] & key_in)
            bias_ref[k * span : (k + 1) * span, :] = jnp.where(allowed, 0.0, MASKED_SCORE)

    kv_t = jnp.concatenate([b0[...], b1[...], b2[...], b3[...]], axis=1)
    keys = kv_t.T[:, 0:HD]
    values_t = kv_t[HD : 2 * HD, :]
    bias = jnp.concatenate([bias_ref[...]] * per, axis=1)
    scores = dot(keys, beside(q_ref)) + bias
    peak = jnp.max(scores, axis=0, keepdims=True)
    exponent = jnp.exp(scores - peak)
    total = jnp.sum(exponent, axis=0, keepdims=True)
    probs = (exponent * (1.0 / total)).astype(LOW)
    p_ref[0] = probs
    mixed = dot(values_t, probs).astype(LOW)
    for i in range(per):
        o_ref[i * HD : (i + 1) * HD, :] = mixed[:, i * span : (i + 1) * span]


def middle_kernel(ranks, att_ref, b0, b1, b2, b3, tok_ref, gain_ref, mid_ref, x_ref, w_ref):
    assemble(ranks[0], (b0, b1, b2, b3), w_ref)
    middle = tok_ref[0].astype(FULL) + dot(w_ref[...], att_ref[...], TN)
    mid_ref[...] = middle
    inverse = lax.rsqrt(jnp.mean(middle * middle, axis=0, keepdims=True) + NORM_EPS)
    x_ref[...] = (middle * inverse * gain_ref[:, 1:2].astype(FULL)).astype(LOW)


def forward_back_step(x, cot, wgut_ref, wgu_ref, wdt_ref, wd_ref, hid_ref, gg_ref, gu_ref, both):
    ff = wd_ref.shape[0]
    gate_up = dot(wgut_ref[...], x)
    grad_hidden = dot(wd_ref[...], cot)
    gate, up = gate_up[0:ff, :], gate_up[ff:, :]
    sig = 1.0 / (1.0 + jnp.exp(-gate))
    swish = gate * sig
    hidden = (swish * up).astype(LOW)
    grad_gate = (grad_hidden * up * sig * (1.0 + gate * (1.0 - sig))).astype(LOW)
    grad_up = (grad_hidden * swish).astype(LOW)
    hid_ref[...] = hidden
    gg_ref[...] = grad_gate
    gu_ref[...] = grad_up
    both[0:ff, :] = grad_gate
    both[ff:, :] = grad_up
    return dot(wgu_ref[...], both[...]).astype(LOW), dot(wdt_ref[...], hidden).astype(LOW)


def own_block_kernel(x_a, x_b, cot_ref, wgut_ref, wgu_ref, wdt_ref, wd_ref, out_ref, grad_ref, hid_ref, gg_ref, gu_ref, held, both):
    s = pl.program_id(0)
    for i, x in enumerate((x_a, x_b)):

        @pl.when(s == i)
        def _(x=x):
            held[...] = x[...]

    grad_x, out = forward_back_step(
        held[...], cot_ref[0], wgut_ref, wgu_ref, wdt_ref, wd_ref, hid_ref.at[0], gg_ref.at[0], gu_ref.at[0], both
    )
    grad_ref[0] = grad_x
    out_ref[0] = out


def other_blocks_kernel(*refs):
    blocks = refs[0:6]
    weights = refs[6:10]
    fo_ref, so_ref, fg_ref, sg_ref, hid_ref, gg_ref, gu_ref, held, both, sem = refs[10:]
    k = pl.program_id(0)
    copies = [pltpu.make_async_copy(block, held.at[i], sem.at[i]) for i, block in enumerate(blocks)]

    @pl.when(k == 0)
    def _():
        for i in range(3):
            copies[i].start()
            copies[3 + i].start()

    for i in range(3):

        @pl.when(k == i)
        def _(i=i):
            copies[i].wait()
            copies[3 + i].wait()

    grad_x, out = forward_back_step(held[k], held[3 + k], *weights, hid_ref, gg_ref, gu_ref, both)

    @pl.when(k == 1)
    def _():
        fg_ref[...] = grad_x
        fo_ref[...] = out

    @pl.when(k != 1)
    def _():
        sg_ref[0] = grad_x
        so_ref[0] = out


def weight_kernel(ranks, *refs):
    blocks = refs[0 : 2 * GROUP]
    own, *others = refs[2 * GROUP : 2 * GROUP + 3]
    outs = refs[2 * GROUP + 3 : 2 * GROUP + 7]
    left, right, acc, sem = refs[2 * GROUP + 7 :]
    span = left.shape[2] // GROUP
    copies = []
    for b, block in enumerate(blocks):
        s, k = divmod(b, GROUP)
        copies.append(pltpu.make_async_copy(block, left.at[s, :, pl.ds(k * span, span)], sem.at[b]))
    for s in range(2):
        for i, (source, part) in enumerate(((own.at[s], slice(0, span)), (others[s], slice(span, GROUP * span)))):
            copy = pltpu.make_async_copy(source, right.at[s, :, part], sem.at[2 * GROUP + 2 * s + i])
            copies.insert(s * (GROUP + 2), copy)
    for copy in copies:
        copy.start()
    for copy in copies[: GROUP + 2]:
        copy.wait()
    acc[...] = dot(left[0], right[0], NT)
    for copy in copies[GROUP + 2 :]:
        copy.wait()
    acc[...] += dot(left[1], right[1], NT)
    part = acc.shape[0] // PARTS
    places = [(outs[0], i) for i in range(4)] + [(outs[1], 0), (outs[1], 1), (outs[2], 0), (outs[3], 0)]
    for (out, i), slot in zip(places, SLOTS):
        start = pl.multiple_of((slot ^ ranks[1]) * part, 8)
        out[i] = acc[pl.ds(start, part), :].astype(LOW)


def branch_kernel(ranks, mid_ref, cot_ref, e0, e1, e2, gain_ref, b0, b1, b2, b3, att_ref, gm_ref, gb_ref, do_ref, delta_ref, gain_out, w_ref):
    width, span = mid_ref.shape
    assemble(ranks[0], (b0, b1, b2, b3), w_ref)
    middle = mid_ref[...]
    grad = e0[0].astype(FULL) + e1[0].astype(FULL) + e2[...].astype(FULL)
    inverse = lax.rsqrt(jnp.mean(middle * middle, axis=0, keepdims=True) + NORM_EPS)
    scaled = grad * gain_ref[:, 1:2].astype(FULL)
    turned = jnp.mean(scaled * middle, axis=0, keepdims=True)
    grad_middle = cot_ref[0].astype(FULL) + inverse * scaled - middle * (inverse * inverse * inverse * turned)
    gain_out[...] = dot(jnp.ones((8, span), LOW), (grad * middle * inverse).astype(LOW), NT)
    gm_ref[...] = grad_middle
    branch = grad_middle.astype(LOW)
    gb_ref[...] = branch
    grad_att = dot(w_ref[...], branch).astype(LOW)
    do_ref[...] = grad_att
    both = grad_att.astype(FULL) * att_ref[...].astype(FULL)
    heads = width // HD
    for h in range(heads):
        delta_ref[h : h + 1, :] = jnp.sum(both[h * HD : (h + 1) * HD, :], axis=0, keepdims=True)
    delta_ref[heads:, :] = jnp.zeros((delta_ref.shape[0] - heads, span), FULL)


def attend_back_kernel(seq, q_ref, b0, b1, b2, b3, p_ref, do_ref, delta_ref, cos_ref, sin_ref, gq_ref, own_ref, far_ref, send_ref):
    span = q_ref.shape[1]
    per = q_ref.shape[0] // HD
    h = pl.program_id(0)
    kv_t = jnp.concatenate([b0[...], b1[...], b2[...], b3[...]], axis=1)
    kv = kv_t.T
    query, out_grad = beside(q_ref), beside(do_ref)
    delta = jnp.concatenate([delta_ref[pl.ds(per * h + i, 1), :] for i in range(per)], axis=1)
    none = jnp.zeros(out_grad.shape, LOW)
    grad_probs = dot(kv, jnp.concatenate([none, out_grad], axis=0))
    grad_scores = (p_ref[0].astype(FULL) * (grad_probs - delta)).astype(LOW)
    grad_q = dot(kv_t[0:HD, :], grad_scores) * SCALE
    for i in range(per):
        one, two = turn(grad_q[:, i * span : (i + 1) * span], cos_ref[seq], sin_ref[seq], -1.0)
        gq_ref[i * HD : i * HD + HD // 2, :] = one.astype(LOW)
        gq_ref[i * HD + HD // 2 : (i + 1) * HD, :] = two.astype(LOW)
    keys = dot(query, grad_scores, NT).astype(LOW)
    values = dot(out_grad, p_ref[0], NT).astype(LOW)
    for k in range(GROUP):
        out = (own_ref, send_ref.at[0], far_ref, send_ref.at[1])[k]
        part = slice(k * span, (k + 1) * span)
        out[0:HD, :] = keys[:, part]
        out[HD:, :] = values[:, part]


def spread(ranks, acc, own_ref, far_ref, send_ref):
    part = acc.shape[1] // PARTS
    for k, out in enumerate((own_ref, send_ref.at[0], far_ref, send_ref.at[1])):
        for i, slot in enumerate(SLOTS):
            start = pl.multiple_of((slot ^ ranks[1]) * part, 8)
            out[i] = acc[ranks[0] ^ k, pl.ds(start, part), :].astype(LOW)


def query_weight_kernel(ranks, norm_ref, gq_a, gq_b, att_a, att_b, gb_a, gb_b, own_ref, far_ref, send_ref, acc):
    width, span = gq_a.shape
    shard = width // GROUP
    for b in range(GROUP):
        rows = slice(b * shard, (b + 1) * shard)
        acc[b, 0:shard, 0:width] = dot(norm_ref[rows, 0:span], gq_a[...], NT) + dot(norm_ref[rows, span:], gq_b[...], NT)
        acc[b, 0:shard, width:] = dot(att_a[rows, :], gb_a[...], NT) + dot(att_b[rows, :], gb_b[...], NT)
        acc[b, shard:, :] = jnp.zeros((acc.shape[1] - shard, acc.shape[2]), FULL)
    spread(ranks, acc, own_ref, far_ref, send_ref)


def key_weight_kernel(ranks, norm_ref, a0, a1, a2, b0, b1, b2, cos_ref, sin_ref, own_ref, far_ref, send_ref, gkv_ref, acc):
    width = norm_ref.shape[0]
    span = a2.shape[1]
    shard = width // GROUP
    kw2 = gkv_ref.shape[0]
    kw = kw2 // 2
    for s, (e0, e1, e2) in enumerate(((a0, a1, a2), (b0, b1, b2))):
        part = slice(s * span, (s + 1) * span)
        grad = e0[...].astype(FULL) + e1[0].astype(FULL) + e2[...].astype(FULL)
        for h in range(kw // HD):
            top = h * 2 * HD
            one, two = turn(grad[top : top + HD, :], cos_ref[s], sin_ref[s], -1.0)
            gkv_ref[h * HD : h * HD + HD // 2, part] = one.astype(LOW)
            gkv_ref[h * HD + HD // 2 : (h + 1) * HD, part] = two.astype(LOW)
            gkv_ref[kw + h * HD : kw + (h + 1) * HD, part] = grad[top + HD : top + 2 * HD, :].astype(LOW)
    for b in range(GROUP):
        rows = slice(b * shard, (b + 1) * shard)
        acc[b, 0:shard, :] = dot(norm_ref[rows, :], gkv_ref[...], NT)
        acc[b, shard:, :] = jnp.zeros((acc.shape[1] - shard, kw2), FULL)
    spread(ranks, acc, own_ref, far_ref, send_ref)


def query_grad_kernel(ranks, gq_a, gq_b, q0, q1, q2, q3, out_ref, wq_ref):
    assemble(ranks[0], (q0, q1, q2, q3), wq_ref)
    out_ref[0] = dot(wq_ref[...], gq_a[...])
    out_ref[1] = dot(wq_ref[...], gq_b[...])


def input_grad_kernel(ranks, part_ref, gkv_ref, k0, k1, k2, k3, tok_ref, gm_a, gm_b, gain_a, gain_b, out_ref, gain_out, wkv_ref):
    span = gm_a.shape[1]
    kw2 = gkv_ref.shape[0]
    assemble(ranks[0], (k0, k1, k2, k3), wkv_ref)
    gain_one = wkv_ref[:, kw2 : kw2 + 1].astype(FULL)
    total = None
    for s in range(2):
        part = slice(s * span, (s + 1) * span)
        grad_norm = part_ref[s] + dot(wkv_ref[:, 0:kw2], gkv_ref[:, part])
        x = tok_ref[s].astype(FULL)
        inverse = lax.rsqrt(jnp.mean(x * x, axis=0, keepdims=True) + NORM_EPS)
        scaled = grad_norm * gain_one
        turned = jnp.mean(scaled * x, axis=0, keepdims=True)
        out_ref[s] = (gm_a, gm_b)[s][...] + inverse * scaled - x * (inverse * inverse * inverse * turned)
        row = dot(jnp.ones((8, span), LOW), (grad_norm * x * inverse).astype(LOW), NT)
        total = row if total is None else total + row
    gain_out[0:1, :] = total[0:1, :]
    gain_out[1:2, :] = gain_a[0:1, :] + gain_b[0:1, :]
    gain_out[2:8, :] = total[2:8, :]


def place(slot):
    return ((slot >> 2) & 1) + ((slot >> 1) & 1) * 2


def gathered(ranks, pairs):
    for a in range(PARTS):
        slot = ranks[1] ^ a
        index = place(slot)
        for parity in range(2):

            @pl.when(slot % 2 == parity)
            def _(parity=parity, index=index, a=a):
                for pair in pairs:
                    part = pair[parity].shape[1]
                    pair[2][a * part : (a + 1) * part, :] = pair[parity][index].astype(FULL)


def forward_weights_kernel(ranks, even, odd, out_ref):
    gathered(ranks, [(even, odd, out_ref)])


def query_done_kernel(ranks, even, odd, q_ref, o_ref, scratch):
    shard, width = q_ref.shape
    gathered(ranks, [(even, odd, scratch)])
    q_ref[...] = scratch[0:shard, 0:width]
    o_ref[...] = scratch[0:shard, width:]


def key_done_kernel(ranks, even, odd, k_ref, v_ref, scratch):
    kw, shard = k_ref.shape
    gathered(ranks, [(even, odd, scratch)])
    k_ref[...] = scratch[0:shard, 0:kw].T
    v_ref[...] = scratch[0:shard, kw:].T


def tables(places):
    half = HD // 2
    frequency = ROPE_BASE ** (-2.0 * jnp.arange(half, dtype=FULL) / HD)
    angles = places.astype(FULL)[:, None, :] * frequency[None, :, None]
    return jnp.cos(angles), jnp.sin(angles)


def body(
    tokens,
    w_query,
    w_key,
    w_value,
    w_out,
    w_gate,
    w_up,
    w_down,
    gain_attn,
    gain_mlp,
    span_order,
    piece_starts,
    cotangent,
):
    ranks = lax.axis_size("rep")
    rank_grp = lax.axis_index("grp")
    seq_count, span, width = tokens.shape
    shard = w_query.shape[0]
    kw = w_key.shape[1]
    kw2 = 2 * kw
    kv_heads = kw // HD
    per = width // kw
    ff = w_gate.shape[1]
    rows = seq_count * span
    length = GROUP * span
    place_of = jnp.stack([rank_grp, lax.axis_index("rep") % PARTS]).astype(jnp.int32)
    tok_t = jnp.swapaxes(tokens, 1, 2)
    cot_t = jnp.swapaxes(cotangent, 1, 2)
    wd_t = w_down.T
    act = whole((width, span))
    seqs = whole((seq_count, width, span))
    one_seq = lambda s: pl.BlockSpec((1, width, span), lambda *_: (s, 0, 0))
    table = whole((seq_count, HD // 2, span))
    gain_spec = whole((width, LANES))
    head = pl.BlockSpec((2 * HD, span), lambda h, *_: (h, 0))
    probs_spec = pl.BlockSpec((1, length, per * span), lambda h, *_: (h, 0, 0))
    q_spec = lambda s: pl.BlockSpec((per * HD, span), lambda h, *_: (h, s))
    per_head = pl.BlockSpec((per * HD, span), lambda h, *_: (h, 0))

    kv_shard = call(
        pack_kernel,
        "pack",
        shape_of((shard, kw2 + LANES)),
        in_specs=[whole((kw, shard))] * 2 + [whole((2, shard))],
        out_specs=whole((shard, kw2 + LANES)),
        micros=2,
    )(w_key.T, w_value.T, jnp.stack([gain_attn, gain_mlp]).astype(FULL))
    kv_flight = Blocks(kv_shard)
    q_flight = Blocks(w_query, kv_shard)
    own_span = lax.dynamic_slice(span_order, (0, rank_grp), (seq_count, 1))
    places = own_span * span + jnp.arange(span, dtype=jnp.int32)[None, :]
    cos_cols, sin_cols = tables(places)
    kv_blocks = kv_flight.finish()
    norm_low, kv_a, kv_b, gain_cols = call(
        keys_values_kernel,
        "keys_values",
        (shape_of((width, rows)), shape_of((kw2, span)), shape_of((kw2, span)), shape_of((width, LANES))),
        prefetch=1,
        in_specs=[seqs] + [whole(kv_shard.shape)] * 4 + [table, table],
        out_specs=(whole((width, rows)), whole((kw2, span)), whole((kw2, span)), gain_spec),
        scratch=[pltpu.VMEM((width, kw2 + LANES), LOW)],
        micros=4.3,
    )(place_of, tok_t, *kv_blocks, cos_cols, sin_cols)
    kv_flight = [Blocks(kv_a), None]
    wgut, wgu = call(
        flip_two_kernel,
        "flip_two",
        (shape_of((2 * ff, width)), shape_of((width, 2 * ff))),
        in_specs=[whole((width, ff))] * 2,
        out_specs=(whole((2 * ff, width)), whole((width, 2 * ff))),
        micros=4,
    )(after(w_gate, norm_low), w_up)
    q_flight.arrive(wgut)
    wd = call(
        flip_one_kernel,
        "flip_one",
        shape_of((ff, width)),
        in_specs=[whole((width, ff))],
        out_specs=whole((ff, width)),
        micros=2,
    )(after(wd_t, *q_flight.ready))
    q_blocks = q_flight.finish(wd)
    queries = call(
        queries_kernel,
        "queries",
        shape_of((width, rows)),
        prefetch=1,
        in_specs=[whole((width, rows))] + [whole((shard, width))] * 4 + [table, table],
        out_specs=whole((width, rows)),
        scratch=[pltpu.VMEM((width, width), LOW)],
        micros=4.9,
    )(place_of, norm_low, *q_blocks, cos_cols, sin_cols)

    o_flight = Blocks(w_out, wgut)
    kv_flight[1] = Blocks(kv_b, o_flight.sent, wgut)
    cot_flight = [Blocks(cot_t[0], queries), None]
    cot_blocks = [None, None]
    kv_all = [kv_flight[0].finish(queries), None]

    def attend_of(s, query):
        return call(
            functools.partial(attend_kernel, s),
            "attend",
            (shape_of((kv_heads, length, per * span)), shape_of((width, span))),
            prefetch=3,
            grid=(kv_heads,),
            in_specs=[q_spec(s)] + [head] * 4,
            out_specs=(probs_spec, per_head),
            scratch=[pltpu.VMEM((length, span), FULL)],
            micros=10,
        )(place_of, span_order, piece_starts, query, *kv_all[s])

    def middle_of(s, att):
        return call(
            middle_kernel,
            "middle",
            (shape_of((width, span), FULL), shape_of((width, span))),
            prefetch=1,
            in_specs=[act] + [whole((shard, width))] * 4 + [one_seq(s), gain_spec],
            out_specs=(act, act),
            scratch=[pltpu.VMEM((width, width), LOW)],
            micros=3,
        )(place_of, att, *o_blocks, tok_t, gain_cols)

    probs_a, att_a = attend_of(0, queries)
    o_blocks = o_flight.finish(att_a)
    kv_all[1] = kv_flight[1].finish(att_a)
    middle_a, x_a = middle_of(0, att_a)
    x_flight = [Blocks(x_a), None]
    cot_flight[1] = Blocks(cot_t[1], x_flight[0].sent, x_a)
    probs_b, att_b = attend_of(1, after(queries, x_a))
    cot_flight[0].arrive(att_b)
    middle_b, x_b = middle_of(1, after(att_b, *cot_flight[0].ready))
    x_flight[1] = Blocks(x_b)
    x_flight[0].arrive(middle_b)
    cot_blocks[0] = cot_flight[0].finish(middle_b)
    stats, attended, middles = (probs_a, probs_b), (att_a, att_b), (middle_a, middle_b)

    each = pl.BlockSpec((1, width, span), lambda s, *_: (s, 0, 0))
    each_ff = pl.BlockSpec((1, ff, span), lambda s, *_: (s, 0, 0))
    two = shape_of((seq_count, width, span))
    two_ff = shape_of((seq_count, ff, span))
    own_out, own_grad, own_hid, own_gg, own_gu = call(
        own_block_kernel,
        "own_blocks",
        (two, two, two_ff, two_ff, two_ff),
        grid=(seq_count,),
        in_specs=[act, act, each] + [NEAR] * 4,
        out_specs=(each, each, each_ff, each_ff, each_ff),
        scratch=[pltpu.VMEM((width, span), LOW), pltpu.VMEM((2 * ff, span), LOW)],
        micros=8,
    )(after(x_a, *x_flight[0].ready, *cot_blocks[0]), x_b, cot_t, wgut, wgu, wd_t, wd)
    x_blocks = [x_flight[0].finish(own_out), None]
    cot_flight[1].arrive(own_out)

    def other_blocks(s, *others):
        half = pl.BlockSpec((1, width, span), lambda k, *_: (k // 2, 0, 0))
        per_block = pl.BlockSpec((ff, span), lambda k, *_: (0, k))
        act_shape, half_shape, ff_shape = shape_of((width, span)), shape_of((2, width, span)), shape_of((ff, 3 * span))
        return call(
            other_blocks_kernel,
            "other_blocks",
            (act_shape, half_shape, act_shape, half_shape, ff_shape, ff_shape, ff_shape),
            grid=(GROUP - 1,),
            in_specs=[ANY] * 6 + [NEAR] * 4,
            out_specs=(act, half, act, half) + (per_block,) * 3,
            scratch=[
                pltpu.VMEM((6, width, span), LOW),
                pltpu.VMEM((2 * ff, span), LOW),
                pltpu.SemaphoreType.DMA((6,)),
            ],
            micros=12,
        )(after(x_blocks[s][1], *others), *x_blocks[s][2:], *cot_blocks[s][1:], wgut, wgu, wd_t, wd)

    fo_a, so_a, fg_a, sg_a, hid_a, gg_a, gu_a = other_blocks(0, *cot_flight[1].ready)
    grad_a = Terms(own_grad[0], fg_a, sg_a)
    out_a = Terms(own_out[0], fo_a, so_a)
    x_flight[1].arrive(fg_a)
    x_blocks[1] = x_flight[1].finish()
    cot_blocks[1] = cot_flight[1].finish(fg_a)
    fo_b, so_b, fg_b, sg_b, hid_b, gg_b, gu_b = other_blocks(1, fg_a)
    grad_b = Terms(own_grad[1], fg_b, sg_b)
    out_b = Terms(own_out[1], fo_b, so_b)
    stage = (grad_a.cross(fg_b), out_a.cross(fg_b))
    grads = (grad_a, grad_b)

    part = width // PARTS

    def sums(name, blocks, rights, *others):
        pieces = call(
            weight_kernel,
            name,
            tuple(shape_of((n, part, ff)) for n in (4, 2, 1, 1)),
            prefetch=1,
            in_specs=[ANY] * (2 * GROUP + 3),
            out_specs=tuple(whole((n, part, ff)) for n in (4, 2, 1, 1)),
            scratch=[
                pltpu.VMEM((2, width, length), LOW),
                pltpu.VMEM((2, ff, length), LOW),
                pltpu.VMEM((width, ff), FULL),
                pltpu.SemaphoreType.DMA((2 * GROUP + 4,)),
            ],
            micros=8,
        )(place_of, after(blocks[0], *others), *blocks[1:], *rights)
        return RepSum(pieces, ranks)

    x_all = x_blocks[0] + x_blocks[1]
    down_sum = sums("down_weights", cot_blocks[0] + cot_blocks[1], (own_hid, hid_a, hid_b), *stage)
    done = down_sum.pieces[0]
    stage = (grad_b.cross(done), out_b.beside, done)
    gate_sum = sums("gate_weights", x_all, (own_gg, gg_a, gg_b), *stage)
    done = gate_sum.pieces[0]
    stage = (grad_a.across, out_b.cross(done), done)
    up_sum = sums("up_weights", x_all, (own_gu, gu_a, gu_b), *stage)
    done = up_sum.pieces[0]
    stage = (down_sum.second(done), out_a.across, done)

    def branch_of(s, middle):
        _, beside_term, across_term = grads[s].all()
        first = whole((1, width, span))
        return call(
            branch_kernel,
            "branch",
            (
                shape_of((width, span), FULL),
                shape_of((width, span)),
                shape_of((width, span)),
                shape_of((16, span), FULL),
                shape_of((8, width), FULL),
            ),
            prefetch=1,
            in_specs=[act, one_seq(s), one_seq(s), first, act, gain_spec] + [whole((shard, width))] * 4 + [act],
            out_specs=(act, act, act, whole((16, span)), whole((8, width))),
            scratch=[pltpu.VMEM((width, width), LOW)],
            micros=4,
        )(place_of, middle, cot_t, own_grad, beside_term, across_term, gain_cols, *o_blocks, attended[s])

    def attend_back_of(s, out_grad, delta):
        halves = pl.BlockSpec((2, 2 * HD, span), lambda h, *_: (0, h, 0))
        grad_q, *kv_parts = call(
            functools.partial(attend_back_kernel, s),
            "attend_back",
            (shape_of((width, span)), shape_of((kw2, span)), shape_of((kw2, span)), shape_of((2, kw2, span))),
            grid=(kv_heads,),
            in_specs=[q_spec(s)] + [head] * 4 + [probs_spec, per_head, whole((16, span)), table, table],
            out_specs=(per_head, head, head, halves),
            micros=11,
        )(queries, *kv_all[s], stats[s], out_grad, delta, cos_cols, sin_cols)
        return grad_q, Terms(*kv_parts)

    mid_a, branch_a, dout_a, delta_a, gain_a = branch_of(0, after(middles[0], *stage))
    gq_a, kv_grad_a = attend_back_of(0, after(dout_a, grad_b.across), delta_a)
    stage = (out_b.across, gate_sum.second(gq_a), down_sum.third(gq_a))
    mid_b, branch_b, dout_b, delta_b, gain_b = branch_of(1, after(middles[1], *stage))
    stage = (kv_grad_a.cross(branch_b), up_sum.second(branch_b))
    gq_b, kv_grad_b = attend_back_of(1, after(dout_b, *stage), delta_b)
    stage = (gate_sum.third(gq_b), down_sum.own(gq_b), up_sum.third(gq_b), kv_grad_a.across)

    grown = shard + GAIN_ROWS
    piece = grown // PARTS
    spread_out = lambda columns: (shape_of((PARTS, piece, columns)),) * 2 + (shape_of((2, PARTS, piece, columns)),)
    spread_spec = lambda columns: (whole((PARTS, piece, columns)),) * 2 + (whole((2, PARTS, piece, columns)),)
    query_parts = call(
        query_weight_kernel,
        "query_weights",
        spread_out(2 * width),
        prefetch=1,
        in_specs=[whole((width, rows))] + [act] * 6,
        out_specs=spread_spec(2 * width),
        scratch=[pltpu.VMEM((GROUP, grown, 2 * width), FULL)],
        micros=8,
    )(place_of, norm_low, after(gq_a, *stage), gq_b, *attended, branch_a, branch_b)
    done = query_parts[0]
    query_terms = Terms(*query_parts)
    stage = (kv_grad_b.cross(done), down_sum.spread(done))
    grad_part = call(
        query_grad_kernel,
        "query_grad",
        shape_of((seq_count, width, span), FULL),
        prefetch=1,
        in_specs=[act, act] + [whole((shard, width))] * 4,
        out_specs=seqs,
        scratch=[pltpu.VMEM((width, width), LOW)],
        micros=4,
    )(place_of, after(gq_a, *stage), gq_b, *q_blocks)
    stage = (query_terms.cross(grad_part), gate_sum.own(grad_part), up_sum.own(grad_part))
    block_out = jnp.stack(
        [middle + three(term.all()) for middle, term in zip(after(middles, *stage), (out_a, out_b))]
    )

    def owned(terms):
        own, beside_term, across = terms.all()
        cuts = (slice(0, 4), slice(4, 6), slice(6, 7), slice(7, 8))
        return [three((own[c], beside_term[:, c], across[c])).astype(LOW) for c in cuts]

    first = whole((1, kw2, span))
    terms = []
    for term in (kv_grad_a, kv_grad_b):
        terms += term.all()
    *key_parts, gkv = call(
        key_weight_kernel,
        "key_weights",
        spread_out(kw2) + (shape_of((kw2, rows)),),
        prefetch=1,
        in_specs=[whole((width, rows))] + [whole((kw2, span)), first, whole((kw2, span))] * 2 + [table, table],
        out_specs=spread_spec(kw2) + (whole((kw2, rows)),),
        scratch=[pltpu.VMEM((GROUP, grown, kw2), FULL)],
        micros=4,
    )(place_of, after(norm_low, block_out), *terms, cos_cols, sin_cols)
    key_terms = Terms(*key_parts)
    down_pair = down_sum.done(gkv)
    grad_tokens, gain_part = call(
        input_grad_kernel,
        "input_grad",
        (shape_of((seq_count, width, span), FULL), shape_of((8, width), FULL)),
        prefetch=1,
        in_specs=[seqs, whole((kw2, rows))]
        + [whole(kv_shard.shape)] * 4
        + [seqs, act, act]
        + [whole((8, width))] * 2,
        out_specs=(seqs, whole((8, width))),
        scratch=[pltpu.VMEM((width, kw2 + LANES), LOW)],
        micros=6,
    )(
        place_of,
        after(grad_part, down_pair[0]),
        gkv,
        *kv_blocks,
        tok_t,
        mid_a,
        mid_b,
        gain_a,
        gain_b,
    )
    small = SmallSum(gain_part, ranks)
    stage = (key_terms.cross(grad_tokens), gate_sum.spread(grad_tokens), up_sum.spread(grad_tokens))
    small.step()
    query_sum = RepSum(owned(query_terms), ranks)
    done = query_sum.pieces[0]
    gate_pair = gate_sum.done(done)
    small.step(done)

    def finished(name, pair, *others):
        return call(
            forward_weights_kernel,
            name,
            shape_of((width, ff), FULL),
            prefetch=1,
            in_specs=[whole((4, part, ff))] * 2,
            out_specs=whole((width, ff)),
            micros=3.5,
        )(place_of, after(pair[0], *others), pair[1])

    grad_down = finished("down_done", down_pair, gate_pair[0])
    key_sum = RepSum(owned(key_terms), ranks)
    stage = (query_sum.second(grad_down), up_sum.done(grad_down), small.step(grad_down))
    up_pair = stage[1]
    grad_gate = finished("gate_done", gate_pair, stage[0], up_pair[0])
    stage = (key_sum.second(grad_gate), query_sum.third(grad_gate))
    small.step(*stage)
    stage = (key_sum.third(*stage), query_sum.own(*stage))
    small.step(*stage)
    grad_up = finished("up_done", up_pair, *stage)
    stage = (key_sum.own(grad_up), query_sum.spread(grad_up))
    query_pair = query_sum.done(*stage)
    key_sum.spread(query_pair[0])
    key_pair = key_sum.done()
    grad_gains = small.finish()
    grad_down = grad_down.T
    grad_query, grad_out = call(
        query_done_kernel,
        "query_done",
        (shape_of((shard, width), FULL),) * 2,
        prefetch=1,
        in_specs=[whole((4, piece, 2 * width))] * 2,
        out_specs=(whole((shard, width)),) * 2,
        scratch=[pltpu.VMEM((grown, 2 * width), FULL)],
        micros=3,
    )(place_of, *query_pair)
    grad_key, grad_value = call(
        key_done_kernel,
        "key_done",
        (shape_of((kw, shard), FULL),) * 2,
        prefetch=1,
        in_specs=[whole((4, piece, kw2))] * 2,
        out_specs=(whole((kw, shard)),) * 2,
        scratch=[pltpu.VMEM((grown, kw2), FULL)],
        micros=2,
    )(place_of, *key_pair)
    own_gains = lax.dynamic_slice(grad_gains, (0, rank_grp * shard), (2, shard))
    return (
        jnp.swapaxes(block_out, 1, 2),
        jnp.swapaxes(grad_tokens, 1, 2),
        grad_query,
        grad_key.T,
        grad_value.T,
        grad_out,
        grad_gate,
        grad_up,
        grad_down,
        own_gains[0],
        own_gains[1],
    )


def solution(mesh):
    placed = (
        P("rep", "grp", None),
        P("grp", None),
        P("grp", None),
        P("grp", None),
        P("grp", None),
        P(None, "grp"),
        P(None, "grp"),
        P("grp", None),
        P("grp"),
        P("grp"),
        P("rep", None),
        P("rep", None),
        P("rep", "grp", None),
    )
    return jax.shard_map(
        body,
        mesh=mesh,
        in_specs=placed,
        out_specs=(
            P("rep", "grp", None),
            P("rep", "grp", None),
            P("grp", None),
            P("grp", None),
            P("grp", None),
            P("grp", None),
            P(None, "grp"),
            P(None, "grp"),
            P("grp", None),
            P("grp"),
            P("grp"),
        ),
        check_vma=False,
    )
```

time: 415 us -> 366 us (0.88); the launches traced: 410 us -> 366 us
  waiting for transfers between devices: 110 us -> 84.2 us
  other arithmetic: 22.2 us -> 10.9 us
  local copies, waits for them, and re-layouts: 21.2 us -> 15.2 us
    ppermute x78, waiting for transfers between devices: 110 us -> 84.2 us  [swap(): return lax.ppermute(values, axis, [(i, i ^ mask) for i in range(count)])]
    unnamed x160 -> x190, local copies, waits for them, and re-layouts: 19.1 us -> 13.2 us
    pallas_call x23 -> x28, Pallas kernels: 197 us -> 194 us  [placed(): return run(*args[:prefetch], *rest)]
  transfers between devices with their start and end apart: 78 -> 78, of which waited for: 31 -> 22; matrix products, arithmetic and copies ran while one was open for 6% -> 3% of each run, Pallas kernels for 47% -> 49%
where the time goes in v4:
time: 366 us
  Pallas kernels  194 us (53%)
  waiting for transfers between devices  84.2 us (23%)
  starting transfers between devices  60.5 us (17%)
  local copies, waits for them, and re-layouts  15.2 us (4%)
  other arithmetic  10.9 us (3%)
    pallas_call x28, Pallas kernels, placed(): return run(*args[:prefetch], *rest)  194 us
    ppermute x78, waiting for transfers between devices, swap(): return lax.ppermute(values, axis, [(i, i ^ mask) for i in range(count)])  84.2 us
    ppermute x78, starting transfers between devices, swap(): return lax.ppermute(values, axis, [(i, i ^ mask) for i in range(count)])  60.5 us
    unnamed x190, local copies, waits for them, and re-layouts  13.2 us
  transfers between devices with their start and end apart: 78, of which 22 were waited for; matrix products, arithmetic and copies ran while one was open for 3% of the time, Pallas kernels for 49%

profile of v4, /device:TPU:0, one launch (start us, length us, event | category | flops | bytes accessed | tf_op | source)
XLA Modules:
  0.0 366.5 jit_solution(4997836391507812805)
XLA Ops:
  2.5 2.1 pack.1.b0.k0
  4.6 3.0 collective-permute-start.1
  8.5 8.7 %collective-permute-done.1.b2.k2 = bf16[240,768]{1,0:T(8,128)(2,1)S(1)} collective-permute-done((bf16[240,768]{1,0:T(8,128)(2,1)}, bf16[240,768]{1,0:T(8,128)(2,1)S(1)}, u32[]{:S(2)}, u32[]{:S(2)}) %collective-permute-start.1) | collective-permute-done | bytes 368672 | tf_op jit(solution)/shard_map/ppermute | solution.py:37
  19.6 4.3 %keys_values.1 = (bf16[960,512]{1,0:T(8,128)(2,1)}, bf16[640,256]{1,0:T(8,128)(2,1)}, bf16[640,256]{1,0:T(8,128)(2,1)}, bf16[960,128]{1,0:T(8,128)(2,1)}) custom-call(s32[2]{0:T(128)S(1)} %pad_add_fusion.ranks, bf16[2,960,256]{2,1,0:T(8,128)(2,1)} %bitcast.107, bf16[240,768]{1,0:T(8,128)(2,1)} %pack.1.b0.k0, bf16[240,768]{1,0:T(8,128)(2,1)} %copy-done.63, ...), custom_call_target="tpu_custom_call" | custom-call | flops 860000000 | bytes 1024 | tf_op jit(solution)/shard_map/keys_values/pallas_call | solution.py:176
  24.0 4.9 %flip_two.1 = (bf16[1280,960]{1,0:T(8,128)(2,1)}, bf16[960,1280]{1,0:T(8,128)(2,1)}) custom-call(bf16[960,640]{1,0:T(8,128)(2,1)} %wg_ref, bf16[960,640]{1,0:T(8,128)(2,1)} %wu_ref.1), custom_call_target="tpu_custom_call" | custom-call | flops 800000000 | bytes 1024 | tf_op jit(solution)/shard_map/flip_two/pallas_call | solution.py:176
  29.4 2.1 collective-permute-start.6
  31.5 2.8 flip_one.1.wd_ref.refs_9_
  35.9 4.9 %queries.1.q_ref = bf16[960,512]{1,0:T(8,128)(2,1)} custom-call(s32[2]{0:T(128)S(1)} %pad_add_fusion.ranks, bf16[960,512]{1,0:T(8,128)(2,1)} %get-tuple-element.326.norm_ref, bf16[240,960]{1,0:T(8,128)(2,1)} %q0.1, bf16[240,960]{1,0:T(8,128)(2,1)} %copy-done.28, bf16[240,960]{1,0:T(8,128)(2,1)} %copy-done.27, bf16[240,960]{1,0:T(8,128)(2,1)} %copy-done.29, ...), custom_call_target="tpu_custom_call" | custom-call | flops 980000000 | bytes 1024 | tf_op jit(solution)/shard_map/queries/pallas_call | solution.py:176
  41.7 1.6 collective-permute-start.12
  44.8 11.5 %attend.2 = (bf16[5,1024,768]{2,1,0:T(8,128)(2,1)}, bf16[960,256]{1,0:T(8,128)(2,1)}) custom-call(s32[2]{0:T(128)S(1)} %pad_add_fusion.ranks, s32[2,4]{1,0:T(2,128)S(1)} %copy-done.4, s32[2,2]{1,0:T(2,128)S(1)} %copy-done.5, bf16[960,512]{1,0:T(8,128)(2,1)} %queries.1.q_ref, bf16[640,256]{1,0:T(8,128)(2,1)} %get-tuple-element.199.b0, ...), custom_call_target="tpu_custom_call" | custom-call | flops 2000000000 | bytes 1024 | tf_op jit(solution)/shard_map/attend/pallas_call | solution.py:176
  56.3 5.2 %collective-permute-done.12.b2 = bf16[640,256]{1,0:T(8,128)(2,1)S(1)} collective-permute-done((bf16[640,256]{1,0:T(8,128)(2,1)S(1)}, bf16[640,256]{1,0:T(8,128)(2,1)S(1)}, u32[]{:S(2)}, u32[]{:S(2)}) %collective-permute-start.12) | collective-permute-done | bytes 327712 | tf_op jit(solution)/shard_map/ppermute | solution.py:37
  65.9 4.4 %middle.2 = (f32[960,256]{1,0:T(8,128)}, bf16[960,256]{1,0:T(8,128)(2,1)}) custom-call(s32[2]{0:T(128)S(1)} %pad_add_fusion.ranks, bf16[960,256]{1,0:T(8,128)(2,1)} %get-tuple-element.203.att_ref.att_a, bf16[240,960]{1,0:T(8,128)(2,1)} %b0.9, bf16[240,960]{1,0:T(8,128)(2,1)} %copy-done.9, bf16[240,960]{1,0:T(8,128)(2,1)} %copy-done.8, ...), custom_call_target="tpu_custom_call" | custom-call | flops 600000000 | bytes 1024 | tf_op jit(solution)/shard_map/middle/pallas_call | solution.py:176
  72.2 11.3 %attend.3 = (bf16[5,1024,768]{2,1,0:T(8,128)(2,1)}, bf16[960,256]{1,0:T(8,128)(2,1)}) custom-call(s32[2]{0:T(128)S(1)} %pad_add_fusion.ranks, s32[2,4]{1,0:T(2,128)S(1)} %copy-done.4, s32[2,2]{1,0:T(2,128)S(1)} %copy-done.5, bf16[960,512]{1,0:T(8,128)(2,1)} %queries.1.q_ref, bf16[640,256]{1,0:T(8,128)(2,1)} %get-tuple-element.215.b0, ...), custom_call_target="tpu_custom_call" | custom-call | flops 2000000000 | bytes 1024 | tf_op jit(solution)/shard_map/attend/pallas_call | solution.py:176
  84.2 1.6 collective-permute-start.21
  85.8 4.4 %middle.3 = (f32[960,256]{1,0:T(8,128)}, bf16[960,256]{1,0:T(8,128)(2,1)}) custom-call(s32[2]{0:T(128)S(1)} %pad_add_fusion.ranks, bf16[960,256]{1,0:T(8,128)(2,1)} %get-tuple-element.223.att_ref.att_b, bf16[240,960]{1,0:T(8,128)(2,1)} %b0.9, bf16[240,960]{1,0:T(8,128)(2,1)} %copy-done.9, bf16[240,960]{1,0:T(8,128)(2,1)} %copy-done.8, ...), custom_call_target="tpu_custom_call" | custom-call | flops 600000000 | bytes 1024 | tf_op jit(solution)/shard_map/middle/pallas_call | solution.py:176
  91.3 8.4 %own_blocks.1 = (bf16[2,960,256]{2,1,0:T(8,128)(2,1)}, bf16[2,960,256]{2,1,0:T(8,128)(2,1)}, bf16[2,640,256]{2,1,0:T(8,128)(2,1)}, bf16[2,640,256]{2,1,0:T(8,128)(2,1)}, bf16[2,640,256]{2,1,0:T(8,128)(2,1)}) custom-call(bf16[960,256]{1,0:T(8,128)(2,1)} %get-tuple-element.272.x_a.refs_0_, bf16[960,256]{1,0:T(8,128)(2,1)} %get-tuple-element.242.x_b.refs_4_, ...), custom_call_target="tpu_custom_call" | custom-call | flops 1600000000 | bytes 1024 | tf_op jit(solution)/shard_map/own_blocks/pallas_call | solution.py:176
  101.9 23.7 %other_blocks.2 = (bf16[960,256]{1,0:T(8,128)(2,1)}, bf16[2,960,256]{2,1,0:T(8,128)(2,1)}, bf16[960,256]{1,0:T(8,128)(2,1)}, bf16[2,960,256]{2,1,0:T(8,128)(2,1)...) custom-call(bf16[960,256]{1,0:T(8,128)(2,1)} %copy-done.14, ...), custom_call_target="tpu_custom_call" | custom-call | flops 2400000000 | bytes 1024 | tf_op jit(solution)/shard_map/other_blocks/pallas_call | solution.py:176
  127.5 1.4 collective-permute-done.25.refs_2_.refs_7_
  129.8 12.0 %other_blocks.3 = (bf16[960,256]{1,0:T(8,128)(2,1)}, bf16[2,960,256]{2,1,0:T(8,128)(2,1)}, bf16[960,256]{1,0:T(8,128)(2,1)}, bf16[2,960,256]{2,1,0:T(8,128)(2,1)...) custom-call(bf16[960,256]{1,0:T(8,128)(2,1)} %copy-done.17, ...), custom_call_target="tpu_custom_call" | custom-call | flops 2400000000 | bytes 1024 | tf_op jit(solution)/shard_map/other_blocks/pallas_call | solution.py:176
  142.5 1.7 collective-permute-start.30
  144.8 7.9 %down_weights.1 = (bf16[4,120,640]{2,1,0:T(8,128)(2,1)}, bf16[2,120,640]{2,1,0:T(8,128)(2,1)}, bf16[1,120,640]{2,1,0:T(8,128)(2,1)}, bf16[1,120,640]{2,1,0:T(8,128)(2,1)}) custom-call(s32[2]{0:T(128)S(1)} %pad_add_fusion.ranks, bf16[960,256]{1,0:T(8,128)(2,1)} %copy-done.37, bf16[960,256]{1,0:T(8,128)(2,1)} %copy-done.31, bf16[960,256]{1,0:T(8,128)(2,1)} %copy-done.30, ...), custom_call_target="tpu_custom_call" | custom-call | flops 1600000000 | bytes 1024 | tf_op jit(solution)/shard_map/down_weights/pallas_call | solution.py:176
  152.7 1.7 collective-permute-start.29
  154.6 1.6 collective-permute-start.34
  156.2 8.0 %gate_weights.1 = (bf16[4,120,640]{2,1,0:T(8,128)(2,1)}, bf16[2,120,640]{2,1,0:T(8,128)(2,1)}, bf16[1,120,640]{2,1,0:T(8,128)(2,1)}, bf16[1,120,640]{2,1,0:T(8,128)(2,1)}) custom-call(s32[2]{0:T(128)S(1)} %pad_add_fusion.ranks, bf16[960,256]{1,0:T(8,128)(2,1)} %get-tuple-element.272.x_a.refs_0_, bf16[960,256]{1,0:T(8,128)(2,1)} %copy-done.14, ...), custom_call_target="tpu_custom_call" | custom-call | flops 1600000000 | bytes 1024 | tf_op jit(solution)/shard_map/gate_weights/pallas_call | solution.py:176
  164.9 7.9 %up_weights.1 = (bf16[4,120,640]{2,1,0:T(8,128)(2,1)}, bf16[2,120,640]{2,1,0:T(8,128)(2,1)}, bf16[1,120,640]{2,1,0:T(8,128)(2,1)}, bf16[1,120,640]{2,1,0:T(8,128)(2,1)}) custom-call(s32[2]{0:T(128)S(1)} %pad_add_fusion.ranks, bf16[960,256]{1,0:T(8,128)(2,1)} %get-tuple-element.272.x_a.refs_0_, bf16[960,256]{1,0:T(8,128)(2,1)} %copy-done.14, ...), custom_call_target="tpu_custom_call" | custom-call | flops 1600000000 | bytes 1024 | tf_op jit(solution)/shard_map/up_weights/pallas_call | solution.py:176
  172.9 1.6 collective-permute-start.38
  175.1 1.5 collective-permute-start.40
  176.6 5.5 %branch.2 = (f32[960,256]{1,0:T(8,128)}, bf16[960,256]{1,0:T(8,128)(2,1)}, bf16[960,256]{1,0:T(8,128)(2,1)}, f32[16,256]{1,0:T(8,128)}, f32[8,960]{1,0:T(8,128)}) custom-call(s32[2]{0:T(128)S(1)} %pad_add_fusion.ranks, f32[960,256]{1,0:T(8,128)} %get-tuple-element.324.mid_ref, bf16[2,960,256]{2,1,0:T(8,128)(2,1)} %bitcast.104, ...), custom_call_target="tpu_custom_call" | custom-call | flops 800000000 | bytes 1024 | tf_op jit(solution)/shard_map/branch/pallas_call | solution.py:176
  182.1 12.0 %attend_back.2 = (bf16[960,256]{1,0:T(8,128)(2,1)}, bf16[640,256]{1,0:T(8,128)(2,1)}, bf16[640,256]{1,0:T(8,128)(2,1)}, bf16[2,640,256]{2,1,0:T(8,128)(2,1)}) custom-call(bf16[960,512]{1,0:T(8,128)(2,1)} %queries.1.q_ref, bf16[640,256]{1,0:T(8,128)(2,1)} %get-tuple-element.199.b0, bf16[640,256]{1,0:T(8,128)(2,1)} %copy-done.76, bf16[640,256]{1,0:T(8,128)(2,1)} %copy-done.75, ...), custom_call_target="tpu_custom_call" | custom-call | flops 2200000000 | bytes 1024 | tf_op jit(solution)/shard_map/attend_back/pallas_call | solution.py:176
  194.3 2.7 collective-permute-start.41
  197.6 5.5 %branch.3 = (f32[960,256]{1,0:T(8,128)}, bf16[960,256]{1,0:T(8,128)(2,1)}, bf16[960,256]{1,0:T(8,128)(2,1)}, f32[16,256]{1,0:T(8,128)}, f32[8,960]{1,0:T(8,128)}) custom-call(s32[2]{0:T(128)S(1)} %pad_add_fusion.ranks, f32[960,256]{1,0:T(8,128)} %get-tuple-element.325.mid_ref, bf16[2,960,256]{2,1,0:T(8,128)(2,1)} %bitcast.105, ...), custom_call_target="tpu_custom_call" | custom-call | flops 800000000 | bytes 1024 | tf_op jit(solution)/shard_map/branch/pallas_call | solution.py:176
  203.2 1.6 collective-permute-start.42
  205.0 1.6 collective-permute-start.43
  206.6 11.5 %attend_back.3 = (bf16[960,256]{1,0:T(8,128)(2,1)}, bf16[640,256]{1,0:T(8,128)(2,1)}, bf16[640,256]{1,0:T(8,128)(2,1)}, bf16[2,640,256]{2,1,0:T(8,128)(2,1)}) custom-call(bf16[960,512]{1,0:T(8,128)(2,1)} %queries.1.q_ref, bf16[640,256]{1,0:T(8,128)(2,1)} %get-tuple-element.215.b0, bf16[640,256]{1,0:T(8,128)(2,1)} %copy-done.72, bf16[640,256]{1,0:T(8,128)(2,1)} %copy-done.71, ...), custom_call_target="tpu_custom_call" | custom-call | flops 2200000000 | bytes 1024 | tf_op jit(solution)/shard_map/attend_back/pallas_call | solution.py:176
  219.8 7.2 %query_weights.1 = (bf16[8,32,1920]{2,1,0:T(8,128)(2,1)}, bf16[8,32,1920]{2,1,0:T(8,128)(2,1)}, bf16[2,8,32,1920]{3,2,1,0:T(8,128)(2,1)}) custom-call(s32[2]{0:T(128)S(1)} %pad_add_fusion.ranks, bf16[960,512]{1,0:T(8,128)(2,1)} %get-tuple-element.326.norm_ref, bf16[960,256]{1,0:T(8,128)(2,1)} %get-tuple-element.317.gq_a, ...), custom_call_target="tpu_custom_call" | custom-call | flops 1600000000 | bytes 1024 | tf_op jit(solution)/shard_map/query_weights/pallas_call | solution.py:176
  227.9 2.6 collective-permute-start.47
  230.8 13.4 %collective-permute-done.46 = bf16[1,120,640]{2,1,0:T(8,128)(2,1)S(1)} collective-permute-done((bf16[1,120,640]{2,1,0:T(8,128)(2,1)S(1)}, bf16[1,120,640]{2,1,0:T(8,128)(2,1)S(1)}, u32[]{:S(2)}, u32[]{:S(2)}) %collective-permute-start.46) | collective-permute-done | bytes 153632 | tf_op jit(solution)/shard_map/ppermute | solution.py:37
  246.3 4.9 %query_grad.1.part_ref = f32[2,960,256]{2,1,0:T(8,128)} custom-call(s32[2]{0:T(128)S(1)} %pad_add_fusion.ranks, bf16[960,256]{1,0:T(8,128)(2,1)} %get-tuple-element.317.gq_a, bf16[960,256]{1,0:T(8,128)(2,1)} %get-tuple-element.301.gq_b, bf16[240,960]{1,0:T(8,128)(2,1)} %q0.1, bf16[240,960]{1,0:T(8,128)(2,1)} %copy-done.28, bf16[240,960]{1,0:T(8,128)(2,1)} %copy-done.27, ...), custom_call_target="tpu_custom_call" | custom-call | flops 800000000 | bytes 1024 | tf_op jit(solution)/shard_map/query_grad/pallas_call | solution.py:176
  251.3 1.7 collective-permute-start.53
  253.3 1.6 collective-permute-start.51
  254.9 1.5 collective-permute-done.50.b2
  257.1 4.9 %key_weights.1 = (bf16[8,32,640]{2,1,0:T(8,128)(2,1)}, bf16[8,32,640]{2,1,0:T(8,128)(2,1)}, bf16[2,8,32,640]{3,2,1,0:T(8,128)(2,1)}, bf16[640,512]{1,0:T(8,128)(2,1)}) custom-call(s32[2]{0:T(128)S(1)} %pad_add_fusion.ranks, bf16[960,512]{1,0:T(8,128)(2,1)} %get-tuple-element.326.norm_ref, bf16[640,256]{1,0:T(8,128)(2,1)} %get-tuple-element.327.a0, ...), custom_call_target="tpu_custom_call" | custom-call | flops 800000000 | bytes 1024 | tf_op jit(solution)/shard_map/key_weights/pallas_call | solution.py:176
  263.8 6.6 %input_grad.1 = (f32[2,960,256]{2,1,0:T(8,128)}, f32[8,960]{1,0:T(8,128)}) custom-call(s32[2]{0:T(128)S(1)} %pad_add_fusion.ranks, f32[2,960,256]{2,1,0:T(8,128)} %query_grad.1.part_ref, bf16[640,512]{1,0:T(8,128)(2,1)} %get-tuple-element.329.gkv_ref, bf16[240,768]{1,0:T(8,128)(2,1)} %pack.1.b0.k0, bf16[240,768]{1,0:T(8,128)(2,1)} %copy-done.63, ...), custom_call_target="tpu_custom_call" | custom-call | flops 1200000000 | bytes 1024 | tf_op jit(solution)/shard_map/input_grad/pallas_call | solution.py:176
  270.3 3.3 collective-permute-done.57
  273.8 2.1 collective-permute-start.54
  277.1 8.5 %collective-permute-done.62 = bf16[8,32,640]{2,1,0:T(8,128)(2,1)S(1)} collective-permute-done((bf16[8,32,640]{2,1,0:T(8,128)(2,1)S(1)}, bf16[8,32,640]{2,1,0:T(8,128)(2,1)S(1)}, u32[]{:S(2)}, u32[]{:S(2)}) %collective-permute-start.62) | collective-permute-done | bytes 327712 | tf_op jit(solution)/shard_map/ppermute | solution.py:37
  286.2 3.8 %collective-permute-done.54 = bf16[2,120,640]{2,1,0:T(8,128)(2,1)S(1)} collective-permute-done((bf16[2,120,640]{2,1,0:T(8,128)(2,1)S(1)}, bf16[2,120,640]{2,1,0:T(8,128)(2,1)S(1)}, u32[]{:S(2)}, u32[]{:S(2)}) %collective-permute-start.54) | collective-permute-done | bytes 307232 | tf_op jit(solution)/shard_map/ppermute | solution.py:37
  290.6 1.6 collective-permute-start.59
  293.0 3.5 down_done.1
  297.3 2.5 collective-permute-done.52
  301.0 13.5 %collective-permute-done.59.odd = bf16[4,120,640]{2,1,0:T(8,128)(2,1)S(1)} collective-permute-done((bf16[4,120,640]{2,1,0:T(8,128)(2,1)S(1)}, bf16[4,120,640]{2,1,0:T(8,128)(2,1)S(1)}, u32[]{:S(2)}, u32[]{:S(2)}) %collective-permute-start.59) | collective-permute-done | bytes 614432 | tf_op jit(solution)/shard_map/ppermute | solution.py:37
  315.3 3.7 %gate_done.1 = f32[960,640]{1,0:T(8,128)} custom-call(s32[2]{0:T(128)S(1)} %pad_add_fusion.ranks, bf16[4,120,640]{2,1,0:T(8,128)(2,1)} %copy-done.23, bf16[4,120,640]{2,1,0:T(8,128)(2,1)} %copy-done.49), custom_call_target="tpu_custom_call" | custom-call | flops 700000000 | bytes 1024 | tf_op jit(solution)/shard_map/gate_done/pallas_call | solution.py:176
  320.7 1.8 collective-permute-start.66
  326.5 1.9 collective-permute-start.68
  328.5 4.6 %collective-permute-done.66.odd = bf16[4,120,640]{2,1,0:T(8,128)(2,1)S(1)} collective-permute-done((bf16[4,120,640]{2,1,0:T(8,128)(2,1)S(1)}, bf16[4,120,640]{2,1,0:T(8,128)(2,1)S(1)}, u32[]{:S(2)}, u32[]{:S(2)}) %collective-permute-start.66) | collective-permute-done | bytes 614432 | tf_op jit(solution)/shard_map/ppermute | solution.py:37
  333.9 3.5 up_done.1
  337.5 1.8 collective-permute-start.67
  340.7 2.7 collective-permute-start.77
  344.2 1.7 collective-permute-start.69
  345.9 2.6 collective-permute-done.70
  348.8 4.2 %collective-permute-done.71 = bf16[2,32,640]{2,1,0:T(8,128)(2,1)S(1)} collective-permute-done((bf16[2,32,640]{2,1,0:T(8,128)(2,1)S(1)}, bf16[2,32,640]{2,1,0:T(8,128)(2,1)S(1)}, u32[]{:S(2)}, u32[]{:S(2)}) %collective-permute-start.71) | collective-permute-done | bytes 81952 | tf_op jit(solution)/shard_map/ppermute | solution.py:37
  354.3 4.2 %collective-permute-done.72.odd = bf16[4,32,640]{2,1,0:T(8,128)(2,1)S(1)} collective-permute-done((bf16[4,32,640]{2,1,0:T(8,128)(2,1)S(1)}, bf16[4,32,640]{2,1,0:T(8,128)(2,1)S(1)}, u32[]{:S(2)}, u32[]{:S(2)}) %collective-permute-start.72) | collective-permute-done | bytes 163872 | tf_op jit(solution)/shard_map/ppermute | solution.py:37
  359.1 2.8 key_done.1
  362.8 3.5 query_done.1
  (361 shorter events, 51.9 us)
Async XLA Ops:
  4.6 12.6 %collective-permute-start.1 = (bf16[240,768]{1,0:T(8,128)(2,1)}, bf16[240,768]{1,0:T(8,128)(2,1)S(1)}, u32[]{:S(2)}, u32[]{:S(2)}) collective-permute-start(bf16[240,768]{1,0:T(8,128)(2,1)} %pack.1.b0.k0), channel_id=1, source_target_pairs={{0,16},{8,24},{16,0},{24,8},{1,17},{9,25},{17,1},{25,9},{2,18},{10... | collective-permute-start | bytes 1105928 | tf_op jit(solution)/shard_map/ppermute | solution.py:37
  7.6 10.7 %collective-permute-start = (bf16[240,768]{1,0:T(8,128)(2,1)}, bf16[240,768]{1,0:T(8,128)(2,1)S(1)}, u32[]{:S(2)}, u32[]{:S(2)}) collective-permute-start(bf16[240,768]{1,0:T(8,128)(2,1)} %pack.1.b0.k0), channel_id=1, source_target_pairs={{0,8},{8,0},{16,24},{24,16},{1,9},{9,1},{17,25},{25,17},{2,10},{10... | collective-permute-start | bytes 1105928 | tf_op jit(solution)/shard_map/ppermute | solution.py:37
  7.6 21.2 %collective-permute-start.3 = (bf16[240,960]{1,0:T(8,128)(2,1)}, bf16[240,960]{1,0:T(8,128)(2,1)S(1)}, u32[]{:S(2)}, u32[]{:S(2)}) collective-permute-start(bf16[240,960]{1,0:T(8,128)(2,1)} %q0.1), channel_id=1, source_target_pairs={{0,16},{8,24},{16,0},{24,8},{1,17},{9,25},{17,1},{25,9},{2,18},{10... | collective-permute-start | bytes 1382408 | tf_op jit(solution)/shard_map/ppermute | solution.py:37
  29.4 11.4 %collective-permute-start.6 = (bf16[640,256]{1,0:T(8,128)(2,1)S(1)}, bf16[640,256]{1,0:T(8,128)(2,1)S(1)}, u32[]{:S(2)}, u32[]{:S(2)}) collective-permute-start(bf16[640,256]{1,0:T(8,128)(2,1)S(1)} %copy-done.74), channel_id=1, source_target_pairs={{0,16},{8,24},{16,0},{24,8},{1,17},{9,25},{17,1},{25,9},{2,18},{10... | collective-permute-start | bytes 983048 | tf_op jit(solution)/shard_map/ppermute | solution.py:37
  41.3 20.2 %collective-permute-start.9 = (bf16[240,960]{1,0:T(8,128)(2,1)S(1)}, bf16[240,960]{1,0:T(8,128)(2,1)S(1)}, u32[]{:S(2)}, u32[]{:S(2)}) collective-permute-start(bf16[240,960]{1,0:T(8,128)(2,1)S(1)} %copy-done.7), channel_id=1, source_target_pairs={{0,16},{8,24},{16,0},{24,8},{1,17},{9,25},{17,1},{25,9},{2,18},{10... | collective-permute-start | bytes 1382408 | tf_op jit(solution)/shard_map/ppermute | solution.py:37
  41.7 19.8 %collective-permute-start.12 = (bf16[640,256]{1,0:T(8,128)(2,1)S(1)}, bf16[640,256]{1,0:T(8,128)(2,1)S(1)}, u32[]{:S(2)}, u32[]{:S(2)}) collective-permute-start(bf16[640,256]{1,0:T(8,128)(2,1)S(1)} %copy-done.70), channel_id=1, source_target_pairs={{0,16},{8,24},{16,0},{24,8},{1,17},{9,25},{17,1},{25,9},{2,18},{10... | collective-permute-start | bytes 983048 | tf_op jit(solution)/shard_map/ppermute | solution.py:37
  61.5 9.2 %collective-permute-start.13 = (bf16[640,256]{1,0:T(8,128)(2,1)S(1)}, bf16[640,256]{1,0:T(8,128)(2,1)S(1)}, u32[]{:S(2)}, u32[]{:S(2)}) collective-permute-start(bf16[640,256]{1,0:T(8,128)(2,1)S(1)} %copy-done.70), channel_id=1, source_target_pairs={{0,8},{8,0},{16,24},{24,16},{1,9},{9,1},{17,25},{25,17},{2,10},{10... | collective-permute-start | bytes 983048 | tf_op jit(solution)/shard_map/ppermute | solution.py:37
  61.6 9.2 %collective-permute-start.14 = (bf16[640,256]{1,0:T(8,128)(2,1)S(1)}, bf16[640,256]{1,0:T(8,128)(2,1)S(1)}, u32[]{:S(2)}, u32[]{:S(2)}) collective-permute-start(bf16[640,256]{1,0:T(8,128)(2,1)S(1)} %collective-permute-done.12.b2), channel_id=1, source_target_pairs={{0,8},{8,0},{16,24},{24,16},{1,9},{9,1},{17,25},{25,17},{2,10},{10... | collective-permute-start | bytes 983048 | tf_op jit(solution)/shard_map/ppermute | solution.py:37
  62.7 20.9 %collective-permute-start.15 = (bf16[960,256]{1,0:T(8,128)(2,1)S(1)}, bf16[960,256]{1,0:T(8,128)(2,1)S(1)}, u32[]{:S(2)}, u32[]{:S(2)}) collective-permute-start(bf16[960,256]{1,0:T(8,128)(2,1)S(1)} %get-tuple-element.254.refs_0_), channel_id=1, source_target_pairs={{0,16},{8,24},{16,0},{24,8},{1,17},{9,25},{17,1},{25,9},{2,18},{10... | collective-permute-start | bytes 1474568 | tf_op jit(solution)/shard_map/ppermute | solution.py:37
  70.4 19.9 %collective-permute-start.16 = (bf16[960,256]{1,0:T(8,128)(2,1)}, bf16[960,256]{1,0:T(8,128)(2,1)S(1)}, u32[]{:S(2)}, u32[]{:S(2)}) collective-permute-start(bf16[960,256]{1,0:T(8,128)(2,1)} %get-tuple-element.272.x_a.refs_0_), channel_id=1, source_target_pairs={{0,16},{8,24},{16,0},{24,8},{1,17},{9,25},{17,1},{25,9},{2,18},{10... | collective-permute-start | bytes 1474568 | tf_op jit(solution)/shard_map/ppermute | solution.py:37
  83.6 7.3 %collective-permute-start.19 = (bf16[960,256]{1,0:T(8,128)(2,1)S(1)}, bf16[960,256]{1,0:T(8,128)(2,1)S(1)}, u32[]{:S(2)}, u32[]{:S(2)}) collective-permute-start(bf16[960,256]{1,0:T(8,128)(2,1)S(1)} %get-tuple-element.254.refs_0_), channel_id=1, source_target_pairs={{0,8},{8,0},{16,24},{24,16},{1,9},{9,1},{17,25},{25,17},{2,10},{10... | collective-permute-start | bytes 1474568 | tf_op jit(solution)/shard_map/ppermute | solution.py:37
  83.7 7.6 %collective-permute-start.20 = (bf16[960,256]{1,0:T(8,128)(2,1)S(1)}, bf16[960,256]{1,0:T(8,128)(2,1)S(1)}, u32[]{:S(2)}, u32[]{:S(2)}) collective-permute-start(bf16[960,256]{1,0:T(8,128)(2,1)S(1)} %collective-permute-done.15.refs_4_.refs_2_), channel_id=1, source_target_pairs={{0,8},{8,0},{16,24},{24,16},{1,9},{9,1},{17,25},{25,17},{2,10},{10... | collective-permute-start | bytes 1474568 | tf_op jit(solution)/shard_map/ppermute | solution.py:37
  84.2 15.5 %collective-permute-start.21 = (bf16[960,256]{1,0:T(8,128)(2,1)S(1)}, bf16[960,256]{1,0:T(8,128)(2,1)S(1)}, u32[]{:S(2)}, u32[]{:S(2)}) collective-permute-start(bf16[960,256]{1,0:T(8,128)(2,1)S(1)} %get-tuple-element.236.refs_4_), channel_id=1, source_target_pairs={{0,16},{8,24},{16,0},{24,8},{1,17},{9,25},{17,1},{25,9},{2,18},{10... | collective-permute-start | bytes 1474568 | tf_op jit(solution)/shard_map/ppermute | solution.py:37
  90.3 10.0 %collective-permute-start.17 = (bf16[960,256]{1,0:T(8,128)(2,1)S(1)}, bf16[960,256]{1,0:T(8,128)(2,1)S(1)}, u32[]{:S(2)}, u32[]{:S(2)}) collective-permute-start(bf16[960,256]{1,0:T(8,128)(2,1)S(1)} %copy-done.11), channel_id=1, source_target_pairs={{0,8},{8,0},{16,24},{24,16},{1,9},{9,1},{17,25},{25,17},{2,10},{10... | collective-permute-start | bytes 1474568 | tf_op jit(solution)/shard_map/ppermute | solution.py:37
  90.3 9.9 %collective-permute-start.18 = (bf16[960,256]{1,0:T(8,128)(2,1)S(1)}, bf16[960,256]{1,0:T(8,128)(2,1)S(1)}, u32[]{:S(2)}, u32[]{:S(2)}) collective-permute-start(bf16[960,256]{1,0:T(8,128)(2,1)S(1)} %collective-permute-done.16.refs_1_.refs_2_), channel_id=1, source_target_pairs={{0,8},{8,0},{16,24},{24,16},{1,9},{9,1},{17,25},{25,17},{2,10},{10... | collective-permute-start | bytes 1474568 | tf_op jit(solution)/shard_map/ppermute | solution.py:37
  90.8 34.7 %collective-permute-start.23 = (bf16[960,256]{1,0:T(8,128)(2,1)}, bf16[960,256]{1,0:T(8,128)(2,1)S(1)}, u32[]{:S(2)}, u32[]{:S(2)}) collective-permute-start(bf16[960,256]{1,0:T(8,128)(2,1)} %get-tuple-element.242.x_b.refs_4_), channel_id=1, source_target_pairs={{0,16},{8,24},{16,0},{24,8},{1,17},{9,25},{17,1},{25,9},{2,18},{10... | collective-permute-start | bytes 1474568 | tf_op jit(solution)/shard_map/ppermute | solution.py:37
  99.7 26.6 %collective-permute-start.26 = (bf16[960,256]{1,0:T(8,128)(2,1)S(1)}, bf16[960,256]{1,0:T(8,128)(2,1)S(1)}, u32[]{:S(2)}, u32[]{:S(2)}) collective-permute-start(bf16[960,256]{1,0:T(8,128)(2,1)S(1)} %get-tuple-element.236.refs_4_), channel_id=1, source_target_pairs={{0,8},{8,0},{16,24},{24,16},{1,9},{9,1},{17,25},{25,17},{2,10},{10... | collective-permute-start | bytes 1474568 | tf_op jit(solution)/shard_map/ppermute | solution.py:37
  99.8 27.0 %collective-permute-start.27 = (bf16[960,256]{1,0:T(8,128)(2,1)S(1)}, bf16[960,256]{1,0:T(8,128)(2,1)S(1)}, u32[]{:S(2)}, u32[]{:S(2)}) collective-permute-start(bf16[960,256]{1,0:T(8,128)(2,1)S(1)} %collective-permute-done.21.refs_4_.refs_6_), channel_id=1, source_target_pairs={{0,8},{8,0},{16,24},{24,16},{1,9},{9,1},{17,25},{25,17},{2,10},{10... | collective-permute-start | bytes 1474568 | tf_op jit(solution)/shard_map/ppermute | solution.py:37
  126.2 16.2 %collective-permute-start.22 = (bf16[2,960,256]{2,1,0:T(8,128)(2,1)}, bf16[2,960,256]{2,1,0:T(8,128)(2,1)S(1)}, u32[]{:S(2)}, u32[]{:S(2)}) collective-permute-start(bf16[2,960,256]{2,1,0:T(8,128)(2,1)} %get-tuple-element.241), channel_id=1, source_target_pairs={{0,8},{8,0},{16,24},{24,16},{1,9},{9,1},{17,25},{25,17},{2,10},{10... | collective-permute-start | bytes 2949128 | tf_op jit(solution)/shard_map/ppermute | solution.py:37
  126.3 17.9 %collective-permute-start.28 = (bf16[2,960,256]{2,1,0:T(8,128)(2,1)}, bf16[2,960,256]{2,1,0:T(8,128)(2,1)S(1)}, u32[]{:S(2)}, u32[]{:S(2)}) collective-permute-start(bf16[2,960,256]{2,1,0:T(8,128)(2,1)} %get-tuple-element.251), channel_id=1, source_target_pairs={{0,8},{8,0},{16,24},{24,16},{1,9},{9,1},{17,25},{25,17},{2,10},{10... | collective-permute-start | bytes 2949128 | tf_op jit(solution)/shard_map/ppermute | solution.py:37
  141.8 12.6 %collective-permute-start.32 = (bf16[2,960,256]{2,1,0:T(8,128)(2,1)}, bf16[2,960,256]{2,1,0:T(8,128)(2,1)S(1)}, u32[]{:S(2)}, u32[]{:S(2)}) collective-permute-start(bf16[2,960,256]{2,1,0:T(8,128)(2,1)} %get-tuple-element.262), channel_id=1, source_target_pairs={{0,8},{8,0},{16,24},{24,16},{1,9},{9,1},{17,25},{25,17},{2,10},{10... | collective-permute-start | bytes 2949128 | tf_op jit(solution)/shard_map/ppermute | solution.py:37
  142.0 14.2 %collective-permute-start.31 = (bf16[2,960,256]{2,1,0:T(8,128)(2,1)}, bf16[2,960,256]{2,1,0:T(8,128)(2,1)S(1)}, u32[]{:S(2)}, u32[]{:S(2)}) collective-permute-start(bf16[2,960,256]{2,1,0:T(8,128)(2,1)} %get-tuple-element.261), channel_id=1, source_target_pairs={{0,8},{8,0},{16,24},{24,16},{1,9},{9,1},{17,25},{25,17},{2,10},{10... | collective-permute-start | bytes 2949128 | tf_op jit(solution)/shard_map/ppermute | solution.py:37
  142.5 22.4 %collective-permute-start.30 = (bf16[960,256]{1,0:T(8,128)(2,1)S(1)}, bf16[960,256]{1,0:T(8,128)(2,1)S(1)}, u32[]{:S(2)}, u32[]{:S(2)}) collective-permute-start(bf16[960,256]{1,0:T(8,128)(2,1)S(1)} %fusion.6), channel_id=1, source_target_pairs={{0,16},{8,24},{16,0},{24,8},{1,17},{9,25},{17,1},{25,9},{2,18},{10... | collective-permute-start | bytes 1474568 | tf_op jit(solution)/shard_map/ppermute | solution.py:37
  144.4 30.7 %collective-permute-start.33 = (bf16[960,256]{1,0:T(8,128)(2,1)S(1)}, bf16[960,256]{1,0:T(8,128)(2,1)S(1)}, u32[]{:S(2)}, u32[]{:S(2)}) collective-permute-start(bf16[960,256]{1,0:T(8,128)(2,1)S(1)} %fusion.5), channel_id=1, source_target_pairs={{0,16},{8,24},{16,0},{24,8},{1,17},{9,25},{17,1},{25,9},{2,18},{10... | collective-permute-start | bytes 1474568 | tf_op jit(solution)/shard_map/ppermute | solution.py:37
  152.7 20.1 %collective-permute-start.29 = (bf16[4,120,640]{2,1,0:T(8,128)(2,1)}, bf16[4,120,640]{2,1,0:T(8,128)(2,1)S(1)}, u32[]{:S(2)}, u32[]{:S(2)}) collective-permute-start(bf16[4,120,640]{2,1,0:T(8,128)(2,1)} %get-tuple-element.259), channel_id=1, source_target_pairs={{0,1},{1,0},{2,3},{3,2},{4,5},{5,4},{6,7},{7,6},{8,9},{9,8},{10,11... | collective-permute-start | bytes 1843208 | tf_op jit(solution)/shard_map/ppermute | solution.py:37
  154.6 27.5 %collective-permute-start.34 = (bf16[960,256]{1,0:T(8,128)(2,1)S(1)}, bf16[960,256]{1,0:T(8,128)(2,1)S(1)}, u32[]{:S(2)}, u32[]{:S(2)}) collective-permute-start(bf16[960,256]{1,0:T(8,128)(2,1)S(1)} %fusion.4), channel_id=1, source_target_pairs={{0,16},{8,24},{16,0},{24,8},{1,17},{9,25},{17,1},{25,9},{2,18},{10... | collective-permute-start | bytes 1474568 | tf_op jit(solution)/shard_map/ppermute | solution.py:37
  164.1 32.9 %collective-permute-start.35 = (bf16[4,120,640]{2,1,0:T(8,128)(2,1)}, bf16[4,120,640]{2,1,0:T(8,128)(2,1)S(1)}, u32[]{:S(2)}, u32[]{:S(2)}) collective-permute-start(bf16[4,120,640]{2,1,0:T(8,128)(2,1)} %get-tuple-element.269), channel_id=1, source_target_pairs={{0,1},{1,0},{2,3},{3,2},{4,5},{5,4},{6,7},{7,6},{8,9},{9,8},{10,11... | collective-permute-start | bytes 1843208 | tf_op jit(solution)/shard_map/ppermute | solution.py:37
  172.9 21.2 %collective-permute-start.38 = (bf16[2,120,640]{2,1,0:T(8,128)(2,1)S(1)}, bf16[2,120,640]{2,1,0:T(8,128)(2,1)S(1)}, u32[]{:S(2)}, u32[]{:S(2)}) collective-permute-start(bf16[2,120,640]{2,1,0:T(8,128)(2,1)S(1)} %add_convert_fusion.2), channel_id=1, source_target_pairs={{0,2},{1,3},{2,0},{3,1},{4,6},{5,7},{6,4},{7,5},{8,10},{9,11},{10,... | collective-permute-start | bytes 921608 | tf_op jit(solution)/shard_map/ppermute | solution.py:37
  174.6 23.0 %collective-permute-start.37 = (bf16[960,256]{1,0:T(8,128)(2,1)S(1)}, bf16[960,256]{1,0:T(8,128)(2,1)S(1)}, u32[]{:S(2)}, u32[]{:S(2)}) collective-permute-start(bf16[960,256]{1,0:T(8,128)(2,1)S(1)} %fusion.3), channel_id=1, source_target_pairs={{0,16},{8,24},{16,0},{24,8},{1,17},{9,25},{17,1},{25,9},{2,18},{10... | collective-permute-start | bytes 1474568 | tf_op jit(solution)/shard_map/ppermute | solution.py:37
  175.1 28.0 %collective-permute-start.40 = (bf16[4,120,640]{2,1,0:T(8,128)(2,1)}, bf16[4,120,640]{2,1,0:T(8,128)(2,1)S(1)}, u32[]{:S(2)}, u32[]{:S(2)}) collective-permute-start(bf16[4,120,640]{2,1,0:T(8,128)(2,1)} %get-tuple-element.276), channel_id=1, source_target_pairs={{0,1},{1,0},{2,3},{3,2},{4,5},{5,4},{6,7},{7,6},{8,9},{9,8},{10,11... | collective-permute-start | bytes 1843208 | tf_op jit(solution)/shard_map/ppermute | solution.py:37
  194.2 10.7 %collective-permute-start.39 = (bf16[2,640,256]{2,1,0:T(8,128)(2,1)}, bf16[2,640,256]{2,1,0:T(8,128)(2,1)S(1)}, u32[]{:S(2)}, u32[]{:S(2)}) collective-permute-start(bf16[2,640,256]{2,1,0:T(8,128)(2,1)} %get-tuple-element.293), channel_id=1, source_target_pairs={{0,8},{8,0},{16,24},{24,16},{1,9},{9,1},{17,25},{25,17},{2,10},{10... | collective-permute-start | bytes 1966088 | tf_op jit(solution)/shard_map/ppermute | solution.py:37
  194.3 24.6 %collective-permute-start.41 = (bf16[1,120,640]{2,1,0:T(8,128)(2,1)S(1)}, bf16[1,120,640]{2,1,0:T(8,128)(2,1)S(1)}, u32[]{:S(2)}, u32[]{:S(2)}) collective-permute-start(bf16[1,120,640]{2,1,0:T(8,128)(2,1)S(1)} %add_convert_fusion.9), channel_id=1, source_target_pairs={{0,4},{1,5},{2,6},{3,7},{4,0},{5,1},{6,2},{7,3},{8,12},{9,13},{10,... | collective-permute-start | bytes 460808 | tf_op jit(solution)/shard_map/ppermute | solution.py:37
  197.1 21.0 %collective-permute-start.36 = (bf16[2,120,640]{2,1,0:T(8,128)(2,1)S(1)}, bf16[2,120,640]{2,1,0:T(8,128)(2,1)S(1)}, u32[]{:S(2)}, u32[]{:S(2)}) collective-permute-start(bf16[2,120,640]{2,1,0:T(8,128)(2,1)S(1)} %add_convert_fusion.1), channel_id=1, source_target_pairs={{0,2},{1,3},{2,0},{3,1},{4,6},{5,7},{6,4},{7,5},{8,10},{9,11},{10,... | collective-permute-start | bytes 921608 | tf_op jit(solution)/shard_map/ppermute | solution.py:37
  203.2 15.7 %collective-permute-start.42 = (bf16[2,120,640]{2,1,0:T(8,128)(2,1)S(1)}, bf16[2,120,640]{2,1,0:T(8,128)(2,1)S(1)}, u32[]{:S(2)}, u32[]{:S(2)}) collective-permute-start(bf16[2,120,640]{2,1,0:T(8,128)(2,1)S(1)} %add_convert_fusion), channel_id=1, source_target_pairs={{0,2},{1,3},{2,0},{3,1},{4,6},{5,7},{6,4},{7,5},{8,10},{9,11},{10,... | collective-permute-start | bytes 921608 | tf_op jit(solution)/shard_map/ppermute | solution.py:37
  205.0 14.8 %collective-permute-start.43 = (bf16[640,256]{1,0:T(8,128)(2,1)S(1)}, bf16[640,256]{1,0:T(8,128)(2,1)S(1)}, u32[]{:S(2)}, u32[]{:S(2)}) collective-permute-start(bf16[640,256]{1,0:T(8,128)(2,1)S(1)} %fusion.13), channel_id=1, source_target_pairs={{0,16},{8,24},{16,0},{24,8},{1,17},{9,25},{17,1},{25,9},{2,18},{10... | collective-permute-start | bytes 983048 | tf_op jit(solution)/shard_map/ppermute | solution.py:37
  226.9 26.0 %collective-permute-start.44 = (bf16[2,8,32,1920]{3,2,1,0:T(8,128)(2,1)}, bf16[2,8,32,1920]{3,2,1,0:T(8,128)(2,1)S(1)}, u32[]{:S(2)}, u32[]{:S(2)}) collective-permute-start(bf16[2,8,32,1920]{3,2,1,0:T(8,128)(2,1)} %get-tuple-element.310), channel_id=1, source_target_pairs={{0,8},{8,0},{16,24},{24,16},{1,9},{9,1},{17,25},{25,17},{2,10},{10... | collective-permute-start | bytes 5898248 | tf_op jit(solution)/shard_map/ppermute | solution.py:37
  227.0 17.3 %collective-permute-start.45 = (bf16[2,640,256]{2,1,0:T(8,128)(2,1)}, bf16[2,640,256]{2,1,0:T(8,128)(2,1)S(1)}, u32[]{:S(2)}, u32[]{:S(2)}) collective-permute-start(bf16[2,640,256]{2,1,0:T(8,128)(2,1)} %get-tuple-element.312), channel_id=1, source_target_pairs={{0,8},{8,0},{16,24},{24,16},{1,9},{9,1},{17,25},{25,17},{2,10},{10... | collective-permute-start | bytes 1966088 | tf_op jit(solution)/shard_map/ppermute | solution.py:37
  227.5 16.7 %collective-permute-start.46 = (bf16[1,120,640]{2,1,0:T(8,128)(2,1)S(1)}, bf16[1,120,640]{2,1,0:T(8,128)(2,1)S(1)}, u32[]{:S(2)}, u32[]{:S(2)}) collective-permute-start(bf16[1,120,640]{2,1,0:T(8,128)(2,1)S(1)} %get-tuple-element.376), channel_id=1, source_target_pairs={{0,4},{1,5},{2,6},{3,7},{4,0},{5,1},{6,2},{7,3},{8,12},{9,13},{10,... | collective-permute-start | bytes 460808 | tf_op jit(solution)/shard_map/ppermute | solution.py:37
  227.9 23.3 %collective-permute-start.47 = (bf16[1,120,640]{2,1,0:T(8,128)(2,1)}, bf16[1,120,640]{2,1,0:T(8,128)(2,1)S(1)}, u32[]{:S(2)}, u32[]{:S(2)}) collective-permute-start(bf16[1,120,640]{2,1,0:T(8,128)(2,1)} %add_convert_fusion.8), channel_id=1, source_target_pairs={{0,4},{1,5},{2,6},{3,7},{4,0},{5,1},{6,2},{7,3},{8,12},{9,13},{10,... | collective-permute-start | bytes 460808 | tf_op jit(solution)/shard_map/ppermute | solution.py:37
  230.4 20.7 %collective-permute-start.48 = (bf16[1,120,640]{2,1,0:T(8,128)(2,1)}, bf16[1,120,640]{2,1,0:T(8,128)(2,1)S(1)}, u32[]{:S(2)}, u32[]{:S(2)}) collective-permute-start(bf16[1,120,640]{2,1,0:T(8,128)(2,1)} %get-tuple-element.375), channel_id=1, source_target_pairs={{0,4},{1,5},{2,6},{3,7},{4,0},{5,1},{6,2},{7,3},{8,12},{9,13},{10,... | collective-permute-start | bytes 460808 | tf_op jit(solution)/shard_map/ppermute | solution.py:37
  244.3 18.8 %collective-permute-start.49 = (bf16[2,120,640]{2,1,0:T(8,128)(2,1)S(1)}, bf16[2,120,640]{2,1,0:T(8,128)(2,1)S(1)}, u32[]{:S(2)}, u32[]{:S(2)}) collective-permute-start(bf16[2,120,640]{2,1,0:T(8,128)(2,1)S(1)} %pad_maximum_fusion.5), channel_id=1, source_target_pairs={{0,2},{1,3},{2,0},{3,1},{4,6},{5,7},{6,4},{7,5},{8,10},{9,11},{10,... | collective-permute-start | bytes 921608 | tf_op jit(solution)/shard_map/ppermute | solution.py:37
  245.7 10.6 %collective-permute-start.50 = (bf16[640,256]{1,0:T(8,128)(2,1)S(1)}, bf16[640,256]{1,0:T(8,128)(2,1)S(1)}, u32[]{:S(2)}, u32[]{:S(2)}) collective-permute-start(bf16[640,256]{1,0:T(8,128)(2,1)S(1)} %fusion.12), channel_id=1, source_target_pairs={{0,16},{8,24},{16,0},{24,8},{1,17},{9,25},{17,1},{25,9},{2,18},{10... | collective-permute-start | bytes 983048 | tf_op jit(solution)/shard_map/ppermute | solution.py:37
  251.3 22.4 %collective-permute-start.53 = (bf16[1,120,640]{2,1,0:T(8,128)(2,1)S(1)}, bf16[1,120,640]{2,1,0:T(8,128)(2,1)S(1)}, u32[]{:S(2)}, u32[]{:S(2)}) collective-permute-start(bf16[1,120,640]{2,1,0:T(8,128)(2,1)S(1)} %add_convert_fusion.5), channel_id=1, source_target_pairs={{0,4},{1,5},{2,6},{3,7},{4,0},{5,1},{6,2},{7,3},{8,12},{9,13},{10,... | collective-permute-start | bytes 460808 | tf_op jit(solution)/shard_map/ppermute | solution.py:37
  253.3 23.1 %collective-permute-start.51 = (bf16[8,32,1920]{2,1,0:T(8,128)(2,1)S(1)}, bf16[8,32,1920]{2,1,0:T(8,128)(2,1)S(1)}, u32[]{:S(2)}, u32[]{:S(2)}) collective-permute-start(bf16[8,32,1920]{2,1,0:T(8,128)(2,1)S(1)} %fusion), channel_id=1, source_target_pairs={{0,16},{8,24},{16,0},{24,8},{1,17},{9,25},{17,1},{25,9},{2,18},{10... | collective-permute-start | bytes 2949128 | tf_op jit(solution)/shard_map/ppermute | solution.py:37
  261.9 11.8 %collective-permute-start.61 = (bf16[2,8,32,640]{3,2,1,0:T(8,128)(2,1)}, bf16[2,8,32,640]{3,2,1,0:T(8,128)(2,1)S(1)}, u32[]{:S(2)}, u32[]{:S(2)}) collective-permute-start(bf16[2,8,32,640]{3,2,1,0:T(8,128)(2,1)} %get-tuple-element.346), channel_id=1, source_target_pairs={{0,8},{8,0},{16,24},{24,16},{1,9},{9,1},{17,25},{25,17},{2,10},{10... | collective-permute-start | bytes 1966088 | tf_op jit(solution)/shard_map/ppermute | solution.py:37
  263.0 10.6 %collective-permute-start.57 = (bf16[1,120,640]{2,1,0:T(8,128)(2,1)S(1)}, bf16[1,120,640]{2,1,0:T(8,128)(2,1)S(1)}, u32[]{:S(2)}, u32[]{:S(2)}) collective-permute-start(bf16[1,120,640]{2,1,0:T(8,128)(2,1)S(1)} %add_convert_fusion.4), channel_id=1, source_target_pairs={{0,4},{1,5},{2,6},{3,7},{4,0},{5,1},{6,2},{7,3},{8,12},{9,13},{10,... | collective-permute-start | bytes 460808 | tf_op jit(solution)/shard_map/ppermute | solution.py:37
  263.2 29.0 %collective-permute-start.55 = (bf16[4,120,640]{2,1,0:T(8,128)(2,1)S(1)}, bf16[4,120,640]{2,1,0:T(8,128)(2,1)S(1)}, u32[]{:S(2)}, u32[]{:S(2)}) collective-permute-start(bf16[4,120,640]{2,1,0:T(8,128)(2,1)S(1)} %pad_maximum_fusion.1.even), channel_id=1, source_target_pairs={{0,1},{1,0},{2,3},{3,2},{4,5},{5,4},{6,7},{7,6},{8,9},{9,8},{10,11... | collective-permute-start | bytes 1843208 | tf_op jit(solution)/shard_map/ppermute | solution.py:37
  273.6 17.0 %collective-permute-start.73 = (f32[8,960]{1,0:T(8,128)}, f32[8,960]{1,0:T(8,128)S(1)}, u32[]{:S(2)}, u32[]{:S(2)}) collective-permute-start(f32[8,960]{1,0:T(8,128)} %get-tuple-element.362), channel_id=1, source_target_pairs={{0,8},{8,0},{16,24},{24,16},{1,9},{9,1},{17,25},{25,17},{2,10},{10... | collective-permute-start | bytes 92168 | tf_op jit(solution)/shard_map/ppermute | solution.py:37
  273.7 22.9 %collective-permute-start.58 = (bf16[2,120,640]{2,1,0:T(8,128)(2,1)S(1)}, bf16[2,120,640]{2,1,0:T(8,128)(2,1)S(1)}, u32[]{:S(2)}, u32[]{:S(2)}) collective-permute-start(bf16[2,120,640]{2,1,0:T(8,128)(2,1)S(1)} %pad_maximum_fusion.7), channel_id=1, source_target_pairs={{0,2},{1,3},{2,0},{3,1},{4,6},{5,7},{6,4},{7,5},{8,10},{9,11},{10,... | collective-permute-start | bytes 921608 | tf_op jit(solution)/shard_map/ppermute | solution.py:37
  273.8 16.2 %collective-permute-start.54 = (bf16[2,120,640]{2,1,0:T(8,128)(2,1)S(1)}, bf16[2,120,640]{2,1,0:T(8,128)(2,1)S(1)}, u32[]{:S(2)}, u32[]{:S(2)}) collective-permute-start(bf16[2,120,640]{2,1,0:T(8,128)(2,1)S(1)} %pad_maximum_fusion.6), channel_id=1, source_target_pairs={{0,2},{1,3},{2,0},{3,1},{4,6},{5,7},{6,4},{7,5},{8,10},{9,11},{10,... | collective-permute-start | bytes 921608 | tf_op jit(solution)/shard_map/ppermute | solution.py:37
  276.4 9.2 %collective-permute-start.62 = (bf16[8,32,640]{2,1,0:T(8,128)(2,1)S(1)}, bf16[8,32,640]{2,1,0:T(8,128)(2,1)S(1)}, u32[]{:S(2)}, u32[]{:S(2)}) collective-permute-start(bf16[8,32,640]{2,1,0:T(8,128)(2,1)S(1)} %fusion.11), channel_id=1, source_target_pairs={{0,16},{8,24},{16,0},{24,8},{1,17},{9,25},{17,1},{25,9},{2,18},{10... | collective-permute-start | bytes 983048 | tf_op jit(solution)/shard_map/ppermute | solution.py:37
  285.6 14.2 %collective-permute-start.52 = (bf16[4,32,1920]{2,1,0:T(8,128)(2,1)S(1)}, bf16[4,32,1920]{2,1,0:T(8,128)(2,1)S(1)}, u32[]{:S(2)}, u32[]{:S(2)}) collective-permute-start(bf16[4,32,1920]{2,1,0:T(8,128)(2,1)S(1)} %fusion.2), channel_id=1, source_target_pairs={{0,1},{1,0},{2,3},{3,2},{4,5},{5,4},{6,7},{7,6},{8,9},{9,8},{10,11... | collective-permute-start | bytes 1474568 | tf_op jit(solution)/shard_map/ppermute | solution.py:37
  290.0 29.0 %collective-permute-start.63 = (bf16[4,32,640]{2,1,0:T(8,128)(2,1)S(1)}, bf16[4,32,640]{2,1,0:T(8,128)(2,1)S(1)}, u32[]{:S(2)}, u32[]{:S(2)}) collective-permute-start(bf16[4,32,640]{2,1,0:T(8,128)(2,1)S(1)} %fusion.17), channel_id=1, source_target_pairs={{0,1},{1,0},{2,3},{3,2},{4,5},{5,4},{6,7},{7,6},{8,9},{9,8},{10,11... | collective-permute-start | bytes 491528 | tf_op jit(solution)/shard_map/ppermute | solution.py:37
  290.6 23.9 %collective-permute-start.59 = (bf16[4,120,640]{2,1,0:T(8,128)(2,1)S(1)}, bf16[4,120,640]{2,1,0:T(8,128)(2,1)S(1)}, u32[]{:S(2)}, u32[]{:S(2)}) collective-permute-start(bf16[4,120,640]{2,1,0:T(8,128)(2,1)S(1)} %pad_maximum_fusion.2.even), channel_id=1, source_target_pairs={{0,1},{1,0},{2,3},{3,2},{4,5},{5,4},{6,7},{7,6},{8,9},{9,8},{10,11... | collective-permute-start | bytes 1843208 | tf_op jit(solution)/shard_map/ppermute | solution.py:37
  296.7 25.8 %collective-permute-start.75 = (f32[8,960]{1,0:T(8,128)S(1)}, f32[8,960]{1,0:T(8,128)S(1)}, u32[]{:S(2)}, u32[]{:S(2)}) collective-permute-start(f32[8,960]{1,0:T(8,128)S(1)} %add.299), channel_id=1, source_target_pairs={{0,1},{1,0},{2,3},{3,2},{4,5},{5,4},{6,7},{7,6},{8,9},{9,8},{10,11... | collective-permute-start | bytes 92168 | tf_op jit(solution)/shard_map/ppermute | solution.py:37
  300.0 19.3 %collective-permute-start.56 = (bf16[2,32,1920]{2,1,0:T(8,128)(2,1)S(1)}, bf16[2,32,1920]{2,1,0:T(8,128)(2,1)S(1)}, u32[]{:S(2)}, u32[]{:S(2)}) collective-permute-start(bf16[2,32,1920]{2,1,0:T(8,128)(2,1)S(1)} %add_convert_fusion.3), channel_id=1, source_target_pairs={{0,2},{1,3},{2,0},{3,1},{4,6},{5,7},{6,4},{7,5},{8,10},{9,11},{10,... | collective-permute-start | bytes 737288 | tf_op jit(solution)/shard_map/ppermute | solution.py:37
  319.4 5.9 %collective-permute-start.60 = (bf16[1,32,1920]{2,1,0:T(8,128)(2,1)S(1)}, bf16[1,32,1920]{2,1,0:T(8,128)(2,1)S(1)}, u32[]{:S(2)}, u32[]{:S(2)}) collective-permute-start(bf16[1,32,1920]{2,1,0:T(8,128)(2,1)S(1)} %add_convert_fusion.11), channel_id=1, source_target_pairs={{0,4},{1,5},{2,6},{3,7},{4,0},{5,1},{6,2},{7,3},{8,12},{9,13},{10,... | collective-permute-start | bytes 368648 | tf_op jit(solution)/shard_map/ppermute | solution.py:37
  320.7 12.4 %collective-permute-start.66 = (bf16[4,120,640]{2,1,0:T(8,128)(2,1)S(1)}, bf16[4,120,640]{2,1,0:T(8,128)(2,1)S(1)}, u32[]{:S(2)}, u32[]{:S(2)}) collective-permute-start(bf16[4,120,640]{2,1,0:T(8,128)(2,1)S(1)} %pad_maximum_fusion.3.even), channel_id=1, source_target_pairs={{0,1},{1,0},{2,3},{3,2},{4,5},{5,4},{6,7},{7,6},{8,9},{9,8},{10,11... | collective-permute-start | bytes 1843208 | tf_op jit(solution)/shard_map/ppermute | solution.py:37
  323.7 17.0 %collective-permute-start.76 = (f32[8,960]{1,0:T(8,128)S(1)}, f32[8,960]{1,0:T(8,128)S(1)}, u32[]{:S(2)}, u32[]{:S(2)}) collective-permute-start(f32[8,960]{1,0:T(8,128)S(1)} %add.300), channel_id=1, source_target_pairs={{0,2},{1,3},{2,0},{3,1},{4,6},{5,7},{6,4},{7,5},{8,10},{9,11},{10,... | collective-permute-start | bytes 92168 | tf_op jit(solution)/shard_map/ppermute | solution.py:37
  325.4 12.1 %collective-permute-start.64 = (bf16[1,32,1920]{2,1,0:T(8,128)(2,1)S(1)}, bf16[1,32,1920]{2,1,0:T(8,128)(2,1)S(1)}, u32[]{:S(2)}, u32[]{:S(2)}) collective-permute-start(bf16[1,32,1920]{2,1,0:T(8,128)(2,1)S(1)} %add_convert_fusion.10), channel_id=1, source_target_pairs={{0,4},{1,5},{2,6},{3,7},{4,0},{5,1},{6,2},{7,3},{8,12},{9,13},{10,... | collective-permute-start | bytes 368648 | tf_op jit(solution)/shard_map/ppermute | solution.py:37
  326.5 16.8 %collective-permute-start.68 = (bf16[1,32,640]{2,1,0:T(8,128)(2,1)S(1)}, bf16[1,32,640]{2,1,0:T(8,128)(2,1)S(1)}, u32[]{:S(2)}, u32[]{:S(2)}) collective-permute-start(bf16[1,32,640]{2,1,0:T(8,128)(2,1)S(1)} %add_convert_fusion.14), channel_id=1, source_target_pairs={{0,4},{1,5},{2,6},{3,7},{4,0},{5,1},{6,2},{7,3},{8,12},{9,13},{10,... | collective-permute-start | bytes 122888 | tf_op jit(solution)/shard_map/ppermute | solution.py:37
  337.5 6.7 %collective-permute-start.67 = (bf16[2,32,1920]{2,1,0:T(8,128)(2,1)S(1)}, bf16[2,32,1920]{2,1,0:T(8,128)(2,1)S(1)}, u32[]{:S(2)}, u32[]{:S(2)}) collective-permute-start(bf16[2,32,1920]{2,1,0:T(8,128)(2,1)S(1)} %pad_maximum_fusion.8), channel_id=1, source_target_pairs={{0,2},{1,3},{2,0},{3,1},{4,6},{5,7},{6,4},{7,5},{8,10},{9,11},{10,... | collective-permute-start | bytes 737288 | tf_op jit(solution)/shard_map/ppermute | solution.py:37
  340.7 8.1 %collective-permute-start.77 = (f32[8,960]{1,0:T(8,128)S(1)}, f32[8,960]{1,0:T(8,128)S(1)}, u32[]{:S(2)}, u32[]{:S(2)}) collective-permute-start(f32[8,960]{1,0:T(8,128)S(1)} %add.301), channel_id=1, source_target_pairs={{0,4},{1,5},{2,6},{3,7},{4,0},{5,1},{6,2},{7,3},{8,12},{9,13},{10,... | collective-permute-start | bytes 92168 | tf_op jit(solution)/shard_map/ppermute | solution.py:37
  344.2 17.7 %collective-permute-start.69 = (bf16[4,32,1920]{2,1,0:T(8,128)(2,1)S(1)}, bf16[4,32,1920]{2,1,0:T(8,128)(2,1)S(1)}, u32[]{:S(2)}, u32[]{:S(2)}) collective-permute-start(bf16[4,32,1920]{2,1,0:T(8,128)(2,1)S(1)} %pad_maximum_fusion.4.even), channel_id=1, source_target_pairs={{0,1},{1,0},{2,3},{3,2},{4,5},{5,4},{6,7},{7,6},{8,9},{9,8},{10,11... | collective-permute-start | bytes 1474568 | tf_op jit(solution)/shard_map/ppermute | solution.py:37
  (109 other events, 951.7 us)

commit v5 on v4

--- a/solution.py
+++ b/solution.py
@@ -13,7 +13,7 @@
 GROUP = 4
 PARTS = 8
 GAIN_ROWS = 16
-RATE = 2.0e8
+RATE = 2.0e9
 SLOTS = (7, 3, 5, 1, 6, 2, 4, 0)
 
 
@@ -61,9 +61,9 @@
 
 
 class Terms:
-    def __init__(self, own, far, send):
+    def __init__(self, own, far, send, *others):
         self.own, self.far = own, far
-        self.beside = swap(send, "grp", GROUP, 1)
+        self.beside = swap(after(send, *others), "grp", GROUP, 1)
 
     def cross(self, *others):
         far, beside = after((self.far, self.beside), *others)
@@ -124,31 +124,7 @@
         return held, swap(held, "rep", self.ranks, 1)
 
 
-class SmallSum:
-    def __init__(self, values, ranks):
-        self.values = values
-        self.steps = [("grp", GROUP, 1), ("grp", GROUP, 2)]
-        mask = 1
-        while mask < ranks:
-            self.steps.append(("rep", ranks, mask))
-            mask *= 2
-        self.flight = None
-
-    def step(self, *others):
-        if self.flight is not None:
-            self.values = self.values + after(self.flight, *others)
-        if self.steps:
-            self.flight = swap(self.values, *self.steps.pop(0))
-        return self.values
-
-    def finish(self):
-        while self.steps:
-            self.step()
-        self.step()
-        return self.values
-
-
-def call(kernel, name, out_shape, *, grid=(1,), prefetch=0, in_specs, out_specs, scratch=(), micros=1, vmem=30):
+def call(kernel, name, out_shape, *, grid=(1,), prefetch=0, in_specs, out_specs, scratch=(), micros=1, vmem=36):
     def lies(shape):
         return pltpu.HBM(shape.shape, shape.dtype)
 
@@ -372,28 +348,46 @@
         so_ref[0] = out
 
 
-def weight_kernel(ranks, *refs):
+def weight_kernel(kinds, ranks, *refs):
     blocks = refs[0 : 2 * GROUP]
-    own, *others = refs[2 * GROUP : 2 * GROUP + 3]
-    outs = refs[2 * GROUP + 3 : 2 * GROUP + 7]
-    left, right, acc, sem = refs[2 * GROUP + 7 :]
+    rights = refs[2 * GROUP : 2 * GROUP + 3 * kinds]
+    outs = refs[2 * GROUP + 3 * kinds : 2 * GROUP + 3 * kinds + 4]
+    left, right, acc, sem = refs[2 * GROUP + 3 * kinds + 4 :]
     span = left.shape[2] // GROUP
-    copies = []
+    kind = pl.program_id(0)
+    lefts, loads = [], []
     for b, block in enumerate(blocks):
         s, k = divmod(b, GROUP)
-        copies.append(pltpu.make_async_copy(block, left.at[s, :, pl.ds(k * span, span)], sem.at[b]))
-    for s in range(2):
-        for i, (source, part) in enumerate(((own.at[s], slice(0, span)), (others[s], slice(span, GROUP * span)))):
-            copy = pltpu.make_async_copy(source, right.at[s, :, part], sem.at[2 * GROUP + 2 * s + i])
-            copies.insert(s * (GROUP + 2), copy)
-    for copy in copies:
-        copy.start()
-    for copy in copies[: GROUP + 2]:
-        copy.wait()
-    acc[...] = dot(left[0], right[0], NT)
-    for copy in copies[GROUP + 2 :]:
-        copy.wait()
-    acc[...] += dot(left[1], right[1], NT)
+        lefts.append(pltpu.make_async_copy(block, left.at[s, :, pl.ds(k * span, span)], sem.at[b]))
+    for n in range(kinds):
+        own, *others = rights[3 * n : 3 * n + 3]
+        for s in range(2):
+            for i, (source, part) in enumerate(((own.at[s], slice(0, span)), (others[s], slice(span, GROUP * span)))):
+                at = sem.at[2 * GROUP + 4 * n + 2 * s + i]
+                loads.append(pltpu.make_async_copy(source, right.at[n, s, :, part], at))
+
+    @pl.when(kind == 0)
+    def _():
+        for copy in loads[0:2] + lefts[:GROUP] + loads[2:4] + lefts[GROUP:] + loads[4:]:
+            copy.start()
+        for copy in loads[0:2] + lefts[:GROUP]:
+            copy.wait()
+
+    for n in range(1, kinds):
+
+        @pl.when(kind == n)
+        def _(n=n):
+            for copy in loads[4 * n : 4 * n + 4]:
+                copy.wait()
+
+    acc[...] = dot(left[0], right[kind, 0], NT)
+
+    @pl.when(kind == 0)
+    def _():
+        for copy in loads[2:4] + lefts[GROUP:]:
+            copy.wait()
+
+    acc[...] += dot(left[1], right[kind, 1], NT)
     part = acc.shape[0] // PARTS
     places = [(outs[0], i) for i in range(4)] + [(outs[1], 0), (outs[1], 1), (outs[2], 0), (outs[3], 0)]
     for (out, i), slot in zip(places, SLOTS):
@@ -401,7 +395,7 @@
         out[i] = acc[pl.ds(start, part), :].astype(LOW)
 
 
-def branch_kernel(ranks, mid_ref, cot_ref, e0, e1, e2, gain_ref, b0, b1, b2, b3, att_ref, gm_ref, gb_ref, do_ref, delta_ref, gain_out, w_ref):
+def branch_kernel(seq, ranks, mid_ref, cot_ref, e0, e1, e2, gain_ref, b0, b1, b2, b3, att_ref, gm_ref, gb_ref, do_ref, delta_ref, gain_out, w_ref):
     width, span = mid_ref.shape
     assemble(ranks[0], (b0, b1, b2, b3), w_ref)
     middle = mid_ref[...]
@@ -409,7 +403,7 @@
     inverse = lax.rsqrt(jnp.mean(middle * middle, axis=0, keepdims=True) + NORM_EPS)
     scaled = grad * gain_ref[:, 1:2].astype(FULL)
     turned = jnp.mean(scaled * middle, axis=0, keepdims=True)
-    grad_middle = cot_ref[0].astype(FULL) + inverse * scaled - middle * (inverse * inverse * inverse * turned)
+    grad_middle = cot_ref[seq].astype(FULL) + inverse * scaled - middle * (inverse * inverse * inverse * turned)
     gain_out[...] = dot(jnp.ones((8, span), LOW), (grad * middle * inverse).astype(LOW), NT)
     gm_ref[...] = grad_middle
     branch = grad_middle.astype(LOW)
@@ -467,13 +461,20 @@
     spread(ranks, acc, own_ref, far_ref, send_ref)
 
 
-def key_weight_kernel(ranks, norm_ref, a0, a1, a2, b0, b1, b2, cos_ref, sin_ref, own_ref, far_ref, send_ref, gkv_ref, acc):
+def key_weight_kernel(ranks, *refs):
+    norm_ref, *terms = refs[0:7]
+    cos_ref, sin_ref, part_ref, k0, k1, k2, k3, tok_ref, gm_a, gm_b, gain_a, gain_b = refs[7:19]
+    own_ref, far_ref, send_ref, out_ref, gkv_ref, wkv_ref, acc = refs[19:]
     width = norm_ref.shape[0]
-    span = a2.shape[1]
+    span = gm_a.shape[1]
     shard = width // GROUP
     kw2 = gkv_ref.shape[0]
     kw = kw2 // 2
-    for s, (e0, e1, e2) in enumerate(((a0, a1, a2), (b0, b1, b2))):
+    assemble(ranks[0], (k0, k1, k2, k3), wkv_ref)
+    gain_one = wkv_ref[:, kw2 : kw2 + 1].astype(FULL)
+    grad_gain = None
+    for s in range(2):
+        e0, e1, e2 = terms[3 * s : 3 * s + 3]
         part = slice(s * span, (s + 1) * span)
         grad = e0[...].astype(FULL) + e1[0].astype(FULL) + e2[...].astype(FULL)
         for h in range(kw // HD):
@@ -482,27 +483,6 @@
             gkv_ref[h * HD : h * HD + HD // 2, part] = one.astype(LOW)
             gkv_ref[h * HD + HD // 2 : (h + 1) * HD, part] = two.astype(LOW)
             gkv_ref[kw + h * HD : kw + (h + 1) * HD, part] = grad[top + HD : top + 2 * HD, :].astype(LOW)
-    for b in range(GROUP):
-        rows = slice(b * shard, (b + 1) * shard)
-        acc[b, 0:shard, :] = dot(norm_ref[rows, :], gkv_ref[...], NT)
-        acc[b, shard:, :] = jnp.zeros((acc.shape[1] - shard, kw2), FULL)
-    spread(ranks, acc, own_ref, far_ref, send_ref)
-
-
-def query_grad_kernel(ranks, gq_a, gq_b, q0, q1, q2, q3, out_ref, wq_ref):
-    assemble(ranks[0], (q0, q1, q2, q3), wq_ref)
-    out_ref[0] = dot(wq_ref[...], gq_a[...])
-    out_ref[1] = dot(wq_ref[...], gq_b[...])
-
-
-def input_grad_kernel(ranks, part_ref, gkv_ref, k0, k1, k2, k3, tok_ref, gm_a, gm_b, gain_a, gain_b, out_ref, gain_out, wkv_ref):
-    span = gm_a.shape[1]
-    kw2 = gkv_ref.shape[0]
-    assemble(ranks[0], (k0, k1, k2, k3), wkv_ref)
-    gain_one = wkv_ref[:, kw2 : kw2 + 1].astype(FULL)
-    total = None
-    for s in range(2):
-        part = slice(s * span, (s + 1) * span)
         grad_norm = part_ref[s] + dot(wkv_ref[:, 0:kw2], gkv_ref[:, part])
         x = tok_ref[s].astype(FULL)
         inverse = lax.rsqrt(jnp.mean(x * x, axis=0, keepdims=True) + NORM_EPS)
@@ -510,10 +490,20 @@
         turned = jnp.mean(scaled * x, axis=0, keepdims=True)
         out_ref[s] = (gm_a, gm_b)[s][...] + inverse * scaled - x * (inverse * inverse * inverse * turned)
         row = dot(jnp.ones((8, span), LOW), (grad_norm * x * inverse).astype(LOW), NT)
-        total = row if total is None else total + row
-    gain_out[0:1, :] = total[0:1, :]
-    gain_out[1:2, :] = gain_a[0:1, :] + gain_b[0:1, :]
-    gain_out[2:8, :] = total[2:8, :]
+        grad_gain = row if grad_gain is None else grad_gain + row
+    gains = jnp.concatenate([grad_gain[0:1, :], gain_a[0:1, :] + gain_b[0:1, :], jnp.zeros((6, width), FULL)], axis=0)
+    for b in range(GROUP):
+        rows = slice(b * shard, (b + 1) * shard)
+        acc[b, 0:shard, :] = dot(norm_ref[rows, :], gkv_ref[...], NT)
+        acc[b, shard:, :] = jnp.zeros((acc.shape[1] - shard, kw2), FULL)
+        acc[b, shard : shard + 8, 0:shard] = gains[:, rows]
+    spread(ranks, acc, own_ref, far_ref, send_ref)
+
+
+def query_grad_kernel(ranks, gq_a, gq_b, q0, q1, q2, q3, out_ref, wq_ref):
+    assemble(ranks[0], (q0, q1, q2, q3), wq_ref)
+    out_ref[0] = dot(wq_ref[...], gq_a[...])
+    out_ref[1] = dot(wq_ref[...], gq_b[...])
 
 
 def place(slot):
@@ -533,22 +523,22 @@
                     pair[2][a * part : (a + 1) * part, :] = pair[parity][index].astype(FULL)
 
 
-def forward_weights_kernel(ranks, even, odd, out_ref):
-    gathered(ranks, [(even, odd, out_ref)])
-
-
-def query_done_kernel(ranks, even, odd, q_ref, o_ref, scratch):
+def forward_weights_kernel(ranks, even, odd, *outs):
+    columns = outs[0].shape[1]
+    for i, out in enumerate(outs):
+        part = slice(i * columns, (i + 1) * columns)
+        gathered(ranks, [(even.at[:, :, part], odd.at[:, :, part], out)])
+
+
+def attention_done_kernel(ranks, even, odd, q_ref, o_ref, k_ref, v_ref, gain_ref, scratch):
     shard, width = q_ref.shape
+    kw = k_ref.shape[0]
     gathered(ranks, [(even, odd, scratch)])
     q_ref[...] = scratch[0:shard, 0:width]
-    o_ref[...] = scratch[0:shard, width:]
-
-
-def key_done_kernel(ranks, even, odd, k_ref, v_ref, scratch):
-    kw, shard = k_ref.shape
-    gathered(ranks, [(even, odd, scratch)])
-    k_ref[...] = scratch[0:shard, 0:kw].T
-    v_ref[...] = scratch[0:shard, kw:].T
+    o_ref[...] = scratch[0:shard, width : 2 * width]
+    k_ref[...] = scratch[0:shard, 2 * width : 2 * width + kw].T
+    v_ref[...] = scratch[0:shard, 2 * width + kw :].T
+    gain_ref[...] = scratch[shard : shard + 8, 2 * width : 2 * width + shard]
 
 
 def tables(places):
@@ -611,18 +601,6 @@
     own_span = lax.dynamic_slice(span_order, (0, rank_grp), (seq_count, 1))
     places = own_span * span + jnp.arange(span, dtype=jnp.int32)[None, :]
     cos_cols, sin_cols = tables(places)
-    kv_blocks = kv_flight.finish()
-    norm_low, kv_a, kv_b, gain_cols = call(
-        keys_values_kernel,
-        "keys_values",
-        (shape_of((width, rows)), shape_of((kw2, span)), shape_of((kw2, span)), shape_of((width, LANES))),
-        prefetch=1,
-        in_specs=[seqs] + [whole(kv_shard.shape)] * 4 + [table, table],
-        out_specs=(whole((width, rows)), whole((kw2, span)), whole((kw2, span)), gain_spec),
-        scratch=[pltpu.VMEM((width, kw2 + LANES), LOW)],
-        micros=4.3,
-    )(place_of, tok_t, *kv_blocks, cos_cols, sin_cols)
-    kv_flight = [Blocks(kv_a), None]
     wgut, wgu = call(
         flip_two_kernel,
         "flip_two",
@@ -630,8 +608,7 @@
         in_specs=[whole((width, ff))] * 2,
         out_specs=(whole((2 * ff, width)), whole((width, 2 * ff))),
         micros=4,
-    )(after(w_gate, norm_low), w_up)
-    q_flight.arrive(wgut)
+    )(after(w_gate, kv_flight.sent), w_up)
     wd = call(
         flip_one_kernel,
         "flip_one",
@@ -639,8 +616,20 @@
         in_specs=[whole((width, ff))],
         out_specs=whole((ff, width)),
         micros=2,
-    )(after(wd_t, *q_flight.ready))
-    q_blocks = q_flight.finish(wd)
+    )(after(wd_t, wgut))
+    kv_blocks = kv_flight.finish(wd)
+    norm_low, kv_a, kv_b, gain_cols = call(
+        keys_values_kernel,
+        "keys_values",
+        (shape_of((width, rows)), shape_of((kw2, span)), shape_of((kw2, span)), shape_of((width, LANES))),
+        prefetch=1,
+        in_specs=[NEAR] + [whole(kv_shard.shape)] * 4 + [table, table],
+        out_specs=(whole((width, rows)), whole((kw2, span)), whole((kw2, span)), gain_spec),
+        scratch=[pltpu.VMEM((width, kw2 + LANES), LOW)],
+        micros=4.3,
+    )(place_of, tok_t, *kv_blocks, cos_cols, sin_cols)
+    kv_flight = [Blocks(kv_a), None]
+    q_blocks = q_flight.finish(norm_low)
     queries = call(
         queries_kernel,
         "queries",
@@ -652,8 +641,8 @@
         micros=4.9,
     )(place_of, norm_low, *q_blocks, cos_cols, sin_cols)
 
-    o_flight = Blocks(w_out, wgut)
-    kv_flight[1] = Blocks(kv_b, o_flight.sent, wgut)
+    o_flight = Blocks(w_out, kv_a)
+    kv_flight[1] = Blocks(kv_b, *q_blocks)
     cot_flight = [Blocks(cot_t[0], queries), None]
     cot_blocks = [None, None]
     kv_all = [kv_flight[0].finish(queries), None]
@@ -747,40 +736,40 @@
 
     part = width // PARTS
 
-    def sums(name, blocks, rights, *others):
+    def sums(name, blocks, kinds, *others):
+        count = len(kinds)
+        columns = count * ff
         pieces = call(
-            weight_kernel,
+            functools.partial(weight_kernel, count),
             name,
-            tuple(shape_of((n, part, ff)) for n in (4, 2, 1, 1)),
+            tuple(shape_of((n, part, columns)) for n in (4, 2, 1, 1)),
             prefetch=1,
-            in_specs=[ANY] * (2 * GROUP + 3),
-            out_specs=tuple(whole((n, part, ff)) for n in (4, 2, 1, 1)),
+            grid=(count,),
+            in_specs=[ANY] * (2 * GROUP + 3 * count),
+            out_specs=tuple(pl.BlockSpec((n, part, ff), lambda m, *_: (0, 0, m)) for n in (4, 2, 1, 1)),
             scratch=[
                 pltpu.VMEM((2, width, length), LOW),
-                pltpu.VMEM((2, ff, length), LOW),
+                pltpu.VMEM((count, 2, ff, length), LOW),
                 pltpu.VMEM((width, ff), FULL),
-                pltpu.SemaphoreType.DMA((2 * GROUP + 4,)),
+                pltpu.SemaphoreType.DMA((2 * GROUP + 4 * count,)),
             ],
-            micros=8,
-        )(place_of, after(blocks[0], *others), *blocks[1:], *rights)
+            micros=2 + 6 * count,
+        )(place_of, after(blocks[0], *others), *blocks[1:], *sum(kinds, ()))
         return RepSum(pieces, ranks)
 
     x_all = x_blocks[0] + x_blocks[1]
-    down_sum = sums("down_weights", cot_blocks[0] + cot_blocks[1], (own_hid, hid_a, hid_b), *stage)
+    down_sum = sums("down_weights", cot_blocks[0] + cot_blocks[1], [(own_hid, hid_a, hid_b)], *stage)
     done = down_sum.pieces[0]
     stage = (grad_b.cross(done), out_b.beside, done)
-    gate_sum = sums("gate_weights", x_all, (own_gg, gg_a, gg_b), *stage)
-    done = gate_sum.pieces[0]
-    stage = (grad_a.across, out_b.cross(done), done)
-    up_sum = sums("up_weights", x_all, (own_gu, gu_a, gu_b), *stage)
+    up_sum = sums("gate_up_weights", x_all, [(own_gg, gg_a, gg_b), (own_gu, gu_a, gu_b)], *stage)
     done = up_sum.pieces[0]
-    stage = (down_sum.second(done), out_a.across, done)
-
-    def branch_of(s, middle):
+    stage = (grad_a.across, out_b.cross(done), down_sum.second(done), out_a.across, done)
+
+    def branch_of(s, *others):
         _, beside_term, across_term = grads[s].all()
         first = whole((1, width, span))
         return call(
-            branch_kernel,
+            functools.partial(branch_kernel, s),
             "branch",
             (
                 shape_of((width, span), FULL),
@@ -790,11 +779,11 @@
                 shape_of((8, width), FULL),
             ),
             prefetch=1,
-            in_specs=[act, one_seq(s), one_seq(s), first, act, gain_spec] + [whole((shard, width))] * 4 + [act],
+            in_specs=[NEAR, NEAR, one_seq(s), first, act, NEAR] + [NEAR] * 5,
             out_specs=(act, act, act, whole((16, span)), whole((8, width))),
             scratch=[pltpu.VMEM((width, width), LOW)],
             micros=4,
-        )(place_of, middle, cot_t, own_grad, beside_term, across_term, gain_cols, *o_blocks, attended[s])
+        )(place_of, middles[s], cot_t, own_grad, beside_term, after(across_term, *others), gain_cols, *o_blocks, attended[s])
 
     def attend_back_of(s, out_grad, delta):
         halves = pl.BlockSpec((2, 2 * HD, span), lambda h, *_: (0, h, 0))
@@ -809,13 +798,14 @@
         )(queries, *kv_all[s], stats[s], out_grad, delta, cos_cols, sin_cols)
         return grad_q, Terms(*kv_parts)
 
-    mid_a, branch_a, dout_a, delta_a, gain_a = branch_of(0, after(middles[0], *stage))
-    gq_a, kv_grad_a = attend_back_of(0, after(dout_a, grad_b.across), delta_a)
-    stage = (out_b.across, gate_sum.second(gq_a), down_sum.third(gq_a))
-    mid_b, branch_b, dout_b, delta_b, gain_b = branch_of(1, after(middles[1], *stage))
+    mid_a, branch_a, dout_a, delta_a, gain_a = branch_of(0, *stage)
+    stage = (down_sum.third(branch_a), grad_b.across)
+    gq_a, kv_grad_a = attend_back_of(0, after(dout_a, *stage), delta_a)
+    stage = (out_b.across, down_sum.own(gq_a))
+    mid_b, branch_b, dout_b, delta_b, gain_b = branch_of(1, *stage)
     stage = (kv_grad_a.cross(branch_b), up_sum.second(branch_b))
     gq_b, kv_grad_b = attend_back_of(1, after(dout_b, *stage), delta_b)
-    stage = (gate_sum.third(gq_b), down_sum.own(gq_b), up_sum.third(gq_b), kv_grad_a.across)
+    stage = (down_sum.spread(gq_b), kv_grad_a.across)
 
     grown = shard + GAIN_ROWS
     piece = grown // PARTS
@@ -826,66 +816,65 @@
         "query_weights",
         spread_out(2 * width),
         prefetch=1,
-        in_specs=[whole((width, rows))] + [act] * 6,
+        in_specs=[NEAR, NEAR, act] + [NEAR] * 4,
         out_specs=spread_spec(2 * width),
         scratch=[pltpu.VMEM((GROUP, grown, 2 * width), FULL)],
         micros=8,
-    )(place_of, norm_low, after(gq_a, *stage), gq_b, *attended, branch_a, branch_b)
+    )(place_of, norm_low, gq_a, after(gq_b, *stage), *attended, branch_a, branch_b)
     done = query_parts[0]
-    query_terms = Terms(*query_parts)
-    stage = (kv_grad_b.cross(done), down_sum.spread(done))
+    stage = (kv_grad_b.cross(done), up_sum.third(done))
+    query_terms = Terms(*query_parts, *stage)
     grad_part = call(
         query_grad_kernel,
         "query_grad",
         shape_of((seq_count, width, span), FULL),
         prefetch=1,
-        in_specs=[act, act] + [whole((shard, width))] * 4,
+        in_specs=[NEAR, act] + [NEAR] * 4,
         out_specs=seqs,
         scratch=[pltpu.VMEM((width, width), LOW)],
         micros=4,
-    )(place_of, after(gq_a, *stage), gq_b, *q_blocks)
-    stage = (query_terms.cross(grad_part), gate_sum.own(grad_part), up_sum.own(grad_part))
+    )(place_of, gq_a, after(gq_b, *stage), *q_blocks)
+    stage = (query_terms.cross(grad_part),)
+    down_pair = down_sum.done(grad_part)
     block_out = jnp.stack(
         [middle + three(term.all()) for middle, term in zip(after(middles, *stage), (out_a, out_b))]
     )
+    stage = (*stage, block_out, down_pair[0], kv_grad_b.across)
 
     def owned(terms):
         own, beside_term, across = terms.all()
         cuts = (slice(0, 4), slice(4, 6), slice(6, 7), slice(7, 8))
-        return [three((own[c], beside_term[:, c], across[c])).astype(LOW) for c in cuts]
+        return [three((own[c], beside_term[:, c], across[c])) for c in cuts]
 
     first = whole((1, kw2, span))
     terms = []
     for term in (kv_grad_a, kv_grad_b):
         terms += term.all()
-    *key_parts, gkv = call(
+    *key_parts, grad_tokens = call(
         key_weight_kernel,
         "key_weights",
-        spread_out(kw2) + (shape_of((kw2, rows)),),
+        spread_out(kw2) + (shape_of((seq_count, width, span), FULL),),
         prefetch=1,
-        in_specs=[whole((width, rows))] + [whole((kw2, span)), first, whole((kw2, span))] * 2 + [table, table],
-        out_specs=spread_spec(kw2) + (whole((kw2, rows)),),
-        scratch=[pltpu.VMEM((GROUP, grown, kw2), FULL)],
-        micros=4,
-    )(place_of, after(norm_low, block_out), *terms, cos_cols, sin_cols)
-    key_terms = Terms(*key_parts)
-    down_pair = down_sum.done(gkv)
-    grad_tokens, gain_part = call(
-        input_grad_kernel,
-        "input_grad",
-        (shape_of((seq_count, width, span), FULL), shape_of((8, width), FULL)),
-        prefetch=1,
-        in_specs=[seqs, whole((kw2, rows))]
-        + [whole(kv_shard.shape)] * 4
-        + [seqs, act, act]
+        in_specs=[NEAR]
+        + [whole((kw2, span)), first, whole((kw2, span))] * 2
+        + [table, table, seqs]
+        + [NEAR] * 7
         + [whole((8, width))] * 2,
-        out_specs=(seqs, whole((8, width))),
-        scratch=[pltpu.VMEM((width, kw2 + LANES), LOW)],
-        micros=6,
+        out_specs=spread_spec(kw2) + (seqs,),
+        scratch=[
+            pltpu.VMEM((kw2, rows), LOW),
+            pltpu.VMEM((width, kw2 + LANES), LOW),
+            pltpu.VMEM((GROUP, grown, kw2), FULL),
+        ],
+        micros=10,
     )(
         place_of,
-        after(grad_part, down_pair[0]),
-        gkv,
+        norm_low,
+        after(terms[0], *stage),
+        *terms[1:],
+        cos_cols,
+        sin_cols,
+        grad_part,
         *kv_blocks,
         tok_t,
         mid_a,
@@ -893,62 +882,48 @@
         gain_a,
         gain_b,
     )
-    small = SmallSum(gain_part, ranks)
-    stage = (key_terms.cross(grad_tokens), gate_sum.spread(grad_tokens), up_sum.spread(grad_tokens))
-    small.step()
-    query_sum = RepSum(owned(query_terms), ranks)
-    done = query_sum.pieces[0]
-    gate_pair = gate_sum.done(done)
-    small.step(done)
-
-    def finished(name, pair, *others):
+    stage = (up_sum.own(grad_tokens), down_pair[1])
+    key_terms = Terms(*key_parts, *stage)
+
+    def finished(name, kernel, pair, outs, *others):
+        columns = pair[0].shape[2]
         return call(
-            forward_weights_kernel,
+            kernel,
             name,
-            shape_of((width, ff), FULL),
+            (shape_of((width, ff), FULL),) * outs,
             prefetch=1,
-            in_specs=[whole((4, part, ff))] * 2,
-            out_specs=whole((width, ff)),
-            micros=3.5,
+            in_specs=[whole((4, part, columns))] * 2,
+            out_specs=(whole((width, ff)),) * outs,
+            micros=3.5 * outs,
         )(place_of, after(pair[0], *others), pair[1])
 
-    grad_down = finished("down_done", down_pair, gate_pair[0])
-    key_sum = RepSum(owned(key_terms), ranks)
-    stage = (query_sum.second(grad_down), up_sum.done(grad_down), small.step(grad_down))
-    up_pair = stage[1]
-    grad_gate = finished("gate_done", gate_pair, stage[0], up_pair[0])
-    stage = (key_sum.second(grad_gate), query_sum.third(grad_gate))
-    small.step(*stage)
-    stage = (key_sum.third(*stage), query_sum.own(*stage))
-    small.step(*stage)
-    grad_up = finished("up_done", up_pair, *stage)
-    stage = (key_sum.own(grad_up), query_sum.spread(grad_up))
-    query_pair = query_sum.done(*stage)
-    key_sum.spread(query_pair[0])
-    key_pair = key_sum.done()
-    grad_gains = small.finish()
+    (grad_down,) = finished("down_done", forward_weights_kernel, down_pair, 1, *stage)
+    key_terms.cross(grad_down)
+    pieces = []
+    for query_piece, key_piece in zip(owned(query_terms), owned(key_terms)):
+        joint = jnp.concatenate([query_piece, key_piece], axis=-1)
+        pieces.append(joint.astype(LOW))
+    query_sum = RepSum(pieces, ranks)
+
+    up_sum.spread(*pieces)
+    step = query_sum.second()
+    up_pair = up_sum.done(step)
+    step = query_sum.third(step)
+    step = query_sum.own(step)
+    step = query_sum.spread(step, up_pair[1])
+    grad_gate, grad_up = finished("gate_up_done", forward_weights_kernel, up_pair, 2, step)
+    query_pair = query_sum.done(grad_up)
     grad_down = grad_down.T
-    grad_query, grad_out = call(
-        query_done_kernel,
-        "query_done",
-        (shape_of((shard, width), FULL),) * 2,
+    grad_query, grad_out, grad_key, grad_value, grad_gains = call(
+        attention_done_kernel,
+        "attention_done",
+        (shape_of((shard, width), FULL),) * 2 + (shape_of((kw, shard), FULL),) * 2 + (shape_of((8, shard), FULL),),
         prefetch=1,
-        in_specs=[whole((4, piece, 2 * width))] * 2,
-        out_specs=(whole((shard, width)),) * 2,
-        scratch=[pltpu.VMEM((grown, 2 * width), FULL)],
-        micros=3,
+        in_specs=[whole((4, piece, 2 * width + kw2))] * 2,
+        out_specs=(whole((shard, width)),) * 2 + (whole((kw, shard)),) * 2 + (whole((8, shard)),),
+        scratch=[pltpu.VMEM((grown, 2 * width + kw2), FULL)],
+        micros=5,
     )(place_of, *query_pair)
-    grad_key, grad_value = call(
-        key_done_kernel,
-        "key_done",
-        (shape_of((kw, shard), FULL),) * 2,
-        prefetch=1,
-        in_specs=[whole((4, piece, kw2))] * 2,
-        out_specs=(whole((kw, shard)),) * 2,
-        scratch=[pltpu.VMEM((grown, kw2), FULL)],
-        micros=2,
-    )(place_of, *key_pair)
-    own_gains = lax.dynamic_slice(grad_gains, (0, rank_grp * shard), (2, shard))
     return (
         jnp.swapaxes(block_out, 1, 2),
         jnp.swapaxes(grad_tokens, 1, 2),
@@ -959,8 +934,8 @@
         grad_gate,
         grad_up,
         grad_down,
-        own_gains[0],
-        own_gains[1],
+        grad_gains[0],
+        grad_gains[1],
     )
 
 

time: 366 us -> 323 us (0.88); the launches traced: 366 us -> 318 us
  Pallas kernels: 194 us -> 166 us
  starting transfers between devices: 60.5 us -> 45.9 us
  other arithmetic: 10.9 us -> 6.79 us
    pallas_call x28 -> x24, Pallas kernels: 194 us -> 166 us  [placed(): return run(*args[:prefetch], *rest)]
    ppermute x78 -> x61, starting transfers between devices: 60.5 us -> 45.9 us  [swap(): return lax.ppermute(values, axis, [(i, i ^ mask) for i in range(count)])]
    unnamed x190 -> x204, local copies, waits for them, and re-layouts: 13.2 us -> 9.52 us
    ppermute x78 -> x61, waiting for transfers between devices: 84.2 us -> 84.6 us  [swap(): return lax.ppermute(values, axis, [(i, i ^ mask) for i in range(count)])]
  transfers between devices with their start and end apart: 78 -> 61, of which waited for: 22 -> 21; matrix products, arithmetic and copies ran while one was open for 3% -> 2% of each run, Pallas kernels for 49% -> 50%
where the time goes in v5:
time: 323 us; the launch traced here: 318 us
  Pallas kernels  166 us (51%)
  waiting for transfers between devices  84.6 us (26%)
  starting transfers between devices  45.9 us (14%)
  local copies, waits for them, and re-layouts  12.2 us (4%)
  other arithmetic  6.79 us (2%)
    pallas_call x24, Pallas kernels, placed(): return run(*args[:prefetch], *rest)  166 us
    ppermute x61, waiting for transfers between devices, swap(): return lax.ppermute(values, axis, [(i, i ^ mask) for i in range(count)])  84.6 us
    ppermute x61, starting transfers between devices, swap(): return lax.ppermute(values, axis, [(i, i ^ mask) for i in range(count)])  45.9 us
    unnamed x204, local copies, waits for them, and re-layouts  9.52 us
  transfers between devices with their start and end apart: 61, of which 21 were waited for; matrix products, arithmetic and copies ran while one was open for 2% of the time, Pallas kernels for 50%

profile of v5, /device:TPU:0, one launch (start us, length us, event | category | flops | bytes accessed | tf_op | source)
XLA Modules:
  0.0 317.8 jit_solution(4007325276662220791)
XLA Ops:
  2.6 2.1 pack.1.b0.refs_10_
  4.7 3.0 collective-permute-start
  7.9 4.8 %flip_two.1 = (bf16[1280,960]{1,0:T(8,128)(2,1)}, bf16[960,1280]{1,0:T(8,128)(2,1)}) custom-call(bf16[960,640]{1,0:T(8,128)(2,1)} %wg_ref, bf16[960,640]{1,0:T(8,128)(2,1)} %wu_ref.1), custom_call_target="tpu_custom_call" | custom-call | flops 8000000000 | bytes 1024 | tf_op jit(solution)/shard_map/flip_two/pallas_call | solution.py:152
  12.7 2.9 flip_one.1.wd_ref.refs_9_
  15.6 1.7 collective-permute-done.b2.refs_12_
  17.9 1.0 multiply_sine_fusion
  20.2 4.0 %keys_values.1 = (bf16[960,512]{1,0:T(8,128)(2,1)}, bf16[640,256]{1,0:T(8,128)(2,1)}, bf16[640,256]{1,0:T(8,128)(2,1)}, bf16[960,128]{1,0:T(8,128)(2,1)}) custom-call(s32[2]{0:T(128)S(1)} %pad_add_fusion.ranks, bf16[2,960,256]{2,1,0:T(8,128)(2,1)S(1)} %bitcast.109, bf16[240,768]{1,0:T(8,128)(2,1)} %pack.1.b0.refs_10_, bf16[240,768]{1,0:T(8,128)(2,1)} %copy-done.28, ...), custom_call_target="tpu_custom_call" | custom-call | flops 8600000512 | bytes 1024 | tf_op jit(solution)/shard_map/keys_values/pallas_call | solution.py:152
  24.3 2.7 collective-permute-done.3.b2.q2
  27.5 1.8 collective-permute-start.6
  30.9 4.9 %queries.1.q_ref = bf16[960,512]{1,0:T(8,128)(2,1)} custom-call(s32[2]{0:T(128)S(1)} %pad_add_fusion.ranks, bf16[960,512]{1,0:T(8,128)(2,1)} %get-tuple-element.182.norm_ref.refs_0_, bf16[240,960]{1,0:T(8,128)(2,1)} %q0.1, bf16[240,960]{1,0:T(8,128)(2,1)} %copy-done.14, bf16[240,960]{1,0:T(8,128)(2,1)} %copy-done.12, bf16[240,960]{1,0:T(8,128)(2,1)} %copy-done.16, ...), custom_call_target="tpu_custom_call" | custom-call | flops 9799999488 | bytes 1024 | tf_op jit(solution)/shard_map/queries/pallas_call | solution.py:152
  35.8 1.6 collective-permute-done.6.b2
  37.9 1.7 collective-permute-start.9
  41.4 11.3 %attend.2 = (bf16[5,1024,768]{2,1,0:T(8,128)(2,1)}, bf16[960,256]{1,0:T(8,128)(2,1)}) custom-call(s32[2]{0:T(128)S(1)} %pad_add_fusion.ranks, s32[2,4]{1,0:T(2,128)S(1)} %copy-done.4, s32[2,2]{1,0:T(2,128)S(1)} %copy-done.32, bf16[960,512]{1,0:T(8,128)(2,1)} %queries.1.q_ref, bf16[640,256]{1,0:T(8,128)(2,1)} %get-tuple-element.189.b0, ...), custom_call_target="tpu_custom_call" | custom-call | flops 20000000000 | bytes 1024 | tf_op jit(solution)/shard_map/attend/pallas_call | solution.py:152
  53.3 4.8 %collective-permute-done.12.b2 = bf16[640,256]{1,0:T(8,128)(2,1)S(1)} collective-permute-done((bf16[640,256]{1,0:T(8,128)(2,1)S(1)}, bf16[640,256]{1,0:T(8,128)(2,1)S(1)}, u32[]{:S(2)}, u32[]{:S(2)}) %collective-permute-start.12) | collective-permute-done | bytes 327712 | tf_op jit(solution)/shard_map/ppermute | solution.py:37
  58.7 1.8 collective-permute-start.15
  61.6 4.4 %middle.2 = (f32[960,256]{1,0:T(8,128)}, bf16[960,256]{1,0:T(8,128)(2,1)}) custom-call(s32[2]{0:T(128)S(1)} %pad_add_fusion.ranks, bf16[960,256]{1,0:T(8,128)(2,1)} %get-tuple-element.193.att_ref.att_a, bf16[240,960]{1,0:T(8,128)(2,1)} %b0.9, bf16[240,960]{1,0:T(8,128)(2,1)} %copy-done.20, bf16[240,960]{1,0:T(8,128)(2,1)} %copy-done.18, ...), custom_call_target="tpu_custom_call" | custom-call | flops 6000000000 | bytes 1024 | tf_op jit(solution)/shard_map/middle/pallas_call | solution.py:152
  66.0 1.5 collective-permute-start.16
  67.5 11.1 %attend.3 = (bf16[5,1024,768]{2,1,0:T(8,128)(2,1)}, bf16[960,256]{1,0:T(8,128)(2,1)}) custom-call(s32[2]{0:T(128)S(1)} %pad_add_fusion.ranks, s32[2,4]{1,0:T(2,128)S(1)} %copy-done.4, s32[2,2]{1,0:T(2,128)S(1)} %copy-done.32, bf16[960,512]{1,0:T(8,128)(2,1)} %queries.1.q_ref, bf16[640,256]{1,0:T(8,128)(2,1)} %get-tuple-element.205.b0, ...), custom_call_target="tpu_custom_call" | custom-call | flops 20000000000 | bytes 1024 | tf_op jit(solution)/shard_map/attend/pallas_call | solution.py:152
  79.9 5.0 %middle.3 = (f32[960,256]{1,0:T(8,128)}, bf16[960,256]{1,0:T(8,128)(2,1)}) custom-call(s32[2]{0:T(128)S(1)} %pad_add_fusion.ranks, bf16[960,256]{1,0:T(8,128)(2,1)} %get-tuple-element.213.att_ref.att_b, bf16[240,960]{1,0:T(8,128)(2,1)} %b0.9, bf16[240,960]{1,0:T(8,128)(2,1)} %copy-done.20, bf16[240,960]{1,0:T(8,128)(2,1)} %copy-done.18, ...), custom_call_target="tpu_custom_call" | custom-call | flops 6000000000 | bytes 1024 | tf_op jit(solution)/shard_map/middle/pallas_call | solution.py:152
  84.9 1.2 collective-permute-start.23
  86.7 8.1 %own_blocks.1 = (bf16[2,960,256]{2,1,0:T(8,128)(2,1)}, bf16[2,960,256]{2,1,0:T(8,128)(2,1)}, bf16[2,640,256]{2,1,0:T(8,128)(2,1)}, bf16[2,640,256]{2,1,0:T(8,128)(2,1)}, bf16[2,640,256]{2,1,0:T(8,128)(2,1)}) custom-call(bf16[960,256]{1,0:T(8,128)(2,1)} %get-tuple-element.255.x_a.refs_0_, bf16[960,256]{1,0:T(8,128)(2,1)} %get-tuple-element.233.x_b.refs_4_, ...), custom_call_target="tpu_custom_call" | custom-call | flops 16000000000 | bytes 1024 | tf_op jit(solution)/shard_map/own_blocks/pallas_call | solution.py:152
  97.1 12.2 %other_blocks.2 = (bf16[960,256]{1,0:T(8,128)(2,1)}, bf16[2,960,256]{2,1,0:T(8,128)(2,1)}, bf16[960,256]{1,0:T(8,128)(2,1)}, bf16[2,960,256]{2,1,0:T(8,128)(2,1)...) custom-call(bf16[960,256]{1,0:T(8,128)(2,1)} %copy-done.81, ...), custom_call_target="tpu_custom_call" | custom-call | flops 24000000000 | bytes 1024 | tf_op jit(solution)/shard_map/other_blocks/pallas_call | solution.py:152
  111.3 1.4 collective-permute-done.25.refs_2_.refs_7_
  113.5 11.9 %other_blocks.3 = (bf16[960,256]{1,0:T(8,128)(2,1)}, bf16[2,960,256]{2,1,0:T(8,128)(2,1)}, bf16[960,256]{1,0:T(8,128)(2,1)}, bf16[2,960,256]{2,1,0:T(8,128)(2,1)...) custom-call(bf16[960,256]{1,0:T(8,128)(2,1)} %copy-done.87, ...), custom_call_target="tpu_custom_call" | custom-call | flops 24000000000 | bytes 1024 | tf_op jit(solution)/shard_map/other_blocks/pallas_call | solution.py:152
  126.1 0.9 collective-permute-start.28
  127.1 1.2 collective-permute-start.33
  128.4 7.9 %down_weights.1 = (bf16[4,120,640]{2,1,0:T(8,128)(2,1)}, bf16[2,120,640]{2,1,0:T(8,128)(2,1)}, bf16[1,120,640]{2,1,0:T(8,128)(2,1)}, bf16[1,120,640]{2,1,0:T(8,128)(2,1)}) custom-call(s32[2]{0:T(128)S(1)} %pad_add_fusion.ranks, bf16[960,256]{1,0:T(8,128)(2,1)} %copy-done.59, bf16[960,256]{1,0:T(8,128)(2,1)} %copy-done.83, bf16[960,256]{1,0:T(8,128)(2,1)} %copy-done.78, ...), custom_call_target="tpu_custom_call" | custom-call | flops 16000000000 | bytes 1024 | tf_op jit(solution)/shard_map/down_weights/pallas_call | solution.py:152
  136.3 1.6 collective-permute-start.32
  139.0 13.2 %gate_up_weights.1 = (bf16[4,120,1280]{2,1,0:T(8,128)(2,1)}, bf16[2,120,1280]{2,1,0:T(8,128)(2,1)}, bf16[1,120,1280]{2,1,0:T(8,128)(2,1)}, bf16[1,120,1280]{2,1,0:T(8,128)(2,1)}) custom-call(s32[2]{0:T(128)S(1)} %pad_add_fusion.ranks, bf16[960,256]{1,0:T(8,128)(2,1)} %get-tuple-element.255.x_a.refs_0_, bf16[960,256]{1,0:T(8,128)(2,1)} %copy-done.81, ...), custom_call_target="tpu_custom_call" | custom-call | flops 28000000000 | bytes 1024 | tf_op jit(solution)/shard_map/gate_up_weights/pallas_call | solution.py:152
  153.0 1.2 collective-permute-start.36
  154.4 1.6 collective-permute-start.34
  156.1 4.3 %branch.2 = (f32[960,256]{1,0:T(8,128)}, bf16[960,256]{1,0:T(8,128)(2,1)}, bf16[960,256]{1,0:T(8,128)(2,1)}, f32[16,256]{1,0:T(8,128)}, f32[8,960]{1,0:T(8,128)}) custom-call(s32[2]{0:T(128)S(1)} %pad_add_fusion.ranks, f32[960,256]{1,0:T(8,128)S(1)} %copy-done.2, bf16[2,960,256]{2,1,0:T(8,128)(2,1)S(1)} %bitcast.101, ...), custom_call_target="tpu_custom_call" | custom-call | flops 8000000000 | bytes 1024 | tf_op jit(solution)/shard_map/branch/pallas_call | solution.py:152
  160.4 1.7 collective-permute-done.34
  162.1 2.7 collective-permute-start.37
  164.8 11.7 %attend_back.2 = (bf16[960,256]{1,0:T(8,128)(2,1)}, bf16[640,256]{1,0:T(8,128)(2,1)}, bf16[640,256]{1,0:T(8,128)(2,1)}, bf16[2,640,256]{2,1,0:T(8,128)(2,1)}) custom-call(bf16[960,512]{1,0:T(8,128)(2,1)} %queries.1.q_ref, bf16[640,256]{1,0:T(8,128)(2,1)} %get-tuple-element.189.b0, bf16[640,256]{1,0:T(8,128)(2,1)} %copy-done.98, bf16[640,256]{1,0:T(8,128)(2,1)} %copy-done.97, ...), custom_call_target="tpu_custom_call" | custom-call | flops 22000001024 | bytes 1024 | tf_op jit(solution)/shard_map/attend_back/pallas_call | solution.py:152
  177.2 4.3 %branch.3 = (f32[960,256]{1,0:T(8,128)}, bf16[960,256]{1,0:T(8,128)(2,1)}, bf16[960,256]{1,0:T(8,128)(2,1)}, f32[16,256]{1,0:T(8,128)}, f32[8,960]{1,0:T(8,128)}) custom-call(s32[2]{0:T(128)S(1)} %pad_add_fusion.ranks, f32[960,256]{1,0:T(8,128)S(1)} %copy-done.3, bf16[2,960,256]{2,1,0:T(8,128)(2,1)S(1)} %bitcast.102, ...), custom_call_target="tpu_custom_call" | custom-call | flops 8000000000 | bytes 1024 | tf_op jit(solution)/shard_map/branch/pallas_call | solution.py:152
  182.7 1.6 collective-permute-start.43
  184.3 11.8 %attend_back.3 = (bf16[960,256]{1,0:T(8,128)(2,1)}, bf16[640,256]{1,0:T(8,128)(2,1)}, bf16[640,256]{1,0:T(8,128)(2,1)}, bf16[2,640,256]{2,1,0:T(8,128)(2,1)}) custom-call(bf16[960,512]{1,0:T(8,128)(2,1)} %queries.1.q_ref, bf16[640,256]{1,0:T(8,128)(2,1)} %get-tuple-element.205.b0, bf16[640,256]{1,0:T(8,128)(2,1)} %copy-done.95, bf16[640,256]{1,0:T(8,128)(2,1)} %copy-done.93, ...), custom_call_target="tpu_custom_call" | custom-call | flops 22000001024 | bytes 1024 | tf_op jit(solution)/shard_map/attend_back/pallas_call | solution.py:152
  196.3 6.1 %query_weights.1 = (bf16[8,32,1920]{2,1,0:T(8,128)(2,1)}, bf16[8,32,1920]{2,1,0:T(8,128)(2,1)}, bf16[2,8,32,1920]{3,2,1,0:T(8,128)(2,1)}) custom-call(s32[2]{0:T(128)S(1)} %pad_add_fusion.ranks, bf16[960,512]{1,0:T(8,128)(2,1)S(1)} %copy-done.40, bf16[960,256]{1,0:T(8,128)(2,1)S(1)} %copy-done.43, bf16[960,256]{1,0:T(8,128)(2,1)} %get-tuple-element.302.gq_b, ...), custom_call_target="tpu_custom_call" | custom-call | flops 16000000000 | bytes 1024 | tf_op jit(solution)/shard_map/query_weights/pallas_call | solution.py:152
  203.8 2.6 collective-permute-start.48
  206.4 1.2 collective-permute-start.46
  207.6 4.1 %query_grad.1.refs_9_ = f32[2,960,256]{2,1,0:T(8,128)} custom-call(s32[2]{0:T(128)S(1)} %pad_add_fusion.ranks, bf16[960,256]{1,0:T(8,128)(2,1)S(1)} %copy-done.43, bf16[960,256]{1,0:T(8,128)(2,1)} %get-tuple-element.302.gq_b, bf16[240,960]{1,0:T(8,128)(2,1)S(1)} %copy-done.11, bf16[240,960]{1,0:T(8,128)(2,1)S(1)} %copy-done.15, ...), custom_call_target="tpu_custom_call" | custom-call | flops 8000000000 | bytes 1024 | tf_op jit(solution)/shard_map/query_grad/pallas_call | solution.py:152
  211.7 7.4 %collective-permute-done.45 = bf16[2,120,640]{2,1,0:T(8,128)(2,1)S(1)} collective-permute-done((bf16[2,120,640]{2,1,0:T(8,128)(2,1)S(1)}, bf16[2,120,640]{2,1,0:T(8,128)(2,1)S(1)}, u32[]{:S(2)}, u32[]{:S(2)}) %collective-permute-start.45) | collective-permute-done | bytes 307232 | tf_op jit(solution)/shard_map/ppermute | solution.py:37
  219.3 1.6 collective-permute-start.49
  221.1 1.2 collective-permute-start.47
  223.1 7.5 %key_weights.1 = (bf16[8,32,640]{2,1,0:T(8,128)(2,1)}, bf16[8,32,640]{2,1,0:T(8,128)(2,1)}, bf16[2,8,32,640]{3,2,1,0:T(8,128)(2,1)}, f32[2,960,256]{2,1,0:T(8,128)}) custom-call(s32[2]{0:T(128)S(1)} %pad_add_fusion.ranks, bf16[960,512]{1,0:T(8,128)(2,1)S(1)} %copy-done.40, bf16[640,256]{1,0:T(8,128)(2,1)} %get-tuple-element.309.refs_1_, ...), custom_call_target="tpu_custom_call" | custom-call | flops 20000000000 | bytes 1024 | tf_op jit(solution)/shard_map/key_weights/pallas_call | solution.py:152
  230.9 3.4 %collective-permute-done.49.odd = bf16[4,120,640]{2,1,0:T(8,128)(2,1)S(1)} collective-permute-done((bf16[4,120,640]{2,1,0:T(8,128)(2,1)S(1)}, bf16[4,120,640]{2,1,0:T(8,128)(2,1)S(1)}, u32[]{:S(2)}, u32[]{:S(2)}) %collective-permute-start.49) | collective-permute-done | bytes 614432 | tf_op jit(solution)/shard_map/ppermute | solution.py:37
  235.1 3.5 %down_done.1 = f32[960,640]{1,0:T(8,128)} custom-call(s32[2]{0:T(128)S(1)} %pad_add_fusion.ranks, bf16[4,120,640]{2,1,0:T(8,128)(2,1)} %copy-done.53, bf16[4,120,640]{2,1,0:T(8,128)(2,1)} %copy-done.75), custom_call_target="tpu_custom_call" | custom-call | flops 7000000000 | bytes 1024 | tf_op jit(solution)/shard_map/down_done/pallas_call | solution.py:152
  238.8 1.2 collective-permute-start.51
  240.0 5.9 %collective-permute-done.47 = bf16[8,32,1920]{2,1,0:T(8,128)(2,1)S(1)} collective-permute-done((bf16[8,32,1920]{2,1,0:T(8,128)(2,1)S(1)}, bf16[8,32,1920]{2,1,0:T(8,128)(2,1)S(1)}, u32[]{:S(2)}, u32[]{:S(2)}) %collective-permute-start.47) | collective-permute-done | bytes 983072 | tf_op jit(solution)/shard_map/ppermute | solution.py:37
  246.1 4.7 %collective-permute-done.51 = bf16[8,32,640]{2,1,0:T(8,128)(2,1)S(1)} collective-permute-done((bf16[8,32,640]{2,1,0:T(8,128)(2,1)S(1)}, bf16[8,32,640]{2,1,0:T(8,128)(2,1)S(1)}, u32[]{:S(2)}, u32[]{:S(2)}) %collective-permute-start.51) | collective-permute-done | bytes 327712 | tf_op jit(solution)/shard_map/ppermute | solution.py:37
  251.9 13.7 %collective-permute-done.52 = bf16[4,32,2560]{2,1,0:T(8,128)(2,1)S(1)} collective-permute-done((bf16[4,32,2560]{2,1,0:T(8,128)(2,1)S(1)}, bf16[4,32,2560]{2,1,0:T(8,128)(2,1)S(1)}, u32[]{:S(2)}, u32[]{:S(2)}) %collective-permute-start.52) | collective-permute-done | bytes 655392 | tf_op jit(solution)/shard_map/ppermute | solution.py:37
  266.0 1.0 collective-permute-start.58
  267.1 5.9 %collective-permute-done.53 = bf16[2,32,2560]{2,1,0:T(8,128)(2,1)S(1)} collective-permute-done((bf16[2,32,2560]{2,1,0:T(8,128)(2,1)S(1)}, bf16[2,32,2560]{2,1,0:T(8,128)(2,1)S(1)}, u32[]{:S(2)}, u32[]{:S(2)}) %collective-permute-start.53) | collective-permute-done | bytes 327712 | tf_op jit(solution)/shard_map/ppermute | solution.py:37
  273.1 11.3 %collective-permute-done.54 = bf16[1,32,2560]{2,1,0:T(8,128)(2,1)S(1)} collective-permute-done((bf16[1,32,2560]{2,1,0:T(8,128)(2,1)S(1)}, bf16[1,32,2560]{2,1,0:T(8,128)(2,1)S(1)}, u32[]{:S(2)}, u32[]{:S(2)}) %collective-permute-start.54) | collective-permute-done | bytes 163872 | tf_op jit(solution)/shard_map/ppermute | solution.py:37
  284.6 6.2 %collective-permute-done.55 = bf16[1,32,2560]{2,1,0:T(8,128)(2,1)S(1)} collective-permute-done((bf16[1,32,2560]{2,1,0:T(8,128)(2,1)S(1)}, bf16[1,32,2560]{2,1,0:T(8,128)(2,1)S(1)}, u32[]{:S(2)}, u32[]{:S(2)}) %collective-permute-start.55) | collective-permute-done | bytes 163872 | tf_op jit(solution)/shard_map/ppermute | solution.py:37
  290.8 1.3 collective-permute-done.58.odd
  292.2 1.8 collective-permute-start.59
  294.0 5.1 %gate_up_done.1 = (f32[960,640]{1,0:T(8,128)}, f32[960,640]{1,0:T(8,128)}) custom-call(s32[2]{0:T(128)S(1)} %pad_add_fusion.ranks, bf16[4,120,1280]{2,1,0:T(8,128)(2,1)} %copy-done.45, bf16[4,120,1280]{2,1,0:T(8,128)(2,1)} %copy-done.73), custom_call_target="tpu_custom_call" | custom-call | flops 14000000000 | bytes 1024 | tf_op jit(solution)/shard_map/gate_up_done/pallas_call | solution.py:152
  299.4 1.5 collective-permute-start.60
  301.4 1.4 fusion.28
  302.8 8.8 %collective-permute-done.60.odd = bf16[4,32,2560]{2,1,0:T(8,128)(2,1)S(1)} collective-permute-done((bf16[4,32,2560]{2,1,0:T(8,128)(2,1)S(1)}, bf16[4,32,2560]{2,1,0:T(8,128)(2,1)S(1)}, u32[]{:S(2)}, u32[]{:S(2)}) %collective-permute-start.60) | collective-permute-done | bytes 655392 | tf_op jit(solution)/shard_map/ppermute | solution.py:37
  312.4 3.9 %attention_done.1 = (f32[240,960]{1,0:T(8,128)}, f32[240,960]{1,0:T(8,128)}, f32[320,240]{1,0:T(8,128)}, f32[320,240]{1,0:T(8,128)}, f32[8,240]{1,0:T(8,128)}) custom-call(s32[2]{0:T(128)S(1)} %pad_add_fusion.ranks, bf16[4,32,2560]{2,1,0:T(8,128)(2,1)} %copy-done.51, bf16[4,32,2560]{2,1,0:T(8,128)(2,1)} %copy-done.74), custom_call_target="tpu_custom_call" | custom-call | flops 10000000000 | bytes 1024 | tf_op jit(solution)/shard_map/attention_done/pallas_call | solution.py:152
  316.3 1.3 fusion.29
  (328 shorter events, 29.3 us)
Async XLA Ops:
  4.7 12.6 %collective-permute-start = (bf16[240,768]{1,0:T(8,128)(2,1)}, bf16[240,768]{1,0:T(8,128)(2,1)S(1)}, u32[]{:S(2)}, u32[]{:S(2)}) collective-permute-start(bf16[240,768]{1,0:T(8,128)(2,1)} %pack.1.b0.refs_10_), channel_id=1, source_target_pairs={{0,16},{8,24},{16,0},{24,8},{1,17},{9,25},{17,1},{25,9},{2,18},{10... | collective-permute-start | bytes 1105928 | tf_op jit(solution)/shard_map/ppermute | solution.py:37
  7.6 19.3 %collective-permute-start.3 = (bf16[240,960]{1,0:T(8,128)(2,1)S(1)}, bf16[240,960]{1,0:T(8,128)(2,1)S(1)}, u32[]{:S(2)}, u32[]{:S(2)}) collective-permute-start(bf16[240,960]{1,0:T(8,128)(2,1)S(1)} %copy-done.10), channel_id=1, source_target_pairs={{0,16},{8,24},{16,0},{24,8},{1,17},{9,25},{17,1},{25,9},{2,18},{10... | collective-permute-start | bytes 1382408 | tf_op jit(solution)/shard_map/ppermute | solution.py:37
  17.3 1.7 collective-permute-start.1
  17.3 2.2 collective-permute-start.2
  27.0 2.3 collective-permute-start.4
  27.0 2.6 collective-permute-start.5
  27.5 9.9 %collective-permute-start.6 = (bf16[640,256]{1,0:T(8,128)(2,1)}, bf16[640,256]{1,0:T(8,128)(2,1)S(1)}, u32[]{:S(2)}, u32[]{:S(2)}) collective-permute-start(bf16[640,256]{1,0:T(8,128)(2,1)} %get-tuple-element.189.b0), channel_id=1, source_target_pairs={{0,16},{8,24},{16,0},{24,8},{1,17},{9,25},{17,1},{25,9},{2,18},{10... | collective-permute-start | bytes 983048 | tf_op jit(solution)/shard_map/ppermute | solution.py:37
  37.4 2.5 collective-permute-start.7
  37.4 2.5 collective-permute-start.8
  37.9 14.8 %collective-permute-start.9 = (bf16[240,960]{1,0:T(8,128)(2,1)S(1)}, bf16[240,960]{1,0:T(8,128)(2,1)S(1)}, u32[]{:S(2)}, u32[]{:S(2)}) collective-permute-start(bf16[240,960]{1,0:T(8,128)(2,1)S(1)} %copy-done.8), channel_id=1, source_target_pairs={{0,16},{8,24},{16,0},{24,8},{1,17},{9,25},{17,1},{25,9},{2,18},{10... | collective-permute-start | bytes 1382408 | tf_op jit(solution)/shard_map/ppermute | solution.py:37
  39.7 18.5 %collective-permute-start.12 = (bf16[640,256]{1,0:T(8,128)(2,1)S(1)}, bf16[640,256]{1,0:T(8,128)(2,1)S(1)}, u32[]{:S(2)}, u32[]{:S(2)}) collective-permute-start(bf16[640,256]{1,0:T(8,128)(2,1)S(1)} %copy-done.92), channel_id=1, source_target_pairs={{0,16},{8,24},{16,0},{24,8},{1,17},{9,25},{17,1},{25,9},{2,18},{10... | collective-permute-start | bytes 983048 | tf_op jit(solution)/shard_map/ppermute | solution.py:37
  52.7 7.9 %collective-permute-start.10 = (bf16[240,960]{1,0:T(8,128)(2,1)S(1)}, bf16[240,960]{1,0:T(8,128)(2,1)S(1)}, u32[]{:S(2)}, u32[]{:S(2)}) collective-permute-start(bf16[240,960]{1,0:T(8,128)(2,1)S(1)} %copy-done.8), channel_id=1, source_target_pairs={{0,8},{8,0},{16,24},{24,16},{1,9},{9,1},{17,25},{25,17},{2,10},{10... | collective-permute-start | bytes 1382408 | tf_op jit(solution)/shard_map/ppermute | solution.py:37
  52.8 7.8 %collective-permute-start.11 = (bf16[240,960]{1,0:T(8,128)(2,1)S(1)}, bf16[240,960]{1,0:T(8,128)(2,1)S(1)}, u32[]{:S(2)}, u32[]{:S(2)}) collective-permute-start(bf16[240,960]{1,0:T(8,128)(2,1)S(1)} %collective-permute-done.9.b2), channel_id=1, source_target_pairs={{0,8},{8,0},{16,24},{24,16},{1,9},{9,1},{17,25},{25,17},{2,10},{10... | collective-permute-start | bytes 1382408 | tf_op jit(solution)/shard_map/ppermute | solution.py:37
  58.1 2.4 collective-permute-start.13
  58.1 2.4 collective-permute-start.14
  58.7 19.8 %copy-start.59 = (bf16[960,256]{1,0:T(8,128)(2,1)}, bf16[960,256]{1,0:T(8,128)(2,1)S(1)}, u32[]{:S(2)}) copy-start(bf16[960,256]{1,0:T(8,128)(2,1)S(1)} %get-tuple-element.248.refs_0_) | copy-start | bytes 1474564
  58.7 36.2 %copy-start.58 = (bf16[960,256]{1,0:T(8,128)(2,1)}, bf16[960,256]{1,0:T(8,128)(2,1)S(1)}, u32[]{:S(2)}) copy-start(bf16[960,256]{1,0:T(8,128)(2,1)S(1)} %get-tuple-element.227.refs_4_) | copy-start | bytes 1474564
  58.7 19.8 %collective-permute-start.15 = (bf16[960,256]{1,0:T(8,128)(2,1)S(1)}, bf16[960,256]{1,0:T(8,128)(2,1)S(1)}, u32[]{:S(2)}, u32[]{:S(2)}) collective-permute-start(bf16[960,256]{1,0:T(8,128)(2,1)S(1)} %get-tuple-element.248.refs_0_), channel_id=1, source_target_pairs={{0,16},{8,24},{16,0},{24,8},{1,17},{9,25},{17,1},{25,9},{2,18},{10... | collective-permute-start | bytes 1474568 | tf_op jit(solution)/shard_map/ppermute | solution.py:37
  66.0 20.1 %collective-permute-start.16 = (bf16[960,256]{1,0:T(8,128)(2,1)}, bf16[960,256]{1,0:T(8,128)(2,1)S(1)}, u32[]{:S(2)}, u32[]{:S(2)}) collective-permute-start(bf16[960,256]{1,0:T(8,128)(2,1)} %get-tuple-element.255.x_a.refs_0_), channel_id=1, source_target_pairs={{0,16},{8,24},{16,0},{24,8},{1,17},{9,25},{17,1},{25,9},{2,18},{10... | collective-permute-start | bytes 1474568 | tf_op jit(solution)/shard_map/ppermute | solution.py:37
  78.6 7.5 %collective-permute-start.17 = (bf16[960,256]{1,0:T(8,128)(2,1)S(1)}, bf16[960,256]{1,0:T(8,128)(2,1)S(1)}, u32[]{:S(2)}, u32[]{:S(2)}) collective-permute-start(bf16[960,256]{1,0:T(8,128)(2,1)S(1)} %get-tuple-element.248.refs_0_), channel_id=1, source_target_pairs={{0,8},{8,0},{16,24},{24,16},{1,9},{9,1},{17,25},{25,17},{2,10},{10... | collective-permute-start | bytes 1474568 | tf_op jit(solution)/shard_map/ppermute | solution.py:37
  78.7 7.4 %collective-permute-start.18 = (bf16[960,256]{1,0:T(8,128)(2,1)S(1)}, bf16[960,256]{1,0:T(8,128)(2,1)S(1)}, u32[]{:S(2)}, u32[]{:S(2)}) collective-permute-start(bf16[960,256]{1,0:T(8,128)(2,1)S(1)} %collective-permute-done.15.refs_4_.refs_2_), channel_id=1, source_target_pairs={{0,8},{8,0},{16,24},{24,16},{1,9},{9,1},{17,25},{25,17},{2,10},{10... | collective-permute-start | bytes 1474568 | tf_op jit(solution)/shard_map/ppermute | solution.py:37
  79.2 15.7 %collective-permute-start.21 = (bf16[960,256]{1,0:T(8,128)(2,1)S(1)}, bf16[960,256]{1,0:T(8,128)(2,1)S(1)}, u32[]{:S(2)}, u32[]{:S(2)}) collective-permute-start(bf16[960,256]{1,0:T(8,128)(2,1)S(1)} %get-tuple-element.227.refs_4_), channel_id=1, source_target_pairs={{0,16},{8,24},{16,0},{24,8},{1,17},{9,25},{17,1},{25,9},{2,18},{10... | collective-permute-start | bytes 1474568 | tf_op jit(solution)/shard_map/ppermute | solution.py:37
  84.9 24.4 %collective-permute-start.23 = (bf16[960,256]{1,0:T(8,128)(2,1)}, bf16[960,256]{1,0:T(8,128)(2,1)S(1)}, u32[]{:S(2)}, u32[]{:S(2)}) collective-permute-start(bf16[960,256]{1,0:T(8,128)(2,1)} %get-tuple-element.233.x_b.refs_4_), channel_id=1, source_target_pairs={{0,16},{8,24},{16,0},{24,8},{1,17},{9,25},{17,1},{25,9},{2,18},{10... | collective-permute-start | bytes 1474568 | tf_op jit(solution)/shard_map/ppermute | solution.py:37
  86.1 9.4 %collective-permute-start.19 = (bf16[960,256]{1,0:T(8,128)(2,1)S(1)}, bf16[960,256]{1,0:T(8,128)(2,1)S(1)}, u32[]{:S(2)}, u32[]{:S(2)}) collective-permute-start(bf16[960,256]{1,0:T(8,128)(2,1)S(1)} %copy-done.76), channel_id=1, source_target_pairs={{0,8},{8,0},{16,24},{24,16},{1,9},{9,1},{17,25},{25,17},{2,10},{10... | collective-permute-start | bytes 1474568 | tf_op jit(solution)/shard_map/ppermute | solution.py:37
  86.2 9.3 %collective-permute-start.20 = (bf16[960,256]{1,0:T(8,128)(2,1)S(1)}, bf16[960,256]{1,0:T(8,128)(2,1)S(1)}, u32[]{:S(2)}, u32[]{:S(2)}) collective-permute-start(bf16[960,256]{1,0:T(8,128)(2,1)S(1)} %collective-permute-done.16.refs_1_.refs_2_), channel_id=1, source_target_pairs={{0,8},{8,0},{16,24},{24,16},{1,9},{9,1},{17,25},{25,17},{2,10},{10... | collective-permute-start | bytes 1474568 | tf_op jit(solution)/shard_map/ppermute | solution.py:37
  94.9 15.0 %collective-permute-start.26 = (bf16[960,256]{1,0:T(8,128)(2,1)S(1)}, bf16[960,256]{1,0:T(8,128)(2,1)S(1)}, u32[]{:S(2)}, u32[]{:S(2)}) collective-permute-start(bf16[960,256]{1,0:T(8,128)(2,1)S(1)} %get-tuple-element.227.refs_4_), channel_id=1, source_target_pairs={{0,8},{8,0},{16,24},{24,16},{1,9},{9,1},{17,25},{25,17},{2,10},{10... | collective-permute-start | bytes 1474568 | tf_op jit(solution)/shard_map/ppermute | solution.py:37
  95.1 14.8 %collective-permute-start.27 = (bf16[960,256]{1,0:T(8,128)(2,1)S(1)}, bf16[960,256]{1,0:T(8,128)(2,1)S(1)}, u32[]{:S(2)}, u32[]{:S(2)}) collective-permute-start(bf16[960,256]{1,0:T(8,128)(2,1)S(1)} %collective-permute-done.21.refs_4_.refs_6_), channel_id=1, source_target_pairs={{0,8},{8,0},{16,24},{24,16},{1,9},{9,1},{17,25},{25,17},{2,10},{10... | collective-permute-start | bytes 1474568 | tf_op jit(solution)/shard_map/ppermute | solution.py:37
  109.3 1.9 collective-permute-start.24
  109.5 3.2 %collective-permute-start.25 = (bf16[960,256]{1,0:T(8,128)(2,1)S(1)}, bf16[960,256]{1,0:T(8,128)(2,1)S(1)}, u32[]{:S(2)}, u32[]{:S(2)}) collective-permute-start(bf16[960,256]{1,0:T(8,128)(2,1)S(1)} %collective-permute-done.23.refs_1_.refs_6_), channel_id=1, source_target_pairs={{0,8},{8,0},{16,24},{24,16},{1,9},{9,1},{17,25},{25,17},{2,10},{10... | collective-permute-start | bytes 1474568 | tf_op jit(solution)/shard_map/ppermute | solution.py:37
  109.9 16.0 %collective-permute-start.22 = (bf16[2,960,256]{2,1,0:T(8,128)(2,1)}, bf16[2,960,256]{2,1,0:T(8,128)(2,1)S(1)}, u32[]{:S(2)}, u32[]{:S(2)}) collective-permute-start(bf16[2,960,256]{2,1,0:T(8,128)(2,1)} %get-tuple-element.231), channel_id=1, source_target_pairs={{0,8},{8,0},{16,24},{24,16},{1,9},{9,1},{17,25},{25,17},{2,10},{10... | collective-permute-start | bytes 2949128 | tf_op jit(solution)/shard_map/ppermute | solution.py:37
  110.1 16.9 %collective-permute-start.31 = (bf16[2,960,256]{2,1,0:T(8,128)(2,1)}, bf16[2,960,256]{2,1,0:T(8,128)(2,1)S(1)}, u32[]{:S(2)}, u32[]{:S(2)}) collective-permute-start(bf16[2,960,256]{2,1,0:T(8,128)(2,1)} %get-tuple-element.245), channel_id=1, source_target_pairs={{0,8},{8,0},{16,24},{24,16},{1,9},{9,1},{17,25},{25,17},{2,10},{10... | collective-permute-start | bytes 2949128 | tf_op jit(solution)/shard_map/ppermute | solution.py:37
  125.4 13.6 %collective-permute-start.29 = (bf16[2,960,256]{2,1,0:T(8,128)(2,1)}, bf16[2,960,256]{2,1,0:T(8,128)(2,1)S(1)}, u32[]{:S(2)}, u32[]{:S(2)}) collective-permute-start(bf16[2,960,256]{2,1,0:T(8,128)(2,1)} %get-tuple-element.242), channel_id=1, source_target_pairs={{0,8},{8,0},{16,24},{24,16},{1,9},{9,1},{17,25},{25,17},{2,10},{10... | collective-permute-start | bytes 2949128 | tf_op jit(solution)/shard_map/ppermute | solution.py:37
  125.5 12.3 %collective-permute-start.30 = (bf16[2,960,256]{2,1,0:T(8,128)(2,1)}, bf16[2,960,256]{2,1,0:T(8,128)(2,1)S(1)}, u32[]{:S(2)}, u32[]{:S(2)}) collective-permute-start(bf16[2,960,256]{2,1,0:T(8,128)(2,1)} %get-tuple-element.243), channel_id=1, source_target_pairs={{0,8},{8,0},{16,24},{24,16},{1,9},{9,1},{17,25},{25,17},{2,10},{10... | collective-permute-start | bytes 2949128 | tf_op jit(solution)/shard_map/ppermute | solution.py:37
  126.1 28.3 %collective-permute-start.28 = (bf16[960,256]{1,0:T(8,128)(2,1)S(1)}, bf16[960,256]{1,0:T(8,128)(2,1)S(1)}, u32[]{:S(2)}, u32[]{:S(2)}) collective-permute-start(bf16[960,256]{1,0:T(8,128)(2,1)S(1)} %fusion.6), channel_id=1, source_target_pairs={{0,16},{8,24},{16,0},{24,8},{1,17},{9,25},{17,1},{25,9},{2,18},{10... | collective-permute-start | bytes 1474568 | tf_op jit(solution)/shard_map/ppermute | solution.py:37
  127.1 28.9 %collective-permute-start.33 = (bf16[960,256]{1,0:T(8,128)(2,1)S(1)}, bf16[960,256]{1,0:T(8,128)(2,1)S(1)}, u32[]{:S(2)}, u32[]{:S(2)}) collective-permute-start(bf16[960,256]{1,0:T(8,128)(2,1)S(1)} %fusion.5), channel_id=1, source_target_pairs={{0,16},{8,24},{16,0},{24,8},{1,17},{9,25},{17,1},{25,9},{2,18},{10... | collective-permute-start | bytes 1474568 | tf_op jit(solution)/shard_map/ppermute | solution.py:37
  136.3 16.7 %collective-permute-start.32 = (bf16[4,120,640]{2,1,0:T(8,128)(2,1)}, bf16[4,120,640]{2,1,0:T(8,128)(2,1)S(1)}, u32[]{:S(2)}, u32[]{:S(2)}) collective-permute-start(bf16[4,120,640]{2,1,0:T(8,128)(2,1)} %get-tuple-element.252), channel_id=1, source_target_pairs={{0,1},{1,0},{2,3},{3,2},{4,5},{5,4},{6,7},{7,6},{8,9},{9,8},{10,11... | collective-permute-start | bytes 1843208 | tf_op jit(solution)/shard_map/ppermute | solution.py:37
  138.0 26.8 %collective-permute-start.35 = (bf16[960,256]{1,0:T(8,128)(2,1)S(1)}, bf16[960,256]{1,0:T(8,128)(2,1)S(1)}, u32[]{:S(2)}, u32[]{:S(2)}) collective-permute-start(bf16[960,256]{1,0:T(8,128)(2,1)S(1)} %fusion.4), channel_id=1, source_target_pairs={{0,16},{8,24},{16,0},{24,8},{1,17},{9,25},{17,1},{25,9},{2,18},{10... | collective-permute-start | bytes 1474568 | tf_op jit(solution)/shard_map/ppermute | solution.py:37
  152.3 30.2 %collective-permute-start.39 = (bf16[4,120,1280]{2,1,0:T(8,128)(2,1)}, bf16[4,120,1280]{2,1,0:T(8,128)(2,1)S(1)}, u32[]{:S(2)}, u32[]{:S(2)}) collective-permute-start(bf16[4,120,1280]{2,1,0:T(8,128)(2,1)} %get-tuple-element.262), channel_id=1, source_target_pairs={{0,1},{1,0},{2,3},{3,2},{4,5},{5,4},{6,7},{7,6},{8,9},{9,8},{10,11... | collective-permute-start | bytes 3686408 | tf_op jit(solution)/shard_map/ppermute | solution.py:37
  153.0 24.1 %collective-permute-start.36 = (bf16[960,256]{1,0:T(8,128)(2,1)S(1)}, bf16[960,256]{1,0:T(8,128)(2,1)S(1)}, u32[]{:S(2)}, u32[]{:S(2)}) collective-permute-start(bf16[960,256]{1,0:T(8,128)(2,1)S(1)} %fusion.3), channel_id=1, source_target_pairs={{0,16},{8,24},{16,0},{24,8},{1,17},{9,25},{17,1},{25,9},{2,18},{10... | collective-permute-start | bytes 1474568 | tf_op jit(solution)/shard_map/ppermute | solution.py:37
  154.4 7.7 %collective-permute-start.34 = (bf16[2,120,640]{2,1,0:T(8,128)(2,1)S(1)}, bf16[2,120,640]{2,1,0:T(8,128)(2,1)S(1)}, u32[]{:S(2)}, u32[]{:S(2)}) collective-permute-start(bf16[2,120,640]{2,1,0:T(8,128)(2,1)S(1)} %add_convert_fusion.4), channel_id=1, source_target_pairs={{0,2},{1,3},{2,0},{3,1},{4,6},{5,7},{6,4},{7,5},{8,10},{9,11},{10,... | collective-permute-start | bytes 921608 | tf_op jit(solution)/shard_map/ppermute | solution.py:37
  162.1 14.5 %collective-permute-start.37 = (bf16[1,120,640]{2,1,0:T(8,128)(2,1)S(1)}, bf16[1,120,640]{2,1,0:T(8,128)(2,1)S(1)}, u32[]{:S(2)}, u32[]{:S(2)}) collective-permute-start(bf16[1,120,640]{2,1,0:T(8,128)(2,1)S(1)} %add_convert_fusion.8), channel_id=1, source_target_pairs={{0,4},{1,5},{2,6},{3,7},{4,0},{5,1},{6,2},{7,3},{8,12},{9,13},{10,... | collective-permute-start | bytes 460808 | tf_op jit(solution)/shard_map/ppermute | solution.py:37
  176.5 4.9 %collective-permute-start.38 = (bf16[2,640,256]{2,1,0:T(8,128)(2,1)}, bf16[2,640,256]{2,1,0:T(8,128)(2,1)S(1)}, u32[]{:S(2)}, u32[]{:S(2)}) collective-permute-start(bf16[2,640,256]{2,1,0:T(8,128)(2,1)} %get-tuple-element.281), channel_id=1, source_target_pairs={{0,8},{8,0},{16,24},{24,16},{1,9},{9,1},{17,25},{25,17},{2,10},{10... | collective-permute-start | bytes 1966088 | tf_op jit(solution)/shard_map/ppermute | solution.py:37
  176.7 19.4 %collective-permute-start.40 = (bf16[1,120,640]{2,1,0:T(8,128)(2,1)S(1)}, bf16[1,120,640]{2,1,0:T(8,128)(2,1)S(1)}, u32[]{:S(2)}, u32[]{:S(2)}) collective-permute-start(bf16[1,120,640]{2,1,0:T(8,128)(2,1)S(1)} %add_convert_fusion.7), channel_id=1, source_target_pairs={{0,4},{1,5},{2,6},{3,7},{4,0},{5,1},{6,2},{7,3},{8,12},{9,13},{10,... | collective-permute-start | bytes 460808 | tf_op jit(solution)/shard_map/ppermute | solution.py:37
  181.6 14.7 %collective-permute-start.41 = (bf16[640,256]{1,0:T(8,128)(2,1)S(1)}, bf16[640,256]{1,0:T(8,128)(2,1)S(1)}, u32[]{:S(2)}, u32[]{:S(2)}) collective-permute-start(bf16[640,256]{1,0:T(8,128)(2,1)S(1)} %fusion.13), channel_id=1, source_target_pairs={{0,16},{8,24},{16,0},{24,8},{1,17},{9,25},{17,1},{25,9},{2,18},{10... | collective-permute-start | bytes 983048 | tf_op jit(solution)/shard_map/ppermute | solution.py:37
  182.7 19.8 %collective-permute-start.43 = (bf16[2,120,1280]{2,1,0:T(8,128)(2,1)S(1)}, bf16[2,120,1280]{2,1,0:T(8,128)(2,1)S(1)}, u32[]{:S(2)}, u32[]{:S(2)}) collective-permute-start(bf16[2,120,1280]{2,1,0:T(8,128)(2,1)S(1)} %add_convert_fusion), channel_id=1, source_target_pairs={{0,2},{1,3},{2,0},{3,1},{4,6},{5,7},{6,4},{7,5},{8,10},{9,11},{10,... | collective-permute-start | bytes 1843208 | tf_op jit(solution)/shard_map/ppermute | solution.py:37
  196.1 6.5 %collective-permute-start.42 = (bf16[2,640,256]{2,1,0:T(8,128)(2,1)}, bf16[2,640,256]{2,1,0:T(8,128)(2,1)S(1)}, u32[]{:S(2)}, u32[]{:S(2)}) collective-permute-start(bf16[2,640,256]{2,1,0:T(8,128)(2,1)} %get-tuple-element.295), channel_id=1, source_target_pairs={{0,8},{8,0},{16,24},{24,16},{1,9},{9,1},{17,25},{25,17},{2,10},{10... | collective-permute-start | bytes 1966088 | tf_op jit(solution)/shard_map/ppermute | solution.py:37
  202.8 18.0 %collective-permute-start.44 = (bf16[2,8,32,1920]{3,2,1,0:T(8,128)(2,1)}, bf16[2,8,32,1920]{3,2,1,0:T(8,128)(2,1)S(1)}, u32[]{:S(2)}, u32[]{:S(2)}) collective-permute-start(bf16[2,8,32,1920]{3,2,1,0:T(8,128)(2,1)} %get-tuple-element.301), channel_id=1, source_target_pairs={{0,8},{8,0},{16,24},{24,16},{1,9},{9,1},{17,25},{25,17},{2,10},{10... | collective-permute-start | bytes 5898248 | tf_op jit(solution)/shard_map/ppermute | solution.py:37
  203.3 15.8 %collective-permute-start.45 = (bf16[2,120,640]{2,1,0:T(8,128)(2,1)S(1)}, bf16[2,120,640]{2,1,0:T(8,128)(2,1)S(1)}, u32[]{:S(2)}, u32[]{:S(2)}) collective-permute-start(bf16[2,120,640]{2,1,0:T(8,128)(2,1)S(1)} %pad_maximum_fusion.8), channel_id=1, source_target_pairs={{0,2},{1,3},{2,0},{3,1},{4,6},{5,7},{6,4},{7,5},{8,10},{9,11},{10,... | collective-permute-start | bytes 921608 | tf_op jit(solution)/shard_map/ppermute | solution.py:37
  203.8 26.8 %collective-permute-start.48 = (bf16[1,120,1280]{2,1,0:T(8,128)(2,1)S(1)}, bf16[1,120,1280]{2,1,0:T(8,128)(2,1)S(1)}, u32[]{:S(2)}, u32[]{:S(2)}) collective-permute-start(bf16[1,120,1280]{2,1,0:T(8,128)(2,1)S(1)} %add_convert_fusion.3), channel_id=1, source_target_pairs={{0,4},{1,5},{2,6},{3,7},{4,0},{5,1},{6,2},{7,3},{8,12},{9,13},{10,... | collective-permute-start | bytes 921608 | tf_op jit(solution)/shard_map/ppermute | solution.py:37
  206.4 16.0 %collective-permute-start.46 = (bf16[640,256]{1,0:T(8,128)(2,1)S(1)}, bf16[640,256]{1,0:T(8,128)(2,1)S(1)}, u32[]{:S(2)}, u32[]{:S(2)}) collective-permute-start(bf16[640,256]{1,0:T(8,128)(2,1)S(1)} %fusion.12), channel_id=1, source_target_pairs={{0,16},{8,24},{16,0},{24,8},{1,17},{9,25},{17,1},{25,9},{2,18},{10... | collective-permute-start | bytes 983048 | tf_op jit(solution)/shard_map/ppermute | solution.py:37
  219.3 15.1 %collective-permute-start.49 = (bf16[4,120,640]{2,1,0:T(8,128)(2,1)S(1)}, bf16[4,120,640]{2,1,0:T(8,128)(2,1)S(1)}, u32[]{:S(2)}, u32[]{:S(2)}) collective-permute-start(bf16[4,120,640]{2,1,0:T(8,128)(2,1)S(1)} %pad_maximum_fusion.4.even), channel_id=1, source_target_pairs={{0,1},{1,0},{2,3},{3,2},{4,5},{5,4},{6,7},{7,6},{8,9},{9,8},{10,11... | collective-permute-start | bytes 1843208 | tf_op jit(solution)/shard_map/ppermute | solution.py:37
  221.1 24.8 %collective-permute-start.47 = (bf16[8,32,1920]{2,1,0:T(8,128)(2,1)S(1)}, bf16[8,32,1920]{2,1,0:T(8,128)(2,1)S(1)}, u32[]{:S(2)}, u32[]{:S(2)}) collective-permute-start(bf16[8,32,1920]{2,1,0:T(8,128)(2,1)S(1)} %fusion), channel_id=1, source_target_pairs={{0,16},{8,24},{16,0},{24,8},{1,17},{9,25},{17,1},{25,9},{2,18},{10... | collective-permute-start | bytes 2949128 | tf_op jit(solution)/shard_map/ppermute | solution.py:37
  230.8 20.7 %collective-permute-start.56 = (bf16[1,120,1280]{2,1,0:T(8,128)(2,1)S(1)}, bf16[1,120,1280]{2,1,0:T(8,128)(2,1)S(1)}, u32[]{:S(2)}, u32[]{:S(2)}) collective-permute-start(bf16[1,120,1280]{2,1,0:T(8,128)(2,1)S(1)} %add_convert_fusion.2), channel_id=1, source_target_pairs={{0,4},{1,5},{2,6},{3,7},{4,0},{5,1},{6,2},{7,3},{8,12},{9,13},{10,... | collective-permute-start | bytes 921608 | tf_op jit(solution)/shard_map/ppermute | solution.py:37
  234.3 4.4 %collective-permute-start.50 = (bf16[2,8,32,640]{3,2,1,0:T(8,128)(2,1)}, bf16[2,8,32,640]{3,2,1,0:T(8,128)(2,1)S(1)}, u32[]{:S(2)}, u32[]{:S(2)}) collective-permute-start(bf16[2,8,32,640]{3,2,1,0:T(8,128)(2,1)} %get-tuple-element.320), channel_id=1, source_target_pairs={{0,8},{8,0},{16,24},{24,16},{1,9},{9,1},{17,25},{25,17},{2,10},{10... | collective-permute-start | bytes 1966088 | tf_op jit(solution)/shard_map/ppermute | solution.py:37
  238.8 12.0 %collective-permute-start.51 = (bf16[8,32,640]{2,1,0:T(8,128)(2,1)S(1)}, bf16[8,32,640]{2,1,0:T(8,128)(2,1)S(1)}, u32[]{:S(2)}, u32[]{:S(2)}) collective-permute-start(bf16[8,32,640]{2,1,0:T(8,128)(2,1)S(1)} %fusion.11), channel_id=1, source_target_pairs={{0,16},{8,24},{16,0},{24,8},{1,17},{9,25},{17,1},{25,9},{2,18},{10... | collective-permute-start | bytes 983048 | tf_op jit(solution)/shard_map/ppermute | solution.py:37
  250.9 14.7 %collective-permute-start.52 = (bf16[4,32,2560]{2,1,0:T(8,128)(2,1)S(1)}, bf16[4,32,2560]{2,1,0:T(8,128)(2,1)S(1)}, u32[]{:S(2)}, u32[]{:S(2)}) collective-permute-start(bf16[4,32,2560]{2,1,0:T(8,128)(2,1)S(1)} %pad_maximum_fusion.2), channel_id=1, source_target_pairs={{0,1},{1,0},{2,3},{3,2},{4,5},{5,4},{6,7},{7,6},{8,9},{9,8},{10,11... | collective-permute-start | bytes 1966088 | tf_op jit(solution)/shard_map/ppermute | solution.py:37
  251.6 14.3 %collective-permute-start.57 = (bf16[2,120,1280]{2,1,0:T(8,128)(2,1)S(1)}, bf16[2,120,1280]{2,1,0:T(8,128)(2,1)S(1)}, u32[]{:S(2)}, u32[]{:S(2)}) collective-permute-start(bf16[2,120,1280]{2,1,0:T(8,128)(2,1)S(1)} %pad_maximum_fusion.5), channel_id=1, source_target_pairs={{0,2},{1,3},{2,0},{3,1},{4,6},{5,7},{6,4},{7,5},{8,10},{9,11},{10,... | collective-permute-start | bytes 1843208 | tf_op jit(solution)/shard_map/ppermute | solution.py:37
  265.8 7.2 %collective-permute-start.53 = (bf16[2,32,2560]{2,1,0:T(8,128)(2,1)S(1)}, bf16[2,32,2560]{2,1,0:T(8,128)(2,1)S(1)}, u32[]{:S(2)}, u32[]{:S(2)}) collective-permute-start(bf16[2,32,2560]{2,1,0:T(8,128)(2,1)S(1)} %add_convert_fusion.1), channel_id=1, source_target_pairs={{0,2},{1,3},{2,0},{3,1},{4,6},{5,7},{6,4},{7,5},{8,10},{9,11},{10,... | collective-permute-start | bytes 983048 | tf_op jit(solution)/shard_map/ppermute | solution.py:37
  266.0 28.0 %copy-start.45 = (bf16[4,120,1280]{2,1,0:T(8,128)(2,1)}, bf16[4,120,1280]{2,1,0:T(8,128)(2,1)S(1)}, u32[]{:S(2)}) copy-start(bf16[4,120,1280]{2,1,0:T(8,128)(2,1)S(1)} %pad_maximum_fusion.1.even) | copy-start | bytes 3686404
  266.0 26.1 %collective-permute-start.58 = (bf16[4,120,1280]{2,1,0:T(8,128)(2,1)S(1)}, bf16[4,120,1280]{2,1,0:T(8,128)(2,1)S(1)}, u32[]{:S(2)}, u32[]{:S(2)}) collective-permute-start(bf16[4,120,1280]{2,1,0:T(8,128)(2,1)S(1)} %pad_maximum_fusion.1.even), channel_id=1, source_target_pairs={{0,1},{1,0},{2,3},{3,2},{4,5},{5,4},{6,7},{7,6},{8,9},{9,8},{10,11... | collective-permute-start | bytes 3686408 | tf_op jit(solution)/shard_map/ppermute | solution.py:37
  273.0 11.4 %collective-permute-start.54 = (bf16[1,32,2560]{2,1,0:T(8,128)(2,1)S(1)}, bf16[1,32,2560]{2,1,0:T(8,128)(2,1)S(1)}, u32[]{:S(2)}, u32[]{:S(2)}) collective-permute-start(bf16[1,32,2560]{2,1,0:T(8,128)(2,1)S(1)} %add_convert_fusion.6), channel_id=1, source_target_pairs={{0,4},{1,5},{2,6},{3,7},{4,0},{5,1},{6,2},{7,3},{8,12},{9,13},{10,... | collective-permute-start | bytes 491528 | tf_op jit(solution)/shard_map/ppermute | solution.py:37
  284.5 6.3 %collective-permute-start.55 = (bf16[1,32,2560]{2,1,0:T(8,128)(2,1)S(1)}, bf16[1,32,2560]{2,1,0:T(8,128)(2,1)S(1)}, u32[]{:S(2)}, u32[]{:S(2)}) collective-permute-start(bf16[1,32,2560]{2,1,0:T(8,128)(2,1)S(1)} %add_convert_fusion.5), channel_id=1, source_target_pairs={{0,4},{1,5},{2,6},{3,7},{4,0},{5,1},{6,2},{7,3},{8,12},{9,13},{10,... | collective-permute-start | bytes 491528 | tf_op jit(solution)/shard_map/ppermute | solution.py:37
  292.2 7.1 %collective-permute-start.59 = (bf16[2,32,2560]{2,1,0:T(8,128)(2,1)S(1)}, bf16[2,32,2560]{2,1,0:T(8,128)(2,1)S(1)}, u32[]{:S(2)}, u32[]{:S(2)}) collective-permute-start(bf16[2,32,2560]{2,1,0:T(8,128)(2,1)S(1)} %pad_maximum_fusion.7), channel_id=1, source_target_pairs={{0,2},{1,3},{2,0},{3,1},{4,6},{5,7},{6,4},{7,5},{8,10},{9,11},{10,... | collective-permute-start | bytes 983048 | tf_op jit(solution)/shard_map/ppermute | solution.py:37
  299.4 12.2 %collective-permute-start.60 = (bf16[4,32,2560]{2,1,0:T(8,128)(2,1)S(1)}, bf16[4,32,2560]{2,1,0:T(8,128)(2,1)S(1)}, u32[]{:S(2)}, u32[]{:S(2)}) collective-permute-start(bf16[4,32,2560]{2,1,0:T(8,128)(2,1)S(1)} %pad_maximum_fusion.3.even), channel_id=1, source_target_pairs={{0,1},{1,0},{2,3},{3,2},{4,5},{5,4},{6,7},{7,6},{8,9},{9,8},{10,11... | collective-permute-start | bytes 1966088 | tf_op jit(solution)/shard_map/ppermute | solution.py:37
  (99 other events, 784.4 us)

commit v6 on v5

--- a/solution.py
+++ b/solution.py
@@ -121,6 +121,33 @@
     def done(self, *others):
         self.wide = after(self.wide, *others)
         held = jnp.concatenate([self.held, self.wide])
+        return held, swap(held, "rep", self.ranks, 1)
+
+
+class ShortSum(RepSum):
+    def second(self, *others):
+        one = after(self.one, *others)
+        self.one = one
+        six = (self.pieces[1][0:1].astype(FULL) + one[0:1].astype(FULL)).astype(LOW)
+        two = (self.pieces[1][1:2].astype(FULL) + one[1:2].astype(FULL)).astype(LOW)
+        four = (self.pieces[2].astype(FULL) + one[2:3].astype(FULL)).astype(LOW)
+        self.terms = [swap(sent, "rep", self.ranks, mask) for sent, mask in ((six, 6), (two, 2), (four, 4))]
+        return six, two, four
+
+    def own(self, *others):
+        ranks = self.ranks
+        terms = after(self.terms, *others)
+        mine = self.pieces[3].astype(FULL) + self.one[3:4].astype(FULL)
+        mine = (mine + terms[0].astype(FULL) + terms[1].astype(FULL) + terms[2].astype(FULL)).astype(LOW)
+        if ranks > PARTS:
+            others = [[j * PARTS + i for j in range(ranks // PARTS)] for i in range(PARTS)]
+            mine = lax.psum(mine, "rep", axis_index_groups=others)
+        self.mine = mine
+        self.back = [swap(mine, "rep", ranks, mask) for mask in (4, 2, 6)]
+        return mine
+
+    def done(self, *others):
+        held = jnp.concatenate([self.mine, *after(self.back, *others)])
         return held, swap(held, "rep", self.ranks, 1)
 
 
@@ -638,7 +665,7 @@
         in_specs=[whole((width, rows))] + [whole((shard, width))] * 4 + [table, table],
         out_specs=whole((width, rows)),
         scratch=[pltpu.VMEM((width, width), LOW)],
-        micros=4.9,
+        micros=0.1,
     )(place_of, norm_low, *q_blocks, cos_cols, sin_cols)
 
     o_flight = Blocks(w_out, kv_a)
@@ -657,7 +684,7 @@
             in_specs=[q_spec(s)] + [head] * 4,
             out_specs=(probs_spec, per_head),
             scratch=[pltpu.VMEM((length, span), FULL)],
-            micros=10,
+            micros=0.1,
         )(place_of, span_order, piece_starts, query, *kv_all[s])
 
     def middle_of(s, att):
@@ -835,11 +862,7 @@
         micros=4,
     )(place_of, gq_a, after(gq_b, *stage), *q_blocks)
     stage = (query_terms.cross(grad_part),)
-    down_pair = down_sum.done(grad_part)
-    block_out = jnp.stack(
-        [middle + three(term.all()) for middle, term in zip(after(middles, *stage), (out_a, out_b))]
-    )
-    stage = (*stage, block_out, down_pair[0], kv_grad_b.across)
+    stage = (*stage, kv_grad_b.across)
 
     def owned(terms):
         own, beside_term, across = terms.all()
@@ -882,8 +905,9 @@
         gain_a,
         gain_b,
     )
-    stage = (up_sum.own(grad_tokens), down_pair[1])
-    key_terms = Terms(*key_parts, *stage)
+    down_pair = down_sum.done(grad_tokens)
+    stage = (up_sum.own(grad_tokens), down_pair[0])
+    key_terms = Terms(*key_parts)
 
     def finished(name, kernel, pair, outs, *others):
         columns = pair[0].shape[2]
@@ -897,22 +921,23 @@
             micros=3.5 * outs,
         )(place_of, after(pair[0], *others), pair[1])
 
-    (grad_down,) = finished("down_done", forward_weights_kernel, down_pair, 1, *stage)
-    key_terms.cross(grad_down)
+    block_out = jnp.stack(
+        [middle + three(term.all()) for middle, term in zip(after(middles, *stage), (out_a, out_b))]
+    )
+    key_terms.cross(block_out)
     pieces = []
     for query_piece, key_piece in zip(owned(query_terms), owned(key_terms)):
         joint = jnp.concatenate([query_piece, key_piece], axis=-1)
         pieces.append(joint.astype(LOW))
-    query_sum = RepSum(pieces, ranks)
+    query_sum = ShortSum(pieces, ranks)
 
     up_sum.spread(*pieces)
-    step = query_sum.second()
-    up_pair = up_sum.done(step)
-    step = query_sum.third(step)
-    step = query_sum.own(step)
-    step = query_sum.spread(step, up_pair[1])
-    grad_gate, grad_up = finished("gate_up_done", forward_weights_kernel, up_pair, 2, step)
-    query_pair = query_sum.done(grad_up)
+    (grad_down,) = finished("down_done", forward_weights_kernel, down_pair, 1, *pieces)
+    step = query_sum.second(grad_down)
+    up_pair = up_sum.done(*step)
+    step = query_sum.own(up_pair[0])
+    query_pair = query_sum.done(step, up_pair[1])
+    grad_gate, grad_up = finished("gate_up_done", forward_weights_kernel, up_pair, 2, query_pair[0])
     grad_down = grad_down.T
     grad_query, grad_out, grad_key, grad_value, grad_gains = call(
         attention_done_kernel,

time: 323 us -> 313 us (0.969)
  waiting for transfers between devices: 84.6 us -> 64.9 us
  starting transfers between devices: 45.9 us -> 54.8 us
    ppermute x61 -> x63, waiting for transfers between devices: 84.6 us -> 64.9 us  [swap(): return lax.ppermute(values, axis, [(i, i ^ mask) for i in range(count)])]
    ppermute x61 -> x63, starting transfers between devices: 45.9 us -> 54.8 us  [swap(): return lax.ppermute(values, axis, [(i, i ^ mask) for i in range(count)])]
  transfers between devices with their start and end apart: 61 -> 63, of which waited for: 21 -> 21; matrix products, arithmetic and copies ran while one was open for 2% -> 2% of each run, Pallas kernels for 50% -> 52%
where the time goes in v6:
time: 313 us; the launch traced here: 308 us
  Pallas kernels  167 us (53%)
  waiting for transfers between devices  64.9 us (21%)
  starting transfers between devices  54.8 us (18%)
  local copies, waits for them, and re-layouts  12.6 us (4%)
  other arithmetic  6.8 us (2%)
    pallas_call x24, Pallas kernels, placed(): return run(*args[:prefetch], *rest)  167 us
    ppermute x63, waiting for transfers between devices, swap(): return lax.ppermute(values, axis, [(i, i ^ mask) for i in range(count)])  64.9 us
    ppermute x63, starting transfers between devices, swap(): return lax.ppermute(values, axis, [(i, i ^ mask) for i in range(count)])  54.8 us
    unnamed x204, local copies, waits for them, and re-layouts  9.84 us
  transfers between devices with their start and end apart: 63, of which 21 were waited for; matrix products, arithmetic and copies ran while one was open for 2% of the time, Pallas kernels for 52%

profile of v6, /device:TPU:0, one launch (start us, length us, event | category | flops | bytes accessed | tf_op | source)
XLA Modules:
  0.0 308.1 jit_solution(10264281887658136775)
XLA Ops:
  2.6 2.1 pack.1.b0.refs_10_
  4.7 3.0 collective-permute-start
  7.9 4.8 %flip_two.1 = (bf16[1280,960]{1,0:T(8,128)(2,1)}, bf16[960,1280]{1,0:T(8,128)(2,1)}) custom-call(bf16[960,640]{1,0:T(8,128)(2,1)} %wg_ref, bf16[960,640]{1,0:T(8,128)(2,1)} %wu_ref.1), custom_call_target="tpu_custom_call" | custom-call | flops 8000000000 | bytes 1024 | tf_op jit(solution)/shard_map/flip_two/pallas_call | solution.py:179
  12.7 2.9 flip_one.1.wd_ref.refs_9_
  15.6 1.7 collective-permute-done.b2.refs_12_
  20.2 4.0 %keys_values.1 = (bf16[960,512]{1,0:T(8,128)(2,1)}, bf16[640,256]{1,0:T(8,128)(2,1)}, bf16[640,256]{1,0:T(8,128)(2,1)}, bf16[960,128]{1,0:T(8,128)(2,1)}) custom-call(s32[2]{0:T(128)S(1)} %pad_add_fusion.ranks, bf16[2,960,256]{2,1,0:T(8,128)(2,1)S(1)} %bitcast.109, bf16[240,768]{1,0:T(8,128)(2,1)} %pack.1.b0.refs_10_, bf16[240,768]{1,0:T(8,128)(2,1)} %copy-done.32, ...), custom_call_target="tpu_custom_call" | custom-call | flops 8600000512 | bytes 1024 | tf_op jit(solution)/shard_map/keys_values/pallas_call | solution.py:179
  24.3 2.7 collective-permute-done.3.b2.q2
  27.5 1.7 collective-permute-start.6
  31.1 4.9 %queries.1.q_ref = bf16[960,512]{1,0:T(8,128)(2,1)} custom-call(s32[2]{0:T(128)S(1)} %pad_add_fusion.ranks, bf16[960,512]{1,0:T(8,128)(2,1)} %get-tuple-element.184.norm_ref.refs_0_, bf16[240,960]{1,0:T(8,128)(2,1)} %q0.1, bf16[240,960]{1,0:T(8,128)(2,1)} %copy-done.9, bf16[240,960]{1,0:T(8,128)(2,1)} %copy-done.7, bf16[240,960]{1,0:T(8,128)(2,1)} %copy-done.11, ...), custom_call_target="tpu_custom_call" | custom-call | flops 200000000 | bytes 1024 | tf_op jit(solution)/shard_map/queries/pallas_call | solution.py:179
  36.0 2.3 collective-permute-done.6.b2
  38.8 1.7 collective-permute-start.12
  42.0 11.3 %attend.2 = (bf16[5,1024,768]{2,1,0:T(8,128)(2,1)}, bf16[960,256]{1,0:T(8,128)(2,1)}) custom-call(s32[2]{0:T(128)S(1)} %pad_add_fusion.ranks, s32[2,4]{1,0:T(2,128)S(1)} %copy-done.13, s32[2,2]{1,0:T(2,128)S(1)} %copy-done.14, bf16[960,512]{1,0:T(8,128)(2,1)} %queries.1.q_ref, bf16[640,256]{1,0:T(8,128)(2,1)} %get-tuple-element.191.b0, ...), custom_call_target="tpu_custom_call" | custom-call | flops 200000000 | bytes 1024 | tf_op jit(solution)/shard_map/attend/pallas_call | solution.py:179
  55.5 1.8 collective-permute-start.15
  58.4 4.5 %middle.2 = (f32[960,256]{1,0:T(8,128)}, bf16[960,256]{1,0:T(8,128)(2,1)}) custom-call(s32[2]{0:T(128)S(1)} %pad_add_fusion.ranks, bf16[960,256]{1,0:T(8,128)(2,1)} %get-tuple-element.195.att_ref.att_a, bf16[240,960]{1,0:T(8,128)(2,1)} %b0.9, bf16[240,960]{1,0:T(8,128)(2,1)} %copy-done.24, bf16[240,960]{1,0:T(8,128)(2,1)} %copy-done.21, ...), custom_call_target="tpu_custom_call" | custom-call | flops 6000000000 | bytes 1024 | tf_op jit(solution)/shard_map/middle/pallas_call | solution.py:179
  62.8 1.5 collective-permute-start.17
  64.3 11.1 %attend.3 = (bf16[5,1024,768]{2,1,0:T(8,128)(2,1)}, bf16[960,256]{1,0:T(8,128)(2,1)}) custom-call(s32[2]{0:T(128)S(1)} %pad_add_fusion.ranks, s32[2,4]{1,0:T(2,128)S(1)} %copy-done.13, s32[2,2]{1,0:T(2,128)S(1)} %copy-done.14, bf16[960,512]{1,0:T(8,128)(2,1)} %queries.1.q_ref, bf16[640,256]{1,0:T(8,128)(2,1)} %get-tuple-element.207.b0, ...), custom_call_target="tpu_custom_call" | custom-call | flops 200000000 | bytes 1024 | tf_op jit(solution)/shard_map/attend/pallas_call | solution.py:179
  76.7 5.0 %middle.3 = (f32[960,256]{1,0:T(8,128)}, bf16[960,256]{1,0:T(8,128)(2,1)}) custom-call(s32[2]{0:T(128)S(1)} %pad_add_fusion.ranks, bf16[960,256]{1,0:T(8,128)(2,1)} %get-tuple-element.215.att_ref.att_b, bf16[240,960]{1,0:T(8,128)(2,1)} %b0.9, bf16[240,960]{1,0:T(8,128)(2,1)} %copy-done.24, bf16[240,960]{1,0:T(8,128)(2,1)} %copy-done.21, ...), custom_call_target="tpu_custom_call" | custom-call | flops 6000000000 | bytes 1024 | tf_op jit(solution)/shard_map/middle/pallas_call | solution.py:179
  81.8 1.2 collective-permute-start.16
  83.6 8.2 %own_blocks.1 = (bf16[2,960,256]{2,1,0:T(8,128)(2,1)}, bf16[2,960,256]{2,1,0:T(8,128)(2,1)}, bf16[2,640,256]{2,1,0:T(8,128)(2,1)}, bf16[2,640,256]{2,1,0:T(8,128)(2,1)}, bf16[2,640,256]{2,1,0:T(8,128)(2,1)}) custom-call(bf16[960,256]{1,0:T(8,128)(2,1)} %get-tuple-element.254.x_a.refs_0_, bf16[960,256]{1,0:T(8,128)(2,1)} %get-tuple-element.232.x_b.refs_4_, ...), custom_call_target="tpu_custom_call" | custom-call | flops 16000000000 | bytes 1024 | tf_op jit(solution)/shard_map/own_blocks/pallas_call | solution.py:179
  94.0 12.3 %other_blocks.2 = (bf16[960,256]{1,0:T(8,128)(2,1)}, bf16[2,960,256]{2,1,0:T(8,128)(2,1)}, bf16[960,256]{1,0:T(8,128)(2,1)}, bf16[2,960,256]{2,1,0:T(8,128)(2,1)...) custom-call(bf16[960,256]{1,0:T(8,128)(2,1)} %copy-done.89, ...), custom_call_target="tpu_custom_call" | custom-call | flops 24000000000 | bytes 1024 | tf_op jit(solution)/shard_map/other_blocks/pallas_call | solution.py:179
  108.3 1.4 collective-permute-done.24.refs_2_.refs_7_
  110.5 12.0 %other_blocks.3 = (bf16[960,256]{1,0:T(8,128)(2,1)}, bf16[2,960,256]{2,1,0:T(8,128)(2,1)}, bf16[960,256]{1,0:T(8,128)(2,1)}, bf16[2,960,256]{2,1,0:T(8,128)(2,1)...) custom-call(bf16[960,256]{1,0:T(8,128)(2,1)} %copy-done.95, ...), custom_call_target="tpu_custom_call" | custom-call | flops 24000000000 | bytes 1024 | tf_op jit(solution)/shard_map/other_blocks/pallas_call | solution.py:179
  124.3 1.2 collective-permute-start.37
  125.6 7.9 %down_weights.1 = (bf16[4,120,640]{2,1,0:T(8,128)(2,1)}, bf16[2,120,640]{2,1,0:T(8,128)(2,1)}, bf16[1,120,640]{2,1,0:T(8,128)(2,1)}, bf16[1,120,640]{2,1,0:T(8,128)(2,1)}) custom-call(s32[2]{0:T(128)S(1)} %pad_add_fusion.ranks, bf16[960,256]{1,0:T(8,128)(2,1)} %copy-done.59, bf16[960,256]{1,0:T(8,128)(2,1)} %copy-done.91, bf16[960,256]{1,0:T(8,128)(2,1)} %copy-done.86, ...), custom_call_target="tpu_custom_call" | custom-call | flops 16000000000 | bytes 1024 | tf_op jit(solution)/shard_map/down_weights/pallas_call | solution.py:179
  133.5 1.6 collective-permute-start.34
  136.2 13.3 %gate_up_weights.1 = (bf16[4,120,1280]{2,1,0:T(8,128)(2,1)}, bf16[2,120,1280]{2,1,0:T(8,128)(2,1)}, bf16[1,120,1280]{2,1,0:T(8,128)(2,1)}, bf16[1,120,1280]{2,1,0:T(8,128)(2,1)}) custom-call(s32[2]{0:T(128)S(1)} %pad_add_fusion.ranks, bf16[960,256]{1,0:T(8,128)(2,1)} %get-tuple-element.254.x_a.refs_0_, bf16[960,256]{1,0:T(8,128)(2,1)} %copy-done.89, ...), custom_call_target="tpu_custom_call" | custom-call | flops 28000000000 | bytes 1024 | tf_op jit(solution)/shard_map/gate_up_weights/pallas_call | solution.py:179
  150.3 1.2 collective-permute-start.33
  151.7 1.6 collective-permute-start.35
  153.4 4.4 %branch.2 = (f32[960,256]{1,0:T(8,128)}, bf16[960,256]{1,0:T(8,128)(2,1)}, bf16[960,256]{1,0:T(8,128)(2,1)}, f32[16,256]{1,0:T(8,128)}, f32[8,960]{1,0:T(8,128)}) custom-call(s32[2]{0:T(128)S(1)} %pad_add_fusion.ranks, f32[960,256]{1,0:T(8,128)S(1)} %copy-done.2, bf16[2,960,256]{2,1,0:T(8,128)(2,1)S(1)} %bitcast.101, ...), custom_call_target="tpu_custom_call" | custom-call | flops 8000000000 | bytes 1024 | tf_op jit(solution)/shard_map/branch/pallas_call | solution.py:179
  157.8 1.6 collective-permute-done.35
  159.4 2.7 collective-permute-start.38
  162.1 11.7 %attend_back.2 = (bf16[960,256]{1,0:T(8,128)(2,1)}, bf16[640,256]{1,0:T(8,128)(2,1)}, bf16[640,256]{1,0:T(8,128)(2,1)}, bf16[2,640,256]{2,1,0:T(8,128)(2,1)}) custom-call(bf16[960,512]{1,0:T(8,128)(2,1)} %queries.1.q_ref, bf16[640,256]{1,0:T(8,128)(2,1)} %get-tuple-element.191.b0, bf16[640,256]{1,0:T(8,128)(2,1)} %copy-done.70, bf16[640,256]{1,0:T(8,128)(2,1)} %copy-done.69, ...), custom_call_target="tpu_custom_call" | custom-call | flops 22000001024 | bytes 1024 | tf_op jit(solution)/shard_map/attend_back/pallas_call | solution.py:179
  174.5 4.3 %branch.3 = (f32[960,256]{1,0:T(8,128)}, bf16[960,256]{1,0:T(8,128)(2,1)}, bf16[960,256]{1,0:T(8,128)(2,1)}, f32[16,256]{1,0:T(8,128)}, f32[8,960]{1,0:T(8,128)}) custom-call(s32[2]{0:T(128)S(1)} %pad_add_fusion.ranks, f32[960,256]{1,0:T(8,128)S(1)} %copy-done.3, bf16[2,960,256]{2,1,0:T(8,128)(2,1)S(1)} %bitcast.102, ...), custom_call_target="tpu_custom_call" | custom-call | flops 8000000000 | bytes 1024 | tf_op jit(solution)/shard_map/branch/pallas_call | solution.py:179
  180.0 1.6 collective-permute-start.39
  181.7 11.8 %attend_back.3 = (bf16[960,256]{1,0:T(8,128)(2,1)}, bf16[640,256]{1,0:T(8,128)(2,1)}, bf16[640,256]{1,0:T(8,128)(2,1)}, bf16[2,640,256]{2,1,0:T(8,128)(2,1)}) custom-call(bf16[960,512]{1,0:T(8,128)(2,1)} %queries.1.q_ref, bf16[640,256]{1,0:T(8,128)(2,1)} %get-tuple-element.207.b0, bf16[640,256]{1,0:T(8,128)(2,1)} %copy-done.67, bf16[640,256]{1,0:T(8,128)(2,1)} %copy-done.65, ...), custom_call_target="tpu_custom_call" | custom-call | flops 22000001024 | bytes 1024 | tf_op jit(solution)/shard_map/attend_back/pallas_call | solution.py:179
  193.7 6.1 %query_weights.1 = (bf16[8,32,1920]{2,1,0:T(8,128)(2,1)}, bf16[8,32,1920]{2,1,0:T(8,128)(2,1)}, bf16[2,8,32,1920]{3,2,1,0:T(8,128)(2,1)}) custom-call(s32[2]{0:T(128)S(1)} %pad_add_fusion.ranks, bf16[960,512]{1,0:T(8,128)(2,1)S(1)} %copy-done.4, bf16[960,256]{1,0:T(8,128)(2,1)S(1)} %copy-done.43, bf16[960,256]{1,0:T(8,128)(2,1)} %get-tuple-element.306.gq_b, ...), custom_call_target="tpu_custom_call" | custom-call | flops 16000000000 | bytes 1024 | tf_op jit(solution)/shard_map/query_weights/pallas_call | solution.py:179
  201.1 2.6 collective-permute-start.43
  203.7 1.2 collective-permute-start.46
  204.9 4.2 %query_grad.1.refs_9_ = f32[2,960,256]{2,1,0:T(8,128)} custom-call(s32[2]{0:T(128)S(1)} %pad_add_fusion.ranks, bf16[960,256]{1,0:T(8,128)(2,1)S(1)} %copy-done.43, bf16[960,256]{1,0:T(8,128)(2,1)} %get-tuple-element.306.gq_b, bf16[240,960]{1,0:T(8,128)(2,1)S(1)} %copy-done.6, bf16[240,960]{1,0:T(8,128)(2,1)S(1)} %copy-done.10, ...), custom_call_target="tpu_custom_call" | custom-call | flops 8000000000 | bytes 1024 | tf_op jit(solution)/shard_map/query_grad/pallas_call | solution.py:179
  210.4 3.9 %collective-permute-done.46.refs_6_ = bf16[640,256]{1,0:T(8,128)(2,1)S(1)} collective-permute-done((bf16[640,256]{1,0:T(8,128)(2,1)S(1)}, bf16[640,256]{1,0:T(8,128)(2,1)S(1)}, u32[]{:S(2)}, u32[]{:S(2)}) %collective-permute-start.46) | collective-permute-done | bytes 327712 | tf_op jit(solution)/shard_map/ppermute | solution.py:37
  215.1 7.6 %key_weights.1 = (bf16[8,32,640]{2,1,0:T(8,128)(2,1)}, bf16[8,32,640]{2,1,0:T(8,128)(2,1)}, bf16[2,8,32,640]{3,2,1,0:T(8,128)(2,1)}, f32[2,960,256]{2,1,0:T(8,128)}) custom-call(s32[2]{0:T(128)S(1)} %pad_add_fusion.ranks, bf16[960,512]{1,0:T(8,128)(2,1)S(1)} %copy-done.4, bf16[640,256]{1,0:T(8,128)(2,1)} %get-tuple-element.309.refs_1_, ...), custom_call_target="tpu_custom_call" | custom-call | flops 20000000000 | bytes 1024 | tf_op jit(solution)/shard_map/key_weights/pallas_call | solution.py:179
  223.3 1.6 collective-permute-start.52
  225.1 1.3 collective-permute-start.50
  226.5 8.9 %collective-permute-done.48 = bf16[8,32,1920]{2,1,0:T(8,128)(2,1)S(1)} collective-permute-done((bf16[8,32,1920]{2,1,0:T(8,128)(2,1)S(1)}, bf16[8,32,1920]{2,1,0:T(8,128)(2,1)S(1)}, u32[]{:S(2)}, u32[]{:S(2)}) %collective-permute-start.48) | collective-permute-done | bytes 983072 | tf_op jit(solution)/shard_map/ppermute | solution.py:37
  235.6 5.4 %collective-permute-done.50 = bf16[8,32,640]{2,1,0:T(8,128)(2,1)S(1)} collective-permute-done((bf16[8,32,640]{2,1,0:T(8,128)(2,1)S(1)}, bf16[8,32,640]{2,1,0:T(8,128)(2,1)S(1)}, u32[]{:S(2)}, u32[]{:S(2)}) %collective-permute-start.50) | collective-permute-done | bytes 327712 | tf_op jit(solution)/shard_map/ppermute | solution.py:37
  241.1 1.6 collective-permute-start.51
  243.0 1.6 collective-permute-start.57
  245.5 3.5 %down_done.1 = f32[960,640]{1,0:T(8,128)} custom-call(s32[2]{0:T(128)S(1)} %pad_add_fusion.ranks, bf16[4,120,640]{2,1,0:T(8,128)(2,1)} %copy-done.53, bf16[4,120,640]{2,1,0:T(8,128)(2,1)} %copy-done.83), custom_call_target="tpu_custom_call" | custom-call | flops 7000000000 | bytes 1024 | tf_op jit(solution)/shard_map/down_done/pallas_call | solution.py:179
  249.0 7.4 %collective-permute-done.51 = bf16[4,32,2560]{2,1,0:T(8,128)(2,1)S(1)} collective-permute-done((bf16[4,32,2560]{2,1,0:T(8,128)(2,1)S(1)}, bf16[4,32,2560]{2,1,0:T(8,128)(2,1)S(1)}, u32[]{:S(2)}, u32[]{:S(2)}) %collective-permute-start.51) | collective-permute-done | bytes 655392 | tf_op jit(solution)/shard_map/ppermute | solution.py:37
  256.6 1.6 collective-permute-start.54
  258.6 1.6 collective-permute-start.55
  260.3 1.6 collective-permute-start.61
  261.9 4.3 %collective-permute-done.54 = bf16[1,32,2560]{2,1,0:T(8,128)(2,1)S(1)} collective-permute-done((bf16[1,32,2560]{2,1,0:T(8,128)(2,1)S(1)}, bf16[1,32,2560]{2,1,0:T(8,128)(2,1)S(1)}, u32[]{:S(2)}, u32[]{:S(2)}) %collective-permute-start.54) | collective-permute-done | bytes 163872 | tf_op jit(solution)/shard_map/ppermute | solution.py:37
  267.2 5.1 %collective-permute-done.55 = bf16[1,32,2560]{2,1,0:T(8,128)(2,1)S(1)} collective-permute-done((bf16[1,32,2560]{2,1,0:T(8,128)(2,1)S(1)}, bf16[1,32,2560]{2,1,0:T(8,128)(2,1)S(1)}, u32[]{:S(2)}, u32[]{:S(2)}) %collective-permute-start.55) | collective-permute-done | bytes 163872 | tf_op jit(solution)/shard_map/ppermute | solution.py:37
  272.4 3.5 %collective-permute-start.60 = (bf16[1,32,2560]{2,1,0:T(8,128)(2,1)S(1)}, bf16[1,32,2560]{2,1,0:T(8,128)(2,1)S(1)}, u32[]{:S(2)}, u32[]{:S(2)}) collective-permute-start(bf16[1,32,2560]{2,1,0:T(8,128)(2,1)S(1)} %add_convert_fusion.4), channel_id=1, source_target_pairs={{0,6},{1,7},{2,4},{3,5},{4,2},{5,3},{6,0},{7,1},{8,14},{9,15},{10,... | collective-permute-start | bytes 491528 | tf_op jit(solution)/shard_map/ppermute | solution.py:37
  277.4 1.4 fusion.30
  278.8 2.4 collective-permute-done.60
  281.1 2.0 collective-permute-done.59
  283.1 3.5 %collective-permute-done.58 = bf16[1,32,2560]{2,1,0:T(8,128)(2,1)S(1)} collective-permute-done((bf16[1,32,2560]{2,1,0:T(8,128)(2,1)S(1)}, bf16[1,32,2560]{2,1,0:T(8,128)(2,1)S(1)}, u32[]{:S(2)}, u32[]{:S(2)}) %collective-permute-start.58) | collective-permute-done | bytes 163872 | tf_op jit(solution)/shard_map/ppermute | solution.py:37
  286.7 1.3 collective-permute-start.62
  288.1 5.1 %gate_up_done.1 = (f32[960,640]{1,0:T(8,128)}, f32[960,640]{1,0:T(8,128)}) custom-call(s32[2]{0:T(128)S(1)} %pad_add_fusion.ranks, bf16[4,120,1280]{2,1,0:T(8,128)(2,1)} %copy-done.45, bf16[4,120,1280]{2,1,0:T(8,128)(2,1)} %copy-done.81), custom_call_target="tpu_custom_call" | custom-call | flops 14000000000 | bytes 1024 | tf_op jit(solution)/shard_map/gate_up_done/pallas_call | solution.py:179
  293.1 8.7 %collective-permute-done.62.odd = bf16[4,32,2560]{2,1,0:T(8,128)(2,1)S(1)} collective-permute-done((bf16[4,32,2560]{2,1,0:T(8,128)(2,1)S(1)}, bf16[4,32,2560]{2,1,0:T(8,128)(2,1)S(1)}, u32[]{:S(2)}, u32[]{:S(2)}) %collective-permute-start.62) | collective-permute-done | bytes 655392 | tf_op jit(solution)/shard_map/ppermute | solution.py:37
  302.7 3.9 %attention_done.1 = (f32[240,960]{1,0:T(8,128)}, f32[240,960]{1,0:T(8,128)}, f32[320,240]{1,0:T(8,128)}, f32[320,240]{1,0:T(8,128)}, f32[8,240]{1,0:T(8,128)}) custom-call(s32[2]{0:T(128)S(1)} %pad_add_fusion.ranks, bf16[4,32,2560]{2,1,0:T(8,128)(2,1)} %copy-done.51, bf16[4,32,2560]{2,1,0:T(8,128)(2,1)} %copy-done.82), custom_call_target="tpu_custom_call" | custom-call | flops 10000000000 | bytes 1024 | tf_op jit(solution)/shard_map/attention_done/pallas_call | solution.py:179
  306.6 1.3 fusion.31
  (330 shorter events, 34.8 us)
Async XLA Ops:
  4.7 12.6 %collective-permute-start = (bf16[240,768]{1,0:T(8,128)(2,1)}, bf16[240,768]{1,0:T(8,128)(2,1)S(1)}, u32[]{:S(2)}, u32[]{:S(2)}) collective-permute-start(bf16[240,768]{1,0:T(8,128)(2,1)} %pack.1.b0.refs_10_), channel_id=1, source_target_pairs={{0,16},{8,24},{16,0},{24,8},{1,17},{9,25},{17,1},{25,9},{2,18},{10... | collective-permute-start | bytes 1105928 | tf_op jit(solution)/shard_map/ppermute | solution.py:37
  7.6 19.3 %collective-permute-start.3 = (bf16[240,960]{1,0:T(8,128)(2,1)S(1)}, bf16[240,960]{1,0:T(8,128)(2,1)S(1)}, u32[]{:S(2)}, u32[]{:S(2)}) collective-permute-start(bf16[240,960]{1,0:T(8,128)(2,1)S(1)} %copy-done.5), channel_id=1, source_target_pairs={{0,16},{8,24},{16,0},{24,8},{1,17},{9,25},{17,1},{25,9},{2,18},{10... | collective-permute-start | bytes 1382408 | tf_op jit(solution)/shard_map/ppermute | solution.py:37
  17.3 1.7 collective-permute-start.1
  17.3 2.2 collective-permute-start.2
  27.0 2.5 collective-permute-start.4
  27.0 2.6 collective-permute-start.5
  27.5 10.8 %collective-permute-start.6 = (bf16[640,256]{1,0:T(8,128)(2,1)}, bf16[640,256]{1,0:T(8,128)(2,1)S(1)}, u32[]{:S(2)}, u32[]{:S(2)}) collective-permute-start(bf16[640,256]{1,0:T(8,128)(2,1)} %get-tuple-element.191.b0), channel_id=1, source_target_pairs={{0,16},{8,24},{16,0},{24,8},{1,17},{9,25},{17,1},{25,9},{2,18},{10... | collective-permute-start | bytes 983048 | tf_op jit(solution)/shard_map/ppermute | solution.py:37
  29.2 24.1 %collective-permute-start.9 = (bf16[240,960]{1,0:T(8,128)(2,1)S(1)}, bf16[240,960]{1,0:T(8,128)(2,1)S(1)}, u32[]{:S(2)}, u32[]{:S(2)}) collective-permute-start(bf16[240,960]{1,0:T(8,128)(2,1)S(1)} %copy-done.18), channel_id=1, source_target_pairs={{0,16},{8,24},{16,0},{24,8},{1,17},{9,25},{17,1},{25,9},{2,18},{10... | collective-permute-start | bytes 1382408 | tf_op jit(solution)/shard_map/ppermute | solution.py:37
  38.3 2.3 collective-permute-start.7
  38.3 2.3 collective-permute-start.8
  38.8 16.2 %collective-permute-start.12 = (bf16[640,256]{1,0:T(8,128)(2,1)S(1)}, bf16[640,256]{1,0:T(8,128)(2,1)S(1)}, u32[]{:S(2)}, u32[]{:S(2)}) collective-permute-start(bf16[640,256]{1,0:T(8,128)(2,1)S(1)} %copy-done.64), channel_id=1, source_target_pairs={{0,16},{8,24},{16,0},{24,8},{1,17},{9,25},{17,1},{25,9},{2,18},{10... | collective-permute-start | bytes 983048 | tf_op jit(solution)/shard_map/ppermute | solution.py:37
  53.3 4.1 %collective-permute-start.10 = (bf16[240,960]{1,0:T(8,128)(2,1)S(1)}, bf16[240,960]{1,0:T(8,128)(2,1)S(1)}, u32[]{:S(2)}, u32[]{:S(2)}) collective-permute-start(bf16[240,960]{1,0:T(8,128)(2,1)S(1)} %copy-done.18), channel_id=1, source_target_pairs={{0,8},{8,0},{16,24},{24,16},{1,9},{9,1},{17,25},{25,17},{2,10},{10... | collective-permute-start | bytes 1382408 | tf_op jit(solution)/shard_map/ppermute | solution.py:37
  53.4 4.0 %collective-permute-start.11 = (bf16[240,960]{1,0:T(8,128)(2,1)S(1)}, bf16[240,960]{1,0:T(8,128)(2,1)S(1)}, u32[]{:S(2)}, u32[]{:S(2)}) collective-permute-start(bf16[240,960]{1,0:T(8,128)(2,1)S(1)} %collective-permute-done.9.b2), channel_id=1, source_target_pairs={{0,8},{8,0},{16,24},{24,16},{1,9},{9,1},{17,25},{25,17},{2,10},{10... | collective-permute-start | bytes 1382408 | tf_op jit(solution)/shard_map/ppermute | solution.py:37
  54.9 2.4 collective-permute-start.13
  54.9 2.4 collective-permute-start.14
  55.5 36.3 %copy-start.58 = (bf16[960,256]{1,0:T(8,128)(2,1)}, bf16[960,256]{1,0:T(8,128)(2,1)S(1)}, u32[]{:S(2)}) copy-start(bf16[960,256]{1,0:T(8,128)(2,1)S(1)} %get-tuple-element.227.refs_4_) | copy-start | bytes 1474564
  55.5 19.9 %collective-permute-start.15 = (bf16[960,256]{1,0:T(8,128)(2,1)S(1)}, bf16[960,256]{1,0:T(8,128)(2,1)S(1)}, u32[]{:S(2)}, u32[]{:S(2)}) collective-permute-start(bf16[960,256]{1,0:T(8,128)(2,1)S(1)} %get-tuple-element.246.refs_0_), channel_id=1, source_target_pairs={{0,16},{8,24},{16,0},{24,8},{1,17},{9,25},{17,1},{25,9},{2,18},{10... | collective-permute-start | bytes 1474568 | tf_op jit(solution)/shard_map/ppermute | solution.py:37
  62.8 20.1 %collective-permute-start.17 = (bf16[960,256]{1,0:T(8,128)(2,1)}, bf16[960,256]{1,0:T(8,128)(2,1)S(1)}, u32[]{:S(2)}, u32[]{:S(2)}) collective-permute-start(bf16[960,256]{1,0:T(8,128)(2,1)} %get-tuple-element.254.x_a.refs_0_), channel_id=1, source_target_pairs={{0,16},{8,24},{16,0},{24,8},{1,17},{9,25},{17,1},{25,9},{2,18},{10... | collective-permute-start | bytes 1474568 | tf_op jit(solution)/shard_map/ppermute | solution.py:37
  75.4 7.5 %collective-permute-start.20 = (bf16[960,256]{1,0:T(8,128)(2,1)S(1)}, bf16[960,256]{1,0:T(8,128)(2,1)S(1)}, u32[]{:S(2)}, u32[]{:S(2)}) collective-permute-start(bf16[960,256]{1,0:T(8,128)(2,1)S(1)} %get-tuple-element.246.refs_0_), channel_id=1, source_target_pairs={{0,8},{8,0},{16,24},{24,16},{1,9},{9,1},{17,25},{25,17},{2,10},{10... | collective-permute-start | bytes 1474568 | tf_op jit(solution)/shard_map/ppermute | solution.py:37
  75.5 7.4 %collective-permute-start.21 = (bf16[960,256]{1,0:T(8,128)(2,1)S(1)}, bf16[960,256]{1,0:T(8,128)(2,1)S(1)}, u32[]{:S(2)}, u32[]{:S(2)}) collective-permute-start(bf16[960,256]{1,0:T(8,128)(2,1)S(1)} %collective-permute-done.15.refs_4_.refs_2_), channel_id=1, source_target_pairs={{0,8},{8,0},{16,24},{24,16},{1,9},{9,1},{17,25},{25,17},{2,10},{10... | collective-permute-start | bytes 1474568 | tf_op jit(solution)/shard_map/ppermute | solution.py:37
  76.0 15.8 %collective-permute-start.22 = (bf16[960,256]{1,0:T(8,128)(2,1)S(1)}, bf16[960,256]{1,0:T(8,128)(2,1)S(1)}, u32[]{:S(2)}, u32[]{:S(2)}) collective-permute-start(bf16[960,256]{1,0:T(8,128)(2,1)S(1)} %get-tuple-element.227.refs_4_), channel_id=1, source_target_pairs={{0,16},{8,24},{16,0},{24,8},{1,17},{9,25},{17,1},{25,9},{2,18},{10... | collective-permute-start | bytes 1474568 | tf_op jit(solution)/shard_map/ppermute | solution.py:37
  81.8 24.6 %collective-permute-start.16 = (bf16[960,256]{1,0:T(8,128)(2,1)}, bf16[960,256]{1,0:T(8,128)(2,1)S(1)}, u32[]{:S(2)}, u32[]{:S(2)}) collective-permute-start(bf16[960,256]{1,0:T(8,128)(2,1)} %get-tuple-element.232.x_b.refs_4_), channel_id=1, source_target_pairs={{0,16},{8,24},{16,0},{24,8},{1,17},{9,25},{17,1},{25,9},{2,18},{10... | collective-permute-start | bytes 1474568 | tf_op jit(solution)/shard_map/ppermute | solution.py:37
  83.0 9.5 %collective-permute-start.18 = (bf16[960,256]{1,0:T(8,128)(2,1)S(1)}, bf16[960,256]{1,0:T(8,128)(2,1)S(1)}, u32[]{:S(2)}, u32[]{:S(2)}) collective-permute-start(bf16[960,256]{1,0:T(8,128)(2,1)S(1)} %copy-done.84), channel_id=1, source_target_pairs={{0,8},{8,0},{16,24},{24,16},{1,9},{9,1},{17,25},{25,17},{2,10},{10... | collective-permute-start | bytes 1474568 | tf_op jit(solution)/shard_map/ppermute | solution.py:37
  83.1 9.4 %collective-permute-start.19 = (bf16[960,256]{1,0:T(8,128)(2,1)S(1)}, bf16[960,256]{1,0:T(8,128)(2,1)S(1)}, u32[]{:S(2)}, u32[]{:S(2)}) collective-permute-start(bf16[960,256]{1,0:T(8,128)(2,1)S(1)} %collective-permute-done.17.refs_1_.refs_2_), channel_id=1, source_target_pairs={{0,8},{8,0},{16,24},{24,16},{1,9},{9,1},{17,25},{25,17},{2,10},{10... | collective-permute-start | bytes 1474568 | tf_op jit(solution)/shard_map/ppermute | solution.py:37
  91.9 15.1 %collective-permute-start.25 = (bf16[960,256]{1,0:T(8,128)(2,1)S(1)}, bf16[960,256]{1,0:T(8,128)(2,1)S(1)}, u32[]{:S(2)}, u32[]{:S(2)}) collective-permute-start(bf16[960,256]{1,0:T(8,128)(2,1)S(1)} %get-tuple-element.227.refs_4_), channel_id=1, source_target_pairs={{0,8},{8,0},{16,24},{24,16},{1,9},{9,1},{17,25},{25,17},{2,10},{10... | collective-permute-start | bytes 1474568 | tf_op jit(solution)/shard_map/ppermute | solution.py:37
  92.0 14.9 %collective-permute-start.26 = (bf16[960,256]{1,0:T(8,128)(2,1)S(1)}, bf16[960,256]{1,0:T(8,128)(2,1)S(1)}, u32[]{:S(2)}, u32[]{:S(2)}) collective-permute-start(bf16[960,256]{1,0:T(8,128)(2,1)S(1)} %collective-permute-done.22.refs_4_.refs_6_), channel_id=1, source_target_pairs={{0,8},{8,0},{16,24},{24,16},{1,9},{9,1},{17,25},{25,17},{2,10},{10... | collective-permute-start | bytes 1474568 | tf_op jit(solution)/shard_map/ppermute | solution.py:37
  106.4 1.9 collective-permute-start.23
  106.5 3.2 %collective-permute-start.24 = (bf16[960,256]{1,0:T(8,128)(2,1)S(1)}, bf16[960,256]{1,0:T(8,128)(2,1)S(1)}, u32[]{:S(2)}, u32[]{:S(2)}) collective-permute-start(bf16[960,256]{1,0:T(8,128)(2,1)S(1)} %collective-permute-done.16.refs_1_.refs_6_), channel_id=1, source_target_pairs={{0,8},{8,0},{16,24},{24,16},{1,9},{9,1},{17,25},{25,17},{2,10},{10... | collective-permute-start | bytes 1474568 | tf_op jit(solution)/shard_map/ppermute | solution.py:37
  107.0 16.1 %collective-permute-start.28 = (bf16[2,960,256]{2,1,0:T(8,128)(2,1)}, bf16[2,960,256]{2,1,0:T(8,128)(2,1)S(1)}, u32[]{:S(2)}, u32[]{:S(2)}) collective-permute-start(bf16[2,960,256]{2,1,0:T(8,128)(2,1)} %get-tuple-element.239), channel_id=1, source_target_pairs={{0,8},{8,0},{16,24},{24,16},{1,9},{9,1},{17,25},{25,17},{2,10},{10... | collective-permute-start | bytes 2949128 | tf_op jit(solution)/shard_map/ppermute | solution.py:37
  107.1 17.1 %collective-permute-start.29 = (bf16[2,960,256]{2,1,0:T(8,128)(2,1)}, bf16[2,960,256]{2,1,0:T(8,128)(2,1)S(1)}, u32[]{:S(2)}, u32[]{:S(2)}) collective-permute-start(bf16[2,960,256]{2,1,0:T(8,128)(2,1)} %get-tuple-element.243), channel_id=1, source_target_pairs={{0,8},{8,0},{16,24},{24,16},{1,9},{9,1},{17,25},{25,17},{2,10},{10... | collective-permute-start | bytes 2949128 | tf_op jit(solution)/shard_map/ppermute | solution.py:37
  122.5 12.6 %collective-permute-start.27 = (bf16[2,960,256]{2,1,0:T(8,128)(2,1)}, bf16[2,960,256]{2,1,0:T(8,128)(2,1)S(1)}, u32[]{:S(2)}, u32[]{:S(2)}) collective-permute-start(bf16[2,960,256]{2,1,0:T(8,128)(2,1)} %get-tuple-element.238), channel_id=1, source_target_pairs={{0,8},{8,0},{16,24},{24,16},{1,9},{9,1},{17,25},{25,17},{2,10},{10... | collective-permute-start | bytes 2949128 | tf_op jit(solution)/shard_map/ppermute | solution.py:37
  122.7 13.4 %collective-permute-start.30 = (bf16[2,960,256]{2,1,0:T(8,128)(2,1)}, bf16[2,960,256]{2,1,0:T(8,128)(2,1)S(1)}, u32[]{:S(2)}, u32[]{:S(2)}) collective-permute-start(bf16[2,960,256]{2,1,0:T(8,128)(2,1)} %get-tuple-element.253), channel_id=1, source_target_pairs={{0,8},{8,0},{16,24},{24,16},{1,9},{9,1},{17,25},{25,17},{2,10},{10... | collective-permute-start | bytes 2949128 | tf_op jit(solution)/shard_map/ppermute | solution.py:37
  123.3 28.4 %collective-permute-start.36 = (bf16[960,256]{1,0:T(8,128)(2,1)S(1)}, bf16[960,256]{1,0:T(8,128)(2,1)S(1)}, u32[]{:S(2)}, u32[]{:S(2)}) collective-permute-start(bf16[960,256]{1,0:T(8,128)(2,1)S(1)} %fusion.6), channel_id=1, source_target_pairs={{0,16},{8,24},{16,0},{24,8},{1,17},{9,25},{17,1},{25,9},{2,18},{10... | collective-permute-start | bytes 1474568 | tf_op jit(solution)/shard_map/ppermute | solution.py:37
  124.3 29.0 %collective-permute-start.37 = (bf16[960,256]{1,0:T(8,128)(2,1)S(1)}, bf16[960,256]{1,0:T(8,128)(2,1)S(1)}, u32[]{:S(2)}, u32[]{:S(2)}) collective-permute-start(bf16[960,256]{1,0:T(8,128)(2,1)S(1)} %fusion.5), channel_id=1, source_target_pairs={{0,16},{8,24},{16,0},{24,8},{1,17},{9,25},{17,1},{25,9},{2,18},{10... | collective-permute-start | bytes 1474568 | tf_op jit(solution)/shard_map/ppermute | solution.py:37
  133.5 16.8 %collective-permute-start.34 = (bf16[4,120,640]{2,1,0:T(8,128)(2,1)}, bf16[4,120,640]{2,1,0:T(8,128)(2,1)S(1)}, u32[]{:S(2)}, u32[]{:S(2)}) collective-permute-start(bf16[4,120,640]{2,1,0:T(8,128)(2,1)} %get-tuple-element.250), channel_id=1, source_target_pairs={{0,1},{1,0},{2,3},{3,2},{4,5},{5,4},{6,7},{7,6},{8,9},{9,8},{10,11... | collective-permute-start | bytes 1843208 | tf_op jit(solution)/shard_map/ppermute | solution.py:37
  135.2 26.9 %collective-permute-start.32 = (bf16[960,256]{1,0:T(8,128)(2,1)S(1)}, bf16[960,256]{1,0:T(8,128)(2,1)S(1)}, u32[]{:S(2)}, u32[]{:S(2)}) collective-permute-start(bf16[960,256]{1,0:T(8,128)(2,1)S(1)} %fusion.4), channel_id=1, source_target_pairs={{0,16},{8,24},{16,0},{24,8},{1,17},{9,25},{17,1},{25,9},{2,18},{10... | collective-permute-start | bytes 1474568 | tf_op jit(solution)/shard_map/ppermute | solution.py:37
  149.6 30.3 %collective-permute-start.31 = (bf16[4,120,1280]{2,1,0:T(8,128)(2,1)}, bf16[4,120,1280]{2,1,0:T(8,128)(2,1)S(1)}, u32[]{:S(2)}, u32[]{:S(2)}) collective-permute-start(bf16[4,120,1280]{2,1,0:T(8,128)(2,1)} %get-tuple-element.262), channel_id=1, source_target_pairs={{0,1},{1,0},{2,3},{3,2},{4,5},{5,4},{6,7},{7,6},{8,9},{9,8},{10,11... | collective-permute-start | bytes 3686408 | tf_op jit(solution)/shard_map/ppermute | solution.py:37
  150.3 24.1 %collective-permute-start.33 = (bf16[960,256]{1,0:T(8,128)(2,1)S(1)}, bf16[960,256]{1,0:T(8,128)(2,1)S(1)}, u32[]{:S(2)}, u32[]{:S(2)}) collective-permute-start(bf16[960,256]{1,0:T(8,128)(2,1)S(1)} %fusion.3), channel_id=1, source_target_pairs={{0,16},{8,24},{16,0},{24,8},{1,17},{9,25},{17,1},{25,9},{2,18},{10... | collective-permute-start | bytes 1474568 | tf_op jit(solution)/shard_map/ppermute | solution.py:37
  151.7 7.7 %collective-permute-start.35 = (bf16[2,120,640]{2,1,0:T(8,128)(2,1)S(1)}, bf16[2,120,640]{2,1,0:T(8,128)(2,1)S(1)}, u32[]{:S(2)}, u32[]{:S(2)}) collective-permute-start(bf16[2,120,640]{2,1,0:T(8,128)(2,1)S(1)} %add_convert_fusion.3), channel_id=1, source_target_pairs={{0,2},{1,3},{2,0},{3,1},{4,6},{5,7},{6,4},{7,5},{8,10},{9,11},{10,... | collective-permute-start | bytes 921608 | tf_op jit(solution)/shard_map/ppermute | solution.py:37
  159.4 14.5 %collective-permute-start.38 = (bf16[1,120,640]{2,1,0:T(8,128)(2,1)S(1)}, bf16[1,120,640]{2,1,0:T(8,128)(2,1)S(1)}, u32[]{:S(2)}, u32[]{:S(2)}) collective-permute-start(bf16[1,120,640]{2,1,0:T(8,128)(2,1)S(1)} %add_convert_fusion.9), channel_id=1, source_target_pairs={{0,4},{1,5},{2,6},{3,7},{4,0},{5,1},{6,2},{7,3},{8,12},{9,13},{10,... | collective-permute-start | bytes 460808 | tf_op jit(solution)/shard_map/ppermute | solution.py:37
  173.9 5.0 %collective-permute-start.40 = (bf16[2,640,256]{2,1,0:T(8,128)(2,1)}, bf16[2,640,256]{2,1,0:T(8,128)(2,1)S(1)}, u32[]{:S(2)}, u32[]{:S(2)}) collective-permute-start(bf16[2,640,256]{2,1,0:T(8,128)(2,1)} %get-tuple-element.287), channel_id=1, source_target_pairs={{0,8},{8,0},{16,24},{24,16},{1,9},{9,1},{17,25},{25,17},{2,10},{10... | collective-permute-start | bytes 1966088 | tf_op jit(solution)/shard_map/ppermute | solution.py:37
  174.1 19.4 %collective-permute-start.41 = (bf16[1,120,640]{2,1,0:T(8,128)(2,1)S(1)}, bf16[1,120,640]{2,1,0:T(8,128)(2,1)S(1)}, u32[]{:S(2)}, u32[]{:S(2)}) collective-permute-start(bf16[1,120,640]{2,1,0:T(8,128)(2,1)S(1)} %add_convert_fusion.8), channel_id=1, source_target_pairs={{0,4},{1,5},{2,6},{3,7},{4,0},{5,1},{6,2},{7,3},{8,12},{9,13},{10,... | collective-permute-start | bytes 460808 | tf_op jit(solution)/shard_map/ppermute | solution.py:37
  178.9 14.7 %collective-permute-start.42 = (bf16[640,256]{1,0:T(8,128)(2,1)S(1)}, bf16[640,256]{1,0:T(8,128)(2,1)S(1)}, u32[]{:S(2)}, u32[]{:S(2)}) collective-permute-start(bf16[640,256]{1,0:T(8,128)(2,1)S(1)} %fusion.13), channel_id=1, source_target_pairs={{0,16},{8,24},{16,0},{24,8},{1,17},{9,25},{17,1},{25,9},{2,18},{10... | collective-permute-start | bytes 983048 | tf_op jit(solution)/shard_map/ppermute | solution.py:37
  180.0 19.9 %collective-permute-start.39 = (bf16[2,120,1280]{2,1,0:T(8,128)(2,1)S(1)}, bf16[2,120,1280]{2,1,0:T(8,128)(2,1)S(1)}, u32[]{:S(2)}, u32[]{:S(2)}) collective-permute-start(bf16[2,120,1280]{2,1,0:T(8,128)(2,1)S(1)} %add_convert_fusion), channel_id=1, source_target_pairs={{0,2},{1,3},{2,0},{3,1},{4,6},{5,7},{6,4},{7,5},{8,10},{9,11},{10,... | collective-permute-start | bytes 1843208 | tf_op jit(solution)/shard_map/ppermute | solution.py:37
  193.5 6.5 %collective-permute-start.44 = (bf16[2,640,256]{2,1,0:T(8,128)(2,1)}, bf16[2,640,256]{2,1,0:T(8,128)(2,1)S(1)}, u32[]{:S(2)}, u32[]{:S(2)}) collective-permute-start(bf16[2,640,256]{2,1,0:T(8,128)(2,1)} %get-tuple-element.302), channel_id=1, source_target_pairs={{0,8},{8,0},{16,24},{24,16},{1,9},{9,1},{17,25},{25,17},{2,10},{10... | collective-permute-start | bytes 1966088 | tf_op jit(solution)/shard_map/ppermute | solution.py:37
  200.1 9.0 %collective-permute-start.45 = (bf16[2,8,32,1920]{3,2,1,0:T(8,128)(2,1)}, bf16[2,8,32,1920]{3,2,1,0:T(8,128)(2,1)S(1)}, u32[]{:S(2)}, u32[]{:S(2)}) collective-permute-start(bf16[2,8,32,1920]{3,2,1,0:T(8,128)(2,1)} %get-tuple-element.305), channel_id=1, source_target_pairs={{0,8},{8,0},{16,24},{24,16},{1,9},{9,1},{17,25},{25,17},{2,10},{10... | collective-permute-start | bytes 5898248 | tf_op jit(solution)/shard_map/ppermute | solution.py:37
  200.7 22.1 %collective-permute-start.47 = (bf16[2,120,640]{2,1,0:T(8,128)(2,1)S(1)}, bf16[2,120,640]{2,1,0:T(8,128)(2,1)S(1)}, u32[]{:S(2)}, u32[]{:S(2)}) collective-permute-start(bf16[2,120,640]{2,1,0:T(8,128)(2,1)S(1)} %pad_maximum_fusion.7), channel_id=1, source_target_pairs={{0,2},{1,3},{2,0},{3,1},{4,6},{5,7},{6,4},{7,5},{8,10},{9,11},{10,... | collective-permute-start | bytes 921608 | tf_op jit(solution)/shard_map/ppermute | solution.py:37
  201.1 21.6 %collective-permute-start.43 = (bf16[1,120,1280]{2,1,0:T(8,128)(2,1)S(1)}, bf16[1,120,1280]{2,1,0:T(8,128)(2,1)S(1)}, u32[]{:S(2)}, u32[]{:S(2)}) collective-permute-start(bf16[1,120,1280]{2,1,0:T(8,128)(2,1)S(1)} %add_convert_fusion.2), channel_id=1, source_target_pairs={{0,4},{1,5},{2,6},{3,7},{4,0},{5,1},{6,2},{7,3},{8,12},{9,13},{10,... | collective-permute-start | bytes 921608 | tf_op jit(solution)/shard_map/ppermute | solution.py:37
  203.7 10.6 %collective-permute-start.46 = (bf16[640,256]{1,0:T(8,128)(2,1)S(1)}, bf16[640,256]{1,0:T(8,128)(2,1)S(1)}, u32[]{:S(2)}, u32[]{:S(2)}) collective-permute-start(bf16[640,256]{1,0:T(8,128)(2,1)S(1)} %fusion.12), channel_id=1, source_target_pairs={{0,16},{8,24},{16,0},{24,8},{1,17},{9,25},{17,1},{25,9},{2,18},{10... | collective-permute-start | bytes 983048 | tf_op jit(solution)/shard_map/ppermute | solution.py:37
  209.5 25.9 %collective-permute-start.48 = (bf16[8,32,1920]{2,1,0:T(8,128)(2,1)S(1)}, bf16[8,32,1920]{2,1,0:T(8,128)(2,1)S(1)}, u32[]{:S(2)}, u32[]{:S(2)}) collective-permute-start(bf16[8,32,1920]{2,1,0:T(8,128)(2,1)S(1)} %fusion), channel_id=1, source_target_pairs={{0,16},{8,24},{16,0},{24,8},{1,17},{9,25},{17,1},{25,9},{2,18},{10... | collective-permute-start | bytes 2949128 | tf_op jit(solution)/shard_map/ppermute | solution.py:37
  222.7 2.4 collective-permute-start.49
  223.0 20.0 %collective-permute-start.56 = (bf16[1,120,1280]{2,1,0:T(8,128)(2,1)S(1)}, bf16[1,120,1280]{2,1,0:T(8,128)(2,1)S(1)}, u32[]{:S(2)}, u32[]{:S(2)}) collective-permute-start(bf16[1,120,1280]{2,1,0:T(8,128)(2,1)S(1)} %add_convert_fusion.1), channel_id=1, source_target_pairs={{0,4},{1,5},{2,6},{3,7},{4,0},{5,1},{6,2},{7,3},{8,12},{9,13},{10,... | collective-permute-start | bytes 921608 | tf_op jit(solution)/shard_map/ppermute | solution.py:37
  223.3 21.3 %collective-permute-start.52 = (bf16[4,120,640]{2,1,0:T(8,128)(2,1)S(1)}, bf16[4,120,640]{2,1,0:T(8,128)(2,1)S(1)}, u32[]{:S(2)}, u32[]{:S(2)}) collective-permute-start(bf16[4,120,640]{2,1,0:T(8,128)(2,1)S(1)} %pad_maximum_fusion.4.even), channel_id=1, source_target_pairs={{0,1},{1,0},{2,3},{3,2},{4,5},{5,4},{6,7},{7,6},{8,9},{9,8},{10,11... | collective-permute-start | bytes 1843208 | tf_op jit(solution)/shard_map/ppermute | solution.py:37
  225.1 15.8 %collective-permute-start.50 = (bf16[8,32,640]{2,1,0:T(8,128)(2,1)S(1)}, bf16[8,32,640]{2,1,0:T(8,128)(2,1)S(1)}, u32[]{:S(2)}, u32[]{:S(2)}) collective-permute-start(bf16[8,32,640]{2,1,0:T(8,128)(2,1)S(1)} %fusion.11), channel_id=1, source_target_pairs={{0,16},{8,24},{16,0},{24,8},{1,17},{9,25},{17,1},{25,9},{2,18},{10... | collective-permute-start | bytes 983048 | tf_op jit(solution)/shard_map/ppermute | solution.py:37
  241.1 15.4 %collective-permute-start.51 = (bf16[4,32,2560]{2,1,0:T(8,128)(2,1)S(1)}, bf16[4,32,2560]{2,1,0:T(8,128)(2,1)S(1)}, u32[]{:S(2)}, u32[]{:S(2)}) collective-permute-start(bf16[4,32,2560]{2,1,0:T(8,128)(2,1)S(1)} %pad_maximum_fusion.2), channel_id=1, source_target_pairs={{0,1},{1,0},{2,3},{3,2},{4,5},{5,4},{6,7},{7,6},{8,9},{9,8},{10,11... | collective-permute-start | bytes 1966088 | tf_op jit(solution)/shard_map/ppermute | solution.py:37
  243.0 17.1 %collective-permute-start.57 = (bf16[2,120,1280]{2,1,0:T(8,128)(2,1)S(1)}, bf16[2,120,1280]{2,1,0:T(8,128)(2,1)S(1)}, u32[]{:S(2)}, u32[]{:S(2)}) collective-permute-start(bf16[2,120,1280]{2,1,0:T(8,128)(2,1)S(1)} %pad_maximum_fusion.5), channel_id=1, source_target_pairs={{0,2},{1,3},{2,0},{3,1},{4,6},{5,7},{6,4},{7,5},{8,10},{9,11},{10,... | collective-permute-start | bytes 1843208 | tf_op jit(solution)/shard_map/ppermute | solution.py:37
  256.6 9.6 %collective-permute-start.54 = (bf16[1,32,2560]{2,1,0:T(8,128)(2,1)S(1)}, bf16[1,32,2560]{2,1,0:T(8,128)(2,1)S(1)}, u32[]{:S(2)}, u32[]{:S(2)}) collective-permute-start(bf16[1,32,2560]{2,1,0:T(8,128)(2,1)S(1)} %get-tuple-element.347), channel_id=1, source_target_pairs={{0,2},{1,3},{2,0},{3,1},{4,6},{5,7},{6,4},{7,5},{8,10},{9,11},{10,... | collective-permute-start | bytes 491528 | tf_op jit(solution)/shard_map/ppermute | solution.py:37
  258.3 8.9 %collective-permute-start.53 = (bf16[1,32,2560]{2,1,0:T(8,128)(2,1)S(1)}, bf16[1,32,2560]{2,1,0:T(8,128)(2,1)S(1)}, u32[]{:S(2)}, u32[]{:S(2)}) collective-permute-start(bf16[1,32,2560]{2,1,0:T(8,128)(2,1)S(1)} %get-tuple-element.348), channel_id=1, source_target_pairs={{0,6},{1,7},{2,4},{3,5},{4,2},{5,3},{6,0},{7,1},{8,14},{9,15},{10,... | collective-permute-start | bytes 491528 | tf_op jit(solution)/shard_map/ppermute | solution.py:37
  258.6 13.7 %collective-permute-start.55 = (bf16[1,32,2560]{2,1,0:T(8,128)(2,1)S(1)}, bf16[1,32,2560]{2,1,0:T(8,128)(2,1)S(1)}, u32[]{:S(2)}, u32[]{:S(2)}) collective-permute-start(bf16[1,32,2560]{2,1,0:T(8,128)(2,1)S(1)} %get-tuple-element.353), channel_id=1, source_target_pairs={{0,4},{1,5},{2,6},{3,7},{4,0},{5,1},{6,2},{7,3},{8,12},{9,13},{10,... | collective-permute-start | bytes 491528 | tf_op jit(solution)/shard_map/ppermute | solution.py:37
  260.3 26.3 %collective-permute-start.61 = (bf16[4,120,1280]{2,1,0:T(8,128)(2,1)S(1)}, bf16[4,120,1280]{2,1,0:T(8,128)(2,1)S(1)}, u32[]{:S(2)}, u32[]{:S(2)}) collective-permute-start(bf16[4,120,1280]{2,1,0:T(8,128)(2,1)S(1)} %pad_maximum_fusion.1.even), channel_id=1, source_target_pairs={{0,1},{1,0},{2,3},{3,2},{4,5},{5,4},{6,7},{7,6},{8,9},{9,8},{10,11... | collective-permute-start | bytes 3686408 | tf_op jit(solution)/shard_map/ppermute | solution.py:37
  272.4 8.7 %collective-permute-start.60 = (bf16[1,32,2560]{2,1,0:T(8,128)(2,1)S(1)}, bf16[1,32,2560]{2,1,0:T(8,128)(2,1)S(1)}, u32[]{:S(2)}, u32[]{:S(2)}) collective-permute-start(bf16[1,32,2560]{2,1,0:T(8,128)(2,1)S(1)} %add_convert_fusion.4), channel_id=1, source_target_pairs={{0,6},{1,7},{2,4},{3,5},{4,2},{5,3},{6,0},{7,1},{8,14},{9,15},{10,... | collective-permute-start | bytes 491528 | tf_op jit(solution)/shard_map/ppermute | solution.py:37
  275.9 7.2 %collective-permute-start.59 = (bf16[1,32,2560]{2,1,0:T(8,128)(2,1)S(1)}, bf16[1,32,2560]{2,1,0:T(8,128)(2,1)S(1)}, u32[]{:S(2)}, u32[]{:S(2)}) collective-permute-start(bf16[1,32,2560]{2,1,0:T(8,128)(2,1)S(1)} %add_convert_fusion.4), channel_id=1, source_target_pairs={{0,2},{1,3},{2,0},{3,1},{4,6},{5,7},{6,4},{7,5},{8,10},{9,11},{10,... | collective-permute-start | bytes 491528 | tf_op jit(solution)/shard_map/ppermute | solution.py:37
  275.9 10.7 %collective-permute-start.58 = (bf16[1,32,2560]{2,1,0:T(8,128)(2,1)S(1)}, bf16[1,32,2560]{2,1,0:T(8,128)(2,1)S(1)}, u32[]{:S(2)}, u32[]{:S(2)}) collective-permute-start(bf16[1,32,2560]{2,1,0:T(8,128)(2,1)S(1)} %add_convert_fusion.4), channel_id=1, source_target_pairs={{0,4},{1,5},{2,6},{3,7},{4,0},{5,1},{6,2},{7,3},{8,12},{9,13},{10,... | collective-permute-start | bytes 491528 | tf_op jit(solution)/shard_map/ppermute | solution.py:37
  286.7 15.1 %collective-permute-start.62 = (bf16[4,32,2560]{2,1,0:T(8,128)(2,1)S(1)}, bf16[4,32,2560]{2,1,0:T(8,128)(2,1)S(1)}, u32[]{:S(2)}, u32[]{:S(2)}) collective-permute-start(bf16[4,32,2560]{2,1,0:T(8,128)(2,1)S(1)} %pad_maximum_fusion.3.even), channel_id=1, source_target_pairs={{0,1},{1,0},{2,3},{3,2},{4,5},{5,4},{6,7},{7,6},{8,9},{9,8},{10,11... | collective-permute-start | bytes 1966088 | tf_op jit(solution)/shard_map/ppermute | solution.py:37
  (101 other events, 821.3 us)

commit v7 on v6

--- a/solution.py
+++ b/solution.py
@@ -151,7 +151,7 @@
         return held, swap(held, "rep", self.ranks, 1)
 
 
-def call(kernel, name, out_shape, *, grid=(1,), prefetch=0, in_specs, out_specs, scratch=(), micros=1, vmem=36):
+def call(kernel, name, out_shape, *, grid=(1,), prefetch=0, in_specs, out_specs, scratch=(), micros=1, vmem=36, free=()):
     def lies(shape):
         return pltpu.HBM(shape.shape, shape.dtype)
 
@@ -173,8 +173,8 @@
 
     def placed(*args):
         rest = [
-            arg if spec is NEAR else pltpu.with_memory_space_constraint(arg, pltpu.HBM)
-            for arg, spec in zip(args[prefetch:], in_specs, strict=True)
+            arg if spec is NEAR or i in free else pltpu.with_memory_space_constraint(arg, pltpu.HBM)
+            for i, (arg, spec) in enumerate(zip(args[prefetch:], in_specs, strict=True))
         ]
         return run(*args[:prefetch], *rest)
 
@@ -649,7 +649,8 @@
         keys_values_kernel,
         "keys_values",
         (shape_of((width, rows)), shape_of((kw2, span)), shape_of((kw2, span)), shape_of((width, LANES))),
-        prefetch=1,
+        free=range(1, 5),
+            prefetch=1,
         in_specs=[NEAR] + [whole(kv_shard.shape)] * 4 + [table, table],
         out_specs=(whole((width, rows)), whole((kw2, span)), whole((kw2, span)), gain_spec),
         scratch=[pltpu.VMEM((width, kw2 + LANES), LOW)],
@@ -661,7 +662,8 @@
         queries_kernel,
         "queries",
         shape_of((width, rows)),
-        prefetch=1,
+        free=range(1, 5),
+            prefetch=1,
         in_specs=[whole((width, rows))] + [whole((shard, width))] * 4 + [table, table],
         out_specs=whole((width, rows)),
         scratch=[pltpu.VMEM((width, width), LOW)],
@@ -679,6 +681,7 @@
             functools.partial(attend_kernel, s),
             "attend",
             (shape_of((kv_heads, length, per * span)), shape_of((width, span))),
+            free=range(1, 5),
             prefetch=3,
             grid=(kv_heads,),
             in_specs=[q_spec(s)] + [head] * 4,
@@ -692,6 +695,7 @@
             middle_kernel,
             "middle",
             (shape_of((width, span), FULL), shape_of((width, span))),
+            free=range(1, 5),
             prefetch=1,
             in_specs=[act] + [whole((shard, width))] * 4 + [one_seq(s), gain_spec],
             out_specs=(act, act),
@@ -738,6 +742,7 @@
             other_blocks_kernel,
             "other_blocks",
             (act_shape, half_shape, act_shape, half_shape, ff_shape, ff_shape, ff_shape),
+            free=range(6),
             grid=(GROUP - 1,),
             in_specs=[ANY] * 6 + [NEAR] * 4,
             out_specs=(act, half, act, half) + (per_block,) * 3,
@@ -805,6 +810,7 @@
                 shape_of((16, span), FULL),
                 shape_of((8, width), FULL),
             ),
+            free=(3, 4),
             prefetch=1,
             in_specs=[NEAR, NEAR, one_seq(s), first, act, NEAR] + [NEAR] * 5,
             out_specs=(act, act, act, whole((16, span)), whole((8, width))),
@@ -877,7 +883,8 @@
         key_weight_kernel,
         "key_weights",
         spread_out(kw2) + (shape_of((seq_count, width, span), FULL),),
-        prefetch=1,
+        free=range(1, 7),
+            prefetch=1,
         in_specs=[NEAR]
         + [whole((kw2, span)), first, whole((kw2, span))] * 2
         + [table, table, seqs]
@@ -915,6 +922,7 @@
             kernel,
             name,
             (shape_of((width, ff), FULL),) * outs,
+            free=range(2),
             prefetch=1,
             in_specs=[whole((4, part, columns))] * 2,
             out_specs=(whole((width, ff)),) * outs,
@@ -943,7 +951,8 @@
         attention_done_kernel,
         "attention_done",
         (shape_of((shard, width), FULL),) * 2 + (shape_of((kw, shard), FULL),) * 2 + (shape_of((8, shard), FULL),),
-        prefetch=1,
+        free=range(2),
+            prefetch=1,
         in_specs=[whole((4, piece, 2 * width + kw2))] * 2,
         out_specs=(whole((shard, width)),) * 2 + (whole((kw, shard)),) * 2 + (whole((8, shard)),),
         scratch=[pltpu.VMEM((grown, 2 * width + kw2), FULL)],

time: 313 us -> 309 us (0.987)
  waiting for transfers between devices: 64.9 us -> 77.5 us
  local copies, waits for them, and re-layouts: 12.6 us -> 3.01 us
  Pallas kernels: 167 us -> 161 us
    ppermute x63, waiting for transfers between devices: 64.9 us -> 77.5 us  [swap(): return lax.ppermute(values, axis, [(i, i ^ mask) for i in range(count)])]
    unnamed x204 -> x146, local copies, waits for them, and re-layouts: 9.84 us -> 0.29 us
    pallas_call x24, Pallas kernels: 167 us -> 161 us  [placed(): return run(*args[:prefetch], *rest)]
  transfers between devices with their start and end apart: 63 -> 63, of which waited for: 21 -> 21; matrix products, arithmetic and copies ran while one was open for 2% -> 2% of each run, Pallas kernels for 52% -> 51%
where the time goes in v7:
time: 309 us; the launch traced here: 305 us
  Pallas kernels  161 us (52%)
  waiting for transfers between devices  77.5 us (25%)
  starting transfers between devices  54.6 us (18%)
  other arithmetic  6.84 us (2%)
    pallas_call x24, Pallas kernels, placed(): return run(*args[:prefetch], *rest)  161 us
    ppermute x63, waiting for transfers between devices, swap(): return lax.ppermute(values, axis, [(i, i ^ mask) for i in range(count)])  77.5 us
    ppermute x63, starting transfers between devices, swap(): return lax.ppermute(values, axis, [(i, i ^ mask) for i in range(count)])  54.6 us
  transfers between devices with their start and end apart: 63, of which 21 were waited for; matrix products, arithmetic and copies ran while one was open for 2% of the time, Pallas kernels for 51%

profile of v7, /device:TPU:0, one launch (start us, length us, event | category | flops | bytes accessed | tf_op | source)
XLA Modules:
  0.0 304.6 jit_solution(2382213461036176453)
XLA Ops:
  2.6 2.1 pack.1.b0.refs_10_
  4.7 3.0 collective-permute-start
  7.9 4.8 %flip_two.1 = (bf16[1280,960]{1,0:T(8,128)(2,1)}, bf16[960,1280]{1,0:T(8,128)(2,1)}) custom-call(bf16[960,640]{1,0:T(8,128)(2,1)} %wg_ref, bf16[960,640]{1,0:T(8,128)(2,1)} %wu_ref.1), custom_call_target="tpu_custom_call" | custom-call | flops 8000000000 | bytes 1024 | tf_op jit(solution)/shard_map/flip_two/pallas_call | solution.py:179
  12.7 2.9 flip_one.1.wd_ref.refs_9_
  15.6 1.7 collective-permute-done.b2.refs_12_
  19.5 3.6 %keys_values.1 = (bf16[960,512]{1,0:T(8,128)(2,1)}, bf16[640,256]{1,0:T(8,128)(2,1)}, bf16[640,256]{1,0:T(8,128)(2,1)}, bf16[960,128]{1,0:T(8,128)(2,1)}) custom-call(s32[2]{0:T(128)S(1)} %pad_add_fusion.ranks, bf16[2,960,256]{2,1,0:T(8,128)(2,1)S(1)} %bitcast.109, bf16[240,768]{1,0:T(8,128)(2,1)S(1)} %copy-done.38, ...), custom_call_target="tpu_custom_call" | custom-call | flops 8600000512 | bytes 1024 | tf_op jit(solution)/shard_map/keys_values/pallas_call | solution.py:179
  23.1 3.9 %collective-permute-done.3.b2.q2 = bf16[240,960]{1,0:T(8,128)(2,1)S(1)} collective-permute-done((bf16[240,960]{1,0:T(8,128)(2,1)S(1)}, bf16[240,960]{1,0:T(8,128)(2,1)S(1)}, u32[]{:S(2)}, u32[]{:S(2)}) %collective-permute-start.3) | collective-permute-done | bytes 460832 | tf_op jit(solution)/shard_map/ppermute | solution.py:37
  27.5 1.7 collective-permute-start.6
  29.5 4.4 %queries.1.q_ref = bf16[960,512]{1,0:T(8,128)(2,1)} custom-call(s32[2]{0:T(128)S(1)} %pad_add_fusion.ranks, bf16[960,512]{1,0:T(8,128)(2,1)} %get-tuple-element.184.norm_ref.refs_0_, bf16[240,960]{1,0:T(8,128)(2,1)S(1)} %copy-done.5, bf16[240,960]{1,0:T(8,128)(2,1)S(1)} %collective-permute-done.4.b1.q1, bf16[240,960]{1,0:T(8,128)(2,1)S(1)} %collective-permute-done.3.b2.q2, ...), custom_call_target="tpu_custom_call" | custom-call | flops 200000000 | bytes 1024 | tf_op jit(solution)/shard_map/queries/pallas_call | solution.py:179
  33.9 4.4 %collective-permute-done.6.b2 = bf16[640,256]{1,0:T(8,128)(2,1)S(1)} collective-permute-done((bf16[640,256]{1,0:T(8,128)(2,1)}, bf16[640,256]{1,0:T(8,128)(2,1)S(1)}, u32[]{:S(2)}, u32[]{:S(2)}) %collective-permute-start.6) | collective-permute-done | bytes 327712 | tf_op jit(solution)/shard_map/ppermute | solution.py:37
  38.8 1.7 collective-permute-start.12
  40.5 11.2 %attend.2 = (bf16[5,1024,768]{2,1,0:T(8,128)(2,1)}, bf16[960,256]{1,0:T(8,128)(2,1)}) custom-call(s32[2]{0:T(128)S(1)} %pad_add_fusion.ranks, s32[2,4]{1,0:T(2,128)S(1)} %copy-done.18, s32[2,2]{1,0:T(2,128)S(1)} %copy-done.19, bf16[960,512]{1,0:T(8,128)(2,1)} %queries.1.q_ref, bf16[640,256]{1,0:T(8,128)(2,1)S(1)} %copy-done.12, ...), custom_call_target="tpu_custom_call" | custom-call | flops 200000000 | bytes 1024 | tf_op jit(solution)/shard_map/attend/pallas_call | solution.py:179
  52.3 2.7 collective-permute-done.12.b2
  55.6 1.8 collective-permute-start.15
  57.4 3.9 %middle.2 = (f32[960,256]{1,0:T(8,128)}, bf16[960,256]{1,0:T(8,128)(2,1)}) custom-call(s32[2]{0:T(128)S(1)} %pad_add_fusion.ranks, bf16[960,256]{1,0:T(8,128)(2,1)} %get-tuple-element.195.att_ref.att_a, bf16[240,960]{1,0:T(8,128)(2,1)S(1)} %copy-done.23, bf16[240,960]{1,0:T(8,128)(2,1)S(1)} %collective-permute-done.10.b1, ...), custom_call_target="tpu_custom_call" | custom-call | flops 6000000000 | bytes 1024 | tf_op jit(solution)/shard_map/middle/pallas_call | solution.py:179
  61.3 1.4 collective-permute-start.17
  62.7 11.0 %attend.3 = (bf16[5,1024,768]{2,1,0:T(8,128)(2,1)}, bf16[960,256]{1,0:T(8,128)(2,1)}) custom-call(s32[2]{0:T(128)S(1)} %pad_add_fusion.ranks, s32[2,4]{1,0:T(2,128)S(1)} %copy-done.18, s32[2,2]{1,0:T(2,128)S(1)} %copy-done.19, bf16[960,512]{1,0:T(8,128)(2,1)} %queries.1.q_ref, bf16[640,256]{1,0:T(8,128)(2,1)S(1)} %copy-done.10, ...), custom_call_target="tpu_custom_call" | custom-call | flops 200000000 | bytes 1024 | tf_op jit(solution)/shard_map/attend/pallas_call | solution.py:179
  75.0 4.5 %middle.3 = (f32[960,256]{1,0:T(8,128)}, bf16[960,256]{1,0:T(8,128)(2,1)}) custom-call(s32[2]{0:T(128)S(1)} %pad_add_fusion.ranks, bf16[960,256]{1,0:T(8,128)(2,1)} %get-tuple-element.215.att_ref.att_b, bf16[240,960]{1,0:T(8,128)(2,1)S(1)} %copy-done.23, bf16[240,960]{1,0:T(8,128)(2,1)S(1)} %collective-permute-done.10.b1, ...), custom_call_target="tpu_custom_call" | custom-call | flops 6000000000 | bytes 1024 | tf_op jit(solution)/shard_map/middle/pallas_call | solution.py:179
  81.2 8.2 %own_blocks.1 = (bf16[2,960,256]{2,1,0:T(8,128)(2,1)}, bf16[2,960,256]{2,1,0:T(8,128)(2,1)}, bf16[2,640,256]{2,1,0:T(8,128)(2,1)}, bf16[2,640,256]{2,1,0:T(8,128)(2,1)}, bf16[2,640,256]{2,1,0:T(8,128)(2,1)}) custom-call(bf16[960,256]{1,0:T(8,128)(2,1)} %get-tuple-element.254.x_a.refs_0_, bf16[960,256]{1,0:T(8,128)(2,1)} %get-tuple-element.232.x_b.refs_4_, ...), custom_call_target="tpu_custom_call" | custom-call | flops 16000000000 | bytes 1024 | tf_op jit(solution)/shard_map/own_blocks/pallas_call | solution.py:179
  89.5 1.3 collective-permute-done.22.refs_4_.refs_6_
  91.4 13.3 %other_blocks.2 = (bf16[960,256]{1,0:T(8,128)(2,1)}, bf16[2,960,256]{2,1,0:T(8,128)(2,1)}, bf16[960,256]{1,0:T(8,128)(2,1)}, bf16[2,960,256]{2,1,0:T(8,128)(2,1)...) custom-call(bf16[960,256]{1,0:T(8,128)(2,1)S(1)} %collective-permute-done.18.refs_0_.refs_1_, ...), custom_call_target="tpu_custom_call" | custom-call | flops 24000000000 | bytes 1024 | tf_op jit(solution)/shard_map/other_blocks/pallas_call | solution.py:179
  106.7 1.4 collective-permute-done.24.refs_2_.refs_7_
  108.1 13.1 %other_blocks.3 = (bf16[960,256]{1,0:T(8,128)(2,1)}, bf16[2,960,256]{2,1,0:T(8,128)(2,1)}, bf16[960,256]{1,0:T(8,128)(2,1)}, bf16[2,960,256]{2,1,0:T(8,128)(2,1)...) custom-call(bf16[960,256]{1,0:T(8,128)(2,1)S(1)} %collective-permute-done.23.refs_0_.refs_5_, ...), custom_call_target="tpu_custom_call" | custom-call | flops 24000000000 | bytes 1024 | tf_op jit(solution)/shard_map/other_blocks/pallas_call | solution.py:179
  122.0 1.8 collective-permute-start.36
  124.3 7.9 %down_weights.1 = (bf16[4,120,640]{2,1,0:T(8,128)(2,1)}, bf16[2,120,640]{2,1,0:T(8,128)(2,1)}, bf16[1,120,640]{2,1,0:T(8,128)(2,1)}, bf16[1,120,640]{2,1,0:T(8,128)(2,1)}) custom-call(s32[2]{0:T(128)S(1)} %pad_add_fusion.ranks, bf16[960,256]{1,0:T(8,128)(2,1)} %copy-done.61, bf16[960,256]{1,0:T(8,128)(2,1)} %copy-done.31, bf16[960,256]{1,0:T(8,128)(2,1)} %copy-done.27, ...), custom_call_target="tpu_custom_call" | custom-call | flops 16000000000 | bytes 1024 | tf_op jit(solution)/shard_map/down_weights/pallas_call | solution.py:179
  132.2 1.8 collective-permute-start.34
  134.2 1.6 collective-permute-start.32
  135.8 13.0 %gate_up_weights.1 = (bf16[4,120,1280]{2,1,0:T(8,128)(2,1)}, bf16[2,120,1280]{2,1,0:T(8,128)(2,1)}, bf16[1,120,1280]{2,1,0:T(8,128)(2,1)}, bf16[1,120,1280]{2,1,0:T(8,128)(2,1)}) custom-call(s32[2]{0:T(128)S(1)} %pad_add_fusion.ranks, bf16[960,256]{1,0:T(8,128)(2,1)} %get-tuple-element.254.x_a.refs_0_, bf16[960,256]{1,0:T(8,128)(2,1)} %copy-done.29, ...), custom_call_target="tpu_custom_call" | custom-call | flops 28000000000 | bytes 1024 | tf_op jit(solution)/shard_map/gate_up_weights/pallas_call | solution.py:179
  150.0 1.9 collective-permute-start.35
  151.9 4.0 %branch.2 = (f32[960,256]{1,0:T(8,128)}, bf16[960,256]{1,0:T(8,128)(2,1)}, bf16[960,256]{1,0:T(8,128)(2,1)}, f32[16,256]{1,0:T(8,128)}, f32[8,960]{1,0:T(8,128)}) custom-call(s32[2]{0:T(128)S(1)} %pad_add_fusion.ranks, f32[960,256]{1,0:T(8,128)S(1)} %copy-done.2, bf16[2,960,256]{2,1,0:T(8,128)(2,1)S(1)} %bitcast.101, ...), custom_call_target="tpu_custom_call" | custom-call | flops 8000000000 | bytes 1024 | tf_op jit(solution)/shard_map/branch/pallas_call | solution.py:179
  155.9 1.8 collective-permute-done.35
  157.8 2.8 collective-permute-start.38
  160.6 11.6 %attend_back.2 = (bf16[960,256]{1,0:T(8,128)(2,1)}, bf16[640,256]{1,0:T(8,128)(2,1)}, bf16[640,256]{1,0:T(8,128)(2,1)}, bf16[2,640,256]{2,1,0:T(8,128)(2,1)}) custom-call(bf16[960,512]{1,0:T(8,128)(2,1)} %queries.1.q_ref, bf16[640,256]{1,0:T(8,128)(2,1)} %get-tuple-element.191.b0, bf16[640,256]{1,0:T(8,128)(2,1)} %copy-done.16, bf16[640,256]{1,0:T(8,128)(2,1)} %copy-done.15, ...), custom_call_target="tpu_custom_call" | custom-call | flops 22000001024 | bytes 1024 | tf_op jit(solution)/shard_map/attend_back/pallas_call | solution.py:179
  172.7 4.0 %branch.3 = (f32[960,256]{1,0:T(8,128)}, bf16[960,256]{1,0:T(8,128)(2,1)}, bf16[960,256]{1,0:T(8,128)(2,1)}, f32[16,256]{1,0:T(8,128)}, f32[8,960]{1,0:T(8,128)}) custom-call(s32[2]{0:T(128)S(1)} %pad_add_fusion.ranks, f32[960,256]{1,0:T(8,128)S(1)} %copy-done.3, bf16[2,960,256]{2,1,0:T(8,128)(2,1)S(1)} %bitcast.102, ...), custom_call_target="tpu_custom_call" | custom-call | flops 8000000000 | bytes 1024 | tf_op jit(solution)/shard_map/branch/pallas_call | solution.py:179
  176.8 1.7 collective-permute-start.42
  178.8 1.6 collective-permute-start.39
  180.4 11.8 %attend_back.3 = (bf16[960,256]{1,0:T(8,128)(2,1)}, bf16[640,256]{1,0:T(8,128)(2,1)}, bf16[640,256]{1,0:T(8,128)(2,1)}, bf16[2,640,256]{2,1,0:T(8,128)(2,1)}) custom-call(bf16[960,512]{1,0:T(8,128)(2,1)} %queries.1.q_ref, bf16[640,256]{1,0:T(8,128)(2,1)} %get-tuple-element.207.b0, bf16[640,256]{1,0:T(8,128)(2,1)} %copy-done.13, bf16[640,256]{1,0:T(8,128)(2,1)} %copy-done.11, ...), custom_call_target="tpu_custom_call" | custom-call | flops 22000001024 | bytes 1024 | tf_op jit(solution)/shard_map/attend_back/pallas_call | solution.py:179
  192.4 6.1 %query_weights.1 = (bf16[8,32,1920]{2,1,0:T(8,128)(2,1)}, bf16[8,32,1920]{2,1,0:T(8,128)(2,1)}, bf16[2,8,32,1920]{3,2,1,0:T(8,128)(2,1)}) custom-call(s32[2]{0:T(128)S(1)} %pad_add_fusion.ranks, bf16[960,512]{1,0:T(8,128)(2,1)S(1)} %copy-done.4, bf16[960,256]{1,0:T(8,128)(2,1)S(1)} %copy-done.46, bf16[960,256]{1,0:T(8,128)(2,1)} %get-tuple-element.306.gq_b, ...), custom_call_target="tpu_custom_call" | custom-call | flops 16000000000 | bytes 1024 | tf_op jit(solution)/shard_map/query_weights/pallas_call | solution.py:179
  199.8 2.6 collective-permute-start.43
  202.9 4.1 %query_grad.1.refs_9_ = f32[2,960,256]{2,1,0:T(8,128)} custom-call(s32[2]{0:T(128)S(1)} %pad_add_fusion.ranks, bf16[960,256]{1,0:T(8,128)(2,1)S(1)} %copy-done.46, bf16[960,256]{1,0:T(8,128)(2,1)} %get-tuple-element.306.gq_b, bf16[240,960]{1,0:T(8,128)(2,1)S(1)} %copy-done.5, bf16[240,960]{1,0:T(8,128)(2,1)S(1)} %copy-done.7, ...), custom_call_target="tpu_custom_call" | custom-call | flops 8000000000 | bytes 1024 | tf_op jit(solution)/shard_map/query_grad/pallas_call | solution.py:179
  207.4 1.6 collective-permute-start.48
  209.0 4.1 %collective-permute-done.46.refs_6_ = bf16[640,256]{1,0:T(8,128)(2,1)S(1)} collective-permute-done((bf16[640,256]{1,0:T(8,128)(2,1)S(1)}, bf16[640,256]{1,0:T(8,128)(2,1)S(1)}, u32[]{:S(2)}, u32[]{:S(2)}) %collective-permute-start.46) | collective-permute-done | bytes 327712 | tf_op jit(solution)/shard_map/ppermute | solution.py:37
  213.1 7.0 %key_weights.1 = (bf16[8,32,640]{2,1,0:T(8,128)(2,1)}, bf16[8,32,640]{2,1,0:T(8,128)(2,1)}, bf16[2,8,32,640]{3,2,1,0:T(8,128)(2,1)}, f32[2,960,256]{2,1,0:T(8,128)}) custom-call(s32[2]{0:T(128)S(1)} %pad_add_fusion.ranks, bf16[960,512]{1,0:T(8,128)(2,1)S(1)} %copy-done.4, bf16[640,256]{1,0:T(8,128)(2,1)S(1)} %copy-done.48, ...), custom_call_target="tpu_custom_call" | custom-call | flops 20000000000 | bytes 1024 | tf_op jit(solution)/shard_map/key_weights/pallas_call | solution.py:179
  220.9 1.6 collective-permute-start.52
  222.8 11.3 %collective-permute-done.48 = bf16[8,32,1920]{2,1,0:T(8,128)(2,1)S(1)} collective-permute-done((bf16[8,32,1920]{2,1,0:T(8,128)(2,1)S(1)}, bf16[8,32,1920]{2,1,0:T(8,128)(2,1)S(1)}, u32[]{:S(2)}, u32[]{:S(2)}) %collective-permute-start.48) | collective-permute-done | bytes 983072 | tf_op jit(solution)/shard_map/ppermute | solution.py:37
  234.3 5.3 %collective-permute-done.50 = bf16[8,32,640]{2,1,0:T(8,128)(2,1)S(1)} collective-permute-done((bf16[8,32,640]{2,1,0:T(8,128)(2,1)S(1)}, bf16[8,32,640]{2,1,0:T(8,128)(2,1)S(1)}, u32[]{:S(2)}, u32[]{:S(2)}) %collective-permute-start.50) | collective-permute-done | bytes 327712 | tf_op jit(solution)/shard_map/ppermute | solution.py:37
  239.8 1.5 collective-permute-start.51
  241.7 1.6 collective-permute-start.57
  243.3 2.3 down_done.1
  245.6 9.4 %collective-permute-done.51 = bf16[4,32,2560]{2,1,0:T(8,128)(2,1)S(1)} collective-permute-done((bf16[4,32,2560]{2,1,0:T(8,128)(2,1)S(1)}, bf16[4,32,2560]{2,1,0:T(8,128)(2,1)S(1)}, u32[]{:S(2)}, u32[]{:S(2)}) %collective-permute-start.51) | collective-permute-done | bytes 655392 | tf_op jit(solution)/shard_map/ppermute | solution.py:37
  255.2 1.6 collective-permute-start.54
  257.1 1.7 collective-permute-start.55
  258.9 1.5 collective-permute-start.61
  260.5 4.2 %collective-permute-done.54 = bf16[1,32,2560]{2,1,0:T(8,128)(2,1)S(1)} collective-permute-done((bf16[1,32,2560]{2,1,0:T(8,128)(2,1)S(1)}, bf16[1,32,2560]{2,1,0:T(8,128)(2,1)S(1)}, u32[]{:S(2)}, u32[]{:S(2)}) %collective-permute-start.54) | collective-permute-done | bytes 163872 | tf_op jit(solution)/shard_map/ppermute | solution.py:37
  265.6 5.2 %collective-permute-done.55 = bf16[1,32,2560]{2,1,0:T(8,128)(2,1)S(1)} collective-permute-done((bf16[1,32,2560]{2,1,0:T(8,128)(2,1)S(1)}, bf16[1,32,2560]{2,1,0:T(8,128)(2,1)S(1)}, u32[]{:S(2)}, u32[]{:S(2)}) %collective-permute-start.55) | collective-permute-done | bytes 163872 | tf_op jit(solution)/shard_map/ppermute | solution.py:37
  270.9 3.6 %collective-permute-start.60 = (bf16[1,32,2560]{2,1,0:T(8,128)(2,1)S(1)}, bf16[1,32,2560]{2,1,0:T(8,128)(2,1)S(1)}, u32[]{:S(2)}, u32[]{:S(2)}) collective-permute-start(bf16[1,32,2560]{2,1,0:T(8,128)(2,1)S(1)} %add_convert_fusion.4), channel_id=1, source_target_pairs={{0,6},{1,7},{2,4},{3,5},{4,2},{5,3},{6,0},{7,1},{8,14},{9,15},{10,... | collective-permute-start | bytes 491528 | tf_op jit(solution)/shard_map/ppermute | solution.py:37
  275.9 1.4 fusion.30
  277.3 2.3 collective-permute-done.60
  279.7 2.0 collective-permute-done.59
  281.7 3.5 %collective-permute-done.58 = bf16[1,32,2560]{2,1,0:T(8,128)(2,1)S(1)} collective-permute-done((bf16[1,32,2560]{2,1,0:T(8,128)(2,1)S(1)}, bf16[1,32,2560]{2,1,0:T(8,128)(2,1)S(1)}, u32[]{:S(2)}, u32[]{:S(2)}) %collective-permute-start.58) | collective-permute-done | bytes 163872 | tf_op jit(solution)/shard_map/ppermute | solution.py:37
  286.6 3.4 %gate_up_done.1 = (f32[960,640]{1,0:T(8,128)}, f32[960,640]{1,0:T(8,128)}) custom-call(s32[2]{0:T(128)S(1)} %pad_add_fusion.ranks, bf16[4,120,1280]{2,1,0:T(8,128)(2,1)S(1)} %pad_maximum_fusion.1.even, bf16[4,120,1280]{2,1,0:T(8,128)(2,1)S(1)} %collective-permute-done.61.odd), custom_call_target="tpu_custom_call" | custom-call | flops 14000000000 | bytes 1024 | tf_op jit(solution)/shard_map/gate_up_done/pallas_call | solution.py:179
  290.0 10.4 %collective-permute-done.62.odd = bf16[4,32,2560]{2,1,0:T(8,128)(2,1)S(1)} collective-permute-done((bf16[4,32,2560]{2,1,0:T(8,128)(2,1)S(1)}, bf16[4,32,2560]{2,1,0:T(8,128)(2,1)S(1)}, u32[]{:S(2)}, u32[]{:S(2)}) %collective-permute-start.62) | collective-permute-done | bytes 655392 | tf_op jit(solution)/shard_map/ppermute | solution.py:37
  300.4 2.6 attention_done.1
  303.1 1.3 fusion.31
  (272 shorter events, 24.0 us)
Async XLA Ops:
  4.7 12.6 %collective-permute-start = (bf16[240,768]{1,0:T(8,128)(2,1)}, bf16[240,768]{1,0:T(8,128)(2,1)S(1)}, u32[]{:S(2)}, u32[]{:S(2)}) collective-permute-start(bf16[240,768]{1,0:T(8,128)(2,1)} %pack.1.b0.refs_10_), channel_id=1, source_target_pairs={{0,16},{8,24},{16,0},{24,8},{1,17},{9,25},{17,1},{25,9},{2,18},{10... | collective-permute-start | bytes 1105928 | tf_op jit(solution)/shard_map/ppermute | solution.py:37
  7.6 19.3 %collective-permute-start.3 = (bf16[240,960]{1,0:T(8,128)(2,1)S(1)}, bf16[240,960]{1,0:T(8,128)(2,1)S(1)}, u32[]{:S(2)}, u32[]{:S(2)}) collective-permute-start(bf16[240,960]{1,0:T(8,128)(2,1)S(1)} %copy-done.5), channel_id=1, source_target_pairs={{0,16},{8,24},{16,0},{24,8},{1,17},{9,25},{17,1},{25,9},{2,18},{10... | collective-permute-start | bytes 1382408 | tf_op jit(solution)/shard_map/ppermute | solution.py:37
  17.3 1.7 collective-permute-start.1
  17.3 2.2 collective-permute-start.2
  27.0 2.5 collective-permute-start.4
  27.0 2.6 collective-permute-start.5
  27.5 10.8 %collective-permute-start.6 = (bf16[640,256]{1,0:T(8,128)(2,1)}, bf16[640,256]{1,0:T(8,128)(2,1)S(1)}, u32[]{:S(2)}, u32[]{:S(2)}) collective-permute-start(bf16[640,256]{1,0:T(8,128)(2,1)} %get-tuple-element.191.b0), channel_id=1, source_target_pairs={{0,16},{8,24},{16,0},{24,8},{1,17},{9,25},{17,1},{25,9},{2,18},{10... | collective-permute-start | bytes 983048 | tf_op jit(solution)/shard_map/ppermute | solution.py:37
  29.2 22.5 %collective-permute-start.9 = (bf16[240,960]{1,0:T(8,128)(2,1)S(1)}, bf16[240,960]{1,0:T(8,128)(2,1)S(1)}, u32[]{:S(2)}, u32[]{:S(2)}) collective-permute-start(bf16[240,960]{1,0:T(8,128)(2,1)S(1)} %copy-done.23), channel_id=1, source_target_pairs={{0,16},{8,24},{16,0},{24,8},{1,17},{9,25},{17,1},{25,9},{2,18},{10... | collective-permute-start | bytes 1382408 | tf_op jit(solution)/shard_map/ppermute | solution.py:37
  38.3 2.3 collective-permute-start.7
  38.3 2.3 collective-permute-start.8
  38.8 16.2 %collective-permute-start.12 = (bf16[640,256]{1,0:T(8,128)(2,1)S(1)}, bf16[640,256]{1,0:T(8,128)(2,1)S(1)}, u32[]{:S(2)}, u32[]{:S(2)}) collective-permute-start(bf16[640,256]{1,0:T(8,128)(2,1)S(1)} %copy-done.10), channel_id=1, source_target_pairs={{0,16},{8,24},{16,0},{24,8},{1,17},{9,25},{17,1},{25,9},{2,18},{10... | collective-permute-start | bytes 983048 | tf_op jit(solution)/shard_map/ppermute | solution.py:37
  51.8 5.6 %collective-permute-start.10 = (bf16[240,960]{1,0:T(8,128)(2,1)S(1)}, bf16[240,960]{1,0:T(8,128)(2,1)S(1)}, u32[]{:S(2)}, u32[]{:S(2)}) collective-permute-start(bf16[240,960]{1,0:T(8,128)(2,1)S(1)} %copy-done.23), channel_id=1, source_target_pairs={{0,8},{8,0},{16,24},{24,16},{1,9},{9,1},{17,25},{25,17},{2,10},{10... | collective-permute-start | bytes 1382408 | tf_op jit(solution)/shard_map/ppermute | solution.py:37
  51.8 5.6 %collective-permute-start.11 = (bf16[240,960]{1,0:T(8,128)(2,1)S(1)}, bf16[240,960]{1,0:T(8,128)(2,1)S(1)}, u32[]{:S(2)}, u32[]{:S(2)}) collective-permute-start(bf16[240,960]{1,0:T(8,128)(2,1)S(1)} %collective-permute-done.9.b2), channel_id=1, source_target_pairs={{0,8},{8,0},{16,24},{24,16},{1,9},{9,1},{17,25},{25,17},{2,10},{10... | collective-permute-start | bytes 1382408 | tf_op jit(solution)/shard_map/ppermute | solution.py:37
  54.9 2.4 collective-permute-start.13
  54.9 2.4 collective-permute-start.14
  55.6 35.2 %copy-start.60 = (bf16[960,256]{1,0:T(8,128)(2,1)}, bf16[960,256]{1,0:T(8,128)(2,1)S(1)}, u32[]{:S(2)}) copy-start(bf16[960,256]{1,0:T(8,128)(2,1)S(1)} %get-tuple-element.227.refs_4_) | copy-start | bytes 1474564
  55.6 18.1 %collective-permute-start.15 = (bf16[960,256]{1,0:T(8,128)(2,1)S(1)}, bf16[960,256]{1,0:T(8,128)(2,1)S(1)}, u32[]{:S(2)}, u32[]{:S(2)}) collective-permute-start(bf16[960,256]{1,0:T(8,128)(2,1)S(1)} %get-tuple-element.246.refs_0_), channel_id=1, source_target_pairs={{0,16},{8,24},{16,0},{24,8},{1,17},{9,25},{17,1},{25,9},{2,18},{10... | collective-permute-start | bytes 1474568 | tf_op jit(solution)/shard_map/ppermute | solution.py:37
  61.3 19.3 %collective-permute-start.17 = (bf16[960,256]{1,0:T(8,128)(2,1)}, bf16[960,256]{1,0:T(8,128)(2,1)S(1)}, u32[]{:S(2)}, u32[]{:S(2)}) collective-permute-start(bf16[960,256]{1,0:T(8,128)(2,1)} %get-tuple-element.254.x_a.refs_0_), channel_id=1, source_target_pairs={{0,16},{8,24},{16,0},{24,8},{1,17},{9,25},{17,1},{25,9},{2,18},{10... | collective-permute-start | bytes 1474568 | tf_op jit(solution)/shard_map/ppermute | solution.py:37
  73.7 6.9 %collective-permute-start.20 = (bf16[960,256]{1,0:T(8,128)(2,1)S(1)}, bf16[960,256]{1,0:T(8,128)(2,1)S(1)}, u32[]{:S(2)}, u32[]{:S(2)}) collective-permute-start(bf16[960,256]{1,0:T(8,128)(2,1)S(1)} %get-tuple-element.246.refs_0_), channel_id=1, source_target_pairs={{0,8},{8,0},{16,24},{24,16},{1,9},{9,1},{17,25},{25,17},{2,10},{10... | collective-permute-start | bytes 1474568 | tf_op jit(solution)/shard_map/ppermute | solution.py:37
  73.8 6.9 %collective-permute-start.21 = (bf16[960,256]{1,0:T(8,128)(2,1)S(1)}, bf16[960,256]{1,0:T(8,128)(2,1)S(1)}, u32[]{:S(2)}, u32[]{:S(2)}) collective-permute-start(bf16[960,256]{1,0:T(8,128)(2,1)S(1)} %collective-permute-done.15.refs_4_.refs_2_), channel_id=1, source_target_pairs={{0,8},{8,0},{16,24},{24,16},{1,9},{9,1},{17,25},{25,17},{2,10},{10... | collective-permute-start | bytes 1474568 | tf_op jit(solution)/shard_map/ppermute | solution.py:37
  74.3 16.5 %collective-permute-start.22 = (bf16[960,256]{1,0:T(8,128)(2,1)S(1)}, bf16[960,256]{1,0:T(8,128)(2,1)S(1)}, u32[]{:S(2)}, u32[]{:S(2)}) collective-permute-start(bf16[960,256]{1,0:T(8,128)(2,1)S(1)} %get-tuple-element.227.refs_4_), channel_id=1, source_target_pairs={{0,16},{8,24},{16,0},{24,8},{1,17},{9,25},{17,1},{25,9},{2,18},{10... | collective-permute-start | bytes 1474568 | tf_op jit(solution)/shard_map/ppermute | solution.py:37
  79.4 25.3 %collective-permute-start.16 = (bf16[960,256]{1,0:T(8,128)(2,1)}, bf16[960,256]{1,0:T(8,128)(2,1)S(1)}, u32[]{:S(2)}, u32[]{:S(2)}) collective-permute-start(bf16[960,256]{1,0:T(8,128)(2,1)} %get-tuple-element.232.x_b.refs_4_), channel_id=1, source_target_pairs={{0,16},{8,24},{16,0},{24,8},{1,17},{9,25},{17,1},{25,9},{2,18},{10... | collective-permute-start | bytes 1474568 | tf_op jit(solution)/shard_map/ppermute | solution.py:37
  80.7 10.7 %collective-permute-start.18 = (bf16[960,256]{1,0:T(8,128)(2,1)S(1)}, bf16[960,256]{1,0:T(8,128)(2,1)S(1)}, u32[]{:S(2)}, u32[]{:S(2)}) collective-permute-start(bf16[960,256]{1,0:T(8,128)(2,1)S(1)} %copy-done.71), channel_id=1, source_target_pairs={{0,8},{8,0},{16,24},{24,16},{1,9},{9,1},{17,25},{25,17},{2,10},{10... | collective-permute-start | bytes 1474568 | tf_op jit(solution)/shard_map/ppermute | solution.py:37
  80.7 10.6 %collective-permute-start.19 = (bf16[960,256]{1,0:T(8,128)(2,1)S(1)}, bf16[960,256]{1,0:T(8,128)(2,1)S(1)}, u32[]{:S(2)}, u32[]{:S(2)}) collective-permute-start(bf16[960,256]{1,0:T(8,128)(2,1)S(1)} %collective-permute-done.17.refs_1_.refs_2_), channel_id=1, source_target_pairs={{0,8},{8,0},{16,24},{24,16},{1,9},{9,1},{17,25},{25,17},{2,10},{10... | collective-permute-start | bytes 1474568 | tf_op jit(solution)/shard_map/ppermute | solution.py:37
  90.8 14.6 %collective-permute-start.25 = (bf16[960,256]{1,0:T(8,128)(2,1)S(1)}, bf16[960,256]{1,0:T(8,128)(2,1)S(1)}, u32[]{:S(2)}, u32[]{:S(2)}) collective-permute-start(bf16[960,256]{1,0:T(8,128)(2,1)S(1)} %get-tuple-element.227.refs_4_), channel_id=1, source_target_pairs={{0,8},{8,0},{16,24},{24,16},{1,9},{9,1},{17,25},{25,17},{2,10},{10... | collective-permute-start | bytes 1474568 | tf_op jit(solution)/shard_map/ppermute | solution.py:37
  90.8 14.6 %collective-permute-start.26 = (bf16[960,256]{1,0:T(8,128)(2,1)S(1)}, bf16[960,256]{1,0:T(8,128)(2,1)S(1)}, u32[]{:S(2)}, u32[]{:S(2)}) collective-permute-start(bf16[960,256]{1,0:T(8,128)(2,1)S(1)} %collective-permute-done.22.refs_4_.refs_6_), channel_id=1, source_target_pairs={{0,8},{8,0},{16,24},{24,16},{1,9},{9,1},{17,25},{25,17},{2,10},{10... | collective-permute-start | bytes 1474568 | tf_op jit(solution)/shard_map/ppermute | solution.py:37
  104.8 1.9 collective-permute-start.23
  104.9 3.2 %collective-permute-start.24 = (bf16[960,256]{1,0:T(8,128)(2,1)S(1)}, bf16[960,256]{1,0:T(8,128)(2,1)S(1)}, u32[]{:S(2)}, u32[]{:S(2)}) collective-permute-start(bf16[960,256]{1,0:T(8,128)(2,1)S(1)} %collective-permute-done.16.refs_1_.refs_6_), channel_id=1, source_target_pairs={{0,8},{8,0},{16,24},{24,16},{1,9},{9,1},{17,25},{25,17},{2,10},{10... | collective-permute-start | bytes 1474568 | tf_op jit(solution)/shard_map/ppermute | solution.py:37
  105.4 16.5 %collective-permute-start.28 = (bf16[2,960,256]{2,1,0:T(8,128)(2,1)}, bf16[2,960,256]{2,1,0:T(8,128)(2,1)S(1)}, u32[]{:S(2)}, u32[]{:S(2)}) collective-permute-start(bf16[2,960,256]{2,1,0:T(8,128)(2,1)} %get-tuple-element.239), channel_id=1, source_target_pairs={{0,8},{8,0},{16,24},{24,16},{1,9},{9,1},{17,25},{25,17},{2,10},{10... | collective-permute-start | bytes 2949128 | tf_op jit(solution)/shard_map/ppermute | solution.py:37
  105.5 18.3 %collective-permute-start.29 = (bf16[2,960,256]{2,1,0:T(8,128)(2,1)}, bf16[2,960,256]{2,1,0:T(8,128)(2,1)S(1)}, u32[]{:S(2)}, u32[]{:S(2)}) collective-permute-start(bf16[2,960,256]{2,1,0:T(8,128)(2,1)} %get-tuple-element.243), channel_id=1, source_target_pairs={{0,8},{8,0},{16,24},{24,16},{1,9},{9,1},{17,25},{25,17},{2,10},{10... | collective-permute-start | bytes 2949128 | tf_op jit(solution)/shard_map/ppermute | solution.py:37
  121.3 12.7 %collective-permute-start.27 = (bf16[2,960,256]{2,1,0:T(8,128)(2,1)}, bf16[2,960,256]{2,1,0:T(8,128)(2,1)S(1)}, u32[]{:S(2)}, u32[]{:S(2)}) collective-permute-start(bf16[2,960,256]{2,1,0:T(8,128)(2,1)} %get-tuple-element.238), channel_id=1, source_target_pairs={{0,8},{8,0},{16,24},{24,16},{1,9},{9,1},{17,25},{25,17},{2,10},{10... | collective-permute-start | bytes 2949128 | tf_op jit(solution)/shard_map/ppermute | solution.py:37
  121.5 14.3 %collective-permute-start.30 = (bf16[2,960,256]{2,1,0:T(8,128)(2,1)}, bf16[2,960,256]{2,1,0:T(8,128)(2,1)S(1)}, u32[]{:S(2)}, u32[]{:S(2)}) collective-permute-start(bf16[2,960,256]{2,1,0:T(8,128)(2,1)} %get-tuple-element.253), channel_id=1, source_target_pairs={{0,8},{8,0},{16,24},{24,16},{1,9},{9,1},{17,25},{25,17},{2,10},{10... | collective-permute-start | bytes 2949128 | tf_op jit(solution)/shard_map/ppermute | solution.py:37
  122.0 28.0 %collective-permute-start.36 = (bf16[960,256]{1,0:T(8,128)(2,1)S(1)}, bf16[960,256]{1,0:T(8,128)(2,1)S(1)}, u32[]{:S(2)}, u32[]{:S(2)}) collective-permute-start(bf16[960,256]{1,0:T(8,128)(2,1)S(1)} %fusion.6), channel_id=1, source_target_pairs={{0,16},{8,24},{16,0},{24,8},{1,17},{9,25},{17,1},{25,9},{2,18},{10... | collective-permute-start | bytes 1474568 | tf_op jit(solution)/shard_map/ppermute | solution.py:37
  124.0 27.9 %collective-permute-start.37 = (bf16[960,256]{1,0:T(8,128)(2,1)S(1)}, bf16[960,256]{1,0:T(8,128)(2,1)S(1)}, u32[]{:S(2)}, u32[]{:S(2)}) collective-permute-start(bf16[960,256]{1,0:T(8,128)(2,1)S(1)} %fusion.5), channel_id=1, source_target_pairs={{0,16},{8,24},{16,0},{24,8},{1,17},{9,25},{17,1},{25,9},{2,18},{10... | collective-permute-start | bytes 1474568 | tf_op jit(solution)/shard_map/ppermute | solution.py:37
  132.2 17.3 %collective-permute-start.34 = (bf16[4,120,640]{2,1,0:T(8,128)(2,1)}, bf16[4,120,640]{2,1,0:T(8,128)(2,1)S(1)}, u32[]{:S(2)}, u32[]{:S(2)}) collective-permute-start(bf16[4,120,640]{2,1,0:T(8,128)(2,1)} %get-tuple-element.250), channel_id=1, source_target_pairs={{0,1},{1,0},{2,3},{3,2},{4,5},{5,4},{6,7},{7,6},{8,9},{9,8},{10,11... | collective-permute-start | bytes 1843208 | tf_op jit(solution)/shard_map/ppermute | solution.py:37
  134.2 26.5 %collective-permute-start.32 = (bf16[960,256]{1,0:T(8,128)(2,1)S(1)}, bf16[960,256]{1,0:T(8,128)(2,1)S(1)}, u32[]{:S(2)}, u32[]{:S(2)}) collective-permute-start(bf16[960,256]{1,0:T(8,128)(2,1)S(1)} %fusion.4), channel_id=1, source_target_pairs={{0,16},{8,24},{16,0},{24,8},{1,17},{9,25},{17,1},{25,9},{2,18},{10... | collective-permute-start | bytes 1474568 | tf_op jit(solution)/shard_map/ppermute | solution.py:37
  148.8 29.8 %collective-permute-start.31 = (bf16[4,120,1280]{2,1,0:T(8,128)(2,1)}, bf16[4,120,1280]{2,1,0:T(8,128)(2,1)S(1)}, u32[]{:S(2)}, u32[]{:S(2)}) collective-permute-start(bf16[4,120,1280]{2,1,0:T(8,128)(2,1)} %get-tuple-element.262), channel_id=1, source_target_pairs={{0,1},{1,0},{2,3},{3,2},{4,5},{5,4},{6,7},{7,6},{8,9},{9,8},{10,11... | collective-permute-start | bytes 3686408 | tf_op jit(solution)/shard_map/ppermute | solution.py:37
  149.6 23.2 %collective-permute-start.33 = (bf16[960,256]{1,0:T(8,128)(2,1)S(1)}, bf16[960,256]{1,0:T(8,128)(2,1)S(1)}, u32[]{:S(2)}, u32[]{:S(2)}) collective-permute-start(bf16[960,256]{1,0:T(8,128)(2,1)S(1)} %fusion.3), channel_id=1, source_target_pairs={{0,16},{8,24},{16,0},{24,8},{1,17},{9,25},{17,1},{25,9},{2,18},{10... | collective-permute-start | bytes 1474568 | tf_op jit(solution)/shard_map/ppermute | solution.py:37
  150.0 7.8 %collective-permute-start.35 = (bf16[2,120,640]{2,1,0:T(8,128)(2,1)S(1)}, bf16[2,120,640]{2,1,0:T(8,128)(2,1)S(1)}, u32[]{:S(2)}, u32[]{:S(2)}) collective-permute-start(bf16[2,120,640]{2,1,0:T(8,128)(2,1)S(1)} %add_convert_fusion.3), channel_id=1, source_target_pairs={{0,2},{1,3},{2,0},{3,1},{4,6},{5,7},{6,4},{7,5},{8,10},{9,11},{10,... | collective-permute-start | bytes 921608 | tf_op jit(solution)/shard_map/ppermute | solution.py:37
  157.8 14.5 %collective-permute-start.38 = (bf16[1,120,640]{2,1,0:T(8,128)(2,1)S(1)}, bf16[1,120,640]{2,1,0:T(8,128)(2,1)S(1)}, u32[]{:S(2)}, u32[]{:S(2)}) collective-permute-start(bf16[1,120,640]{2,1,0:T(8,128)(2,1)S(1)} %add_convert_fusion.9), channel_id=1, source_target_pairs={{0,4},{1,5},{2,6},{3,7},{4,0},{5,1},{6,2},{7,3},{8,12},{9,13},{10,... | collective-permute-start | bytes 460808 | tf_op jit(solution)/shard_map/ppermute | solution.py:37
  172.2 4.5 %collective-permute-start.40 = (bf16[2,640,256]{2,1,0:T(8,128)(2,1)}, bf16[2,640,256]{2,1,0:T(8,128)(2,1)S(1)}, u32[]{:S(2)}, u32[]{:S(2)}) collective-permute-start(bf16[2,640,256]{2,1,0:T(8,128)(2,1)} %get-tuple-element.287), channel_id=1, source_target_pairs={{0,8},{8,0},{16,24},{24,16},{1,9},{9,1},{17,25},{25,17},{2,10},{10... | collective-permute-start | bytes 1966088 | tf_op jit(solution)/shard_map/ppermute | solution.py:37
  172.5 19.7 %collective-permute-start.41 = (bf16[1,120,640]{2,1,0:T(8,128)(2,1)S(1)}, bf16[1,120,640]{2,1,0:T(8,128)(2,1)S(1)}, u32[]{:S(2)}, u32[]{:S(2)}) collective-permute-start(bf16[1,120,640]{2,1,0:T(8,128)(2,1)S(1)} %add_convert_fusion.8), channel_id=1, source_target_pairs={{0,4},{1,5},{2,6},{3,7},{4,0},{5,1},{6,2},{7,3},{8,12},{9,13},{10,... | collective-permute-start | bytes 460808 | tf_op jit(solution)/shard_map/ppermute | solution.py:37
  176.8 15.5 %collective-permute-start.42 = (bf16[640,256]{1,0:T(8,128)(2,1)S(1)}, bf16[640,256]{1,0:T(8,128)(2,1)S(1)}, u32[]{:S(2)}, u32[]{:S(2)}) collective-permute-start(bf16[640,256]{1,0:T(8,128)(2,1)S(1)} %fusion.13), channel_id=1, source_target_pairs={{0,16},{8,24},{16,0},{24,8},{1,17},{9,25},{17,1},{25,9},{2,18},{10... | collective-permute-start | bytes 983048 | tf_op jit(solution)/shard_map/ppermute | solution.py:37
  178.8 19.8 %collective-permute-start.39 = (bf16[2,120,1280]{2,1,0:T(8,128)(2,1)S(1)}, bf16[2,120,1280]{2,1,0:T(8,128)(2,1)S(1)}, u32[]{:S(2)}, u32[]{:S(2)}) collective-permute-start(bf16[2,120,1280]{2,1,0:T(8,128)(2,1)S(1)} %add_convert_fusion), channel_id=1, source_target_pairs={{0,2},{1,3},{2,0},{3,1},{4,6},{5,7},{6,4},{7,5},{8,10},{9,11},{10,... | collective-permute-start | bytes 1843208 | tf_op jit(solution)/shard_map/ppermute | solution.py:37
  192.2 6.5 %collective-permute-start.44 = (bf16[2,640,256]{2,1,0:T(8,128)(2,1)}, bf16[2,640,256]{2,1,0:T(8,128)(2,1)S(1)}, u32[]{:S(2)}, u32[]{:S(2)}) collective-permute-start(bf16[2,640,256]{2,1,0:T(8,128)(2,1)} %get-tuple-element.302), channel_id=1, source_target_pairs={{0,8},{8,0},{16,24},{24,16},{1,9},{9,1},{17,25},{25,17},{2,10},{10... | collective-permute-start | bytes 1966088 | tf_op jit(solution)/shard_map/ppermute | solution.py:37
  198.8 8.3 %collective-permute-start.45 = (bf16[2,8,32,1920]{3,2,1,0:T(8,128)(2,1)}, bf16[2,8,32,1920]{3,2,1,0:T(8,128)(2,1)S(1)}, u32[]{:S(2)}, u32[]{:S(2)}) collective-permute-start(bf16[2,8,32,1920]{3,2,1,0:T(8,128)(2,1)} %get-tuple-element.305), channel_id=1, source_target_pairs={{0,8},{8,0},{16,24},{24,16},{1,9},{9,1},{17,25},{25,17},{2,10},{10... | collective-permute-start | bytes 5898248 | tf_op jit(solution)/shard_map/ppermute | solution.py:37
  199.4 20.8 %collective-permute-start.47 = (bf16[2,120,640]{2,1,0:T(8,128)(2,1)S(1)}, bf16[2,120,640]{2,1,0:T(8,128)(2,1)S(1)}, u32[]{:S(2)}, u32[]{:S(2)}) collective-permute-start(bf16[2,120,640]{2,1,0:T(8,128)(2,1)S(1)} %pad_maximum_fusion.7), channel_id=1, source_target_pairs={{0,2},{1,3},{2,0},{3,1},{4,6},{5,7},{6,4},{7,5},{8,10},{9,11},{10,... | collective-permute-start | bytes 921608 | tf_op jit(solution)/shard_map/ppermute | solution.py:37
  199.8 20.4 %collective-permute-start.43 = (bf16[1,120,1280]{2,1,0:T(8,128)(2,1)S(1)}, bf16[1,120,1280]{2,1,0:T(8,128)(2,1)S(1)}, u32[]{:S(2)}, u32[]{:S(2)}) collective-permute-start(bf16[1,120,1280]{2,1,0:T(8,128)(2,1)S(1)} %add_convert_fusion.2), channel_id=1, source_target_pairs={{0,4},{1,5},{2,6},{3,7},{4,0},{5,1},{6,2},{7,3},{8,12},{9,13},{10,... | collective-permute-start | bytes 921608 | tf_op jit(solution)/shard_map/ppermute | solution.py:37
  202.4 10.6 %collective-permute-start.46 = (bf16[640,256]{1,0:T(8,128)(2,1)S(1)}, bf16[640,256]{1,0:T(8,128)(2,1)S(1)}, u32[]{:S(2)}, u32[]{:S(2)}) collective-permute-start(bf16[640,256]{1,0:T(8,128)(2,1)S(1)} %fusion.12), channel_id=1, source_target_pairs={{0,16},{8,24},{16,0},{24,8},{1,17},{9,25},{17,1},{25,9},{2,18},{10... | collective-permute-start | bytes 983048 | tf_op jit(solution)/shard_map/ppermute | solution.py:37
  207.4 26.7 %collective-permute-start.48 = (bf16[8,32,1920]{2,1,0:T(8,128)(2,1)S(1)}, bf16[8,32,1920]{2,1,0:T(8,128)(2,1)S(1)}, u32[]{:S(2)}, u32[]{:S(2)}) collective-permute-start(bf16[8,32,1920]{2,1,0:T(8,128)(2,1)S(1)} %fusion), channel_id=1, source_target_pairs={{0,16},{8,24},{16,0},{24,8},{1,17},{9,25},{17,1},{25,9},{2,18},{10... | collective-permute-start | bytes 2949128 | tf_op jit(solution)/shard_map/ppermute | solution.py:37
  220.1 2.4 collective-permute-start.49
  220.4 21.2 %collective-permute-start.56 = (bf16[1,120,1280]{2,1,0:T(8,128)(2,1)S(1)}, bf16[1,120,1280]{2,1,0:T(8,128)(2,1)S(1)}, u32[]{:S(2)}, u32[]{:S(2)}) collective-permute-start(bf16[1,120,1280]{2,1,0:T(8,128)(2,1)S(1)} %add_convert_fusion.1), channel_id=1, source_target_pairs={{0,4},{1,5},{2,6},{3,7},{4,0},{5,1},{6,2},{7,3},{8,12},{9,13},{10,... | collective-permute-start | bytes 921608 | tf_op jit(solution)/shard_map/ppermute | solution.py:37
  220.9 22.5 %collective-permute-start.52 = (bf16[4,120,640]{2,1,0:T(8,128)(2,1)S(1)}, bf16[4,120,640]{2,1,0:T(8,128)(2,1)S(1)}, u32[]{:S(2)}, u32[]{:S(2)}) collective-permute-start(bf16[4,120,640]{2,1,0:T(8,128)(2,1)S(1)} %pad_maximum_fusion.4.even), channel_id=1, source_target_pairs={{0,1},{1,0},{2,3},{3,2},{4,5},{5,4},{6,7},{7,6},{8,9},{9,8},{10,11... | collective-permute-start | bytes 1843208 | tf_op jit(solution)/shard_map/ppermute | solution.py:37
  222.6 17.1 %collective-permute-start.50 = (bf16[8,32,640]{2,1,0:T(8,128)(2,1)S(1)}, bf16[8,32,640]{2,1,0:T(8,128)(2,1)S(1)}, u32[]{:S(2)}, u32[]{:S(2)}) collective-permute-start(bf16[8,32,640]{2,1,0:T(8,128)(2,1)S(1)} %fusion.11), channel_id=1, source_target_pairs={{0,16},{8,24},{16,0},{24,8},{1,17},{9,25},{17,1},{25,9},{2,18},{10... | collective-permute-start | bytes 983048 | tf_op jit(solution)/shard_map/ppermute | solution.py:37
  239.8 15.3 %collective-permute-start.51 = (bf16[4,32,2560]{2,1,0:T(8,128)(2,1)S(1)}, bf16[4,32,2560]{2,1,0:T(8,128)(2,1)S(1)}, u32[]{:S(2)}, u32[]{:S(2)}) collective-permute-start(bf16[4,32,2560]{2,1,0:T(8,128)(2,1)S(1)} %pad_maximum_fusion.2), channel_id=1, source_target_pairs={{0,1},{1,0},{2,3},{3,2},{4,5},{5,4},{6,7},{7,6},{8,9},{9,8},{10,11... | collective-permute-start | bytes 1966088 | tf_op jit(solution)/shard_map/ppermute | solution.py:37
  241.7 17.1 %collective-permute-start.57 = (bf16[2,120,1280]{2,1,0:T(8,128)(2,1)S(1)}, bf16[2,120,1280]{2,1,0:T(8,128)(2,1)S(1)}, u32[]{:S(2)}, u32[]{:S(2)}) collective-permute-start(bf16[2,120,1280]{2,1,0:T(8,128)(2,1)S(1)} %pad_maximum_fusion.5), channel_id=1, source_target_pairs={{0,2},{1,3},{2,0},{3,1},{4,6},{5,7},{6,4},{7,5},{8,10},{9,11},{10,... | collective-permute-start | bytes 1843208 | tf_op jit(solution)/shard_map/ppermute | solution.py:37
  255.2 9.4 %collective-permute-start.54 = (bf16[1,32,2560]{2,1,0:T(8,128)(2,1)S(1)}, bf16[1,32,2560]{2,1,0:T(8,128)(2,1)S(1)}, u32[]{:S(2)}, u32[]{:S(2)}) collective-permute-start(bf16[1,32,2560]{2,1,0:T(8,128)(2,1)S(1)} %get-tuple-element.347), channel_id=1, source_target_pairs={{0,2},{1,3},{2,0},{3,1},{4,6},{5,7},{6,4},{7,5},{8,10},{9,11},{10,... | collective-permute-start | bytes 491528 | tf_op jit(solution)/shard_map/ppermute | solution.py:37
  256.9 8.8 %collective-permute-start.53 = (bf16[1,32,2560]{2,1,0:T(8,128)(2,1)S(1)}, bf16[1,32,2560]{2,1,0:T(8,128)(2,1)S(1)}, u32[]{:S(2)}, u32[]{:S(2)}) collective-permute-start(bf16[1,32,2560]{2,1,0:T(8,128)(2,1)S(1)} %get-tuple-element.348), channel_id=1, source_target_pairs={{0,6},{1,7},{2,4},{3,5},{4,2},{5,3},{6,0},{7,1},{8,14},{9,15},{10,... | collective-permute-start | bytes 491528 | tf_op jit(solution)/shard_map/ppermute | solution.py:37
  257.1 13.7 %collective-permute-start.55 = (bf16[1,32,2560]{2,1,0:T(8,128)(2,1)S(1)}, bf16[1,32,2560]{2,1,0:T(8,128)(2,1)S(1)}, u32[]{:S(2)}, u32[]{:S(2)}) collective-permute-start(bf16[1,32,2560]{2,1,0:T(8,128)(2,1)S(1)} %get-tuple-element.353), channel_id=1, source_target_pairs={{0,4},{1,5},{2,6},{3,7},{4,0},{5,1},{6,2},{7,3},{8,12},{9,13},{10,... | collective-permute-start | bytes 491528 | tf_op jit(solution)/shard_map/ppermute | solution.py:37
  258.9 26.3 %collective-permute-start.61 = (bf16[4,120,1280]{2,1,0:T(8,128)(2,1)S(1)}, bf16[4,120,1280]{2,1,0:T(8,128)(2,1)S(1)}, u32[]{:S(2)}, u32[]{:S(2)}) collective-permute-start(bf16[4,120,1280]{2,1,0:T(8,128)(2,1)S(1)} %pad_maximum_fusion.1.even), channel_id=1, source_target_pairs={{0,1},{1,0},{2,3},{3,2},{4,5},{5,4},{6,7},{7,6},{8,9},{9,8},{10,11... | collective-permute-start | bytes 3686408 | tf_op jit(solution)/shard_map/ppermute | solution.py:37
  270.9 8.7 %collective-permute-start.60 = (bf16[1,32,2560]{2,1,0:T(8,128)(2,1)S(1)}, bf16[1,32,2560]{2,1,0:T(8,128)(2,1)S(1)}, u32[]{:S(2)}, u32[]{:S(2)}) collective-permute-start(bf16[1,32,2560]{2,1,0:T(8,128)(2,1)S(1)} %add_convert_fusion.4), channel_id=1, source_target_pairs={{0,6},{1,7},{2,4},{3,5},{4,2},{5,3},{6,0},{7,1},{8,14},{9,15},{10,... | collective-permute-start | bytes 491528 | tf_op jit(solution)/shard_map/ppermute | solution.py:37
  274.5 7.2 %collective-permute-start.59 = (bf16[1,32,2560]{2,1,0:T(8,128)(2,1)S(1)}, bf16[1,32,2560]{2,1,0:T(8,128)(2,1)S(1)}, u32[]{:S(2)}, u32[]{:S(2)}) collective-permute-start(bf16[1,32,2560]{2,1,0:T(8,128)(2,1)S(1)} %add_convert_fusion.4), channel_id=1, source_target_pairs={{0,2},{1,3},{2,0},{3,1},{4,6},{5,7},{6,4},{7,5},{8,10},{9,11},{10,... | collective-permute-start | bytes 491528 | tf_op jit(solution)/shard_map/ppermute | solution.py:37
  274.5 10.7 %collective-permute-start.58 = (bf16[1,32,2560]{2,1,0:T(8,128)(2,1)S(1)}, bf16[1,32,2560]{2,1,0:T(8,128)(2,1)S(1)}, u32[]{:S(2)}, u32[]{:S(2)}) collective-permute-start(bf16[1,32,2560]{2,1,0:T(8,128)(2,1)S(1)} %add_convert_fusion.4), channel_id=1, source_target_pairs={{0,4},{1,5},{2,6},{3,7},{4,0},{5,1},{6,2},{7,3},{8,12},{9,13},{10,... | collective-permute-start | bytes 491528 | tf_op jit(solution)/shard_map/ppermute | solution.py:37
  285.3 15.1 %collective-permute-start.62 = (bf16[4,32,2560]{2,1,0:T(8,128)(2,1)S(1)}, bf16[4,32,2560]{2,1,0:T(8,128)(2,1)S(1)}, u32[]{:S(2)}, u32[]{:S(2)}) collective-permute-start(bf16[4,32,2560]{2,1,0:T(8,128)(2,1)S(1)} %pad_maximum_fusion.3.even), channel_id=1, source_target_pairs={{0,1},{1,0},{2,3},{3,2},{4,5},{5,4},{6,7},{7,6},{8,9},{9,8},{10,11... | collective-permute-start | bytes 1966088 | tf_op jit(solution)/shard_map/ppermute | solution.py:37
  (72 other events, 755.7 us)

commit v8 on v7

--- a/solution.py
+++ b/solution.py
@@ -469,12 +469,22 @@
         out[HD:, :] = values[:, part]
 
 
+def slot_at(i):
+    n = PARTS - 1 - i
+    return ((n & 1) << 2) | (n & 2) | ((n >> 2) & 1)
+
+
 def spread(ranks, acc, own_ref, far_ref, send_ref):
     part = acc.shape[1] // PARTS
-    for k, out in enumerate((own_ref, send_ref.at[0], far_ref, send_ref.at[1])):
-        for i, slot in enumerate(SLOTS):
-            start = pl.multiple_of((slot ^ ranks[1]) * part, 8)
+    outs = (own_ref, send_ref.at[0], far_ref, send_ref.at[1])
+
+    def move(i, carry):
+        start = pl.multiple_of((slot_at(i) ^ ranks[1]) * part, 8)
+        for k, out in enumerate(outs):
             out[i] = acc[ranks[0] ^ k, pl.ds(start, part), :].astype(LOW)
+        return carry
+
+    lax.fori_loop(0, PARTS, move, 0)
 
 
 def query_weight_kernel(ranks, norm_ref, gq_a, gq_b, att_a, att_b, gb_a, gb_b, own_ref, far_ref, send_ref, acc):
@@ -538,16 +548,21 @@
 
 
 def gathered(ranks, pairs):
-    for a in range(PARTS):
+    def move(a, carry):
         slot = ranks[1] ^ a
         index = place(slot)
         for parity in range(2):
 
             @pl.when(slot % 2 == parity)
-            def _(parity=parity, index=index, a=a):
+            def _(parity=parity):
                 for pair in pairs:
                     part = pair[parity].shape[1]
-                    pair[2][a * part : (a + 1) * part, :] = pair[parity][index].astype(FULL)
+                    rows = pl.ds(pl.multiple_of(a * part, 8), part)
+                    pair[2][rows, :] = pair[parity][index].astype(FULL)
+
+        return carry
+
+    lax.fori_loop(0, PARTS, move, 0)
 
 
 def forward_weights_kernel(ranks, even, odd, *outs):
@@ -742,7 +757,7 @@
             other_blocks_kernel,
             "other_blocks",
             (act_shape, half_shape, act_shape, half_shape, ff_shape, ff_shape, ff_shape),
-            free=range(6),
+            free=(0, 2),
             grid=(GROUP - 1,),
             in_specs=[ANY] * 6 + [NEAR] * 4,
             out_specs=(act, half, act, half) + (per_block,) * 3,

time: 309 us -> 308 us (level)
  no operation moved by 1% of the time
where the time goes in v8:
time: 308 us; the launch traced here: 303 us
  Pallas kernels  160 us (52%)
  waiting for transfers between devices  77.3 us (25%)
  starting transfers between devices  54.6 us (18%)
  other arithmetic  6.84 us (2%)
    pallas_call x24, Pallas kernels, placed(): return run(*args[:prefetch], *rest)  160 us
    ppermute x63, waiting for transfers between devices, swap(): return lax.ppermute(values, axis, [(i, i ^ mask) for i in range(count)])  77.3 us
    ppermute x63, starting transfers between devices, swap(): return lax.ppermute(values, axis, [(i, i ^ mask) for i in range(count)])  54.6 us
  transfers between devices with their start and end apart: 63, of which 21 were waited for; matrix products, arithmetic and copies ran while one was open for 2% of the time, Pallas kernels for 51%

profile of v8, /device:TPU:0, one launch (start us, length us, event | category | flops | bytes accessed | tf_op | source)
XLA Modules:
  0.0 303.2 jit_solution(13221343835219128956)
XLA Ops:
  2.6 2.1 pack.1.b0.refs_10_
  4.7 3.0 collective-permute-start
  7.9 4.8 %flip_two.1 = (bf16[1280,960]{1,0:T(8,128)(2,1)}, bf16[960,1280]{1,0:T(8,128)(2,1)}) custom-call(bf16[960,640]{1,0:T(8,128)(2,1)} %wg_ref, bf16[960,640]{1,0:T(8,128)(2,1)} %wu_ref.1), custom_call_target="tpu_custom_call" | custom-call | flops 8000000000 | bytes 1024 | tf_op jit(solution)/shard_map/flip_two/pallas_call | solution.py:179
  12.7 2.9 flip_one.1.wd_ref.refs_9_
  15.6 1.7 collective-permute-done.b2.refs_12_
  19.5 3.6 %keys_values.1 = (bf16[960,512]{1,0:T(8,128)(2,1)}, bf16[640,256]{1,0:T(8,128)(2,1)}, bf16[640,256]{1,0:T(8,128)(2,1)}, bf16[960,128]{1,0:T(8,128)(2,1)}) custom-call(s32[2]{0:T(128)S(1)} %pad_add_fusion.ranks, bf16[2,960,256]{2,1,0:T(8,128)(2,1)S(1)} %bitcast.109, bf16[240,768]{1,0:T(8,128)(2,1)S(1)} %copy-done.30, ...), custom_call_target="tpu_custom_call" | custom-call | flops 8600000512 | bytes 1024 | tf_op jit(solution)/shard_map/keys_values/pallas_call | solution.py:179
  23.1 3.9 %collective-permute-done.3.b2.q2 = bf16[240,960]{1,0:T(8,128)(2,1)S(1)} collective-permute-done((bf16[240,960]{1,0:T(8,128)(2,1)S(1)}, bf16[240,960]{1,0:T(8,128)(2,1)S(1)}, u32[]{:S(2)}, u32[]{:S(2)}) %collective-permute-start.3) | collective-permute-done | bytes 460832 | tf_op jit(solution)/shard_map/ppermute | solution.py:37
  27.5 1.7 collective-permute-start.6
  29.5 4.4 %queries.1.q_ref = bf16[960,512]{1,0:T(8,128)(2,1)} custom-call(s32[2]{0:T(128)S(1)} %pad_add_fusion.ranks, bf16[960,512]{1,0:T(8,128)(2,1)} %get-tuple-element.184.norm_ref.refs_0_, bf16[240,960]{1,0:T(8,128)(2,1)S(1)} %copy-done.5, bf16[240,960]{1,0:T(8,128)(2,1)S(1)} %collective-permute-done.4.b1.q1, bf16[240,960]{1,0:T(8,128)(2,1)S(1)} %collective-permute-done.3.b2.q2, ...), custom_call_target="tpu_custom_call" | custom-call | flops 200000000 | bytes 1024 | tf_op jit(solution)/shard_map/queries/pallas_call | solution.py:179
  33.9 4.4 %collective-permute-done.6.b2 = bf16[640,256]{1,0:T(8,128)(2,1)S(1)} collective-permute-done((bf16[640,256]{1,0:T(8,128)(2,1)}, bf16[640,256]{1,0:T(8,128)(2,1)S(1)}, u32[]{:S(2)}, u32[]{:S(2)}) %collective-permute-start.6) | collective-permute-done | bytes 327712 | tf_op jit(solution)/shard_map/ppermute | solution.py:37
  38.8 1.7 collective-permute-start.12
  40.5 11.2 %attend.2 = (bf16[5,1024,768]{2,1,0:T(8,128)(2,1)}, bf16[960,256]{1,0:T(8,128)(2,1)}) custom-call(s32[2]{0:T(128)S(1)} %pad_add_fusion.ranks, s32[2,4]{1,0:T(2,128)S(1)} %copy-done.18, s32[2,2]{1,0:T(2,128)S(1)} %copy-done.19, bf16[960,512]{1,0:T(8,128)(2,1)} %queries.1.q_ref, bf16[640,256]{1,0:T(8,128)(2,1)S(1)} %copy-done.12, ...), custom_call_target="tpu_custom_call" | custom-call | flops 200000000 | bytes 1024 | tf_op jit(solution)/shard_map/attend/pallas_call | solution.py:179
  52.2 2.7 collective-permute-done.12.b2
  55.6 1.8 collective-permute-start.15
  57.4 3.9 %middle.2 = (f32[960,256]{1,0:T(8,128)}, bf16[960,256]{1,0:T(8,128)(2,1)}) custom-call(s32[2]{0:T(128)S(1)} %pad_add_fusion.ranks, bf16[960,256]{1,0:T(8,128)(2,1)} %get-tuple-element.195.att_ref.att_a, bf16[240,960]{1,0:T(8,128)(2,1)S(1)} %copy-done.23, bf16[240,960]{1,0:T(8,128)(2,1)S(1)} %collective-permute-done.10.b1, ...), custom_call_target="tpu_custom_call" | custom-call | flops 6000000000 | bytes 1024 | tf_op jit(solution)/shard_map/middle/pallas_call | solution.py:179
  61.3 1.4 collective-permute-start.17
  62.7 11.0 %attend.3 = (bf16[5,1024,768]{2,1,0:T(8,128)(2,1)}, bf16[960,256]{1,0:T(8,128)(2,1)}) custom-call(s32[2]{0:T(128)S(1)} %pad_add_fusion.ranks, s32[2,4]{1,0:T(2,128)S(1)} %copy-done.18, s32[2,2]{1,0:T(2,128)S(1)} %copy-done.19, bf16[960,512]{1,0:T(8,128)(2,1)} %queries.1.q_ref, bf16[640,256]{1,0:T(8,128)(2,1)S(1)} %copy-done.10, ...), custom_call_target="tpu_custom_call" | custom-call | flops 200000000 | bytes 1024 | tf_op jit(solution)/shard_map/attend/pallas_call | solution.py:179
  75.0 4.5 %middle.3 = (f32[960,256]{1,0:T(8,128)}, bf16[960,256]{1,0:T(8,128)(2,1)}) custom-call(s32[2]{0:T(128)S(1)} %pad_add_fusion.ranks, bf16[960,256]{1,0:T(8,128)(2,1)} %get-tuple-element.215.att_ref.att_b, bf16[240,960]{1,0:T(8,128)(2,1)S(1)} %copy-done.23, bf16[240,960]{1,0:T(8,128)(2,1)S(1)} %collective-permute-done.10.b1, ...), custom_call_target="tpu_custom_call" | custom-call | flops 6000000000 | bytes 1024 | tf_op jit(solution)/shard_map/middle/pallas_call | solution.py:179
  81.3 8.2 %own_blocks.1 = (bf16[2,960,256]{2,1,0:T(8,128)(2,1)}, bf16[2,960,256]{2,1,0:T(8,128)(2,1)}, bf16[2,640,256]{2,1,0:T(8,128)(2,1)}, bf16[2,640,256]{2,1,0:T(8,128)(2,1)}, bf16[2,640,256]{2,1,0:T(8,128)(2,1)}) custom-call(bf16[960,256]{1,0:T(8,128)(2,1)} %get-tuple-element.254.x_a.refs_0_, bf16[960,256]{1,0:T(8,128)(2,1)} %get-tuple-element.232.x_b.refs_4_, ...), custom_call_target="tpu_custom_call" | custom-call | flops 16000000000 | bytes 1024 | tf_op jit(solution)/shard_map/own_blocks/pallas_call | solution.py:179
  91.3 12.5 %other_blocks.2 = (bf16[960,256]{1,0:T(8,128)(2,1)}, bf16[2,960,256]{2,1,0:T(8,128)(2,1)}, bf16[960,256]{1,0:T(8,128)(2,1)}, bf16[2,960,256]{2,1,0:T(8,128)(2,1)...) custom-call(bf16[960,256]{1,0:T(8,128)(2,1)S(1)} %collective-permute-done.18.refs_0_.refs_1_, ...), custom_call_target="tpu_custom_call" | custom-call | flops 24000000000 | bytes 1024 | tf_op jit(solution)/shard_map/other_blocks/pallas_call | solution.py:179
  105.8 1.4 collective-permute-done.24.refs_2_.refs_7_
  107.2 12.3 %other_blocks.3 = (bf16[960,256]{1,0:T(8,128)(2,1)}, bf16[2,960,256]{2,1,0:T(8,128)(2,1)}, bf16[960,256]{1,0:T(8,128)(2,1)}, bf16[2,960,256]{2,1,0:T(8,128)(2,1)...) custom-call(bf16[960,256]{1,0:T(8,128)(2,1)S(1)} %collective-permute-done.23.refs_0_.refs_5_, ...), custom_call_target="tpu_custom_call" | custom-call | flops 24000000000 | bytes 1024 | tf_op jit(solution)/shard_map/other_blocks/pallas_call | solution.py:179
  120.3 1.8 collective-permute-start.36
  122.6 7.9 %down_weights.1 = (bf16[4,120,640]{2,1,0:T(8,128)(2,1)}, bf16[2,120,640]{2,1,0:T(8,128)(2,1)}, bf16[1,120,640]{2,1,0:T(8,128)(2,1)}, bf16[1,120,640]{2,1,0:T(8,128)(2,1)}) custom-call(s32[2]{0:T(128)S(1)} %pad_add_fusion.ranks, bf16[960,256]{1,0:T(8,128)(2,1)} %copy-done.53, bf16[960,256]{1,0:T(8,128)(2,1)} %copy-done.68, bf16[960,256]{1,0:T(8,128)(2,1)} %copy-done.65, ...), custom_call_target="tpu_custom_call" | custom-call | flops 16000000000 | bytes 1024 | tf_op jit(solution)/shard_map/down_weights/pallas_call | solution.py:179
  130.5 1.8 collective-permute-start.34
  132.4 1.6 collective-permute-start.32
  134.0 12.9 %gate_up_weights.1 = (bf16[4,120,1280]{2,1,0:T(8,128)(2,1)}, bf16[2,120,1280]{2,1,0:T(8,128)(2,1)}, bf16[1,120,1280]{2,1,0:T(8,128)(2,1)}, bf16[1,120,1280]{2,1,0:T(8,128)(2,1)}) custom-call(s32[2]{0:T(128)S(1)} %pad_add_fusion.ranks, bf16[960,256]{1,0:T(8,128)(2,1)} %get-tuple-element.254.x_a.refs_0_, bf16[960,256]{1,0:T(8,128)(2,1)} %copy-done.26, ...), custom_call_target="tpu_custom_call" | custom-call | flops 28000000000 | bytes 1024 | tf_op jit(solution)/shard_map/gate_up_weights/pallas_call | solution.py:179
  148.2 1.9 collective-permute-start.35
  150.1 4.0 %branch.2 = (f32[960,256]{1,0:T(8,128)}, bf16[960,256]{1,0:T(8,128)(2,1)}, bf16[960,256]{1,0:T(8,128)(2,1)}, f32[16,256]{1,0:T(8,128)}, f32[8,960]{1,0:T(8,128)}) custom-call(s32[2]{0:T(128)S(1)} %pad_add_fusion.ranks, f32[960,256]{1,0:T(8,128)S(1)} %copy-done.2, bf16[2,960,256]{2,1,0:T(8,128)(2,1)S(1)} %bitcast.101, ...), custom_call_target="tpu_custom_call" | custom-call | flops 8000000000 | bytes 1024 | tf_op jit(solution)/shard_map/branch/pallas_call | solution.py:179
  154.1 1.8 collective-permute-done.35
  156.0 2.8 collective-permute-start.38
  158.8 11.6 %attend_back.2 = (bf16[960,256]{1,0:T(8,128)(2,1)}, bf16[640,256]{1,0:T(8,128)(2,1)}, bf16[640,256]{1,0:T(8,128)(2,1)}, bf16[2,640,256]{2,1,0:T(8,128)(2,1)}) custom-call(bf16[960,512]{1,0:T(8,128)(2,1)} %queries.1.q_ref, bf16[640,256]{1,0:T(8,128)(2,1)} %get-tuple-element.191.b0, bf16[640,256]{1,0:T(8,128)(2,1)} %copy-done.16, bf16[640,256]{1,0:T(8,128)(2,1)} %copy-done.15, ...), custom_call_target="tpu_custom_call" | custom-call | flops 22000001024 | bytes 1024 | tf_op jit(solution)/shard_map/attend_back/pallas_call | solution.py:179
  170.9 4.0 %branch.3 = (f32[960,256]{1,0:T(8,128)}, bf16[960,256]{1,0:T(8,128)(2,1)}, bf16[960,256]{1,0:T(8,128)(2,1)}, f32[16,256]{1,0:T(8,128)}, f32[8,960]{1,0:T(8,128)}) custom-call(s32[2]{0:T(128)S(1)} %pad_add_fusion.ranks, f32[960,256]{1,0:T(8,128)S(1)} %copy-done.3, bf16[2,960,256]{2,1,0:T(8,128)(2,1)S(1)} %bitcast.102, ...), custom_call_target="tpu_custom_call" | custom-call | flops 8000000000 | bytes 1024 | tf_op jit(solution)/shard_map/branch/pallas_call | solution.py:179
  175.0 1.8 collective-permute-start.42
  176.9 1.6 collective-permute-start.39
  178.6 11.6 %attend_back.3 = (bf16[960,256]{1,0:T(8,128)(2,1)}, bf16[640,256]{1,0:T(8,128)(2,1)}, bf16[640,256]{1,0:T(8,128)(2,1)}, bf16[2,640,256]{2,1,0:T(8,128)(2,1)}) custom-call(bf16[960,512]{1,0:T(8,128)(2,1)} %queries.1.q_ref, bf16[640,256]{1,0:T(8,128)(2,1)} %get-tuple-element.207.b0, bf16[640,256]{1,0:T(8,128)(2,1)} %copy-done.13, bf16[640,256]{1,0:T(8,128)(2,1)} %copy-done.11, ...), custom_call_target="tpu_custom_call" | custom-call | flops 22000001024 | bytes 1024 | tf_op jit(solution)/shard_map/attend_back/pallas_call | solution.py:179
  190.4 6.7 %query_weights.1 = (bf16[8,32,1920]{2,1,0:T(8,128)(2,1)}, bf16[8,32,1920]{2,1,0:T(8,128)(2,1)}, bf16[2,8,32,1920]{3,2,1,0:T(8,128)(2,1)}) custom-call(s32[2]{0:T(128)S(1)} %pad_add_fusion.ranks, bf16[960,512]{1,0:T(8,128)(2,1)S(1)} %copy-done.4, bf16[960,256]{1,0:T(8,128)(2,1)S(1)} %copy-done.38, bf16[960,256]{1,0:T(8,128)(2,1)} %get-tuple-element.306.gq_b, ...), custom_call_target="tpu_custom_call" | custom-call | flops 16000000000 | bytes 1024 | tf_op jit(solution)/shard_map/query_weights/pallas_call | solution.py:179
  198.4 2.6 collective-permute-start.43
  201.5 4.1 %query_grad.1.refs_9_ = f32[2,960,256]{2,1,0:T(8,128)} custom-call(s32[2]{0:T(128)S(1)} %pad_add_fusion.ranks, bf16[960,256]{1,0:T(8,128)(2,1)S(1)} %copy-done.38, bf16[960,256]{1,0:T(8,128)(2,1)} %get-tuple-element.306.gq_b, bf16[240,960]{1,0:T(8,128)(2,1)S(1)} %copy-done.5, bf16[240,960]{1,0:T(8,128)(2,1)S(1)} %copy-done.7, ...), custom_call_target="tpu_custom_call" | custom-call | flops 8000000000 | bytes 1024 | tf_op jit(solution)/shard_map/query_grad/pallas_call | solution.py:179
  206.0 1.6 collective-permute-start.48
  207.5 4.1 %collective-permute-done.46.refs_6_ = bf16[640,256]{1,0:T(8,128)(2,1)S(1)} collective-permute-done((bf16[640,256]{1,0:T(8,128)(2,1)S(1)}, bf16[640,256]{1,0:T(8,128)(2,1)S(1)}, u32[]{:S(2)}, u32[]{:S(2)}) %collective-permute-start.46) | collective-permute-done | bytes 327712 | tf_op jit(solution)/shard_map/ppermute | solution.py:37
  211.7 7.1 %key_weights.1 = (bf16[8,32,640]{2,1,0:T(8,128)(2,1)}, bf16[8,32,640]{2,1,0:T(8,128)(2,1)}, bf16[2,8,32,640]{3,2,1,0:T(8,128)(2,1)}, f32[2,960,256]{2,1,0:T(8,128)}) custom-call(s32[2]{0:T(128)S(1)} %pad_add_fusion.ranks, bf16[960,512]{1,0:T(8,128)(2,1)S(1)} %copy-done.4, bf16[640,256]{1,0:T(8,128)(2,1)S(1)} %copy-done.40, ...), custom_call_target="tpu_custom_call" | custom-call | flops 20000000000 | bytes 1024 | tf_op jit(solution)/shard_map/key_weights/pallas_call | solution.py:179
  219.4 1.6 collective-permute-start.52
  221.4 11.3 %collective-permute-done.48 = bf16[8,32,1920]{2,1,0:T(8,128)(2,1)S(1)} collective-permute-done((bf16[8,32,1920]{2,1,0:T(8,128)(2,1)S(1)}, bf16[8,32,1920]{2,1,0:T(8,128)(2,1)S(1)}, u32[]{:S(2)}, u32[]{:S(2)}) %collective-permute-start.48) | collective-permute-done | bytes 983072 | tf_op jit(solution)/shard_map/ppermute | solution.py:37
  232.9 5.3 %collective-permute-done.50 = bf16[8,32,640]{2,1,0:T(8,128)(2,1)S(1)} collective-permute-done((bf16[8,32,640]{2,1,0:T(8,128)(2,1)S(1)}, bf16[8,32,640]{2,1,0:T(8,128)(2,1)S(1)}, u32[]{:S(2)}, u32[]{:S(2)}) %collective-permute-start.50) | collective-permute-done | bytes 327712 | tf_op jit(solution)/shard_map/ppermute | solution.py:37
  238.3 1.6 collective-permute-start.51
  240.3 1.6 collective-permute-start.57
  241.9 2.3 down_done.1
  244.2 9.4 %collective-permute-done.51 = bf16[4,32,2560]{2,1,0:T(8,128)(2,1)S(1)} collective-permute-done((bf16[4,32,2560]{2,1,0:T(8,128)(2,1)S(1)}, bf16[4,32,2560]{2,1,0:T(8,128)(2,1)S(1)}, u32[]{:S(2)}, u32[]{:S(2)}) %collective-permute-start.51) | collective-permute-done | bytes 655392 | tf_op jit(solution)/shard_map/ppermute | solution.py:37
  253.8 1.6 collective-permute-start.54
  255.6 1.7 collective-permute-start.55
  257.4 1.6 collective-permute-start.61
  259.0 4.2 %collective-permute-done.54 = bf16[1,32,2560]{2,1,0:T(8,128)(2,1)S(1)} collective-permute-done((bf16[1,32,2560]{2,1,0:T(8,128)(2,1)S(1)}, bf16[1,32,2560]{2,1,0:T(8,128)(2,1)S(1)}, u32[]{:S(2)}, u32[]{:S(2)}) %collective-permute-start.54) | collective-permute-done | bytes 163872 | tf_op jit(solution)/shard_map/ppermute | solution.py:37
  264.2 5.1 %collective-permute-done.55 = bf16[1,32,2560]{2,1,0:T(8,128)(2,1)S(1)} collective-permute-done((bf16[1,32,2560]{2,1,0:T(8,128)(2,1)S(1)}, bf16[1,32,2560]{2,1,0:T(8,128)(2,1)S(1)}, u32[]{:S(2)}, u32[]{:S(2)}) %collective-permute-start.55) | collective-permute-done | bytes 163872 | tf_op jit(solution)/shard_map/ppermute | solution.py:37
  269.5 3.6 %collective-permute-start.60 = (bf16[1,32,2560]{2,1,0:T(8,128)(2,1)S(1)}, bf16[1,32,2560]{2,1,0:T(8,128)(2,1)S(1)}, u32[]{:S(2)}, u32[]{:S(2)}) collective-permute-start(bf16[1,32,2560]{2,1,0:T(8,128)(2,1)S(1)} %add_convert_fusion.4), channel_id=1, source_target_pairs={{0,6},{1,7},{2,4},{3,5},{4,2},{5,3},{6,0},{7,1},{8,14},{9,15},{10,... | collective-permute-start | bytes 491528 | tf_op jit(solution)/shard_map/ppermute | solution.py:37
  274.5 1.4 fusion.30
  275.9 2.3 collective-permute-done.60
  278.2 2.0 collective-permute-done.59
  280.2 3.5 %collective-permute-done.58 = bf16[1,32,2560]{2,1,0:T(8,128)(2,1)S(1)} collective-permute-done((bf16[1,32,2560]{2,1,0:T(8,128)(2,1)S(1)}, bf16[1,32,2560]{2,1,0:T(8,128)(2,1)S(1)}, u32[]{:S(2)}, u32[]{:S(2)}) %collective-permute-start.58) | collective-permute-done | bytes 163872 | tf_op jit(solution)/shard_map/ppermute | solution.py:37
  283.9 1.3 collective-permute-start.62
  285.1 3.5 %gate_up_done.1 = (f32[960,640]{1,0:T(8,128)}, f32[960,640]{1,0:T(8,128)}) custom-call(s32[2]{0:T(128)S(1)} %pad_add_fusion.ranks, bf16[4,120,1280]{2,1,0:T(8,128)(2,1)S(1)} %pad_maximum_fusion.1.even, bf16[4,120,1280]{2,1,0:T(8,128)(2,1)S(1)} %collective-permute-done.61.odd), custom_call_target="tpu_custom_call" | custom-call | flops 14000000000 | bytes 1024 | tf_op jit(solution)/shard_map/gate_up_done/pallas_call | solution.py:179
  288.6 10.3 %collective-permute-done.62.odd = bf16[4,32,2560]{2,1,0:T(8,128)(2,1)S(1)} collective-permute-done((bf16[4,32,2560]{2,1,0:T(8,128)(2,1)S(1)}, bf16[4,32,2560]{2,1,0:T(8,128)(2,1)S(1)}, u32[]{:S(2)}, u32[]{:S(2)}) %collective-permute-start.62) | collective-permute-done | bytes 655392 | tf_op jit(solution)/shard_map/ppermute | solution.py:37
  299.0 2.7 attention_done.1
  301.7 1.3 fusion.31
  (272 shorter events, 24.0 us)
Async XLA Ops:
  4.7 12.6 %collective-permute-start = (bf16[240,768]{1,0:T(8,128)(2,1)}, bf16[240,768]{1,0:T(8,128)(2,1)S(1)}, u32[]{:S(2)}, u32[]{:S(2)}) collective-permute-start(bf16[240,768]{1,0:T(8,128)(2,1)} %pack.1.b0.refs_10_), channel_id=1, source_target_pairs={{0,16},{8,24},{16,0},{24,8},{1,17},{9,25},{17,1},{25,9},{2,18},{10... | collective-permute-start | bytes 1105928 | tf_op jit(solution)/shard_map/ppermute | solution.py:37
  7.6 19.3 %collective-permute-start.3 = (bf16[240,960]{1,0:T(8,128)(2,1)S(1)}, bf16[240,960]{1,0:T(8,128)(2,1)S(1)}, u32[]{:S(2)}, u32[]{:S(2)}) collective-permute-start(bf16[240,960]{1,0:T(8,128)(2,1)S(1)} %copy-done.5), channel_id=1, source_target_pairs={{0,16},{8,24},{16,0},{24,8},{1,17},{9,25},{17,1},{25,9},{2,18},{10... | collective-permute-start | bytes 1382408 | tf_op jit(solution)/shard_map/ppermute | solution.py:37
  17.3 1.7 collective-permute-start.1
  17.3 2.2 collective-permute-start.2
  27.0 2.5 collective-permute-start.4
  27.0 2.6 collective-permute-start.5
  27.5 10.8 %collective-permute-start.6 = (bf16[640,256]{1,0:T(8,128)(2,1)}, bf16[640,256]{1,0:T(8,128)(2,1)S(1)}, u32[]{:S(2)}, u32[]{:S(2)}) collective-permute-start(bf16[640,256]{1,0:T(8,128)(2,1)} %get-tuple-element.191.b0), channel_id=1, source_target_pairs={{0,16},{8,24},{16,0},{24,8},{1,17},{9,25},{17,1},{25,9},{2,18},{10... | collective-permute-start | bytes 983048 | tf_op jit(solution)/shard_map/ppermute | solution.py:37
  29.2 22.5 %collective-permute-start.9 = (bf16[240,960]{1,0:T(8,128)(2,1)S(1)}, bf16[240,960]{1,0:T(8,128)(2,1)S(1)}, u32[]{:S(2)}, u32[]{:S(2)}) collective-permute-start(bf16[240,960]{1,0:T(8,128)(2,1)S(1)} %copy-done.23), channel_id=1, source_target_pairs={{0,16},{8,24},{16,0},{24,8},{1,17},{9,25},{17,1},{25,9},{2,18},{10... | collective-permute-start | bytes 1382408 | tf_op jit(solution)/shard_map/ppermute | solution.py:37
  38.3 2.3 collective-permute-start.7
  38.3 2.3 collective-permute-start.8
  38.8 16.2 %collective-permute-start.12 = (bf16[640,256]{1,0:T(8,128)(2,1)S(1)}, bf16[640,256]{1,0:T(8,128)(2,1)S(1)}, u32[]{:S(2)}, u32[]{:S(2)}) collective-permute-start(bf16[640,256]{1,0:T(8,128)(2,1)S(1)} %copy-done.10), channel_id=1, source_target_pairs={{0,16},{8,24},{16,0},{24,8},{1,17},{9,25},{17,1},{25,9},{2,18},{10... | collective-permute-start | bytes 983048 | tf_op jit(solution)/shard_map/ppermute | solution.py:37
  51.7 5.7 %collective-permute-start.10 = (bf16[240,960]{1,0:T(8,128)(2,1)S(1)}, bf16[240,960]{1,0:T(8,128)(2,1)S(1)}, u32[]{:S(2)}, u32[]{:S(2)}) collective-permute-start(bf16[240,960]{1,0:T(8,128)(2,1)S(1)} %copy-done.23), channel_id=1, source_target_pairs={{0,8},{8,0},{16,24},{24,16},{1,9},{9,1},{17,25},{25,17},{2,10},{10... | collective-permute-start | bytes 1382408 | tf_op jit(solution)/shard_map/ppermute | solution.py:37
  51.7 5.7 %collective-permute-start.11 = (bf16[240,960]{1,0:T(8,128)(2,1)S(1)}, bf16[240,960]{1,0:T(8,128)(2,1)S(1)}, u32[]{:S(2)}, u32[]{:S(2)}) collective-permute-start(bf16[240,960]{1,0:T(8,128)(2,1)S(1)} %collective-permute-done.9.b2), channel_id=1, source_target_pairs={{0,8},{8,0},{16,24},{24,16},{1,9},{9,1},{17,25},{25,17},{2,10},{10... | collective-permute-start | bytes 1382408 | tf_op jit(solution)/shard_map/ppermute | solution.py:37
  54.9 2.4 collective-permute-start.13
  54.9 2.4 collective-permute-start.14
  55.6 35.2 %copy-start.52 = (bf16[960,256]{1,0:T(8,128)(2,1)}, bf16[960,256]{1,0:T(8,128)(2,1)S(1)}, u32[]{:S(2)}) copy-start(bf16[960,256]{1,0:T(8,128)(2,1)S(1)} %get-tuple-element.227.refs_4_) | copy-start | bytes 1474564
  55.6 18.1 %collective-permute-start.15 = (bf16[960,256]{1,0:T(8,128)(2,1)S(1)}, bf16[960,256]{1,0:T(8,128)(2,1)S(1)}, u32[]{:S(2)}, u32[]{:S(2)}) collective-permute-start(bf16[960,256]{1,0:T(8,128)(2,1)S(1)} %get-tuple-element.246.refs_0_), channel_id=1, source_target_pairs={{0,16},{8,24},{16,0},{24,8},{1,17},{9,25},{17,1},{25,9},{2,18},{10... | collective-permute-start | bytes 1474568 | tf_op jit(solution)/shard_map/ppermute | solution.py:37
  61.3 19.4 %collective-permute-start.17 = (bf16[960,256]{1,0:T(8,128)(2,1)}, bf16[960,256]{1,0:T(8,128)(2,1)S(1)}, u32[]{:S(2)}, u32[]{:S(2)}) collective-permute-start(bf16[960,256]{1,0:T(8,128)(2,1)} %get-tuple-element.254.x_a.refs_0_), channel_id=1, source_target_pairs={{0,16},{8,24},{16,0},{24,8},{1,17},{9,25},{17,1},{25,9},{2,18},{10... | collective-permute-start | bytes 1474568 | tf_op jit(solution)/shard_map/ppermute | solution.py:37
  73.7 6.9 %collective-permute-start.20 = (bf16[960,256]{1,0:T(8,128)(2,1)S(1)}, bf16[960,256]{1,0:T(8,128)(2,1)S(1)}, u32[]{:S(2)}, u32[]{:S(2)}) collective-permute-start(bf16[960,256]{1,0:T(8,128)(2,1)S(1)} %get-tuple-element.246.refs_0_), channel_id=1, source_target_pairs={{0,8},{8,0},{16,24},{24,16},{1,9},{9,1},{17,25},{25,17},{2,10},{10... | collective-permute-start | bytes 1474568 | tf_op jit(solution)/shard_map/ppermute | solution.py:37
  73.8 6.9 %collective-permute-start.21 = (bf16[960,256]{1,0:T(8,128)(2,1)S(1)}, bf16[960,256]{1,0:T(8,128)(2,1)S(1)}, u32[]{:S(2)}, u32[]{:S(2)}) collective-permute-start(bf16[960,256]{1,0:T(8,128)(2,1)S(1)} %collective-permute-done.15.refs_4_.refs_2_), channel_id=1, source_target_pairs={{0,8},{8,0},{16,24},{24,16},{1,9},{9,1},{17,25},{25,17},{2,10},{10... | collective-permute-start | bytes 1474568 | tf_op jit(solution)/shard_map/ppermute | solution.py:37
  74.3 16.5 %collective-permute-start.22 = (bf16[960,256]{1,0:T(8,128)(2,1)S(1)}, bf16[960,256]{1,0:T(8,128)(2,1)S(1)}, u32[]{:S(2)}, u32[]{:S(2)}) collective-permute-start(bf16[960,256]{1,0:T(8,128)(2,1)S(1)} %get-tuple-element.227.refs_4_), channel_id=1, source_target_pairs={{0,16},{8,24},{16,0},{24,8},{1,17},{9,25},{17,1},{25,9},{2,18},{10... | collective-permute-start | bytes 1474568 | tf_op jit(solution)/shard_map/ppermute | solution.py:37
  79.5 24.4 %collective-permute-start.16 = (bf16[960,256]{1,0:T(8,128)(2,1)}, bf16[960,256]{1,0:T(8,128)(2,1)S(1)}, u32[]{:S(2)}, u32[]{:S(2)}) collective-permute-start(bf16[960,256]{1,0:T(8,128)(2,1)} %get-tuple-element.232.x_b.refs_4_), channel_id=1, source_target_pairs={{0,16},{8,24},{16,0},{24,8},{1,17},{9,25},{17,1},{25,9},{2,18},{10... | collective-permute-start | bytes 1474568 | tf_op jit(solution)/shard_map/ppermute | solution.py:37
  80.7 10.6 %collective-permute-start.18 = (bf16[960,256]{1,0:T(8,128)(2,1)S(1)}, bf16[960,256]{1,0:T(8,128)(2,1)S(1)}, u32[]{:S(2)}, u32[]{:S(2)}) collective-permute-start(bf16[960,256]{1,0:T(8,128)(2,1)S(1)} %copy-done.63), channel_id=1, source_target_pairs={{0,8},{8,0},{16,24},{24,16},{1,9},{9,1},{17,25},{25,17},{2,10},{10... | collective-permute-start | bytes 1474568 | tf_op jit(solution)/shard_map/ppermute | solution.py:37
  80.8 10.6 %collective-permute-start.19 = (bf16[960,256]{1,0:T(8,128)(2,1)S(1)}, bf16[960,256]{1,0:T(8,128)(2,1)S(1)}, u32[]{:S(2)}, u32[]{:S(2)}) collective-permute-start(bf16[960,256]{1,0:T(8,128)(2,1)S(1)} %collective-permute-done.17.refs_1_.refs_2_), channel_id=1, source_target_pairs={{0,8},{8,0},{16,24},{24,16},{1,9},{9,1},{17,25},{25,17},{2,10},{10... | collective-permute-start | bytes 1474568 | tf_op jit(solution)/shard_map/ppermute | solution.py:37
  90.8 13.6 %collective-permute-start.25 = (bf16[960,256]{1,0:T(8,128)(2,1)S(1)}, bf16[960,256]{1,0:T(8,128)(2,1)S(1)}, u32[]{:S(2)}, u32[]{:S(2)}) collective-permute-start(bf16[960,256]{1,0:T(8,128)(2,1)S(1)} %get-tuple-element.227.refs_4_), channel_id=1, source_target_pairs={{0,8},{8,0},{16,24},{24,16},{1,9},{9,1},{17,25},{25,17},{2,10},{10... | collective-permute-start | bytes 1474568 | tf_op jit(solution)/shard_map/ppermute | solution.py:37
  90.8 13.6 %collective-permute-start.26 = (bf16[960,256]{1,0:T(8,128)(2,1)S(1)}, bf16[960,256]{1,0:T(8,128)(2,1)S(1)}, u32[]{:S(2)}, u32[]{:S(2)}) collective-permute-start(bf16[960,256]{1,0:T(8,128)(2,1)S(1)} %collective-permute-done.22.refs_4_.refs_6_), channel_id=1, source_target_pairs={{0,8},{8,0},{16,24},{24,16},{1,9},{9,1},{17,25},{25,17},{2,10},{10... | collective-permute-start | bytes 1474568 | tf_op jit(solution)/shard_map/ppermute | solution.py:37
  103.9 1.9 collective-permute-start.23
  104.0 3.2 %collective-permute-start.24 = (bf16[960,256]{1,0:T(8,128)(2,1)S(1)}, bf16[960,256]{1,0:T(8,128)(2,1)S(1)}, u32[]{:S(2)}, u32[]{:S(2)}) collective-permute-start(bf16[960,256]{1,0:T(8,128)(2,1)S(1)} %collective-permute-done.16.refs_1_.refs_6_), channel_id=1, source_target_pairs={{0,8},{8,0},{16,24},{24,16},{1,9},{9,1},{17,25},{25,17},{2,10},{10... | collective-permute-start | bytes 1474568 | tf_op jit(solution)/shard_map/ppermute | solution.py:37
  104.5 15.7 %collective-permute-start.28 = (bf16[2,960,256]{2,1,0:T(8,128)(2,1)}, bf16[2,960,256]{2,1,0:T(8,128)(2,1)S(1)}, u32[]{:S(2)}, u32[]{:S(2)}) collective-permute-start(bf16[2,960,256]{2,1,0:T(8,128)(2,1)} %get-tuple-element.239), channel_id=1, source_target_pairs={{0,8},{8,0},{16,24},{24,16},{1,9},{9,1},{17,25},{25,17},{2,10},{10... | collective-permute-start | bytes 2949128 | tf_op jit(solution)/shard_map/ppermute | solution.py:37
  104.6 17.5 %collective-permute-start.29 = (bf16[2,960,256]{2,1,0:T(8,128)(2,1)}, bf16[2,960,256]{2,1,0:T(8,128)(2,1)S(1)}, u32[]{:S(2)}, u32[]{:S(2)}) collective-permute-start(bf16[2,960,256]{2,1,0:T(8,128)(2,1)} %get-tuple-element.243), channel_id=1, source_target_pairs={{0,8},{8,0},{16,24},{24,16},{1,9},{9,1},{17,25},{25,17},{2,10},{10... | collective-permute-start | bytes 2949128 | tf_op jit(solution)/shard_map/ppermute | solution.py:37
  119.6 12.7 %collective-permute-start.27 = (bf16[2,960,256]{2,1,0:T(8,128)(2,1)}, bf16[2,960,256]{2,1,0:T(8,128)(2,1)S(1)}, u32[]{:S(2)}, u32[]{:S(2)}) collective-permute-start(bf16[2,960,256]{2,1,0:T(8,128)(2,1)} %get-tuple-element.238), channel_id=1, source_target_pairs={{0,8},{8,0},{16,24},{24,16},{1,9},{9,1},{17,25},{25,17},{2,10},{10... | collective-permute-start | bytes 2949128 | tf_op jit(solution)/shard_map/ppermute | solution.py:37
  119.8 14.3 %collective-permute-start.30 = (bf16[2,960,256]{2,1,0:T(8,128)(2,1)}, bf16[2,960,256]{2,1,0:T(8,128)(2,1)S(1)}, u32[]{:S(2)}, u32[]{:S(2)}) collective-permute-start(bf16[2,960,256]{2,1,0:T(8,128)(2,1)} %get-tuple-element.253), channel_id=1, source_target_pairs={{0,8},{8,0},{16,24},{24,16},{1,9},{9,1},{17,25},{25,17},{2,10},{10... | collective-permute-start | bytes 2949128 | tf_op jit(solution)/shard_map/ppermute | solution.py:37
  120.3 27.9 %collective-permute-start.36 = (bf16[960,256]{1,0:T(8,128)(2,1)S(1)}, bf16[960,256]{1,0:T(8,128)(2,1)S(1)}, u32[]{:S(2)}, u32[]{:S(2)}) collective-permute-start(bf16[960,256]{1,0:T(8,128)(2,1)S(1)} %fusion.6), channel_id=1, source_target_pairs={{0,16},{8,24},{16,0},{24,8},{1,17},{9,25},{17,1},{25,9},{2,18},{10... | collective-permute-start | bytes 1474568 | tf_op jit(solution)/shard_map/ppermute | solution.py:37
  122.3 27.8 %collective-permute-start.37 = (bf16[960,256]{1,0:T(8,128)(2,1)S(1)}, bf16[960,256]{1,0:T(8,128)(2,1)S(1)}, u32[]{:S(2)}, u32[]{:S(2)}) collective-permute-start(bf16[960,256]{1,0:T(8,128)(2,1)S(1)} %fusion.5), channel_id=1, source_target_pairs={{0,16},{8,24},{16,0},{24,8},{1,17},{9,25},{17,1},{25,9},{2,18},{10... | collective-permute-start | bytes 1474568 | tf_op jit(solution)/shard_map/ppermute | solution.py:37
  130.5 17.2 %collective-permute-start.34 = (bf16[4,120,640]{2,1,0:T(8,128)(2,1)}, bf16[4,120,640]{2,1,0:T(8,128)(2,1)S(1)}, u32[]{:S(2)}, u32[]{:S(2)}) collective-permute-start(bf16[4,120,640]{2,1,0:T(8,128)(2,1)} %get-tuple-element.250), channel_id=1, source_target_pairs={{0,1},{1,0},{2,3},{3,2},{4,5},{5,4},{6,7},{7,6},{8,9},{9,8},{10,11... | collective-permute-start | bytes 1843208 | tf_op jit(solution)/shard_map/ppermute | solution.py:37
  132.4 26.4 %collective-permute-start.32 = (bf16[960,256]{1,0:T(8,128)(2,1)S(1)}, bf16[960,256]{1,0:T(8,128)(2,1)S(1)}, u32[]{:S(2)}, u32[]{:S(2)}) collective-permute-start(bf16[960,256]{1,0:T(8,128)(2,1)S(1)} %fusion.4), channel_id=1, source_target_pairs={{0,16},{8,24},{16,0},{24,8},{1,17},{9,25},{17,1},{25,9},{2,18},{10... | collective-permute-start | bytes 1474568 | tf_op jit(solution)/shard_map/ppermute | solution.py:37
  147.0 29.8 %collective-permute-start.31 = (bf16[4,120,1280]{2,1,0:T(8,128)(2,1)}, bf16[4,120,1280]{2,1,0:T(8,128)(2,1)S(1)}, u32[]{:S(2)}, u32[]{:S(2)}) collective-permute-start(bf16[4,120,1280]{2,1,0:T(8,128)(2,1)} %get-tuple-element.262), channel_id=1, source_target_pairs={{0,1},{1,0},{2,3},{3,2},{4,5},{5,4},{6,7},{7,6},{8,9},{9,8},{10,11... | collective-permute-start | bytes 3686408 | tf_op jit(solution)/shard_map/ppermute | solution.py:37
  147.8 23.1 %collective-permute-start.33 = (bf16[960,256]{1,0:T(8,128)(2,1)S(1)}, bf16[960,256]{1,0:T(8,128)(2,1)S(1)}, u32[]{:S(2)}, u32[]{:S(2)}) collective-permute-start(bf16[960,256]{1,0:T(8,128)(2,1)S(1)} %fusion.3), channel_id=1, source_target_pairs={{0,16},{8,24},{16,0},{24,8},{1,17},{9,25},{17,1},{25,9},{2,18},{10... | collective-permute-start | bytes 1474568 | tf_op jit(solution)/shard_map/ppermute | solution.py:37
  148.2 7.7 %collective-permute-start.35 = (bf16[2,120,640]{2,1,0:T(8,128)(2,1)S(1)}, bf16[2,120,640]{2,1,0:T(8,128)(2,1)S(1)}, u32[]{:S(2)}, u32[]{:S(2)}) collective-permute-start(bf16[2,120,640]{2,1,0:T(8,128)(2,1)S(1)} %add_convert_fusion.3), channel_id=1, source_target_pairs={{0,2},{1,3},{2,0},{3,1},{4,6},{5,7},{6,4},{7,5},{8,10},{9,11},{10,... | collective-permute-start | bytes 921608 | tf_op jit(solution)/shard_map/ppermute | solution.py:37
  156.0 14.5 %collective-permute-start.38 = (bf16[1,120,640]{2,1,0:T(8,128)(2,1)S(1)}, bf16[1,120,640]{2,1,0:T(8,128)(2,1)S(1)}, u32[]{:S(2)}, u32[]{:S(2)}) collective-permute-start(bf16[1,120,640]{2,1,0:T(8,128)(2,1)S(1)} %add_convert_fusion.9), channel_id=1, source_target_pairs={{0,4},{1,5},{2,6},{3,7},{4,0},{5,1},{6,2},{7,3},{8,12},{9,13},{10,... | collective-permute-start | bytes 460808 | tf_op jit(solution)/shard_map/ppermute | solution.py:37
  170.4 4.5 %collective-permute-start.40 = (bf16[2,640,256]{2,1,0:T(8,128)(2,1)}, bf16[2,640,256]{2,1,0:T(8,128)(2,1)S(1)}, u32[]{:S(2)}, u32[]{:S(2)}) collective-permute-start(bf16[2,640,256]{2,1,0:T(8,128)(2,1)} %get-tuple-element.287), channel_id=1, source_target_pairs={{0,8},{8,0},{16,24},{24,16},{1,9},{9,1},{17,25},{25,17},{2,10},{10... | collective-permute-start | bytes 1966088 | tf_op jit(solution)/shard_map/ppermute | solution.py:37
  170.7 19.6 %collective-permute-start.41 = (bf16[1,120,640]{2,1,0:T(8,128)(2,1)S(1)}, bf16[1,120,640]{2,1,0:T(8,128)(2,1)S(1)}, u32[]{:S(2)}, u32[]{:S(2)}) collective-permute-start(bf16[1,120,640]{2,1,0:T(8,128)(2,1)S(1)} %add_convert_fusion.8), channel_id=1, source_target_pairs={{0,4},{1,5},{2,6},{3,7},{4,0},{5,1},{6,2},{7,3},{8,12},{9,13},{10,... | collective-permute-start | bytes 460808 | tf_op jit(solution)/shard_map/ppermute | solution.py:37
  175.0 15.4 %collective-permute-start.42 = (bf16[640,256]{1,0:T(8,128)(2,1)S(1)}, bf16[640,256]{1,0:T(8,128)(2,1)S(1)}, u32[]{:S(2)}, u32[]{:S(2)}) collective-permute-start(bf16[640,256]{1,0:T(8,128)(2,1)S(1)} %fusion.13), channel_id=1, source_target_pairs={{0,16},{8,24},{16,0},{24,8},{1,17},{9,25},{17,1},{25,9},{2,18},{10... | collective-permute-start | bytes 983048 | tf_op jit(solution)/shard_map/ppermute | solution.py:37
  176.9 20.2 %collective-permute-start.39 = (bf16[2,120,1280]{2,1,0:T(8,128)(2,1)S(1)}, bf16[2,120,1280]{2,1,0:T(8,128)(2,1)S(1)}, u32[]{:S(2)}, u32[]{:S(2)}) collective-permute-start(bf16[2,120,1280]{2,1,0:T(8,128)(2,1)S(1)} %add_convert_fusion), channel_id=1, source_target_pairs={{0,2},{1,3},{2,0},{3,1},{4,6},{5,7},{6,4},{7,5},{8,10},{9,11},{10,... | collective-permute-start | bytes 1843208 | tf_op jit(solution)/shard_map/ppermute | solution.py:37
  190.2 7.0 %collective-permute-start.44 = (bf16[2,640,256]{2,1,0:T(8,128)(2,1)}, bf16[2,640,256]{2,1,0:T(8,128)(2,1)S(1)}, u32[]{:S(2)}, u32[]{:S(2)}) collective-permute-start(bf16[2,640,256]{2,1,0:T(8,128)(2,1)} %get-tuple-element.302), channel_id=1, source_target_pairs={{0,8},{8,0},{16,24},{24,16},{1,9},{9,1},{17,25},{25,17},{2,10},{10... | collective-permute-start | bytes 1966088 | tf_op jit(solution)/shard_map/ppermute | solution.py:37
  197.4 8.3 %collective-permute-start.45 = (bf16[2,8,32,1920]{3,2,1,0:T(8,128)(2,1)}, bf16[2,8,32,1920]{3,2,1,0:T(8,128)(2,1)S(1)}, u32[]{:S(2)}, u32[]{:S(2)}) collective-permute-start(bf16[2,8,32,1920]{3,2,1,0:T(8,128)(2,1)} %get-tuple-element.305), channel_id=1, source_target_pairs={{0,8},{8,0},{16,24},{24,16},{1,9},{9,1},{17,25},{25,17},{2,10},{10... | collective-permute-start | bytes 5898248 | tf_op jit(solution)/shard_map/ppermute | solution.py:37
  197.9 20.8 %collective-permute-start.47 = (bf16[2,120,640]{2,1,0:T(8,128)(2,1)S(1)}, bf16[2,120,640]{2,1,0:T(8,128)(2,1)S(1)}, u32[]{:S(2)}, u32[]{:S(2)}) collective-permute-start(bf16[2,120,640]{2,1,0:T(8,128)(2,1)S(1)} %pad_maximum_fusion.7), channel_id=1, source_target_pairs={{0,2},{1,3},{2,0},{3,1},{4,6},{5,7},{6,4},{7,5},{8,10},{9,11},{10,... | collective-permute-start | bytes 921608 | tf_op jit(solution)/shard_map/ppermute | solution.py:37
  198.4 20.4 %collective-permute-start.43 = (bf16[1,120,1280]{2,1,0:T(8,128)(2,1)S(1)}, bf16[1,120,1280]{2,1,0:T(8,128)(2,1)S(1)}, u32[]{:S(2)}, u32[]{:S(2)}) collective-permute-start(bf16[1,120,1280]{2,1,0:T(8,128)(2,1)S(1)} %add_convert_fusion.2), channel_id=1, source_target_pairs={{0,4},{1,5},{2,6},{3,7},{4,0},{5,1},{6,2},{7,3},{8,12},{9,13},{10,... | collective-permute-start | bytes 921608 | tf_op jit(solution)/shard_map/ppermute | solution.py:37
  201.0 10.6 %collective-permute-start.46 = (bf16[640,256]{1,0:T(8,128)(2,1)S(1)}, bf16[640,256]{1,0:T(8,128)(2,1)S(1)}, u32[]{:S(2)}, u32[]{:S(2)}) collective-permute-start(bf16[640,256]{1,0:T(8,128)(2,1)S(1)} %fusion.12), channel_id=1, source_target_pairs={{0,16},{8,24},{16,0},{24,8},{1,17},{9,25},{17,1},{25,9},{2,18},{10... | collective-permute-start | bytes 983048 | tf_op jit(solution)/shard_map/ppermute | solution.py:37
  206.0 26.7 %collective-permute-start.48 = (bf16[8,32,1920]{2,1,0:T(8,128)(2,1)S(1)}, bf16[8,32,1920]{2,1,0:T(8,128)(2,1)S(1)}, u32[]{:S(2)}, u32[]{:S(2)}) collective-permute-start(bf16[8,32,1920]{2,1,0:T(8,128)(2,1)S(1)} %fusion), channel_id=1, source_target_pairs={{0,16},{8,24},{16,0},{24,8},{1,17},{9,25},{17,1},{25,9},{2,18},{10... | collective-permute-start | bytes 2949128 | tf_op jit(solution)/shard_map/ppermute | solution.py:37
  218.7 2.3 collective-permute-start.49
  219.0 21.2 %collective-permute-start.56 = (bf16[1,120,1280]{2,1,0:T(8,128)(2,1)S(1)}, bf16[1,120,1280]{2,1,0:T(8,128)(2,1)S(1)}, u32[]{:S(2)}, u32[]{:S(2)}) collective-permute-start(bf16[1,120,1280]{2,1,0:T(8,128)(2,1)S(1)} %add_convert_fusion.1), channel_id=1, source_target_pairs={{0,4},{1,5},{2,6},{3,7},{4,0},{5,1},{6,2},{7,3},{8,12},{9,13},{10,... | collective-permute-start | bytes 921608 | tf_op jit(solution)/shard_map/ppermute | solution.py:37
  219.4 22.4 %collective-permute-start.52 = (bf16[4,120,640]{2,1,0:T(8,128)(2,1)S(1)}, bf16[4,120,640]{2,1,0:T(8,128)(2,1)S(1)}, u32[]{:S(2)}, u32[]{:S(2)}) collective-permute-start(bf16[4,120,640]{2,1,0:T(8,128)(2,1)S(1)} %pad_maximum_fusion.4.even), channel_id=1, source_target_pairs={{0,1},{1,0},{2,3},{3,2},{4,5},{5,4},{6,7},{7,6},{8,9},{9,8},{10,11... | collective-permute-start | bytes 1843208 | tf_op jit(solution)/shard_map/ppermute | solution.py:37
  221.1 17.1 %collective-permute-start.50 = (bf16[8,32,640]{2,1,0:T(8,128)(2,1)S(1)}, bf16[8,32,640]{2,1,0:T(8,128)(2,1)S(1)}, u32[]{:S(2)}, u32[]{:S(2)}) collective-permute-start(bf16[8,32,640]{2,1,0:T(8,128)(2,1)S(1)} %fusion.11), channel_id=1, source_target_pairs={{0,16},{8,24},{16,0},{24,8},{1,17},{9,25},{17,1},{25,9},{2,18},{10... | collective-permute-start | bytes 983048 | tf_op jit(solution)/shard_map/ppermute | solution.py:37
  238.3 15.3 %collective-permute-start.51 = (bf16[4,32,2560]{2,1,0:T(8,128)(2,1)S(1)}, bf16[4,32,2560]{2,1,0:T(8,128)(2,1)S(1)}, u32[]{:S(2)}, u32[]{:S(2)}) collective-permute-start(bf16[4,32,2560]{2,1,0:T(8,128)(2,1)S(1)} %pad_maximum_fusion.2), channel_id=1, source_target_pairs={{0,1},{1,0},{2,3},{3,2},{4,5},{5,4},{6,7},{7,6},{8,9},{9,8},{10,11... | collective-permute-start | bytes 1966088 | tf_op jit(solution)/shard_map/ppermute | solution.py:37
  240.3 17.1 %collective-permute-start.57 = (bf16[2,120,1280]{2,1,0:T(8,128)(2,1)S(1)}, bf16[2,120,1280]{2,1,0:T(8,128)(2,1)S(1)}, u32[]{:S(2)}, u32[]{:S(2)}) collective-permute-start(bf16[2,120,1280]{2,1,0:T(8,128)(2,1)S(1)} %pad_maximum_fusion.5), channel_id=1, source_target_pairs={{0,2},{1,3},{2,0},{3,1},{4,6},{5,7},{6,4},{7,5},{8,10},{9,11},{10,... | collective-permute-start | bytes 1843208 | tf_op jit(solution)/shard_map/ppermute | solution.py:37
  253.8 9.4 %collective-permute-start.54 = (bf16[1,32,2560]{2,1,0:T(8,128)(2,1)S(1)}, bf16[1,32,2560]{2,1,0:T(8,128)(2,1)S(1)}, u32[]{:S(2)}, u32[]{:S(2)}) collective-permute-start(bf16[1,32,2560]{2,1,0:T(8,128)(2,1)S(1)} %get-tuple-element.347), channel_id=1, source_target_pairs={{0,2},{1,3},{2,0},{3,1},{4,6},{5,7},{6,4},{7,5},{8,10},{9,11},{10,... | collective-permute-start | bytes 491528 | tf_op jit(solution)/shard_map/ppermute | solution.py:37
  255.4 8.8 %collective-permute-start.53 = (bf16[1,32,2560]{2,1,0:T(8,128)(2,1)S(1)}, bf16[1,32,2560]{2,1,0:T(8,128)(2,1)S(1)}, u32[]{:S(2)}, u32[]{:S(2)}) collective-permute-start(bf16[1,32,2560]{2,1,0:T(8,128)(2,1)S(1)} %get-tuple-element.348), channel_id=1, source_target_pairs={{0,6},{1,7},{2,4},{3,5},{4,2},{5,3},{6,0},{7,1},{8,14},{9,15},{10,... | collective-permute-start | bytes 491528 | tf_op jit(solution)/shard_map/ppermute | solution.py:37
  255.6 13.7 %collective-permute-start.55 = (bf16[1,32,2560]{2,1,0:T(8,128)(2,1)S(1)}, bf16[1,32,2560]{2,1,0:T(8,128)(2,1)S(1)}, u32[]{:S(2)}, u32[]{:S(2)}) collective-permute-start(bf16[1,32,2560]{2,1,0:T(8,128)(2,1)S(1)} %get-tuple-element.353), channel_id=1, source_target_pairs={{0,4},{1,5},{2,6},{3,7},{4,0},{5,1},{6,2},{7,3},{8,12},{9,13},{10,... | collective-permute-start | bytes 491528 | tf_op jit(solution)/shard_map/ppermute | solution.py:37
  257.4 26.3 %collective-permute-start.61 = (bf16[4,120,1280]{2,1,0:T(8,128)(2,1)S(1)}, bf16[4,120,1280]{2,1,0:T(8,128)(2,1)S(1)}, u32[]{:S(2)}, u32[]{:S(2)}) collective-permute-start(bf16[4,120,1280]{2,1,0:T(8,128)(2,1)S(1)} %pad_maximum_fusion.1.even), channel_id=1, source_target_pairs={{0,1},{1,0},{2,3},{3,2},{4,5},{5,4},{6,7},{7,6},{8,9},{9,8},{10,11... | collective-permute-start | bytes 3686408 | tf_op jit(solution)/shard_map/ppermute | solution.py:37
  269.5 8.7 %collective-permute-start.60 = (bf16[1,32,2560]{2,1,0:T(8,128)(2,1)S(1)}, bf16[1,32,2560]{2,1,0:T(8,128)(2,1)S(1)}, u32[]{:S(2)}, u32[]{:S(2)}) collective-permute-start(bf16[1,32,2560]{2,1,0:T(8,128)(2,1)S(1)} %add_convert_fusion.4), channel_id=1, source_target_pairs={{0,6},{1,7},{2,4},{3,5},{4,2},{5,3},{6,0},{7,1},{8,14},{9,15},{10,... | collective-permute-start | bytes 491528 | tf_op jit(solution)/shard_map/ppermute | solution.py:37
  273.0 7.2 %collective-permute-start.59 = (bf16[1,32,2560]{2,1,0:T(8,128)(2,1)S(1)}, bf16[1,32,2560]{2,1,0:T(8,128)(2,1)S(1)}, u32[]{:S(2)}, u32[]{:S(2)}) collective-permute-start(bf16[1,32,2560]{2,1,0:T(8,128)(2,1)S(1)} %add_convert_fusion.4), channel_id=1, source_target_pairs={{0,2},{1,3},{2,0},{3,1},{4,6},{5,7},{6,4},{7,5},{8,10},{9,11},{10,... | collective-permute-start | bytes 491528 | tf_op jit(solution)/shard_map/ppermute | solution.py:37
  273.0 10.7 %collective-permute-start.58 = (bf16[1,32,2560]{2,1,0:T(8,128)(2,1)S(1)}, bf16[1,32,2560]{2,1,0:T(8,128)(2,1)S(1)}, u32[]{:S(2)}, u32[]{:S(2)}) collective-permute-start(bf16[1,32,2560]{2,1,0:T(8,128)(2,1)S(1)} %add_convert_fusion.4), channel_id=1, source_target_pairs={{0,4},{1,5},{2,6},{3,7},{4,0},{5,1},{6,2},{7,3},{8,12},{9,13},{10,... | collective-permute-start | bytes 491528 | tf_op jit(solution)/shard_map/ppermute | solution.py:37
  283.9 15.1 %collective-permute-start.62 = (bf16[4,32,2560]{2,1,0:T(8,128)(2,1)S(1)}, bf16[4,32,2560]{2,1,0:T(8,128)(2,1)S(1)}, u32[]{:S(2)}, u32[]{:S(2)}) collective-permute-start(bf16[4,32,2560]{2,1,0:T(8,128)(2,1)S(1)} %pad_maximum_fusion.3.even), channel_id=1, source_target_pairs={{0,1},{1,0},{2,3},{3,2},{4,5},{5,4},{6,7},{7,6},{8,9},{9,8},{10,11... | collective-permute-start | bytes 1966088 | tf_op jit(solution)/shard_map/ppermute | solution.py:37
  (72 other events, 688.5 us)

commit v9 on v8

--- a/solution.py
+++ b/solution.py
@@ -380,18 +380,19 @@
     rights = refs[2 * GROUP : 2 * GROUP + 3 * kinds]
     outs = refs[2 * GROUP + 3 * kinds : 2 * GROUP + 3 * kinds + 4]
     left, right, acc, sem = refs[2 * GROUP + 3 * kinds + 4 :]
-    span = left.shape[2] // GROUP
+    length = left.shape[1] // 2
+    span = length // GROUP
     kind = pl.program_id(0)
     lefts, loads = [], []
     for b, block in enumerate(blocks):
         s, k = divmod(b, GROUP)
-        lefts.append(pltpu.make_async_copy(block, left.at[s, :, pl.ds(k * span, span)], sem.at[b]))
+        lefts.append(pltpu.make_async_copy(block, left.at[:, pl.ds(b * span, span)], sem.at[b]))
     for n in range(kinds):
         own, *others = rights[3 * n : 3 * n + 3]
         for s in range(2):
-            for i, (source, part) in enumerate(((own.at[s], slice(0, span)), (others[s], slice(span, GROUP * span)))):
+            for i, (source, part) in enumerate(((own.at[s], pl.ds(s * length, span)), (others[s], pl.ds(s * length + span, length - span)))):
                 at = sem.at[2 * GROUP + 4 * n + 2 * s + i]
-                loads.append(pltpu.make_async_copy(source, right.at[n, s, :, part], at))
+                loads.append(pltpu.make_async_copy(source, right.at[n, :, part], at))
 
     @pl.when(kind == 0)
     def _():
@@ -407,14 +408,17 @@
             for copy in loads[4 * n : 4 * n + 4]:
                 copy.wait()
 
-    acc[...] = dot(left[0], right[kind, 0], NT)
-
     @pl.when(kind == 0)
     def _():
+        acc[...] = dot(left[:, 0:length], right[0, :, 0:length], NT)
         for copy in loads[2:4] + lefts[GROUP:]:
             copy.wait()
-
-    acc[...] += dot(left[1], right[kind, 1], NT)
+        acc[...] += dot(left[:, length:], right[0, :, length:], NT)
+
+    @pl.when(kind > 0)
+    def _():
+        acc[...] = dot(left[...], right[kind], NT)
+
     part = acc.shape[0] // PARTS
     places = [(outs[0], i) for i in range(4)] + [(outs[1], 0), (outs[1], 1), (outs[2], 0), (outs[3], 0)]
     for (out, i), slot in zip(places, SLOTS):
@@ -795,8 +799,8 @@
             in_specs=[ANY] * (2 * GROUP + 3 * count),
             out_specs=tuple(pl.BlockSpec((n, part, ff), lambda m, *_: (0, 0, m)) for n in (4, 2, 1, 1)),
             scratch=[
-                pltpu.VMEM((2, width, length), LOW),
-                pltpu.VMEM((count, 2, ff, length), LOW),
+                pltpu.VMEM((width, 2 * length), LOW),
+                pltpu.VMEM((count, ff, 2 * length), LOW),
                 pltpu.VMEM((width, ff), FULL),
                 pltpu.SemaphoreType.DMA((2 * GROUP + 4 * count,)),
             ],

time: 308 us -> 307 us (level)
  waiting for transfers between devices: 77.3 us -> 73.9 us
    ppermute x63, waiting for transfers between devices: 77.3 us -> 73.9 us  [swap(): return lax.ppermute(values, axis, [(i, i ^ mask) for i in range(count)])]
where the time goes in v9:
time: 307 us; the launch traced here: 301 us
  Pallas kernels  159 us (52%)
  waiting for transfers between devices  73.9 us (24%)
  starting transfers between devices  56.8 us (19%)
  other arithmetic  6.84 us (2%)
    pallas_call x24, Pallas kernels, placed(): return run(*args[:prefetch], *rest)  159 us
    ppermute x63, waiting for transfers between devices, swap(): return lax.ppermute(values, axis, [(i, i ^ mask) for i in range(count)])  73.9 us
    ppermute x63, starting transfers between devices, swap(): return lax.ppermute(values, axis, [(i, i ^ mask) for i in range(count)])  56.8 us
  transfers between devices with their start and end apart: 63, of which 21 were waited for; matrix products, arithmetic and copies ran while one was open for 2% of the time, Pallas kernels for 51%

profile of v9, /device:TPU:0, one launch (start us, length us, event | category | flops | bytes accessed | tf_op | source)
XLA Modules:
  0.0 301.5 jit_solution(8196063299087184012)
XLA Ops:
  2.6 2.1 pack.1.b0.refs_10_
  4.7 3.0 collective-permute-start
  7.9 4.8 %flip_two.1 = (bf16[1280,960]{1,0:T(8,128)(2,1)}, bf16[960,1280]{1,0:T(8,128)(2,1)}) custom-call(bf16[960,640]{1,0:T(8,128)(2,1)} %wg_ref, bf16[960,640]{1,0:T(8,128)(2,1)} %wu_ref.1), custom_call_target="tpu_custom_call" | custom-call | flops 8000000000 | bytes 1024 | tf_op jit(solution)/shard_map/flip_two/pallas_call | solution.py:179
  12.7 2.9 flip_one.1.wd_ref.refs_9_
  15.6 1.7 collective-permute-done.b2.refs_12_
  19.5 3.6 %keys_values.1 = (bf16[960,512]{1,0:T(8,128)(2,1)}, bf16[640,256]{1,0:T(8,128)(2,1)}, bf16[640,256]{1,0:T(8,128)(2,1)}, bf16[960,128]{1,0:T(8,128)(2,1)}) custom-call(s32[2]{0:T(128)S(1)} %pad_add_fusion.ranks, bf16[2,960,256]{2,1,0:T(8,128)(2,1)S(1)} %bitcast.109, bf16[240,768]{1,0:T(8,128)(2,1)S(1)} %copy-done.30, ...), custom_call_target="tpu_custom_call" | custom-call | flops 8600000512 | bytes 1024 | tf_op jit(solution)/shard_map/keys_values/pallas_call | solution.py:179
  23.1 3.9 %collective-permute-done.3.b2.q2 = bf16[240,960]{1,0:T(8,128)(2,1)S(1)} collective-permute-done((bf16[240,960]{1,0:T(8,128)(2,1)S(1)}, bf16[240,960]{1,0:T(8,128)(2,1)S(1)}, u32[]{:S(2)}, u32[]{:S(2)}) %collective-permute-start.3) | collective-permute-done | bytes 460832 | tf_op jit(solution)/shard_map/ppermute | solution.py:37
  27.5 1.7 collective-permute-start.6
  29.5 4.4 %queries.1.q_ref = bf16[960,512]{1,0:T(8,128)(2,1)} custom-call(s32[2]{0:T(128)S(1)} %pad_add_fusion.ranks, bf16[960,512]{1,0:T(8,128)(2,1)} %get-tuple-element.184.norm_ref.refs_0_, bf16[240,960]{1,0:T(8,128)(2,1)S(1)} %copy-done.5, bf16[240,960]{1,0:T(8,128)(2,1)S(1)} %collective-permute-done.4.b1.q1, bf16[240,960]{1,0:T(8,128)(2,1)S(1)} %collective-permute-done.3.b2.q2, ...), custom_call_target="tpu_custom_call" | custom-call | flops 200000000 | bytes 1024 | tf_op jit(solution)/shard_map/queries/pallas_call | solution.py:179
  33.9 4.4 %collective-permute-done.6.b2 = bf16[640,256]{1,0:T(8,128)(2,1)S(1)} collective-permute-done((bf16[640,256]{1,0:T(8,128)(2,1)}, bf16[640,256]{1,0:T(8,128)(2,1)S(1)}, u32[]{:S(2)}, u32[]{:S(2)}) %collective-permute-start.6) | collective-permute-done | bytes 327712 | tf_op jit(solution)/shard_map/ppermute | solution.py:37
  38.8 1.7 collective-permute-start.12
  40.5 11.5 %attend.2 = (bf16[5,1024,768]{2,1,0:T(8,128)(2,1)}, bf16[960,256]{1,0:T(8,128)(2,1)}) custom-call(s32[2]{0:T(128)S(1)} %pad_add_fusion.ranks, s32[2,4]{1,0:T(2,128)S(1)} %copy-done.18, s32[2,2]{1,0:T(2,128)S(1)} %copy-done.19, bf16[960,512]{1,0:T(8,128)(2,1)} %queries.1.q_ref, bf16[640,256]{1,0:T(8,128)(2,1)S(1)} %copy-done.12, ...), custom_call_target="tpu_custom_call" | custom-call | flops 200000000 | bytes 1024 | tf_op jit(solution)/shard_map/attend/pallas_call | solution.py:179
  52.5 2.4 collective-permute-done.12.b2
  55.6 1.8 collective-permute-start.15
  57.4 3.9 %middle.2 = (f32[960,256]{1,0:T(8,128)}, bf16[960,256]{1,0:T(8,128)(2,1)}) custom-call(s32[2]{0:T(128)S(1)} %pad_add_fusion.ranks, bf16[960,256]{1,0:T(8,128)(2,1)} %get-tuple-element.195.att_ref.att_a, bf16[240,960]{1,0:T(8,128)(2,1)S(1)} %copy-done.23, bf16[240,960]{1,0:T(8,128)(2,1)S(1)} %collective-permute-done.10.b1, ...), custom_call_target="tpu_custom_call" | custom-call | flops 6000000000 | bytes 1024 | tf_op jit(solution)/shard_map/middle/pallas_call | solution.py:179
  61.3 1.4 collective-permute-start.17
  62.7 11.0 %attend.3 = (bf16[5,1024,768]{2,1,0:T(8,128)(2,1)}, bf16[960,256]{1,0:T(8,128)(2,1)}) custom-call(s32[2]{0:T(128)S(1)} %pad_add_fusion.ranks, s32[2,4]{1,0:T(2,128)S(1)} %copy-done.18, s32[2,2]{1,0:T(2,128)S(1)} %copy-done.19, bf16[960,512]{1,0:T(8,128)(2,1)} %queries.1.q_ref, bf16[640,256]{1,0:T(8,128)(2,1)S(1)} %copy-done.10, ...), custom_call_target="tpu_custom_call" | custom-call | flops 200000000 | bytes 1024 | tf_op jit(solution)/shard_map/attend/pallas_call | solution.py:179
  75.0 4.5 %middle.3 = (f32[960,256]{1,0:T(8,128)}, bf16[960,256]{1,0:T(8,128)(2,1)}) custom-call(s32[2]{0:T(128)S(1)} %pad_add_fusion.ranks, bf16[960,256]{1,0:T(8,128)(2,1)} %get-tuple-element.215.att_ref.att_b, bf16[240,960]{1,0:T(8,128)(2,1)S(1)} %copy-done.23, bf16[240,960]{1,0:T(8,128)(2,1)S(1)} %collective-permute-done.10.b1, ...), custom_call_target="tpu_custom_call" | custom-call | flops 6000000000 | bytes 1024 | tf_op jit(solution)/shard_map/middle/pallas_call | solution.py:179
  81.3 8.2 %own_blocks.1 = (bf16[2,960,256]{2,1,0:T(8,128)(2,1)}, bf16[2,960,256]{2,1,0:T(8,128)(2,1)}, bf16[2,640,256]{2,1,0:T(8,128)(2,1)}, bf16[2,640,256]{2,1,0:T(8,128)(2,1)}, bf16[2,640,256]{2,1,0:T(8,128)(2,1)}) custom-call(bf16[960,256]{1,0:T(8,128)(2,1)} %get-tuple-element.254.x_a.refs_0_, bf16[960,256]{1,0:T(8,128)(2,1)} %get-tuple-element.232.x_b.refs_4_, ...), custom_call_target="tpu_custom_call" | custom-call | flops 16000000000 | bytes 1024 | tf_op jit(solution)/shard_map/own_blocks/pallas_call | solution.py:179
  91.3 12.4 %other_blocks.2 = (bf16[960,256]{1,0:T(8,128)(2,1)}, bf16[2,960,256]{2,1,0:T(8,128)(2,1)}, bf16[960,256]{1,0:T(8,128)(2,1)}, bf16[2,960,256]{2,1,0:T(8,128)(2,1)...) custom-call(bf16[960,256]{1,0:T(8,128)(2,1)S(1)} %collective-permute-done.18.refs_0_.refs_1_, ...), custom_call_target="tpu_custom_call" | custom-call | flops 24000000000 | bytes 1024 | tf_op jit(solution)/shard_map/other_blocks/pallas_call | solution.py:179
  105.8 1.4 collective-permute-done.24.refs_2_.refs_7_
  107.2 12.3 %other_blocks.3 = (bf16[960,256]{1,0:T(8,128)(2,1)}, bf16[2,960,256]{2,1,0:T(8,128)(2,1)}, bf16[960,256]{1,0:T(8,128)(2,1)}, bf16[2,960,256]{2,1,0:T(8,128)(2,1)...) custom-call(bf16[960,256]{1,0:T(8,128)(2,1)S(1)} %collective-permute-done.23.refs_0_.refs_5_, ...), custom_call_target="tpu_custom_call" | custom-call | flops 24000000000 | bytes 1024 | tf_op jit(solution)/shard_map/other_blocks/pallas_call | solution.py:179
  120.3 1.8 collective-permute-start.36
  122.6 7.9 %down_weights.1 = (bf16[4,120,640]{2,1,0:T(8,128)(2,1)}, bf16[2,120,640]{2,1,0:T(8,128)(2,1)}, bf16[1,120,640]{2,1,0:T(8,128)(2,1)}, bf16[1,120,640]{2,1,0:T(8,128)(2,1)}) custom-call(s32[2]{0:T(128)S(1)} %pad_add_fusion.ranks, bf16[960,256]{1,0:T(8,128)(2,1)} %copy-done.53, bf16[960,256]{1,0:T(8,128)(2,1)} %copy-done.68, bf16[960,256]{1,0:T(8,128)(2,1)} %copy-done.65, ...), custom_call_target="tpu_custom_call" | custom-call | flops 16000000000 | bytes 1024 | tf_op jit(solution)/shard_map/down_weights/pallas_call | solution.py:179
  130.5 1.8 collective-permute-start.34
  132.4 1.6 collective-permute-start.32
  134.0 11.7 %gate_up_weights.1 = (bf16[4,120,1280]{2,1,0:T(8,128)(2,1)}, bf16[2,120,1280]{2,1,0:T(8,128)(2,1)}, bf16[1,120,1280]{2,1,0:T(8,128)(2,1)}, bf16[1,120,1280]{2,1,0:T(8,128)(2,1)}) custom-call(s32[2]{0:T(128)S(1)} %pad_add_fusion.ranks, bf16[960,256]{1,0:T(8,128)(2,1)} %get-tuple-element.254.x_a.refs_0_, bf16[960,256]{1,0:T(8,128)(2,1)} %copy-done.26, ...), custom_call_target="tpu_custom_call" | custom-call | flops 28000000000 | bytes 1024 | tf_op jit(solution)/shard_map/gate_up_weights/pallas_call | solution.py:179
  147.9 1.6 collective-permute-start.35
  149.6 4.0 %branch.2 = (f32[960,256]{1,0:T(8,128)}, bf16[960,256]{1,0:T(8,128)(2,1)}, bf16[960,256]{1,0:T(8,128)(2,1)}, f32[16,256]{1,0:T(8,128)}, f32[8,960]{1,0:T(8,128)}) custom-call(s32[2]{0:T(128)S(1)} %pad_add_fusion.ranks, f32[960,256]{1,0:T(8,128)S(1)} %copy-done.2, bf16[2,960,256]{2,1,0:T(8,128)(2,1)S(1)} %bitcast.101, ...), custom_call_target="tpu_custom_call" | custom-call | flops 8000000000 | bytes 1024 | tf_op jit(solution)/shard_map/branch/pallas_call | solution.py:179
  153.6 1.9 collective-permute-done.35
  155.6 2.7 collective-permute-start.38
  158.3 11.6 %attend_back.2 = (bf16[960,256]{1,0:T(8,128)(2,1)}, bf16[640,256]{1,0:T(8,128)(2,1)}, bf16[640,256]{1,0:T(8,128)(2,1)}, bf16[2,640,256]{2,1,0:T(8,128)(2,1)}) custom-call(bf16[960,512]{1,0:T(8,128)(2,1)} %queries.1.q_ref, bf16[640,256]{1,0:T(8,128)(2,1)} %get-tuple-element.191.b0, bf16[640,256]{1,0:T(8,128)(2,1)} %copy-done.16, bf16[640,256]{1,0:T(8,128)(2,1)} %copy-done.15, ...), custom_call_target="tpu_custom_call" | custom-call | flops 22000001024 | bytes 1024 | tf_op jit(solution)/shard_map/attend_back/pallas_call | solution.py:179
  170.5 4.0 %branch.3 = (f32[960,256]{1,0:T(8,128)}, bf16[960,256]{1,0:T(8,128)(2,1)}, bf16[960,256]{1,0:T(8,128)(2,1)}, f32[16,256]{1,0:T(8,128)}, f32[8,960]{1,0:T(8,128)}) custom-call(s32[2]{0:T(128)S(1)} %pad_add_fusion.ranks, f32[960,256]{1,0:T(8,128)S(1)} %copy-done.3, bf16[2,960,256]{2,1,0:T(8,128)(2,1)S(1)} %bitcast.102, ...), custom_call_target="tpu_custom_call" | custom-call | flops 8000000000 | bytes 1024 | tf_op jit(solution)/shard_map/branch/pallas_call | solution.py:179
  176.0 1.6 collective-permute-start.39
  177.7 11.9 %attend_back.3 = (bf16[960,256]{1,0:T(8,128)(2,1)}, bf16[640,256]{1,0:T(8,128)(2,1)}, bf16[640,256]{1,0:T(8,128)(2,1)}, bf16[2,640,256]{2,1,0:T(8,128)(2,1)}) custom-call(bf16[960,512]{1,0:T(8,128)(2,1)} %queries.1.q_ref, bf16[640,256]{1,0:T(8,128)(2,1)} %get-tuple-element.207.b0, bf16[640,256]{1,0:T(8,128)(2,1)} %copy-done.13, bf16[640,256]{1,0:T(8,128)(2,1)} %copy-done.11, ...), custom_call_target="tpu_custom_call" | custom-call | flops 22000001024 | bytes 1024 | tf_op jit(solution)/shard_map/attend_back/pallas_call | solution.py:179
  189.8 6.5 %query_weights.1 = (bf16[8,32,1920]{2,1,0:T(8,128)(2,1)}, bf16[8,32,1920]{2,1,0:T(8,128)(2,1)}, bf16[2,8,32,1920]{3,2,1,0:T(8,128)(2,1)}) custom-call(s32[2]{0:T(128)S(1)} %pad_add_fusion.ranks, bf16[960,512]{1,0:T(8,128)(2,1)S(1)} %copy-done.4, bf16[960,256]{1,0:T(8,128)(2,1)S(1)} %copy-done.38, bf16[960,256]{1,0:T(8,128)(2,1)} %get-tuple-element.306.gq_b, ...), custom_call_target="tpu_custom_call" | custom-call | flops 16000000000 | bytes 1024 | tf_op jit(solution)/shard_map/query_weights/pallas_call | solution.py:179
  197.6 2.2 collective-permute-start.43
  201.0 4.1 %query_grad.1.refs_9_ = f32[2,960,256]{2,1,0:T(8,128)} custom-call(s32[2]{0:T(128)S(1)} %pad_add_fusion.ranks, bf16[960,256]{1,0:T(8,128)(2,1)S(1)} %copy-done.38, bf16[960,256]{1,0:T(8,128)(2,1)} %get-tuple-element.306.gq_b, bf16[240,960]{1,0:T(8,128)(2,1)S(1)} %copy-done.5, bf16[240,960]{1,0:T(8,128)(2,1)S(1)} %copy-done.7, ...), custom_call_target="tpu_custom_call" | custom-call | flops 8000000000 | bytes 1024 | tf_op jit(solution)/shard_map/query_grad/pallas_call | solution.py:179
  206.4 4.1 %collective-permute-done.46.refs_6_ = bf16[640,256]{1,0:T(8,128)(2,1)S(1)} collective-permute-done((bf16[640,256]{1,0:T(8,128)(2,1)S(1)}, bf16[640,256]{1,0:T(8,128)(2,1)S(1)}, u32[]{:S(2)}, u32[]{:S(2)}) %collective-permute-start.46) | collective-permute-done | bytes 327712 | tf_op jit(solution)/shard_map/ppermute | solution.py:37
  210.5 7.1 %key_weights.1 = (bf16[8,32,640]{2,1,0:T(8,128)(2,1)}, bf16[8,32,640]{2,1,0:T(8,128)(2,1)}, bf16[2,8,32,640]{3,2,1,0:T(8,128)(2,1)}, f32[2,960,256]{2,1,0:T(8,128)}) custom-call(s32[2]{0:T(128)S(1)} %pad_add_fusion.ranks, bf16[960,512]{1,0:T(8,128)(2,1)S(1)} %copy-done.4, bf16[640,256]{1,0:T(8,128)(2,1)S(1)} %copy-done.40, ...), custom_call_target="tpu_custom_call" | custom-call | flops 20000000000 | bytes 1024 | tf_op jit(solution)/shard_map/key_weights/pallas_call | solution.py:179
  218.6 1.6 collective-permute-start.52
  221.3 10.2 %collective-permute-done.48 = bf16[8,32,1920]{2,1,0:T(8,128)(2,1)S(1)} collective-permute-done((bf16[8,32,1920]{2,1,0:T(8,128)(2,1)S(1)}, bf16[8,32,1920]{2,1,0:T(8,128)(2,1)S(1)}, u32[]{:S(2)}, u32[]{:S(2)}) %collective-permute-start.48) | collective-permute-done | bytes 983072 | tf_op jit(solution)/shard_map/ppermute | solution.py:37
  231.7 5.3 %collective-permute-done.50 = bf16[8,32,640]{2,1,0:T(8,128)(2,1)S(1)} collective-permute-done((bf16[8,32,640]{2,1,0:T(8,128)(2,1)S(1)}, bf16[8,32,640]{2,1,0:T(8,128)(2,1)S(1)}, u32[]{:S(2)}, u32[]{:S(2)}) %collective-permute-start.50) | collective-permute-done | bytes 327712 | tf_op jit(solution)/shard_map/ppermute | solution.py:37
  237.2 1.5 collective-permute-start.51
  239.1 1.6 collective-permute-start.57
  240.7 2.3 down_done.1
  243.1 9.6 %collective-permute-done.51 = bf16[4,32,2560]{2,1,0:T(8,128)(2,1)S(1)} collective-permute-done((bf16[4,32,2560]{2,1,0:T(8,128)(2,1)S(1)}, bf16[4,32,2560]{2,1,0:T(8,128)(2,1)S(1)}, u32[]{:S(2)}, u32[]{:S(2)}) %collective-permute-start.51) | collective-permute-done | bytes 655392 | tf_op jit(solution)/shard_map/ppermute | solution.py:37
  252.8 1.4 collective-permute-start.54
  254.8 1.6 collective-permute-start.55
  256.5 1.8 collective-permute-start.61
  258.3 3.2 %collective-permute-done.54 = bf16[1,32,2560]{2,1,0:T(8,128)(2,1)S(1)} collective-permute-done((bf16[1,32,2560]{2,1,0:T(8,128)(2,1)S(1)}, bf16[1,32,2560]{2,1,0:T(8,128)(2,1)S(1)}, u32[]{:S(2)}, u32[]{:S(2)}) %collective-permute-start.54) | collective-permute-done | bytes 163872 | tf_op jit(solution)/shard_map/ppermute | solution.py:37
  261.5 1.5 collective-permute-done.53
  263.1 5.6 %collective-permute-done.55 = bf16[1,32,2560]{2,1,0:T(8,128)(2,1)S(1)} collective-permute-done((bf16[1,32,2560]{2,1,0:T(8,128)(2,1)S(1)}, bf16[1,32,2560]{2,1,0:T(8,128)(2,1)S(1)}, u32[]{:S(2)}, u32[]{:S(2)}) %collective-permute-start.55) | collective-permute-done | bytes 163872 | tf_op jit(solution)/shard_map/ppermute | solution.py:37
  268.8 3.1 %collective-permute-start.60 = (bf16[1,32,2560]{2,1,0:T(8,128)(2,1)S(1)}, bf16[1,32,2560]{2,1,0:T(8,128)(2,1)S(1)}, u32[]{:S(2)}, u32[]{:S(2)}) collective-permute-start(bf16[1,32,2560]{2,1,0:T(8,128)(2,1)S(1)} %add_convert_fusion.4), channel_id=1, source_target_pairs={{0,6},{1,7},{2,4},{3,5},{4,2},{5,3},{6,0},{7,1},{8,14},{9,15},{10,... | collective-permute-start | bytes 491528 | tf_op jit(solution)/shard_map/ppermute | solution.py:37
  271.9 1.3 collective-permute-start.58
  273.8 1.4 fusion.30
  275.2 2.5 collective-permute-done.60
  277.8 1.6 collective-permute-done.59
  279.4 3.5 %collective-permute-done.58 = bf16[1,32,2560]{2,1,0:T(8,128)(2,1)S(1)} collective-permute-done((bf16[1,32,2560]{2,1,0:T(8,128)(2,1)S(1)}, bf16[1,32,2560]{2,1,0:T(8,128)(2,1)S(1)}, u32[]{:S(2)}, u32[]{:S(2)}) %collective-permute-start.58) | collective-permute-done | bytes 163872 | tf_op jit(solution)/shard_map/ppermute | solution.py:37
  283.0 2.2 collective-permute-start.62
  285.2 3.5 %gate_up_done.1 = (f32[960,640]{1,0:T(8,128)}, f32[960,640]{1,0:T(8,128)}) custom-call(s32[2]{0:T(128)S(1)} %pad_add_fusion.ranks, bf16[4,120,1280]{2,1,0:T(8,128)(2,1)S(1)} %pad_maximum_fusion.1.even, bf16[4,120,1280]{2,1,0:T(8,128)(2,1)S(1)} %collective-permute-done.61.odd), custom_call_target="tpu_custom_call" | custom-call | flops 14000000000 | bytes 1024 | tf_op jit(solution)/shard_map/gate_up_done/pallas_call | solution.py:179
  288.7 8.3 %collective-permute-done.62.odd = bf16[4,32,2560]{2,1,0:T(8,128)(2,1)S(1)} collective-permute-done((bf16[4,32,2560]{2,1,0:T(8,128)(2,1)S(1)}, bf16[4,32,2560]{2,1,0:T(8,128)(2,1)S(1)}, u32[]{:S(2)}, u32[]{:S(2)}) %collective-permute-start.62) | collective-permute-done | bytes 655392 | tf_op jit(solution)/shard_map/ppermute | solution.py:37
  297.0 2.7 attention_done.1
  299.7 1.3 fusion.31
  (272 shorter events, 27.5 us)
Async XLA Ops:
  4.7 12.6 %collective-permute-start = (bf16[240,768]{1,0:T(8,128)(2,1)}, bf16[240,768]{1,0:T(8,128)(2,1)S(1)}, u32[]{:S(2)}, u32[]{:S(2)}) collective-permute-start(bf16[240,768]{1,0:T(8,128)(2,1)} %pack.1.b0.refs_10_), channel_id=1, source_target_pairs={{0,16},{8,24},{16,0},{24,8},{1,17},{9,25},{17,1},{25,9},{2,18},{10... | collective-permute-start | bytes 1105928 | tf_op jit(solution)/shard_map/ppermute | solution.py:37
  7.6 19.3 %collective-permute-start.3 = (bf16[240,960]{1,0:T(8,128)(2,1)S(1)}, bf16[240,960]{1,0:T(8,128)(2,1)S(1)}, u32[]{:S(2)}, u32[]{:S(2)}) collective-permute-start(bf16[240,960]{1,0:T(8,128)(2,1)S(1)} %copy-done.5), channel_id=1, source_target_pairs={{0,16},{8,24},{16,0},{24,8},{1,17},{9,25},{17,1},{25,9},{2,18},{10... | collective-permute-start | bytes 1382408 | tf_op jit(solution)/shard_map/ppermute | solution.py:37
  17.3 1.7 collective-permute-start.1
  17.3 2.2 collective-permute-start.2
  27.0 2.5 collective-permute-start.4
  27.0 2.6 collective-permute-start.5
  27.5 10.8 %collective-permute-start.6 = (bf16[640,256]{1,0:T(8,128)(2,1)}, bf16[640,256]{1,0:T(8,128)(2,1)S(1)}, u32[]{:S(2)}, u32[]{:S(2)}) collective-permute-start(bf16[640,256]{1,0:T(8,128)(2,1)} %get-tuple-element.191.b0), channel_id=1, source_target_pairs={{0,16},{8,24},{16,0},{24,8},{1,17},{9,25},{17,1},{25,9},{2,18},{10... | collective-permute-start | bytes 983048 | tf_op jit(solution)/shard_map/ppermute | solution.py:37
  29.2 22.8 %collective-permute-start.9 = (bf16[240,960]{1,0:T(8,128)(2,1)S(1)}, bf16[240,960]{1,0:T(8,128)(2,1)S(1)}, u32[]{:S(2)}, u32[]{:S(2)}) collective-permute-start(bf16[240,960]{1,0:T(8,128)(2,1)S(1)} %copy-done.23), channel_id=1, source_target_pairs={{0,16},{8,24},{16,0},{24,8},{1,17},{9,25},{17,1},{25,9},{2,18},{10... | collective-permute-start | bytes 1382408 | tf_op jit(solution)/shard_map/ppermute | solution.py:37
  38.3 2.3 collective-permute-start.7
  38.3 2.3 collective-permute-start.8
  38.8 16.2 %collective-permute-start.12 = (bf16[640,256]{1,0:T(8,128)(2,1)S(1)}, bf16[640,256]{1,0:T(8,128)(2,1)S(1)}, u32[]{:S(2)}, u32[]{:S(2)}) collective-permute-start(bf16[640,256]{1,0:T(8,128)(2,1)S(1)} %copy-done.10), channel_id=1, source_target_pairs={{0,16},{8,24},{16,0},{24,8},{1,17},{9,25},{17,1},{25,9},{2,18},{10... | collective-permute-start | bytes 983048 | tf_op jit(solution)/shard_map/ppermute | solution.py:37
  52.0 5.4 %collective-permute-start.10 = (bf16[240,960]{1,0:T(8,128)(2,1)S(1)}, bf16[240,960]{1,0:T(8,128)(2,1)S(1)}, u32[]{:S(2)}, u32[]{:S(2)}) collective-permute-start(bf16[240,960]{1,0:T(8,128)(2,1)S(1)} %copy-done.23), channel_id=1, source_target_pairs={{0,8},{8,0},{16,24},{24,16},{1,9},{9,1},{17,25},{25,17},{2,10},{10... | collective-permute-start | bytes 1382408 | tf_op jit(solution)/shard_map/ppermute | solution.py:37
  52.0 5.4 %collective-permute-start.11 = (bf16[240,960]{1,0:T(8,128)(2,1)S(1)}, bf16[240,960]{1,0:T(8,128)(2,1)S(1)}, u32[]{:S(2)}, u32[]{:S(2)}) collective-permute-start(bf16[240,960]{1,0:T(8,128)(2,1)S(1)} %collective-permute-done.9.b2), channel_id=1, source_target_pairs={{0,8},{8,0},{16,24},{24,16},{1,9},{9,1},{17,25},{25,17},{2,10},{10... | collective-permute-start | bytes 1382408 | tf_op jit(solution)/shard_map/ppermute | solution.py:37
  54.9 2.4 collective-permute-start.13
  54.9 2.4 collective-permute-start.14
  55.6 35.2 %copy-start.52 = (bf16[960,256]{1,0:T(8,128)(2,1)}, bf16[960,256]{1,0:T(8,128)(2,1)S(1)}, u32[]{:S(2)}) copy-start(bf16[960,256]{1,0:T(8,128)(2,1)S(1)} %get-tuple-element.227.refs_4_) | copy-start | bytes 1474564
  55.6 18.1 %collective-permute-start.15 = (bf16[960,256]{1,0:T(8,128)(2,1)S(1)}, bf16[960,256]{1,0:T(8,128)(2,1)S(1)}, u32[]{:S(2)}, u32[]{:S(2)}) collective-permute-start(bf16[960,256]{1,0:T(8,128)(2,1)S(1)} %get-tuple-element.246.refs_0_), channel_id=1, source_target_pairs={{0,16},{8,24},{16,0},{24,8},{1,17},{9,25},{17,1},{25,9},{2,18},{10... | collective-permute-start | bytes 1474568 | tf_op jit(solution)/shard_map/ppermute | solution.py:37
  61.3 19.4 %collective-permute-start.17 = (bf16[960,256]{1,0:T(8,128)(2,1)}, bf16[960,256]{1,0:T(8,128)(2,1)S(1)}, u32[]{:S(2)}, u32[]{:S(2)}) collective-permute-start(bf16[960,256]{1,0:T(8,128)(2,1)} %get-tuple-element.254.x_a.refs_0_), channel_id=1, source_target_pairs={{0,16},{8,24},{16,0},{24,8},{1,17},{9,25},{17,1},{25,9},{2,18},{10... | collective-permute-start | bytes 1474568 | tf_op jit(solution)/shard_map/ppermute | solution.py:37
  73.7 6.9 %collective-permute-start.20 = (bf16[960,256]{1,0:T(8,128)(2,1)S(1)}, bf16[960,256]{1,0:T(8,128)(2,1)S(1)}, u32[]{:S(2)}, u32[]{:S(2)}) collective-permute-start(bf16[960,256]{1,0:T(8,128)(2,1)S(1)} %get-tuple-element.246.refs_0_), channel_id=1, source_target_pairs={{0,8},{8,0},{16,24},{24,16},{1,9},{9,1},{17,25},{25,17},{2,10},{10... | collective-permute-start | bytes 1474568 | tf_op jit(solution)/shard_map/ppermute | solution.py:37
  73.8 6.9 %collective-permute-start.21 = (bf16[960,256]{1,0:T(8,128)(2,1)S(1)}, bf16[960,256]{1,0:T(8,128)(2,1)S(1)}, u32[]{:S(2)}, u32[]{:S(2)}) collective-permute-start(bf16[960,256]{1,0:T(8,128)(2,1)S(1)} %collective-permute-done.15.refs_4_.refs_2_), channel_id=1, source_target_pairs={{0,8},{8,0},{16,24},{24,16},{1,9},{9,1},{17,25},{25,17},{2,10},{10... | collective-permute-start | bytes 1474568 | tf_op jit(solution)/shard_map/ppermute | solution.py:37
  74.3 16.5 %collective-permute-start.22 = (bf16[960,256]{1,0:T(8,128)(2,1)S(1)}, bf16[960,256]{1,0:T(8,128)(2,1)S(1)}, u32[]{:S(2)}, u32[]{:S(2)}) collective-permute-start(bf16[960,256]{1,0:T(8,128)(2,1)S(1)} %get-tuple-element.227.refs_4_), channel_id=1, source_target_pairs={{0,16},{8,24},{16,0},{24,8},{1,17},{9,25},{17,1},{25,9},{2,18},{10... | collective-permute-start | bytes 1474568 | tf_op jit(solution)/shard_map/ppermute | solution.py:37
  79.5 24.3 %collective-permute-start.16 = (bf16[960,256]{1,0:T(8,128)(2,1)}, bf16[960,256]{1,0:T(8,128)(2,1)S(1)}, u32[]{:S(2)}, u32[]{:S(2)}) collective-permute-start(bf16[960,256]{1,0:T(8,128)(2,1)} %get-tuple-element.232.x_b.refs_4_), channel_id=1, source_target_pairs={{0,16},{8,24},{16,0},{24,8},{1,17},{9,25},{17,1},{25,9},{2,18},{10... | collective-permute-start | bytes 1474568 | tf_op jit(solution)/shard_map/ppermute | solution.py:37
  80.7 10.6 %collective-permute-start.18 = (bf16[960,256]{1,0:T(8,128)(2,1)S(1)}, bf16[960,256]{1,0:T(8,128)(2,1)S(1)}, u32[]{:S(2)}, u32[]{:S(2)}) collective-permute-start(bf16[960,256]{1,0:T(8,128)(2,1)S(1)} %copy-done.63), channel_id=1, source_target_pairs={{0,8},{8,0},{16,24},{24,16},{1,9},{9,1},{17,25},{25,17},{2,10},{10... | collective-permute-start | bytes 1474568 | tf_op jit(solution)/shard_map/ppermute | solution.py:37
  80.8 10.6 %collective-permute-start.19 = (bf16[960,256]{1,0:T(8,128)(2,1)S(1)}, bf16[960,256]{1,0:T(8,128)(2,1)S(1)}, u32[]{:S(2)}, u32[]{:S(2)}) collective-permute-start(bf16[960,256]{1,0:T(8,128)(2,1)S(1)} %collective-permute-done.17.refs_1_.refs_2_), channel_id=1, source_target_pairs={{0,8},{8,0},{16,24},{24,16},{1,9},{9,1},{17,25},{25,17},{2,10},{10... | collective-permute-start | bytes 1474568 | tf_op jit(solution)/shard_map/ppermute | solution.py:37
  90.8 13.6 %collective-permute-start.25 = (bf16[960,256]{1,0:T(8,128)(2,1)S(1)}, bf16[960,256]{1,0:T(8,128)(2,1)S(1)}, u32[]{:S(2)}, u32[]{:S(2)}) collective-permute-start(bf16[960,256]{1,0:T(8,128)(2,1)S(1)} %get-tuple-element.227.refs_4_), channel_id=1, source_target_pairs={{0,8},{8,0},{16,24},{24,16},{1,9},{9,1},{17,25},{25,17},{2,10},{10... | collective-permute-start | bytes 1474568 | tf_op jit(solution)/shard_map/ppermute | solution.py:37
  90.8 13.6 %collective-permute-start.26 = (bf16[960,256]{1,0:T(8,128)(2,1)S(1)}, bf16[960,256]{1,0:T(8,128)(2,1)S(1)}, u32[]{:S(2)}, u32[]{:S(2)}) collective-permute-start(bf16[960,256]{1,0:T(8,128)(2,1)S(1)} %collective-permute-done.22.refs_4_.refs_6_), channel_id=1, source_target_pairs={{0,8},{8,0},{16,24},{24,16},{1,9},{9,1},{17,25},{25,17},{2,10},{10... | collective-permute-start | bytes 1474568 | tf_op jit(solution)/shard_map/ppermute | solution.py:37
  103.8 1.9 collective-permute-start.23
  104.0 3.2 %collective-permute-start.24 = (bf16[960,256]{1,0:T(8,128)(2,1)S(1)}, bf16[960,256]{1,0:T(8,128)(2,1)S(1)}, u32[]{:S(2)}, u32[]{:S(2)}) collective-permute-start(bf16[960,256]{1,0:T(8,128)(2,1)S(1)} %collective-permute-done.16.refs_1_.refs_6_), channel_id=1, source_target_pairs={{0,8},{8,0},{16,24},{24,16},{1,9},{9,1},{17,25},{25,17},{2,10},{10... | collective-permute-start | bytes 1474568 | tf_op jit(solution)/shard_map/ppermute | solution.py:37
  104.4 15.7 %collective-permute-start.28 = (bf16[2,960,256]{2,1,0:T(8,128)(2,1)}, bf16[2,960,256]{2,1,0:T(8,128)(2,1)S(1)}, u32[]{:S(2)}, u32[]{:S(2)}) collective-permute-start(bf16[2,960,256]{2,1,0:T(8,128)(2,1)} %get-tuple-element.239), channel_id=1, source_target_pairs={{0,8},{8,0},{16,24},{24,16},{1,9},{9,1},{17,25},{25,17},{2,10},{10... | collective-permute-start | bytes 2949128 | tf_op jit(solution)/shard_map/ppermute | solution.py:37
  104.6 17.5 %collective-permute-start.29 = (bf16[2,960,256]{2,1,0:T(8,128)(2,1)}, bf16[2,960,256]{2,1,0:T(8,128)(2,1)S(1)}, u32[]{:S(2)}, u32[]{:S(2)}) collective-permute-start(bf16[2,960,256]{2,1,0:T(8,128)(2,1)} %get-tuple-element.243), channel_id=1, source_target_pairs={{0,8},{8,0},{16,24},{24,16},{1,9},{9,1},{17,25},{25,17},{2,10},{10... | collective-permute-start | bytes 2949128 | tf_op jit(solution)/shard_map/ppermute | solution.py:37
  119.5 12.7 %collective-permute-start.27 = (bf16[2,960,256]{2,1,0:T(8,128)(2,1)}, bf16[2,960,256]{2,1,0:T(8,128)(2,1)S(1)}, u32[]{:S(2)}, u32[]{:S(2)}) collective-permute-start(bf16[2,960,256]{2,1,0:T(8,128)(2,1)} %get-tuple-element.238), channel_id=1, source_target_pairs={{0,8},{8,0},{16,24},{24,16},{1,9},{9,1},{17,25},{25,17},{2,10},{10... | collective-permute-start | bytes 2949128 | tf_op jit(solution)/shard_map/ppermute | solution.py:37
  119.7 14.3 %collective-permute-start.30 = (bf16[2,960,256]{2,1,0:T(8,128)(2,1)}, bf16[2,960,256]{2,1,0:T(8,128)(2,1)S(1)}, u32[]{:S(2)}, u32[]{:S(2)}) collective-permute-start(bf16[2,960,256]{2,1,0:T(8,128)(2,1)} %get-tuple-element.253), channel_id=1, source_target_pairs={{0,8},{8,0},{16,24},{24,16},{1,9},{9,1},{17,25},{25,17},{2,10},{10... | collective-permute-start | bytes 2949128 | tf_op jit(solution)/shard_map/ppermute | solution.py:37
  120.3 27.6 %collective-permute-start.36 = (bf16[960,256]{1,0:T(8,128)(2,1)S(1)}, bf16[960,256]{1,0:T(8,128)(2,1)S(1)}, u32[]{:S(2)}, u32[]{:S(2)}) collective-permute-start(bf16[960,256]{1,0:T(8,128)(2,1)S(1)} %fusion.6), channel_id=1, source_target_pairs={{0,16},{8,24},{16,0},{24,8},{1,17},{9,25},{17,1},{25,9},{2,18},{10... | collective-permute-start | bytes 1474568 | tf_op jit(solution)/shard_map/ppermute | solution.py:37
  122.2 27.3 %collective-permute-start.37 = (bf16[960,256]{1,0:T(8,128)(2,1)S(1)}, bf16[960,256]{1,0:T(8,128)(2,1)S(1)}, u32[]{:S(2)}, u32[]{:S(2)}) collective-permute-start(bf16[960,256]{1,0:T(8,128)(2,1)S(1)} %fusion.5), channel_id=1, source_target_pairs={{0,16},{8,24},{16,0},{24,8},{1,17},{9,25},{17,1},{25,9},{2,18},{10... | collective-permute-start | bytes 1474568 | tf_op jit(solution)/shard_map/ppermute | solution.py:37
  130.5 16.0 %collective-permute-start.34 = (bf16[4,120,640]{2,1,0:T(8,128)(2,1)}, bf16[4,120,640]{2,1,0:T(8,128)(2,1)S(1)}, u32[]{:S(2)}, u32[]{:S(2)}) collective-permute-start(bf16[4,120,640]{2,1,0:T(8,128)(2,1)} %get-tuple-element.250), channel_id=1, source_target_pairs={{0,1},{1,0},{2,3},{3,2},{4,5},{5,4},{6,7},{7,6},{8,9},{9,8},{10,11... | collective-permute-start | bytes 1843208 | tf_op jit(solution)/shard_map/ppermute | solution.py:37
  132.4 25.9 %collective-permute-start.32 = (bf16[960,256]{1,0:T(8,128)(2,1)S(1)}, bf16[960,256]{1,0:T(8,128)(2,1)S(1)}, u32[]{:S(2)}, u32[]{:S(2)}) collective-permute-start(bf16[960,256]{1,0:T(8,128)(2,1)S(1)} %fusion.4), channel_id=1, source_target_pairs={{0,16},{8,24},{16,0},{24,8},{1,17},{9,25},{17,1},{25,9},{2,18},{10... | collective-permute-start | bytes 1474568 | tf_op jit(solution)/shard_map/ppermute | solution.py:37
  145.7 30.1 %collective-permute-start.31 = (bf16[4,120,1280]{2,1,0:T(8,128)(2,1)}, bf16[4,120,1280]{2,1,0:T(8,128)(2,1)S(1)}, u32[]{:S(2)}, u32[]{:S(2)}) collective-permute-start(bf16[4,120,1280]{2,1,0:T(8,128)(2,1)} %get-tuple-element.262), channel_id=1, source_target_pairs={{0,1},{1,0},{2,3},{3,2},{4,5},{5,4},{6,7},{7,6},{8,9},{9,8},{10,11... | collective-permute-start | bytes 3686408 | tf_op jit(solution)/shard_map/ppermute | solution.py:37
  146.5 24.0 %collective-permute-start.33 = (bf16[960,256]{1,0:T(8,128)(2,1)S(1)}, bf16[960,256]{1,0:T(8,128)(2,1)S(1)}, u32[]{:S(2)}, u32[]{:S(2)}) collective-permute-start(bf16[960,256]{1,0:T(8,128)(2,1)S(1)} %fusion.3), channel_id=1, source_target_pairs={{0,16},{8,24},{16,0},{24,8},{1,17},{9,25},{17,1},{25,9},{2,18},{10... | collective-permute-start | bytes 1474568 | tf_op jit(solution)/shard_map/ppermute | solution.py:37
  147.9 7.6 %collective-permute-start.35 = (bf16[2,120,640]{2,1,0:T(8,128)(2,1)S(1)}, bf16[2,120,640]{2,1,0:T(8,128)(2,1)S(1)}, u32[]{:S(2)}, u32[]{:S(2)}) collective-permute-start(bf16[2,120,640]{2,1,0:T(8,128)(2,1)S(1)} %add_convert_fusion.3), channel_id=1, source_target_pairs={{0,2},{1,3},{2,0},{3,1},{4,6},{5,7},{6,4},{7,5},{8,10},{9,11},{10,... | collective-permute-start | bytes 921608 | tf_op jit(solution)/shard_map/ppermute | solution.py:37
  155.6 14.4 %collective-permute-start.38 = (bf16[1,120,640]{2,1,0:T(8,128)(2,1)S(1)}, bf16[1,120,640]{2,1,0:T(8,128)(2,1)S(1)}, u32[]{:S(2)}, u32[]{:S(2)}) collective-permute-start(bf16[1,120,640]{2,1,0:T(8,128)(2,1)S(1)} %add_convert_fusion.9), channel_id=1, source_target_pairs={{0,4},{1,5},{2,6},{3,7},{4,0},{5,1},{6,2},{7,3},{8,12},{9,13},{10,... | collective-permute-start | bytes 460808 | tf_op jit(solution)/shard_map/ppermute | solution.py:37
  169.9 4.6 %collective-permute-start.40 = (bf16[2,640,256]{2,1,0:T(8,128)(2,1)}, bf16[2,640,256]{2,1,0:T(8,128)(2,1)S(1)}, u32[]{:S(2)}, u32[]{:S(2)}) collective-permute-start(bf16[2,640,256]{2,1,0:T(8,128)(2,1)} %get-tuple-element.287), channel_id=1, source_target_pairs={{0,8},{8,0},{16,24},{24,16},{1,9},{9,1},{17,25},{25,17},{2,10},{10... | collective-permute-start | bytes 1966088 | tf_op jit(solution)/shard_map/ppermute | solution.py:37
  170.1 19.5 %collective-permute-start.41 = (bf16[1,120,640]{2,1,0:T(8,128)(2,1)S(1)}, bf16[1,120,640]{2,1,0:T(8,128)(2,1)S(1)}, u32[]{:S(2)}, u32[]{:S(2)}) collective-permute-start(bf16[1,120,640]{2,1,0:T(8,128)(2,1)S(1)} %add_convert_fusion.8), channel_id=1, source_target_pairs={{0,4},{1,5},{2,6},{3,7},{4,0},{5,1},{6,2},{7,3},{8,12},{9,13},{10,... | collective-permute-start | bytes 460808 | tf_op jit(solution)/shard_map/ppermute | solution.py:37
  174.6 15.1 %collective-permute-start.42 = (bf16[640,256]{1,0:T(8,128)(2,1)S(1)}, bf16[640,256]{1,0:T(8,128)(2,1)S(1)}, u32[]{:S(2)}, u32[]{:S(2)}) collective-permute-start(bf16[640,256]{1,0:T(8,128)(2,1)S(1)} %fusion.13), channel_id=1, source_target_pairs={{0,16},{8,24},{16,0},{24,8},{1,17},{9,25},{17,1},{25,9},{2,18},{10... | collective-permute-start | bytes 983048 | tf_op jit(solution)/shard_map/ppermute | solution.py:37
  176.0 20.3 %collective-permute-start.39 = (bf16[2,120,1280]{2,1,0:T(8,128)(2,1)S(1)}, bf16[2,120,1280]{2,1,0:T(8,128)(2,1)S(1)}, u32[]{:S(2)}, u32[]{:S(2)}) collective-permute-start(bf16[2,120,1280]{2,1,0:T(8,128)(2,1)S(1)} %add_convert_fusion), channel_id=1, source_target_pairs={{0,2},{1,3},{2,0},{3,1},{4,6},{5,7},{6,4},{7,5},{8,10},{9,11},{10,... | collective-permute-start | bytes 1843208 | tf_op jit(solution)/shard_map/ppermute | solution.py:37
  189.6 6.8 %collective-permute-start.44 = (bf16[2,640,256]{2,1,0:T(8,128)(2,1)}, bf16[2,640,256]{2,1,0:T(8,128)(2,1)S(1)}, u32[]{:S(2)}, u32[]{:S(2)}) collective-permute-start(bf16[2,640,256]{2,1,0:T(8,128)(2,1)} %get-tuple-element.302), channel_id=1, source_target_pairs={{0,8},{8,0},{16,24},{24,16},{1,9},{9,1},{17,25},{25,17},{2,10},{10... | collective-permute-start | bytes 1966088 | tf_op jit(solution)/shard_map/ppermute | solution.py:37
  196.6 8.6 %collective-permute-start.45 = (bf16[2,8,32,1920]{3,2,1,0:T(8,128)(2,1)}, bf16[2,8,32,1920]{3,2,1,0:T(8,128)(2,1)S(1)}, u32[]{:S(2)}, u32[]{:S(2)}) collective-permute-start(bf16[2,8,32,1920]{3,2,1,0:T(8,128)(2,1)} %get-tuple-element.305), channel_id=1, source_target_pairs={{0,8},{8,0},{16,24},{24,16},{1,9},{9,1},{17,25},{25,17},{2,10},{10... | collective-permute-start | bytes 5898248 | tf_op jit(solution)/shard_map/ppermute | solution.py:37
  197.1 20.5 %collective-permute-start.47 = (bf16[2,120,640]{2,1,0:T(8,128)(2,1)S(1)}, bf16[2,120,640]{2,1,0:T(8,128)(2,1)S(1)}, u32[]{:S(2)}, u32[]{:S(2)}) collective-permute-start(bf16[2,120,640]{2,1,0:T(8,128)(2,1)S(1)} %pad_maximum_fusion.7), channel_id=1, source_target_pairs={{0,2},{1,3},{2,0},{3,1},{4,6},{5,7},{6,4},{7,5},{8,10},{9,11},{10,... | collective-permute-start | bytes 921608 | tf_op jit(solution)/shard_map/ppermute | solution.py:37
  197.6 20.0 %collective-permute-start.43 = (bf16[1,120,1280]{2,1,0:T(8,128)(2,1)S(1)}, bf16[1,120,1280]{2,1,0:T(8,128)(2,1)S(1)}, u32[]{:S(2)}, u32[]{:S(2)}) collective-permute-start(bf16[1,120,1280]{2,1,0:T(8,128)(2,1)S(1)} %add_convert_fusion.2), channel_id=1, source_target_pairs={{0,4},{1,5},{2,6},{3,7},{4,0},{5,1},{6,2},{7,3},{8,12},{9,13},{10,... | collective-permute-start | bytes 921608 | tf_op jit(solution)/shard_map/ppermute | solution.py:37
  199.8 10.6 %collective-permute-start.46 = (bf16[640,256]{1,0:T(8,128)(2,1)S(1)}, bf16[640,256]{1,0:T(8,128)(2,1)S(1)}, u32[]{:S(2)}, u32[]{:S(2)}) collective-permute-start(bf16[640,256]{1,0:T(8,128)(2,1)S(1)} %fusion.12), channel_id=1, source_target_pairs={{0,16},{8,24},{16,0},{24,8},{1,17},{9,25},{17,1},{25,9},{2,18},{10... | collective-permute-start | bytes 983048 | tf_op jit(solution)/shard_map/ppermute | solution.py:37
  205.5 26.0 %collective-permute-start.48 = (bf16[8,32,1920]{2,1,0:T(8,128)(2,1)S(1)}, bf16[8,32,1920]{2,1,0:T(8,128)(2,1)S(1)}, u32[]{:S(2)}, u32[]{:S(2)}) collective-permute-start(bf16[8,32,1920]{2,1,0:T(8,128)(2,1)S(1)} %fusion), channel_id=1, source_target_pairs={{0,16},{8,24},{16,0},{24,8},{1,17},{9,25},{17,1},{25,9},{2,18},{10... | collective-permute-start | bytes 2949128 | tf_op jit(solution)/shard_map/ppermute | solution.py:37
  217.6 2.6 collective-permute-start.49
  217.8 21.2 %collective-permute-start.56 = (bf16[1,120,1280]{2,1,0:T(8,128)(2,1)S(1)}, bf16[1,120,1280]{2,1,0:T(8,128)(2,1)S(1)}, u32[]{:S(2)}, u32[]{:S(2)}) collective-permute-start(bf16[1,120,1280]{2,1,0:T(8,128)(2,1)S(1)} %add_convert_fusion.1), channel_id=1, source_target_pairs={{0,4},{1,5},{2,6},{3,7},{4,0},{5,1},{6,2},{7,3},{8,12},{9,13},{10,... | collective-permute-start | bytes 921608 | tf_op jit(solution)/shard_map/ppermute | solution.py:37
  218.6 22.1 %collective-permute-start.52 = (bf16[4,120,640]{2,1,0:T(8,128)(2,1)S(1)}, bf16[4,120,640]{2,1,0:T(8,128)(2,1)S(1)}, u32[]{:S(2)}, u32[]{:S(2)}) collective-permute-start(bf16[4,120,640]{2,1,0:T(8,128)(2,1)S(1)} %pad_maximum_fusion.4.even), channel_id=1, source_target_pairs={{0,1},{1,0},{2,3},{3,2},{4,5},{5,4},{6,7},{7,6},{8,9},{9,8},{10,11... | collective-permute-start | bytes 1843208 | tf_op jit(solution)/shard_map/ppermute | solution.py:37
  220.3 16.7 %collective-permute-start.50 = (bf16[8,32,640]{2,1,0:T(8,128)(2,1)S(1)}, bf16[8,32,640]{2,1,0:T(8,128)(2,1)S(1)}, u32[]{:S(2)}, u32[]{:S(2)}) collective-permute-start(bf16[8,32,640]{2,1,0:T(8,128)(2,1)S(1)} %fusion.11), channel_id=1, source_target_pairs={{0,16},{8,24},{16,0},{24,8},{1,17},{9,25},{17,1},{25,9},{2,18},{10... | collective-permute-start | bytes 983048 | tf_op jit(solution)/shard_map/ppermute | solution.py:37
  237.2 15.5 %collective-permute-start.51 = (bf16[4,32,2560]{2,1,0:T(8,128)(2,1)S(1)}, bf16[4,32,2560]{2,1,0:T(8,128)(2,1)S(1)}, u32[]{:S(2)}, u32[]{:S(2)}) collective-permute-start(bf16[4,32,2560]{2,1,0:T(8,128)(2,1)S(1)} %pad_maximum_fusion.2), channel_id=1, source_target_pairs={{0,1},{1,0},{2,3},{3,2},{4,5},{5,4},{6,7},{7,6},{8,9},{9,8},{10,11... | collective-permute-start | bytes 1966088 | tf_op jit(solution)/shard_map/ppermute | solution.py:37
  239.1 17.3 %collective-permute-start.57 = (bf16[2,120,1280]{2,1,0:T(8,128)(2,1)S(1)}, bf16[2,120,1280]{2,1,0:T(8,128)(2,1)S(1)}, u32[]{:S(2)}, u32[]{:S(2)}) collective-permute-start(bf16[2,120,1280]{2,1,0:T(8,128)(2,1)S(1)} %pad_maximum_fusion.5), channel_id=1, source_target_pairs={{0,2},{1,3},{2,0},{3,1},{4,6},{5,7},{6,4},{7,5},{8,10},{9,11},{10,... | collective-permute-start | bytes 1843208 | tf_op jit(solution)/shard_map/ppermute | solution.py:37
  252.8 8.7 %collective-permute-start.54 = (bf16[1,32,2560]{2,1,0:T(8,128)(2,1)S(1)}, bf16[1,32,2560]{2,1,0:T(8,128)(2,1)S(1)}, u32[]{:S(2)}, u32[]{:S(2)}) collective-permute-start(bf16[1,32,2560]{2,1,0:T(8,128)(2,1)S(1)} %get-tuple-element.347), channel_id=1, source_target_pairs={{0,2},{1,3},{2,0},{3,1},{4,6},{5,7},{6,4},{7,5},{8,10},{9,11},{10,... | collective-permute-start | bytes 491528 | tf_op jit(solution)/shard_map/ppermute | solution.py:37
  254.2 8.8 %collective-permute-start.53 = (bf16[1,32,2560]{2,1,0:T(8,128)(2,1)S(1)}, bf16[1,32,2560]{2,1,0:T(8,128)(2,1)S(1)}, u32[]{:S(2)}, u32[]{:S(2)}) collective-permute-start(bf16[1,32,2560]{2,1,0:T(8,128)(2,1)S(1)} %get-tuple-element.348), channel_id=1, source_target_pairs={{0,6},{1,7},{2,4},{3,5},{4,2},{5,3},{6,0},{7,1},{8,14},{9,15},{10,... | collective-permute-start | bytes 491528 | tf_op jit(solution)/shard_map/ppermute | solution.py:37
  254.8 13.9 %collective-permute-start.55 = (bf16[1,32,2560]{2,1,0:T(8,128)(2,1)S(1)}, bf16[1,32,2560]{2,1,0:T(8,128)(2,1)S(1)}, u32[]{:S(2)}, u32[]{:S(2)}) collective-permute-start(bf16[1,32,2560]{2,1,0:T(8,128)(2,1)S(1)} %get-tuple-element.353), channel_id=1, source_target_pairs={{0,4},{1,5},{2,6},{3,7},{4,0},{5,1},{6,2},{7,3},{8,12},{9,13},{10,... | collective-permute-start | bytes 491528 | tf_op jit(solution)/shard_map/ppermute | solution.py:37
  256.5 26.4 %collective-permute-start.61 = (bf16[4,120,1280]{2,1,0:T(8,128)(2,1)S(1)}, bf16[4,120,1280]{2,1,0:T(8,128)(2,1)S(1)}, u32[]{:S(2)}, u32[]{:S(2)}) collective-permute-start(bf16[4,120,1280]{2,1,0:T(8,128)(2,1)S(1)} %pad_maximum_fusion.1.even), channel_id=1, source_target_pairs={{0,1},{1,0},{2,3},{3,2},{4,5},{5,4},{6,7},{7,6},{8,9},{9,8},{10,11... | collective-permute-start | bytes 3686408 | tf_op jit(solution)/shard_map/ppermute | solution.py:37
  268.8 9.0 %collective-permute-start.60 = (bf16[1,32,2560]{2,1,0:T(8,128)(2,1)S(1)}, bf16[1,32,2560]{2,1,0:T(8,128)(2,1)S(1)}, u32[]{:S(2)}, u32[]{:S(2)}) collective-permute-start(bf16[1,32,2560]{2,1,0:T(8,128)(2,1)S(1)} %add_convert_fusion.4), channel_id=1, source_target_pairs={{0,6},{1,7},{2,4},{3,5},{4,2},{5,3},{6,0},{7,1},{8,14},{9,15},{10,... | collective-permute-start | bytes 491528 | tf_op jit(solution)/shard_map/ppermute | solution.py:37
  271.9 7.5 %collective-permute-start.59 = (bf16[1,32,2560]{2,1,0:T(8,128)(2,1)S(1)}, bf16[1,32,2560]{2,1,0:T(8,128)(2,1)S(1)}, u32[]{:S(2)}, u32[]{:S(2)}) collective-permute-start(bf16[1,32,2560]{2,1,0:T(8,128)(2,1)S(1)} %add_convert_fusion.4), channel_id=1, source_target_pairs={{0,2},{1,3},{2,0},{3,1},{4,6},{5,7},{6,4},{7,5},{8,10},{9,11},{10,... | collective-permute-start | bytes 491528 | tf_op jit(solution)/shard_map/ppermute | solution.py:37
  271.9 11.0 %collective-permute-start.58 = (bf16[1,32,2560]{2,1,0:T(8,128)(2,1)S(1)}, bf16[1,32,2560]{2,1,0:T(8,128)(2,1)S(1)}, u32[]{:S(2)}, u32[]{:S(2)}) collective-permute-start(bf16[1,32,2560]{2,1,0:T(8,128)(2,1)S(1)} %add_convert_fusion.4), channel_id=1, source_target_pairs={{0,4},{1,5},{2,6},{3,7},{4,0},{5,1},{6,2},{7,3},{8,12},{9,13},{10,... | collective-permute-start | bytes 491528 | tf_op jit(solution)/shard_map/ppermute | solution.py:37
  283.0 14.0 %collective-permute-start.62 = (bf16[4,32,2560]{2,1,0:T(8,128)(2,1)S(1)}, bf16[4,32,2560]{2,1,0:T(8,128)(2,1)S(1)}, u32[]{:S(2)}, u32[]{:S(2)}) collective-permute-start(bf16[4,32,2560]{2,1,0:T(8,128)(2,1)S(1)} %pad_maximum_fusion.3.even), channel_id=1, source_target_pairs={{0,1},{1,0},{2,3},{3,2},{4,5},{5,4},{6,7},{7,6},{8,9},{9,8},{10,11... | collective-permute-start | bytes 1966088 | tf_op jit(solution)/shard_map/ppermute | solution.py:37
  (72 other events, 688.1 us)
